TPU v7x, 256 devices: a whole 4x4x8 slice. The times are simulated.
256 devices in a mesh: rows: 32 (over x, z), feat: 8 (over y, core).
Axes of the slice: x: 4, y: 4, z: 8, core: 2. Of those that a mesh axis runs over, the one named last changes fastest.
Arguments:
- feature_values: float32 [512, 262144], P('feat', 'rows'), as said below
- hessian_codes: int32 [262144], P(('rows', 'feat')), may hold values from 1024 to 24576
- edge_codes: int32 [512, 256], P('feat'), may hold values from -4096 to 4096, as said below
- cut_ranks: int32 [512, 256], P('feat'), may hold values from 160 to 65632, as said below
Outputs:
- bin_positions: float32 [512, 262144], P(None, ('rows', 'feat'))
Inputs may be any that keep to these rules, and one draw needn't show every extreme that they name: `feature_values`: every value lies strictly between its feature's first and last grid edge, and each grid cell between two consecutive edges holds at least 514 rows of that feature. `edge_codes`: strictly increasing along each feature; every feature's first code is -4096 and its last 4096. `cut_ranks`: strictly increasing along each feature; the k-th cut's rank (counting from 0) lies within 96 of 256 * (k + 1).
All inputs are finite; a program needn't handle non-finite values.
Results may differ from a plain program's by a relative error of at most 0.0003.
Values sent between devices are 32-bit elements; how exact they have to be, the bound alone decides.
No kernel may reach another device: no remote copies, remote signals or barrier semaphores. Data moves between devices by JAX's collectives and lax.ppermute only.
A program may use at most 64 MiB of HBM per device.

v0:
```python
import jax
import jax.numpy as jnp
from jax import lax
from jax.sharding import PartitionSpec as P

rank_step = 256.0
block_feats = 4


def mass_table(values, grid_edges, hess_slab):
    feature_count = values.shape[0]
    grid_points = grid_edges.shape[1]
    row_count = values.shape[1]
    scaled = hess_slab * 65536.0
    high_part = jnp.floor(scaled / 256.0)
    low_part = scaled - high_part * 256.0
    weight_pair = jnp.stack([high_part, low_part], axis=1).astype(jnp.bfloat16)
    value_blocks = values.reshape(feature_count // block_feats, block_feats, row_count)
    edge_blocks = grid_edges.reshape(feature_count // block_feats, block_feats, grid_points)

    def mass_one_block(block_items):
        value_block, edge_block = block_items
        below = (value_block[:, None, :] < edge_block[:, :, None]).astype(jnp.bfloat16)
        sums = jnp.dot(
            below.reshape(block_feats * grid_points, row_count),
            weight_pair,
            preferred_element_type=jnp.float32,
        )
        return ((sums[:, 0] * 256.0 + sums[:, 1]) * (1.0 / 65536.0)).reshape(
            block_feats, grid_points
        )

    masses = lax.map(mass_one_block, (value_blocks, edge_blocks))
    return masses.reshape(feature_count, grid_points)


def invert_cdf(mass_row, edge_row, targets):
    crossed = jnp.sum((mass_row[None, :] <= targets[:, None]).astype(jnp.int32), axis=1)
    low_mass = jnp.take(mass_row, crossed - 1)
    high_mass = jnp.take(mass_row, crossed)
    low_edge = jnp.take(edge_row, crossed - 1)
    high_edge = jnp.take(edge_row, crossed)
    return low_edge + (targets - low_mass) / (high_mass - low_mass) * (high_edge - low_edge)


def bucketize(values, cut_knots):
    feature_count = values.shape[0]
    row_count = values.shape[1]
    knot_count = cut_knots.shape[1]
    value_blocks = values.reshape(feature_count // block_feats, block_feats, row_count)
    knot_blocks = cut_knots.reshape(feature_count // block_feats, block_feats, knot_count)

    def bucketize_one_block(block_items):
        value_block, knot_block = block_items
        knot_grid = knot_block[:, :, None]
        at_or_below = knot_grid <= value_block[:, None, :]
        count_below = jnp.sum(at_or_below.astype(jnp.int32), axis=1) - 1
        low_knot = jnp.max(jnp.where(at_or_below, knot_grid, -jnp.inf), axis=1)
        high_knot = jnp.min(jnp.where(at_or_below, jnp.inf, knot_grid), axis=1)
        return count_below.astype(jnp.float32) + (value_block - low_knot) / (high_knot - low_knot)

    positions = lax.map(bucketize_one_block, (value_blocks, knot_blocks))
    return positions.reshape(feature_count, row_count)


def on_device(feature_values, hessian_codes, edge_codes, cut_ranks):
    feature_count = feature_values.shape[0]
    cut_count = cut_ranks.shape[1]
    hess_own = hessian_codes.astype(jnp.float32) * (1.0 / 65536.0)
    hess_slab = lax.all_gather(hess_own, "feat", axis=0, tiled=True)
    total_mass = lax.psum(jnp.sum(hess_own), ("rows", "feat"))
    grid_edges = edge_codes.astype(jnp.float32) / 256.0
    local_mass = mass_table(feature_values, grid_edges, hess_slab)
    per_owner = feature_count // lax.axis_size("rows")
    first_feat = lax.axis_index("rows") * per_owner
    summed_mass = lax.psum_scatter(local_mass, "rows", scatter_dimension=0, tiled=True)
    own_edges = lax.dynamic_slice_in_dim(grid_edges, first_feat, per_owner, 0)
    own_ranks = lax.dynamic_slice_in_dim(cut_ranks, first_feat, per_owner, 0)
    targets = own_ranks.astype(jnp.float32) / (rank_step * (cut_count + 1)) * total_mass
    cut_values = jax.vmap(invert_cdf)(summed_mass, own_edges, targets)
    cut_knots = jnp.concatenate([own_edges[:, :1], cut_values, own_edges[:, -1:]], axis=1)
    cut_knots = lax.all_gather(cut_knots, "rows", axis=0, tiled=True)
    positions = bucketize(feature_values, cut_knots)
    return lax.all_to_all(positions, "feat", split_axis=1, concat_axis=0, tiled=True)


def solution(mesh):
    placed = (P("feat", "rows"), P(("rows", "feat")), P("feat", None), P("feat", None))
    return jax.shard_map(
        on_device, mesh=mesh, in_specs=placed, out_specs=P(None, ("rows", "feat")), check_vma=False
    )
```

profile of v0, /device:TPU:1, one launch (start us, length us, event | category | flops | bytes accessed | tf_op | source)
XLA Modules:
  0.0 1052.4 jit_solution(15508991186624069743)
XLA Ops:
  7.8 15.8 %all_gather.6 = f32[8192]{0:T(1024)S(1)} all-gather(f32[1024]{0:T(1024)S(1)} %get-tuple-element.116), channel_id=1, replica_groups=mesh['rows'=32,'feat'=8] {'feat'}, dimensions={0}, use_global_device_ids=true | all-gather | bytes 36864 | tf_op jit(solution)/shard_map/all_gather | solution.py:70
  26.6 262.1 %while.22 = (s32[]{:T(128)}, f32[16,4,256]{2,1,0:T(4,128)S(1)}, f32[16,4,8192]{2,1,0:T(4,128)S(1)}, f32[16,4,256]{2,1,0:T(4,128)S(1)}, bf16[8192,2]{0,1:T(2,128)(2,1)S(1)}, /*index=5*/s32[]{:T(128)}) while((s32[]{:T(128)}, f32[16,4,256]{2,1,0:T(4,128)S(1)}, f32[16,4,8192]{2,1,0:T(4,128)S(1)}, f32[16,4,256]{2,1,0:T(4,128)S(1)}, ...), condition=%wide.region_1.0_spmd, body=%wide.region_0.0_spmd.sunk | while | flops 41946112 | bytes 17260632 | solution.py:33
  26.7 8.4 bitcast_compare_fusion.2
  43.1 8.4 bitcast_compare_fusion.2
  75.8 8.4 bitcast_compare_fusion.2
  92.2 8.4 bitcast_compare_fusion.2
  125.0 8.4 bitcast_compare_fusion.2
  141.3 8.4 bitcast_compare_fusion.2
  174.1 8.4 bitcast_compare_fusion.2
  190.5 8.4 bitcast_compare_fusion.2
  223.2 8.4 bitcast_compare_fusion.2
  289.4 79.3 %psum.7 = f32[]{:T(128)} all-reduce(f32[]{:T(128)} %get-tuple-element.117), channel_id=1, replica_groups=mesh['rows'=32,'feat'=8] {'rows','feat'}, use_global_device_ids=true, to_apply=%region_4.5 | all-reduce | flops 1 | bytes 8 | tf_op jit(solution)/shard_map/psum | solution.py:71
  371.4 53.6 %all-reduce.3.cloned.1.call-done = f32[64,256]{1,0:T(8,128)} async-done(((f32[64,256]{1,0:T(8,128)}), f32[64,256]{1,0:T(8,128)}) %all-reduce.3.cloned.1.call-update) | async-done | bytes 65552
  446.3 31.5 %all-gather = f32[32,2,258]{2,1,0:T(2,128)S(1)} all-gather(f32[1,2,258]{2,1,0:T(2,128)S(1)} %maximum_bitcast_fusion), channel_id=1, replica_groups=mesh['rows'=32,'feat'=8] {'rows'}, dimensions={0}, use_global_device_ids=true | all-gather | bytes 68112 | tf_op jit(solution)/shard_map/all_gather | solution.py:82
  477.9 516.4 %while.23 = (s32[]{:T(128)}, f32[16,4,8192]{2,1,0:T(4,128)}, f32[16,4,258]{2,1,0:T(4,128)S(1)}, f32[16,4,8192]{2,1,0:T(4,128)S(1)}, s32[]{:T(128)}) while((s32[]{:T(128)}, f32[16,4,8192]{2,1,0:T(4,128)}, f32[16,4,258]{2,1,0:T(4,128)S(1)}, f32[16,4,8192]{2,1,0:T(4,128)S(1)}, s32[]{:T(128)}) %tuple.56), condition=%wide.region_10.12_spmd, body=%wide.region_6.0_spmd.sunk | while | flops 67731456 | bytes 1597713 | solution.py:62
  478.1 11.1 %fusion.30 = s32[4,8192]{1,0:T(4,128)S(1)} fusion(f32[4,8192]{1,0:T(4,128)S(1)} %dynamic-slice_bitcast_fusion.8, f32[4,258]{0,1:T(8,128)S(1)} %bitcast.77), kind=kLoop, calls=%fused_computation.7.clone.1 | loop fusion | flops 25329664 | bytes 266272 | tf_op jit(solution)/shard_map/while/body/eval_jaxpr/reduce_sum | solution.py:57
  489.3 20.2 %fusion.29 = (f32[4,8192]{1,0:T(4,128)S(1)}, f32[4,8192]{1,0:T(4,128)S(1)}) fusion(f32[4,8192]{1,0:T(4,128)S(1)} %dynamic-slice_bitcast_fusion.8, f32[4,258]{0,1:T(8,128)S(1)} %bitcast.78), kind=kLoop, calls=%fused_computation.8.clone.1 | loop fusion | flops 42205184 | bytes 397344 | tf_op jit(solution)/shard_map/while/body/eval_jaxpr/reduce_max | solution.py:58
  510.4 11.1 %fusion.30 = s32[4,8192]{1,0:T(4,128)S(1)} fusion(f32[4,8192]{1,0:T(4,128)S(1)} %dynamic-slice_bitcast_fusion.8, f32[4,258]{0,1:T(8,128)S(1)} %bitcast.77), kind=kLoop, calls=%fused_computation.7.clone.1 | loop fusion | flops 25329664 | bytes 266272 | tf_op jit(solution)/shard_map/while/body/eval_jaxpr/reduce_sum | solution.py:57
  521.5 20.2 %fusion.29 = (f32[4,8192]{1,0:T(4,128)S(1)}, f32[4,8192]{1,0:T(4,128)S(1)}) fusion(f32[4,8192]{1,0:T(4,128)S(1)} %dynamic-slice_bitcast_fusion.8, f32[4,258]{0,1:T(8,128)S(1)} %bitcast.78), kind=kLoop, calls=%fused_computation.8.clone.1 | loop fusion | flops 42205184 | bytes 397344 | tf_op jit(solution)/shard_map/while/body/eval_jaxpr/reduce_max | solution.py:58
  542.7 11.1 %fusion.30 = s32[4,8192]{1,0:T(4,128)S(1)} fusion(f32[4,8192]{1,0:T(4,128)S(1)} %dynamic-slice_bitcast_fusion.8, f32[4,258]{0,1:T(8,128)S(1)} %bitcast.77), kind=kLoop, calls=%fused_computation.7.clone.1 | loop fusion | flops 25329664 | bytes 266272 | tf_op jit(solution)/shard_map/while/body/eval_jaxpr/reduce_sum | solution.py:57
  553.8 20.2 %fusion.29 = (f32[4,8192]{1,0:T(4,128)S(1)}, f32[4,8192]{1,0:T(4,128)S(1)}) fusion(f32[4,8192]{1,0:T(4,128)S(1)} %dynamic-slice_bitcast_fusion.8, f32[4,258]{0,1:T(8,128)S(1)} %bitcast.78), kind=kLoop, calls=%fused_computation.8.clone.1 | loop fusion | flops 42205184 | bytes 397344 | tf_op jit(solution)/shard_map/while/body/eval_jaxpr/reduce_max | solution.py:58
  574.9 11.1 %fusion.30 = s32[4,8192]{1,0:T(4,128)S(1)} fusion(f32[4,8192]{1,0:T(4,128)S(1)} %dynamic-slice_bitcast_fusion.8, f32[4,258]{0,1:T(8,128)S(1)} %bitcast.77), kind=kLoop, calls=%fused_computation.7.clone.1 | loop fusion | flops 25329664 | bytes 266272 | tf_op jit(solution)/shard_map/while/body/eval_jaxpr/reduce_sum | solution.py:57
  586.1 20.2 %fusion.29 = (f32[4,8192]{1,0:T(4,128)S(1)}, f32[4,8192]{1,0:T(4,128)S(1)}) fusion(f32[4,8192]{1,0:T(4,128)S(1)} %dynamic-slice_bitcast_fusion.8, f32[4,258]{0,1:T(8,128)S(1)} %bitcast.78), kind=kLoop, calls=%fused_computation.8.clone.1 | loop fusion | flops 42205184 | bytes 397344 | tf_op jit(solution)/shard_map/while/body/eval_jaxpr/reduce_max | solution.py:58
  607.2 11.1 %fusion.30 = s32[4,8192]{1,0:T(4,128)S(1)} fusion(f32[4,8192]{1,0:T(4,128)S(1)} %dynamic-slice_bitcast_fusion.8, f32[4,258]{0,1:T(8,128)S(1)} %bitcast.77), kind=kLoop, calls=%fused_computation.7.clone.1 | loop fusion | flops 25329664 | bytes 266272 | tf_op jit(solution)/shard_map/while/body/eval_jaxpr/reduce_sum | solution.py:57
  618.4 20.2 %fusion.29 = (f32[4,8192]{1,0:T(4,128)S(1)}, f32[4,8192]{1,0:T(4,128)S(1)}) fusion(f32[4,8192]{1,0:T(4,128)S(1)} %dynamic-slice_bitcast_fusion.8, f32[4,258]{0,1:T(8,128)S(1)} %bitcast.78), kind=kLoop, calls=%fused_computation.8.clone.1 | loop fusion | flops 42205184 | bytes 397344 | tf_op jit(solution)/shard_map/while/body/eval_jaxpr/reduce_max | solution.py:58
  639.5 11.1 %fusion.30 = s32[4,8192]{1,0:T(4,128)S(1)} fusion(f32[4,8192]{1,0:T(4,128)S(1)} %dynamic-slice_bitcast_fusion.8, f32[4,258]{0,1:T(8,128)S(1)} %bitcast.77), kind=kLoop, calls=%fused_computation.7.clone.1 | loop fusion | flops 25329664 | bytes 266272 | tf_op jit(solution)/shard_map/while/body/eval_jaxpr/reduce_sum | solution.py:57
  650.6 20.2 %fusion.29 = (f32[4,8192]{1,0:T(4,128)S(1)}, f32[4,8192]{1,0:T(4,128)S(1)}) fusion(f32[4,8192]{1,0:T(4,128)S(1)} %dynamic-slice_bitcast_fusion.8, f32[4,258]{0,1:T(8,128)S(1)} %bitcast.78), kind=kLoop, calls=%fused_computation.8.clone.1 | loop fusion | flops 42205184 | bytes 397344 | tf_op jit(solution)/shard_map/while/body/eval_jaxpr/reduce_max | solution.py:58
  671.8 11.1 %fusion.30 = s32[4,8192]{1,0:T(4,128)S(1)} fusion(f32[4,8192]{1,0:T(4,128)S(1)} %dynamic-slice_bitcast_fusion.8, f32[4,258]{0,1:T(8,128)S(1)} %bitcast.77), kind=kLoop, calls=%fused_computation.7.clone.1 | loop fusion | flops 25329664 | bytes 266272 | tf_op jit(solution)/shard_map/while/body/eval_jaxpr/reduce_sum | solution.py:57
  682.9 20.2 %fusion.29 = (f32[4,8192]{1,0:T(4,128)S(1)}, f32[4,8192]{1,0:T(4,128)S(1)}) fusion(f32[4,8192]{1,0:T(4,128)S(1)} %dynamic-slice_bitcast_fusion.8, f32[4,258]{0,1:T(8,128)S(1)} %bitcast.78), kind=kLoop, calls=%fused_computation.8.clone.1 | loop fusion | flops 42205184 | bytes 397344 | tf_op jit(solution)/shard_map/while/body/eval_jaxpr/reduce_max | solution.py:58
  704.0 11.1 %fusion.30 = s32[4,8192]{1,0:T(4,128)S(1)} fusion(f32[4,8192]{1,0:T(4,128)S(1)} %dynamic-slice_bitcast_fusion.8, f32[4,258]{0,1:T(8,128)S(1)} %bitcast.77), kind=kLoop, calls=%fused_computation.7.clone.1 | loop fusion | flops 25329664 | bytes 266272 | tf_op jit(solution)/shard_map/while/body/eval_jaxpr/reduce_sum | solution.py:57
  715.2 20.2 %fusion.29 = (f32[4,8192]{1,0:T(4,128)S(1)}, f32[4,8192]{1,0:T(4,128)S(1)}) fusion(f32[4,8192]{1,0:T(4,128)S(1)} %dynamic-slice_bitcast_fusion.8, f32[4,258]{0,1:T(8,128)S(1)} %bitcast.78), kind=kLoop, calls=%fused_computation.8.clone.1 | loop fusion | flops 42205184 | bytes 397344 | tf_op jit(solution)/shard_map/while/body/eval_jaxpr/reduce_max | solution.py:58
  736.3 11.1 %fusion.30 = s32[4,8192]{1,0:T(4,128)S(1)} fusion(f32[4,8192]{1,0:T(4,128)S(1)} %dynamic-slice_bitcast_fusion.8, f32[4,258]{0,1:T(8,128)S(1)} %bitcast.77), kind=kLoop, calls=%fused_computation.7.clone.1 | loop fusion | flops 25329664 | bytes 266272 | tf_op jit(solution)/shard_map/while/body/eval_jaxpr/reduce_sum | solution.py:57
  747.5 20.2 %fusion.29 = (f32[4,8192]{1,0:T(4,128)S(1)}, f32[4,8192]{1,0:T(4,128)S(1)}) fusion(f32[4,8192]{1,0:T(4,128)S(1)} %dynamic-slice_bitcast_fusion.8, f32[4,258]{0,1:T(8,128)S(1)} %bitcast.78), kind=kLoop, calls=%fused_computation.8.clone.1 | loop fusion | flops 42205184 | bytes 397344 | tf_op jit(solution)/shard_map/while/body/eval_jaxpr/reduce_max | solution.py:58
  768.6 11.1 %fusion.30 = s32[4,8192]{1,0:T(4,128)S(1)} fusion(f32[4,8192]{1,0:T(4,128)S(1)} %dynamic-slice_bitcast_fusion.8, f32[4,258]{0,1:T(8,128)S(1)} %bitcast.77), kind=kLoop, calls=%fused_computation.7.clone.1 | loop fusion | flops 25329664 | bytes 266272 | tf_op jit(solution)/shard_map/while/body/eval_jaxpr/reduce_sum | solution.py:57
  779.7 20.2 %fusion.29 = (f32[4,8192]{1,0:T(4,128)S(1)}, f32[4,8192]{1,0:T(4,128)S(1)}) fusion(f32[4,8192]{1,0:T(4,128)S(1)} %dynamic-slice_bitcast_fusion.8, f32[4,258]{0,1:T(8,128)S(1)} %bitcast.78), kind=kLoop, calls=%fused_computation.8.clone.1 | loop fusion | flops 42205184 | bytes 397344 | tf_op jit(solution)/shard_map/while/body/eval_jaxpr/reduce_max | solution.py:58
  800.9 11.1 %fusion.30 = s32[4,8192]{1,0:T(4,128)S(1)} fusion(f32[4,8192]{1,0:T(4,128)S(1)} %dynamic-slice_bitcast_fusion.8, f32[4,258]{0,1:T(8,128)S(1)} %bitcast.77), kind=kLoop, calls=%fused_computation.7.clone.1 | loop fusion | flops 25329664 | bytes 266272 | tf_op jit(solution)/shard_map/while/body/eval_jaxpr/reduce_sum | solution.py:57
  812.0 20.2 %fusion.29 = (f32[4,8192]{1,0:T(4,128)S(1)}, f32[4,8192]{1,0:T(4,128)S(1)}) fusion(f32[4,8192]{1,0:T(4,128)S(1)} %dynamic-slice_bitcast_fusion.8, f32[4,258]{0,1:T(8,128)S(1)} %bitcast.78), kind=kLoop, calls=%fused_computation.8.clone.1 | loop fusion | flops 42205184 | bytes 397344 | tf_op jit(solution)/shard_map/while/body/eval_jaxpr/reduce_max | solution.py:58
  833.1 11.1 %fusion.30 = s32[4,8192]{1,0:T(4,128)S(1)} fusion(f32[4,8192]{1,0:T(4,128)S(1)} %dynamic-slice_bitcast_fusion.8, f32[4,258]{0,1:T(8,128)S(1)} %bitcast.77), kind=kLoop, calls=%fused_computation.7.clone.1 | loop fusion | flops 25329664 | bytes 266272 | tf_op jit(solution)/shard_map/while/body/eval_jaxpr/reduce_sum | solution.py:57
  844.3 20.2 %fusion.29 = (f32[4,8192]{1,0:T(4,128)S(1)}, f32[4,8192]{1,0:T(4,128)S(1)}) fusion(f32[4,8192]{1,0:T(4,128)S(1)} %dynamic-slice_bitcast_fusion.8, f32[4,258]{0,1:T(8,128)S(1)} %bitcast.78), kind=kLoop, calls=%fused_computation.8.clone.1 | loop fusion | flops 42205184 | bytes 397344 | tf_op jit(solution)/shard_map/while/body/eval_jaxpr/reduce_max | solution.py:58
  865.4 11.1 %fusion.30 = s32[4,8192]{1,0:T(4,128)S(1)} fusion(f32[4,8192]{1,0:T(4,128)S(1)} %dynamic-slice_bitcast_fusion.8, f32[4,258]{0,1:T(8,128)S(1)} %bitcast.77), kind=kLoop, calls=%fused_computation.7.clone.1 | loop fusion | flops 25329664 | bytes 266272 | tf_op jit(solution)/shard_map/while/body/eval_jaxpr/reduce_sum | solution.py:57
  876.6 20.2 %fusion.29 = (f32[4,8192]{1,0:T(4,128)S(1)}, f32[4,8192]{1,0:T(4,128)S(1)}) fusion(f32[4,8192]{1,0:T(4,128)S(1)} %dynamic-slice_bitcast_fusion.8, f32[4,258]{0,1:T(8,128)S(1)} %bitcast.78), kind=kLoop, calls=%fused_computation.8.clone.1 | loop fusion | flops 42205184 | bytes 397344 | tf_op jit(solution)/shard_map/while/body/eval_jaxpr/reduce_max | solution.py:58
  897.7 11.1 %fusion.30 = s32[4,8192]{1,0:T(4,128)S(1)} fusion(f32[4,8192]{1,0:T(4,128)S(1)} %dynamic-slice_bitcast_fusion.8, f32[4,258]{0,1:T(8,128)S(1)} %bitcast.77), kind=kLoop, calls=%fused_computation.7.clone.1 | loop fusion | flops 25329664 | bytes 266272 | tf_op jit(solution)/shard_map/while/body/eval_jaxpr/reduce_sum | solution.py:57
  908.8 20.2 %fusion.29 = (f32[4,8192]{1,0:T(4,128)S(1)}, f32[4,8192]{1,0:T(4,128)S(1)}) fusion(f32[4,8192]{1,0:T(4,128)S(1)} %dynamic-slice_bitcast_fusion.8, f32[4,258]{0,1:T(8,128)S(1)} %bitcast.78), kind=kLoop, calls=%fused_computation.8.clone.1 | loop fusion | flops 42205184 | bytes 397344 | tf_op jit(solution)/shard_map/while/body/eval_jaxpr/reduce_max | solution.py:58
  930.0 11.1 %fusion.30 = s32[4,8192]{1,0:T(4,128)S(1)} fusion(f32[4,8192]{1,0:T(4,128)S(1)} %dynamic-slice_bitcast_fusion.8, f32[4,258]{0,1:T(8,128)S(1)} %bitcast.77), kind=kLoop, calls=%fused_computation.7.clone.1 | loop fusion | flops 25329664 | bytes 266272 | tf_op jit(solution)/shard_map/while/body/eval_jaxpr/reduce_sum | solution.py:57
  941.1 20.2 %fusion.29 = (f32[4,8192]{1,0:T(4,128)S(1)}, f32[4,8192]{1,0:T(4,128)S(1)}) fusion(f32[4,8192]{1,0:T(4,128)S(1)} %dynamic-slice_bitcast_fusion.8, f32[4,258]{0,1:T(8,128)S(1)} %bitcast.78), kind=kLoop, calls=%fused_computation.8.clone.1 | loop fusion | flops 42205184 | bytes 397344 | tf_op jit(solution)/shard_map/while/body/eval_jaxpr/reduce_max | solution.py:58
  962.2 11.1 %fusion.30 = s32[4,8192]{1,0:T(4,128)S(1)} fusion(f32[4,8192]{1,0:T(4,128)S(1)} %dynamic-slice_bitcast_fusion.8, f32[4,258]{0,1:T(8,128)S(1)} %bitcast.77), kind=kLoop, calls=%fused_computation.7.clone.1 | loop fusion | flops 25329664 | bytes 266272 | tf_op jit(solution)/shard_map/while/body/eval_jaxpr/reduce_sum | solution.py:57
  973.4 20.2 %fusion.29 = (f32[4,8192]{1,0:T(4,128)S(1)}, f32[4,8192]{1,0:T(4,128)S(1)}) fusion(f32[4,8192]{1,0:T(4,128)S(1)} %dynamic-slice_bitcast_fusion.8, f32[4,258]{0,1:T(8,128)S(1)} %bitcast.78), kind=kLoop, calls=%fused_computation.8.clone.1 | loop fusion | flops 42205184 | bytes 397344 | tf_op jit(solution)/shard_map/while/body/eval_jaxpr/reduce_max | solution.py:58
  998.3 45.9 %all_to_all.19 = f32[64,8,1024]{2,0,1:T(8,128)S(1)} all-to-all(f32[64,8,1024]{2,0,1:T(8,128)S(1)} %copy.9), channel_id=1, replica_groups=mesh['rows'=32,'feat'=8] {'feat'}, dimensions={1} | all-to-all | bytes 4194304 | tf_op jit(solution)/shard_map/all_to_all | solution.py:84
  (221 shorter events, 232.4 us)
Async XLA Ops:
  6.5 418.5 %all-reduce.3.cloned.1.call-start = ((), (), s32[]{:S(2)}) async-start(), calls=%async_computation.1 | async-start | bytes 131072
  26.6 342.2 %copy-start = (u32[256]{0:T(256)S(1)}, u32[256]{0:T(256)}, u32[]{:S(2)}) copy-start(u32[256]{0:T(256)} %constant.162) | copy-start | bytes 3076
Sparse Core Ops, SparseCore 0:
  289.5 135.4 all-reduce.2
where the time goes:
time: 1050 us
  other arithmetic  653 us (62%)
  blocking collectives  173 us (16%)
  matrix products  125 us (12%)
  waiting for transfers between devices  53.7 us (5%)
  local copies, waits for them, and re-layouts  32.1 us (3%)
  between operations  14.8 us (1%)
    reduce_max x16, other arithmetic, bucketize_one_block(): low_knot = jnp.max(jnp.where(at_or_below, knot_grid, -jnp.inf), axis=1)  323 us
    reduce_sum x16, other arithmetic, bucketize_one_block(): count_below = jnp.sum(at_or_below.astype(jnp.int32), axis=1) - 1  178 us
    lt x16, other arithmetic, mass_one_block(): value_block[:, None, :] < edge_block[:, :, None]  135 us
    dot_general x16, matrix products, mass_one_block(): jnp.dot(below.reshape(block_feats * grid_points, row_count), weight_pair,...  125 us
    psum x1, blocking collectives, on_device(): total_mass = lax.psum(jnp.sum(hess_own), ('rows', 'feat'))  79.3 us
    unnamed x2, waiting for transfers between devices  53.7 us
    all_to_all x1, blocking collectives, on_device(): lax.all_to_all(positions, 'feat', split_axis=1, concat_axis=0, tiled=True)  45.9 us
    all_gather x1, blocking collectives, on_device(): cut_knots = lax.all_gather(cut_knots, 'rows', axis=0, tiled=True)  31.5 us
  transfers between devices with their start and end apart: 1, of which 1 were waited for; matrix products, arithmetic and copies ran while one was open for 0% of the time, Pallas kernels for 0%

commit v1 on v0

v1 whole, which is shorter than its diff:
```python
import jax
import jax.numpy as jnp
from jax import lax
from jax.experimental import pallas as pl
from jax.experimental.pallas import tpu as pltpu
from jax.sharding import PartitionSpec as P

LANES = 128


def lane_take(table, index):
    return jnp.take_along_axis(table, index, axis=1, mode="promise_in_bounds")


def pick_columns(wide, index):
    low = lane_take(wide[:, :LANES], index & (LANES - 1))
    high = lane_take(wide[:, LANES:], index & (LANES - 1))
    return jnp.where(index < LANES, low, high)


def lane_iota(shape):
    return lax.broadcasted_iota(jnp.int32, shape, 1)


def search_pair(even, middle, value):
    base = jnp.where(value >= middle, 64, 0)
    for step in (32, 16, 8, 4, 2, 1):
        probe = base + step
        base = jnp.where(value >= lane_take(even, probe), probe, base)
    return base


def mass_kernel(codes_ref, hess_ref, values_ref, mass_ref, a_ref, b_ref, w_ref):
    feats, rows = values_ref.shape
    shape = (feats, LANES)
    lane = lane_iota(shape)
    feat = lax.broadcasted_iota(jnp.int32, shape, 0)
    edges = codes_ref[...].astype(jnp.float32) * (1.0 / 256.0)
    even = pick_columns(edges, 2 * lane)
    odd = pick_columns(edges, 2 * lane + 1)
    middle = jnp.broadcast_to(even[:, 64:65], shape)

    @pl.when(pl.program_id(0) == 0)
    def _():
        scaled = jnp.broadcast_to(hess_ref[...] * 65536.0, (feats, rows))
        high = jnp.floor(scaled * (1.0 / 256.0))
        w_ref[0] = high.astype(jnp.bfloat16)
        w_ref[1] = (scaled - high * 256.0).astype(jnp.bfloat16)

    def chunk(step, carry):
        for part in range(4):
            at = pl.multiple_of(step * (4 * LANES) + part * LANES, LANES)
            value = values_ref[:, pl.ds(at, LANES)]
            pair = search_pair(even, middle, value)
            top = (pair >> 3).astype(jnp.float32).astype(jnp.bfloat16)
            bit = jnp.where(value >= lane_take(odd, pair), 1, 0)
            low = (2 * (pair & 7) + bit).astype(jnp.float32).astype(jnp.bfloat16)
            w_high = w_ref[0, :, pl.ds(at, LANES)]
            w_low = w_ref[1, :, pl.ds(at, LANES)]
            zero = jnp.zeros(shape, jnp.bfloat16)
            one = jnp.ones(shape, jnp.bfloat16)
            for k in range(16):
                hit = top == k
                a_ref[k * feats:(k + 1) * feats, pl.ds(at, LANES)] = jnp.where(hit, w_high, zero)
                a_ref[(16 + k) * feats:(17 + k) * feats, pl.ds(at, LANES)] = jnp.where(hit, w_low, zero)
                b_ref[k * feats:(k + 1) * feats, pl.ds(at, LANES)] = jnp.where(low <= k, one, zero)
        return carry

    lax.fori_loop(0, rows // (4 * LANES), chunk, 0)
    sums = lax.dot_general(a_ref[...], b_ref[...], (((1,), (1,)), ((), ())), preferred_element_type=jnp.float32)
    half = 16 * feats
    table = (sums[:half] * 256.0 + sums[half:]) * (1.0 / 65536.0)
    for parity in range(2):
        point = 2 * lane + parity - 1
        column = (point & 7) * feats + feat
        result = jnp.zeros(shape, jnp.float32)
        before = jnp.zeros(shape, jnp.float32)
        for k in range(16):
            block = table[k * feats:(k + 1) * feats]
            here = jnp.where((point & 15) < 8, lane_take(block[:, :LANES], column), lane_take(block[:, LANES:], column))
            result = jnp.where((point >> 4) == k, before + here, result)
            before = before + lane_take(block[:, LANES:], 7 * feats + feat)
        mass_ref[:, parity * LANES:(parity + 1) * LANES] = result


def local_mass(values, edge_codes, hess):
    feats, rows = values.shape
    group = 16
    return pl.pallas_call(
        mass_kernel,
        grid=(feats // group,),
        in_specs=[
            pl.BlockSpec((group, 256), lambda i: (i, 0)),
            pl.BlockSpec((1, rows), lambda i: (0, 0)),
            pl.BlockSpec((group, rows), lambda i: (i, 0)),
        ],
        out_specs=pl.BlockSpec((group, 256), lambda i: (i, 0)),
        out_shape=jax.ShapeDtypeStruct((feats, 256), jnp.float32),
        scratch_shapes=[
            pltpu.VMEM((32 * group, rows), jnp.bfloat16),
            pltpu.VMEM((16 * group, rows), jnp.bfloat16),
            pltpu.VMEM((2, group, rows), jnp.bfloat16),
        ],
        compiler_params=pltpu.CompilerParams(vmem_limit_bytes=40 << 20),
    )(edge_codes, hess.reshape(1, rows), values)


def next_even(even, lane, last):
    return jnp.where(lane == LANES - 1, last, lane_take(even, (lane + 1) & (LANES - 1)))


def cuts_kernel(codes_ref, ranks_ref, mass_ref, cuts_ref):
    feats = codes_ref.shape[0]
    shape = (feats, LANES)
    lane = lane_iota(shape)
    edges = codes_ref[...].astype(jnp.float32) * (1.0 / 256.0)
    edge_even = pick_columns(edges, 2 * lane)
    edge_odd = pick_columns(edges, 2 * lane + 1)
    edge_next = lane_take(edge_even, (lane + 1) & (LANES - 1))
    mass_even = mass_ref[:, :LANES]
    mass_odd = mass_ref[:, LANES:]
    mass_next = lane_take(mass_even, (lane + 1) & (LANES - 1))
    middle = jnp.broadcast_to(mass_even[:, 64:65], shape)
    total = jnp.broadcast_to(mass_odd[:, LANES - 1:], shape)
    ranks = ranks_ref[...].astype(jnp.float32)
    for side in range(2):
        order = 2 * lane if side else jnp.where(lane == 0, 255, 2 * lane - 1)
        target = pick_columns(ranks, order) * (1.0 / 65792.0) * total
        pair = search_pair(mass_even, middle, target)
        mid_mass = lane_take(mass_odd, pair)
        mid_edge = lane_take(edge_odd, pair)
        above = target >= mid_mass
        low_mass = jnp.where(above, mid_mass, lane_take(mass_even, pair))
        high_mass = jnp.where(above, lane_take(mass_next, pair), mid_mass)
        low_edge = jnp.where(above, mid_edge, lane_take(edge_even, pair))
        high_edge = jnp.where(above, lane_take(edge_next, pair), mid_edge)
        cuts_ref[:, side * LANES:(side + 1) * LANES] = low_edge + (target - low_mass) / (high_mass - low_mass) * (high_edge - low_edge)


def find_cuts(edge_codes, cut_ranks, mass):
    return pl.pallas_call(
        cuts_kernel,
        out_shape=jax.ShapeDtypeStruct(mass.shape, jnp.float32),
    )(edge_codes, cut_ranks, mass)


def place_kernel(cuts_ref, values_ref, out_ref):
    feats, rows = values_ref.shape
    shape = (8, LANES)
    lane = lane_iota(shape)
    for group in range(feats // 8):
        some = slice(group * 8, group * 8 + 8)
        raw = cuts_ref[some, :LANES]
        odd = cuts_ref[some, LANES:]
        last = jnp.broadcast_to(raw[:, :1], shape)
        even = jnp.where(lane == 0, -16.0, raw)
        after = next_even(even, lane, last)
        inv_low = 1.0 / (odd - even)
        inv_high = 1.0 / (after - odd)
        inv_last = 1.0 / (16.0 - last)
        middle = jnp.broadcast_to(raw[:, 64:65], shape)

        def chunk(step, carry):
            for part in range(8):
                at = pl.multiple_of(step * (8 * LANES) + part * LANES, LANES)
                value = values_ref[some, pl.ds(at, LANES)]
                pair = search_pair(even, middle, value)
                knot = lane_take(odd, pair)
                slope = jnp.where(value >= knot, lane_take(inv_high, pair), lane_take(inv_low, pair))
                whole = (2 * pair + 1).astype(jnp.float32)
                inside = whole + (value - knot) * slope
                out_ref[some, pl.ds(at, LANES)] = jnp.where(value >= last, 256.0 + (value - last) * inv_last, inside)
            return carry

        lax.fori_loop(0, rows // (8 * LANES), chunk, 0)


def place(cuts, values):
    feats, rows = values.shape
    group = 16 if rows > 1024 else feats
    return pl.pallas_call(
        place_kernel,
        grid=(feats // group,),
        in_specs=[
            pl.BlockSpec((group, 256), lambda i: (i, 0)),
            pl.BlockSpec((group, rows), lambda i: (i, 0)),
        ],
        out_specs=pl.BlockSpec((group, rows), lambda i: (i, 0)),
        out_shape=jax.ShapeDtypeStruct((feats, rows), jnp.float32),
    )(cuts, values)


def swap_rows(array, flip):
    count = lax.axis_size("rows")
    return lax.ppermute(array, "rows", [(i, i ^ flip) for i in range(count)])


def sum_rows(array):
    for flip in (1, 2, 4, 8, 16):
        array = array + swap_rows(array, flip)
    return array


def on_device(feature_values, hessian_codes, edge_codes, cut_ranks):
    hess_own = hessian_codes.astype(jnp.float32) * (1.0 / 65536.0)
    hess_slab = lax.all_gather(hess_own, "feat", axis=0, tiled=True)
    mass = sum_rows(local_mass(feature_values, edge_codes, hess_slab))
    cuts = find_cuts(edge_codes, cut_ranks, mass)
    positions = place(cuts, feature_values)
    return lax.all_to_all(positions, "feat", split_axis=1, concat_axis=0, tiled=True)


def solution(mesh):
    placed = (P("feat", "rows"), P(("rows", "feat")), P("feat", None), P("feat", None))
    return jax.shard_map(
        on_device, mesh=mesh, in_specs=placed, out_specs=P(None, ("rows", "feat")), check_vma=False
    )
```

time: 1050 us -> 178 us (0.17)
  other arithmetic: 653 us -> 1.37 us
  matrix products: 125 us -> 0 us
  blocking collectives: 173 us -> 51.3 us
  Pallas kernels: 0 us -> 96.1 us
  waiting for transfers between devices: 53.7 us -> 10.4 us
  local copies, waits for them, and re-layouts: 32.1 us -> 5.48 us
  between operations: 14.8 us -> 0.03 us
  starting transfers between devices: 0.01 us -> 13.4 us
    reduce_max x16 -> x0, other arithmetic: 323 us -> none  [bucketize_one_block(): low_knot = jnp.max(jnp.where(at_or_below, knot_grid, -jnp.inf), axis=1)]
    reduce_sum x17 -> x0, other arithmetic: 179 us -> none  [the longest x16 178 us: bucketize_one_block(): count_below = jnp.sum(at_or_below.astype(jnp.int32), axis=1) - 1]
    lt x16 -> x0, other arithmetic: 135 us -> none  [mass_one_block(): value_block[:, None, :] < edge_block[:, :, None]]
    dot_general x16 -> x0, matrix products: 125 us -> none  [mass_one_block(): jnp.dot(below.reshape(block_feats * grid_points, row_count), weight_pair,...]
    pallas_call x0 -> x3, Pallas kernels: none -> 96.1 us  [the longest x1 55.1 us: local_mass(): pl.pallas_call(mass_kernel, grid=(feats // group,), in_specs=[pl.BlockSpe...]
    psum x1 -> x0, blocking collectives: 79.3 us -> none  [on_device(): total_mass = lax.psum(jnp.sum(hess_own), ('rows', 'feat'))]
    unnamed x2 -> x0, waiting for transfers between devices: 53.7 us -> none
    all_gather x1 -> x0, blocking collectives: 31.5 us -> none  [on_device(): cut_knots = lax.all_gather(cut_knots, 'rows', axis=0, tiled=True)]
  transfers between devices with their start and end apart: 1 -> 5, of which waited for: 1 -> 5; matrix products, arithmetic and copies ran while one was open for 0% -> 0% of each run, Pallas kernels for 0% -> 0%
where the time goes in v1:
time: 178 us
  Pallas kernels  96.1 us (54%)
  blocking collectives  51.3 us (29%)
  starting transfers between devices  13.4 us (8%)
  waiting for transfers between devices  10.4 us (6%)
  local copies, waits for them, and re-layouts  5.48 us (3%)
    pallas_call x1, Pallas kernels, local_mass(): pl.pallas_call(mass_kernel, grid=(feats // group,), in_specs=[pl.BlockSpe...  55.1 us
    pallas_call x1, Pallas kernels, place(): pl.pallas_call(place_kernel, grid=(feats // group,), in_specs=[pl.BlockSp...  38.4 us
    all_to_all x1, blocking collectives, on_device(): lax.all_to_all(positions, 'feat', split_axis=1, concat_axis=0, tiled=True)  35.5 us
    all_gather x1, blocking collectives, on_device(): hess_slab = lax.all_gather(hess_own, 'feat', axis=0, tiled=True)  15.8 us
    ppermute x5, starting transfers between devices, swap_rows(): return lax.ppermute(array, 'rows', [(i, i ^ flip) for i in range(count)])  13.4 us
    ppermute x5, waiting for transfers between devices, swap_rows(): return lax.ppermute(array, 'rows', [(i, i ^ flip) for i in range(count)])  10.4 us
    unnamed x5, local copies, waits for them, and re-layouts  3.75 us
  transfers between devices with their start and end apart: 5, of which 5 were waited for; matrix products, arithmetic and copies ran while one was open for 0% of the time, Pallas kernels for 0%

profile of v1, /device:TPU:1, one launch (start us, length us, event | category | flops | bytes accessed | tf_op | source)
XLA Modules:
  0.0 178.0 jit_solution(15704262856420592672)
XLA Ops:
  0.0 0.7 convert_multiply_fusion
  0.7 15.8 %all_gather.3 = f32[8192]{0:T(1024)S(1)} all-gather(f32[1024]{0:T(1024)S(1)} %convert_multiply_fusion), channel_id=1, replica_groups=mesh['rows'=32,'feat'=8] {'feat'}, dimensions={0}, use_global_device_ids=true | all-gather | bytes 36864 | tf_op jit(solution)/shard_map/all_gather | solution.py:206
  16.5 0.0 copy-start
  16.5 1.6 copy-done
  18.1 0.0 copy-start.1
  18.1 0.8 copy-done.1
  19.0 55.1 %shard_map.46 = f32[64,256]{1,0:T(8,128)S(1)} custom-call(s32[64,256]{1,0:T(8,128)S(1)} %copy-done.1, f32[1,8192]{1,0:T(1,128)S(1)} %bitcast.8, f32[64,8192]{1,0:T(8,128)S(1)} %copy-done), custom_call_target="tpu_custom_call" | custom-call | tf_op jit(solution)/shard_map/pallas_call | solution.py:89
  74.1 0.5 collective-permute-start
  74.6 3.1 %collective-permute-done = f32[64,256]{1,0:T(8,128)S(1)} collective-permute-done((f32[64,256]{1,0:T(8,128)S(1)}, f32[64,256]{1,0:T(8,128)S(1)}, u32[]{:S(2)}, u32[]{:S(2)}) %collective-permute-start) | collective-permute-done | bytes 65568 | tf_op jit(solution)/shard_map/ppermute | solution.py:195
  77.6 2.2 %collective-permute-start.1 = (f32[64,256]{1,0:T(8,128)S(1)}, f32[64,256]{1,0:T(8,128)S(1)}, u32[]{:S(2)}, u32[]{:S(2)}) collective-permute-start(f32[64,256]{1,0:T(8,128)S(1)} %add.15), channel_id=1, source_target_pairs={{0,16},{8,24},{16,0},{24,8},{32,48},{40,56},{48,32},{56,40},{64,80... | collective-permute-start | bytes 196616 | tf_op jit(solution)/shard_map/ppermute | solution.py:195
  79.9 1.9 %collective-permute-done.1 = f32[64,256]{1,0:T(8,128)S(1)} collective-permute-done((f32[64,256]{1,0:T(8,128)S(1)}, f32[64,256]{1,0:T(8,128)S(1)}, u32[]{:S(2)}, u32[]{:S(2)}) %collective-permute-start.1) | collective-permute-done | bytes 65568 | tf_op jit(solution)/shard_map/ppermute | solution.py:195
  81.8 6.5 %collective-permute-start.2 = (f32[64,256]{1,0:T(8,128)S(1)}, f32[64,256]{1,0:T(8,128)S(1)}, u32[]{:S(2)}, u32[]{:S(2)}) collective-permute-start(f32[64,256]{1,0:T(8,128)S(1)} %add.16), channel_id=1, source_target_pairs={{0,32},{8,40},{16,48},{24,56},{32,0},{40,8},{48,16},{56,24},{64,96... | collective-permute-start | bytes 196616 | tf_op jit(solution)/shard_map/ppermute | solution.py:195
  88.2 1.7 collective-permute-done.2
  89.9 1.3 collective-permute-start.3
  91.2 1.9 %collective-permute-done.3 = f32[64,256]{1,0:T(8,128)S(1)} collective-permute-done((f32[64,256]{1,0:T(8,128)S(1)}, f32[64,256]{1,0:T(8,128)S(1)}, u32[]{:S(2)}, u32[]{:S(2)}) %collective-permute-start.3) | collective-permute-done | bytes 65568 | tf_op jit(solution)/shard_map/ppermute | solution.py:195
  93.1 2.8 %collective-permute-start.4 = (f32[64,256]{1,0:T(8,128)S(1)}, f32[64,256]{1,0:T(8,128)S(1)}, u32[]{:S(2)}, u32[]{:S(2)}) collective-permute-start(f32[64,256]{1,0:T(8,128)S(1)} %add.18), channel_id=1, source_target_pairs={{0,128},{8,136},{16,144},{24,152},{32,160},{40,168},{48,176},{56,1... | collective-permute-start | bytes 196616 | tf_op jit(solution)/shard_map/ppermute | solution.py:195
  96.0 1.9 %collective-permute-done.4 = f32[64,256]{1,0:T(8,128)S(1)} collective-permute-done((f32[64,256]{1,0:T(8,128)S(1)}, f32[64,256]{1,0:T(8,128)S(1)}, u32[]{:S(2)}, u32[]{:S(2)}) %collective-permute-start.4) | collective-permute-done | bytes 65568 | tf_op jit(solution)/shard_map/ppermute | solution.py:195
  97.8 0.6 add.19.mass_ref
  98.5 2.6 %shard_map.47.cuts_ref = f32[64,256]{1,0:T(8,128)} custom-call(s32[64,256]{1,0:T(8,128)} %codes_ref.3, s32[64,256]{1,0:T(8,128)} %ranks_ref.1, f32[64,256]{1,0:T(8,128)} %add.19.mass_ref), custom_call_target="tpu_custom_call" | custom-call | tf_op jit(solution)/shard_map/pallas_call | solution.py:141
  101.1 38.4 %shard_map.48 = f32[64,8192]{1,0:T(8,128)} custom-call(f32[64,256]{1,0:T(8,128)} %shard_map.47.cuts_ref, f32[64,8192]{1,0:T(8,128)} %values_ref.3), custom_call_target="tpu_custom_call" | custom-call | tf_op jit(solution)/shard_map/pallas_call | solution.py:181
  139.5 1.7 copy.9
  141.2 35.5 %all_to_all.19 = f32[64,8,1024]{2,0,1:T(8,128)S(1)} all-to-all(f32[64,8,1024]{2,0,1:T(8,128)S(1)} %bitcast.10), channel_id=1, replica_groups=mesh['rows'=32,'feat'=8] {'feat'}, dimensions={1} | all-to-all | bytes 4194304 | tf_op jit(solution)/shard_map/all_to_all | solution.py:210
  176.7 1.3 copy.11
  (4 shorter events, 0.0 us)
Async XLA Ops:
  16.5 1.6 copy-start
  18.1 0.8 copy-start.1
  74.1 3.6 %collective-permute-start = (f32[64,256]{1,0:T(8,128)S(1)}, f32[64,256]{1,0:T(8,128)S(1)}, u32[]{:S(2)}, u32[]{:S(2)}) collective-permute-start(f32[64,256]{1,0:T(8,128)S(1)} %shard_map.46), channel_id=1, source_target_pairs={{0,8},{8,0},{16,24},{24,16},{32,40},{40,32},{48,56},{56,48},{64,72... | collective-permute-start | bytes 196616 | tf_op jit(solution)/shard_map/ppermute | solution.py:195
  77.6 4.1 %collective-permute-start.1 = (f32[64,256]{1,0:T(8,128)S(1)}, f32[64,256]{1,0:T(8,128)S(1)}, u32[]{:S(2)}, u32[]{:S(2)}) collective-permute-start(f32[64,256]{1,0:T(8,128)S(1)} %add.15), channel_id=1, source_target_pairs={{0,16},{8,24},{16,0},{24,8},{32,48},{40,56},{48,32},{56,40},{64,80... | collective-permute-start | bytes 196616 | tf_op jit(solution)/shard_map/ppermute | solution.py:195
  81.8 8.1 %collective-permute-start.2 = (f32[64,256]{1,0:T(8,128)S(1)}, f32[64,256]{1,0:T(8,128)S(1)}, u32[]{:S(2)}, u32[]{:S(2)}) collective-permute-start(f32[64,256]{1,0:T(8,128)S(1)} %add.16), channel_id=1, source_target_pairs={{0,32},{8,40},{16,48},{24,56},{32,0},{40,8},{48,16},{56,24},{64,96... | collective-permute-start | bytes 196616 | tf_op jit(solution)/shard_map/ppermute | solution.py:195
  89.9 3.2 %collective-permute-start.3 = (f32[64,256]{1,0:T(8,128)S(1)}, f32[64,256]{1,0:T(8,128)S(1)}, u32[]{:S(2)}, u32[]{:S(2)}) collective-permute-start(f32[64,256]{1,0:T(8,128)S(1)} %add.17), channel_id=1, source_target_pairs={{0,64},{8,72},{16,80},{24,88},{32,96},{40,104},{48,112},{56,120},{... | collective-permute-start | bytes 196616 | tf_op jit(solution)/shard_map/ppermute | solution.py:195
  93.1 4.7 %collective-permute-start.4 = (f32[64,256]{1,0:T(8,128)S(1)}, f32[64,256]{1,0:T(8,128)S(1)}, u32[]{:S(2)}, u32[]{:S(2)}) collective-permute-start(f32[64,256]{1,0:T(8,128)S(1)} %add.18), channel_id=1, source_target_pairs={{0,128},{8,136},{16,144},{24,152},{32,160},{40,168},{48,176},{56,1... | collective-permute-start | bytes 196616 | tf_op jit(solution)/shard_map/ppermute | solution.py:195

commit v2 on v0

v2 whole, which is shorter than its diff:
```python
import jax
import jax.numpy as jnp
from jax import lax
from jax.experimental import pallas as pl
from jax.experimental.pallas import tpu as pltpu
from jax.sharding import PartitionSpec as P

LANES = 128
FEATS = 16
DEPTH = 4
SPAN = 2048


def in_vmem(count):
    return [pl.BlockSpec(memory_space=pltpu.VMEM)] * count


def lane_take(table, index):
    return jnp.take_along_axis(table, index, axis=1, mode="promise_in_bounds")


def pick_columns(wide, index):
    low = lane_take(wide[:, :LANES], index & (LANES - 1))
    high = lane_take(wide[:, LANES:], index & (LANES - 1))
    return jnp.where(index < LANES, low, high)


def lane_iota(shape):
    return lax.broadcasted_iota(jnp.int32, shape, 1)


def choose(marks, low, high, masks):
    middle = (low + high) // 2
    if not masks:
        return marks[middle]
    upper = choose(marks, middle, high, masks[1:])
    return jnp.where(masks[0], upper, choose(marks, low, middle, masks[1:]))


def spread(even):
    return {i: jnp.broadcast_to(even[:, i : i + 1], even.shape) for i in range(128 >> DEPTH, 128, 128 >> DEPTH)}


def search_pairs(tables, values):
    masks = [[] for _ in values]
    for _ in range(DEPTH):
        for (_, marks), mask, value in zip(tables, masks, values):
            mask.append(value >= choose(marks, 0, LANES, mask))
    bases = []
    for mask in masks:
        base = jnp.where(mask[0], 64, 0)
        for level in range(1, DEPTH):
            base = base + jnp.where(mask[level], 64 >> level, 0)
        bases.append(base)
    step = 64 >> DEPTH
    while step:
        probes = [base + step for base in bases]
        entries = [lane_take(even, probe) for (even, _), probe in zip(tables, probes)]
        bases = [jnp.where(v >= e, p, b) for v, e, p, b in zip(values, entries, probes, bases)]
        step //= 2
    return bases


def even_odd(codes):
    lane = lane_iota((codes.shape[0], LANES))
    edges = codes.astype(jnp.float32) * (1.0 / 256.0)
    return pick_columns(edges, 2 * lane), pick_columns(edges, 2 * lane + 1)


def slot_kernel(turn, codes_ref, values_ref, top_ref, low_ref):
    rows = values_ref.shape[1]
    width = 32
    group = (lax.axis_index("rows") // 8 + turn) % 4
    tables = []
    for half in range(2):
        at = pl.ds(pl.multiple_of(group * FEATS + 8 * half, 8), 8)
        even, odd = even_odd(codes_ref[at, :])
        tables.append((at, odd, (even, spread(even))))

    def chunk(step, carry):
        columns = [pl.ds(pl.multiple_of((step * width + part) * LANES, LANES), LANES) for part in range(width)]
        tops, lows = [[] for _ in columns], [[] for _ in columns]
        for at, odd, table in tables:
            values = [values_ref[at, column] for column in columns]
            pairs = search_pairs([table] * width, values)
            entries = [lane_take(odd, pair) for pair in pairs]
            for top, low, value, pair, entry in zip(tops, lows, values, pairs, entries):
                top.append((pair >> 3).astype(jnp.float32))
                low.append((2 * (pair & 7) + jnp.where(value >= entry, 1, 0)).astype(jnp.float32))
        for column, top, low in zip(columns, tops, lows):
            top_ref[:, column] = jnp.concatenate(top, axis=0).astype(jnp.bfloat16)
            low_ref[:, column] = jnp.concatenate(low, axis=0).astype(jnp.bfloat16)
        return carry

    lax.fori_loop(0, rows // (width * LANES), chunk, 0)


def find_slots(turn, edge_codes, values):
    slots = jax.ShapeDtypeStruct((FEATS, values.shape[1]), jnp.bfloat16)
    return pl.pallas_call(
        lambda *refs: slot_kernel(turn, *refs),
        in_specs=in_vmem(2),
        out_specs=in_vmem(2),
        out_shape=[slots, slots],
        compiler_params=pltpu.CompilerParams(vmem_limit_bytes=16 << 20),
        cost_estimate=pl.CostEstimate(flops=10**7, bytes_accessed=10**7, transcendentals=0),
        name="slots",
    )(edge_codes, values)


def hist_kernel(hess_ref, top_ref, low_ref, mass_ref, high_ref, rest_ref, sum_ref, a0, b0):
    rows = top_ref.shape[1]
    shape = (FEATS, LANES)
    lane = lane_iota(shape)
    feat = lax.broadcasted_iota(jnp.int32, shape, 0)
    zero = jnp.zeros(shape, jnp.bfloat16)
    one = jnp.ones(shape, jnp.bfloat16)
    scaled = hess_ref[...] * 65536.0
    high = jnp.floor(scaled * (1.0 / 256.0))
    rest = scaled - high * 256.0
    wide = hess_ref.shape[1]
    for part in range(rows // wide):
        own = slice(part * wide, (part + 1) * wide)
        high_ref[:, own] = jnp.broadcast_to(high[part : part + 1], (FEATS, wide)).astype(jnp.bfloat16)
        rest_ref[:, own] = jnp.broadcast_to(rest[part : part + 1], (FEATS, wide)).astype(jnp.bfloat16)

    def make(step, a_ref, b_ref):
        for off in range(0, SPAN, LANES):
            at = pl.ds(pl.multiple_of(step * SPAN + off, LANES), LANES)
            own = slice(off, off + LANES)
            top, low, w_high, w_rest = top_ref[:, at], low_ref[:, at], high_ref[:, at], rest_ref[:, at]
            for k in range(16):
                hit = top == k
                a_ref[k * FEATS : (k + 1) * FEATS, own] = jnp.where(hit, w_high, zero)
                a_ref[(16 + k) * FEATS : (17 + k) * FEATS, own] = jnp.where(hit, w_rest, zero)
                b_ref[k * FEATS : (k + 1) * FEATS, own] = jnp.where(low <= k, one, zero)

    def add(a_ref, b_ref):
        sum_ref[...] += lax.dot_general(
            a_ref[...], b_ref[...], (((1,), (1,)), ((), ())), preferred_element_type=jnp.float32
        )

    sum_ref[...] = jnp.zeros_like(sum_ref)

    def step(index, carry):
        make(index, a0, b0)
        add(a0, b0)
        return carry

    lax.fori_loop(0, rows // SPAN, step, 0)

    for parity in range(2):
        point = 2 * lane + parity - 1
        column = (point & 7) * FEATS + feat
        result = jnp.zeros(shape, jnp.float32)
        before = jnp.zeros(shape, jnp.float32)
        for k in range(16):
            large = sum_ref[k * FEATS : (k + 1) * FEATS]
            small = sum_ref[(16 + k) * FEATS : (17 + k) * FEATS]
            block = (large * 256.0 + small) * (1.0 / 65536.0)
            here = jnp.where((point & 15) < 8, lane_take(block[:, :LANES], column), lane_take(block[:, LANES:], column))
            result = jnp.where((point >> 4) == k, before + here, result)
            before = before + lane_take(block[:, LANES:], 7 * FEATS + feat)
        mass_ref[:, parity * LANES : (parity + 1) * LANES] = result


def find_mass(hess, top, low):
    rows = top.shape[1]
    return pl.pallas_call(
        hist_kernel,
        in_specs=in_vmem(3),
        out_specs=in_vmem(1)[0],
        out_shape=jax.ShapeDtypeStruct((FEATS, 256), jnp.float32),
        scratch_shapes=[pltpu.VMEM((FEATS, rows), jnp.bfloat16)] * 2
        + [pltpu.VMEM((512, 256), jnp.float32)]
        + [pltpu.VMEM((512, SPAN), jnp.bfloat16), pltpu.VMEM((256, SPAN), jnp.bfloat16)],
        compiler_params=pltpu.CompilerParams(vmem_limit_bytes=24 << 20),
        cost_estimate=pl.CostEstimate(flops=4 * 10**9, bytes_accessed=10**7, transcendentals=0),
        name="hist",
    )(hess, top, low)


def cuts_kernel(codes_ref, ranks_ref, first_ref, second_ref, cuts_ref):
    shape = (FEATS, LANES)
    lane = lane_iota(shape)
    group = lax.axis_index("rows") // 8
    at = pl.ds(pl.multiple_of(group * FEATS, FEATS), FEATS)
    edge_even, edge_odd = even_odd(codes_ref[at, :])
    edge_next = lane_take(edge_even, (lane + 1) & (LANES - 1))
    mass = first_ref[...] + second_ref[...]
    mass_even, mass_odd = mass[:, :LANES], mass[:, LANES:]
    mass_next = lane_take(mass_even, (lane + 1) & (LANES - 1))
    total = jnp.broadcast_to(mass_odd[:, LANES - 1 :], shape)
    ranks = ranks_ref[at, :].astype(jnp.float32)
    orders = [jnp.where(lane == 0, 255, 2 * lane - 1), 2 * lane]
    targets = [pick_columns(ranks, order) * (1.0 / 65792.0) * total for order in orders]
    pairs = search_pairs([(mass_even, spread(mass_even))] * 2, targets)
    for side, (target, pair) in enumerate(zip(targets, pairs)):
        mid_mass = lane_take(mass_odd, pair)
        mid_edge = lane_take(edge_odd, pair)
        above = target >= mid_mass
        low_mass = jnp.where(above, mid_mass, lane_take(mass_even, pair))
        high_mass = jnp.where(above, lane_take(mass_next, pair), mid_mass)
        low_edge = jnp.where(above, mid_edge, lane_take(edge_even, pair))
        high_edge = jnp.where(above, lane_take(edge_next, pair), mid_edge)
        part = (target - low_mass) / (high_mass - low_mass)
        cuts_ref[:, side * LANES : (side + 1) * LANES] = low_edge + part * (high_edge - low_edge)


def find_cuts(edge_codes, cut_ranks, first, second):
    return pl.pallas_call(
        cuts_kernel,
        in_specs=in_vmem(4),
        out_specs=in_vmem(1)[0],
        out_shape=jax.ShapeDtypeStruct((FEATS, 256), jnp.float32),
        name="cuts",
    )(edge_codes, cut_ranks, first, second)


def place_group(raw, odd, values, write):
    shape = odd.shape
    lane = lane_iota(shape)
    last = jnp.broadcast_to(raw[:, :1], shape)
    even = jnp.where(lane == 0, -16.0, raw)
    after = jnp.where(lane == LANES - 1, last, lane_take(even, (lane + 1) & (LANES - 1)))
    inv_low = 1.0 / (odd - even)
    inv_high = 1.0 / (after - odd)
    inv_last = 1.0 / (16.0 - last)
    table = (even, spread(even))
    pairs = search_pairs([table] * len(values), values)
    knots = [lane_take(odd, pair) for pair in pairs]
    highs = [lane_take(inv_high, pair) for pair in pairs]
    lows = [lane_take(inv_low, pair) for pair in pairs]
    for index, (value, pair, knot, high, low) in enumerate(zip(values, pairs, knots, highs, lows)):
        inside = (2 * pair + 1).astype(jnp.float32) + (value - knot) * jnp.where(value >= knot, high, low)
        write(index, jnp.where(value >= last, 256.0 + (value - last) * inv_last, inside))


def place_kernel(c0, c1, c2, c3, values_ref, out_ref, cuts_ref):
    blocks, feats, wide = out_ref.shape
    mine = lax.axis_index("rows") // 8
    for turn, c_ref in enumerate((c0, c1, c2, c3)):
        group = (mine + 4 - turn) % 4
        cuts_ref[pl.ds(pl.multiple_of(group * FEATS, FEATS), FEATS), :] = c_ref[...]

    def step(index, carry):
        at = pl.ds(pl.multiple_of(index * 8, 8), 8)
        values = [values_ref[at, part * LANES : (part + 1) * LANES] for part in range(blocks * wide // LANES)]

        def write(part, value):
            lanes = part * LANES % wide
            out_ref[part * LANES // wide, at, lanes : lanes + LANES] = value

        place_group(cuts_ref[at, :LANES], cuts_ref[at, LANES:], values, write)
        return carry

    lax.fori_loop(0, feats // 8, step, 0)


def place(cuts, values):
    feats, rows = values.shape
    return pl.pallas_call(
        place_kernel,
        in_specs=in_vmem(5),
        out_specs=in_vmem(1)[0],
        out_shape=jax.ShapeDtypeStruct((8, feats, rows // 8), jnp.float32),
        scratch_shapes=[pltpu.VMEM((feats, 256), jnp.float32)],
        compiler_params=pltpu.CompilerParams(vmem_limit_bytes=16 << 20),
        name="place",
    )(*cuts, values)


def flip_rows(array, flip):
    return lax.ppermute(array, "rows", [(i, i ^ flip) for i in range(32)])


def turn_rows(array, turn):
    return lax.ppermute(array, "rows", [(i, (i + 8 * turn) % 32) for i in range(32)])


def on_device(feature_values, hessian_codes, edge_codes, cut_ranks):
    hess_own = hessian_codes.astype(jnp.float32) * (1.0 / 65536.0)
    hess = lax.all_gather(hess_own, "feat", axis=0)
    slots = [find_slots(turn, edge_codes, feature_values) for turn in range(4)]
    parts = [turn_rows(find_mass(hess, *slots[turn]), turn) for turn in (1, 2, 3)]
    mass = find_mass(hess, *slots[0]) + parts[0] + parts[1] + parts[2]
    for flip in (1, 2):
        mass = mass + flip_rows(mass, flip)
    cuts = find_cuts(edge_codes, cut_ranks, mass, flip_rows(mass, 4))
    cuts = [cuts] + [turn_rows(cuts, turn) for turn in (1, 2, 3)]
    positions = place(cuts, feature_values)
    return lax.all_to_all(positions, "feat", split_axis=0, concat_axis=0, tiled=True).reshape(512, -1)


def solution(mesh):
    placed = (P("feat", "rows"), P(("rows", "feat")), P("feat", None), P("feat", None))
    return jax.shard_map(
        on_device, mesh=mesh, in_specs=placed, out_specs=P(None, ("rows", "feat")), check_vma=False
    )
```

time: 1050 us -> 122 us (0.12)
  other arithmetic: 653 us -> 0.71 us
  matrix products: 125 us -> 0 us
  blocking collectives: 173 us -> 51.4 us
  waiting for transfers between devices: 53.7 us -> 7.22 us
  Pallas kernels: 0 us -> 40 us
  local copies, waits for them, and re-layouts: 32.1 us -> 5.09 us
  starting transfers between devices: 0.01 us -> 16.9 us
  between operations: 14.8 us -> 0.14 us
    reduce_max x16 -> x0, other arithmetic: 323 us -> none  [bucketize_one_block(): low_knot = jnp.max(jnp.where(at_or_below, knot_grid, -jnp.inf), axis=1)]
    reduce_sum x17 -> x0, other arithmetic: 179 us -> none  [the longest x16 178 us: bucketize_one_block(): count_below = jnp.sum(at_or_below.astype(jnp.int32), axis=1) - 1]
    lt x16 -> x0, other arithmetic: 135 us -> none  [mass_one_block(): value_block[:, None, :] < edge_block[:, :, None]]
    dot_general x16 -> x0, matrix products: 125 us -> none  [mass_one_block(): jnp.dot(below.reshape(block_feats * grid_points, row_count), weight_pair,...]
    psum x1 -> x0, blocking collectives: 79.3 us -> none  [on_device(): total_mass = lax.psum(jnp.sum(hess_own), ('rows', 'feat'))]
    unnamed x2 -> x0, waiting for transfers between devices: 53.7 us -> none
    pallas_call x0 -> x10, Pallas kernels: none -> 40 us  [the longest x4 20.2 us: find_mass(): pl.pallas_call(hist_kernel, in_specs=in_vmem(3), out_specs=in_vmem(1)[0],...]
    all_gather x2 -> x1, blocking collectives: 47.4 us -> 15.8 us  [on_device(): hess = lax.all_gather(hess_own, 'feat', axis=0)]
  transfers between devices with their start and end apart: 1 -> 9, of which waited for: 1 -> 6; matrix products, arithmetic and copies ran while one was open for 0% -> 0% of each run, Pallas kernels for 0% -> 17%
where the time goes in v2:
time: 122 us
  blocking collectives  51.4 us (42%)
  Pallas kernels  40 us (33%)
  starting transfers between devices  16.9 us (14%)
  waiting for transfers between devices  7.22 us (6%)
  local copies, waits for them, and re-layouts  5.09 us (4%)
    all_to_all x1, blocking collectives, on_device(): lax.all_to_all(positions, 'feat', split_axis=0, concat_axis=0, tiled=True)  35.6 us
    pallas_call x4, Pallas kernels, find_mass(): pl.pallas_call(hist_kernel, in_specs=in_vmem(3), out_specs=in_vmem(1)[0],...  20.2 us
    all_gather x1, blocking collectives, on_device(): hess = lax.all_gather(hess_own, 'feat', axis=0)  15.8 us
    ppermute x3, starting transfers between devices, flip_rows(): return lax.ppermute(array, 'rows', [(i, i ^ flip) for i in range(32)])  10.8 us
    pallas_call x1, Pallas kernels, place(): pl.pallas_call(place_kernel, in_specs=in_vmem(5), out_specs=in_vmem(1)[0]...  10.5 us
    pallas_call x4, Pallas kernels, find_slots(): pl.pallas_call(lambda *refs: slot_kernel(turn, *refs), in_specs=in_vmem(2...  7.44 us
    ppermute x6, starting transfers between devices, turn_rows(): lax.ppermute(array, 'rows', [(i, (i + 8 * turn) % 32) for i in range(32)])  6.09 us
    unnamed x15, local copies, waits for them, and re-layouts  5.08 us
  transfers between devices with their start and end apart: 9, of which 6 were waited for; matrix products, arithmetic and copies ran while one was open for 0% of the time, Pallas kernels for 17%

profile of v2, /device:TPU:1, one launch (start us, length us, event | category | flops | bytes accessed | tf_op | source)
XLA Modules:
  0.0 121.5 jit_solution(4714360933912266975)
XLA Ops:
  0.0 0.7 convert_multiply_fusion
  0.7 15.8 %all-gather = f32[8192]{0:T(1024)S(1)} all-gather(f32[1024]{0:T(1024)S(1)} %convert_multiply_fusion), channel_id=2, replica_groups=mesh['rows'=32,'feat'=8] {'feat'}, dimensions={0}, use_global_device_ids=true | all-gather | bytes 36864 | tf_op jit(solution)/shard_map/all_gather | solution.py:283
  16.5 0.0 copy-start
  16.6 1.6 %copy-done = f32[64,8192]{1,0:T(8,128)S(1)} copy-done((f32[64,8192]{1,0:T(8,128)S(1)}, f32[64,8192]{1,0:T(8,128)}, u32[]{:S(2)}) %copy-start) | copy-done | bytes 2097176
  18.1 0.0 copy-start.2
  18.1 0.8 copy-done.2
  19.0 1.9 %slots.6 = (bf16[16,8192]{1,0:T(8,128)(2,1)S(1)}, bf16[16,8192]{1,0:T(8,128)(2,1)S(1)}) custom-call(s32[64,256]{1,0:T(8,128)S(1)} %copy-done.2, f32[64,8192]{1,0:T(8,128)S(1)} %copy-done), custom_call_target="tpu_custom_call" | custom-call | flops 10000000 | bytes 10000000 | tf_op jit(solution)/shard_map/slots/pallas_call | solution.py:100
  20.8 0.0 copy-start.1
  20.9 0.0 copy-start.3
  20.9 5.0 %hist.6 = f32[16,256]{1,0:T(8,128)S(1)} custom-call(f32[8,1024]{1,0:T(8,128)S(1)} %reshape.4.hess_ref, bf16[16,8192]{1,0:T(8,128)(2,1)S(1)} %get-tuple-element.17.top_ref, bf16[16,8192]{1,0:T(8,128)(2,1)S(1)} %get-tuple-element.18.low_ref), custom_call_target="tpu_custom_call" | custom-call | flops 4000000000 | bytes 10000000 | tf_op jit(solution)/shard_map/hist/pallas_call | solution.py:169
  25.9 1.6 %collective-permute-start.1 = (f32[16,256]{1,0:T(8,128)S(1)}, f32[16,256]{1,0:T(8,128)S(1)}, u32[]{:S(2)}, u32[]{:S(2)}) collective-permute-start(f32[16,256]{1,0:T(8,128)S(1)} %hist.6), channel_id=1, source_target_pairs={{0,128},{8,136},{16,144},{24,152},{32,160},{40,168},{48,176},{56,1... | collective-permute-start | bytes 49160 | tf_op jit(solution)/shard_map/ppermute | solution.py:278
  27.5 0.0 copy-done.1
  27.5 0.0 copy-done.3
  27.5 1.9 %slots.5 = (bf16[16,8192]{1,0:T(8,128)(2,1)S(1)}, bf16[16,8192]{1,0:T(8,128)(2,1)S(1)}) custom-call(s32[64,256]{1,0:T(8,128)S(1)} %copy-done.3, f32[64,8192]{1,0:T(8,128)S(1)} %copy-done.1), custom_call_target="tpu_custom_call" | custom-call | flops 10000000 | bytes 10000000 | tf_op jit(solution)/shard_map/slots/pallas_call | solution.py:100
  29.4 5.0 %hist.5 = f32[16,256]{1,0:T(8,128)S(1)} custom-call(f32[8,1024]{1,0:T(8,128)S(1)} %reshape.4.hess_ref, bf16[16,8192]{1,0:T(8,128)(2,1)S(1)} %get-tuple-element.15.top_ref, bf16[16,8192]{1,0:T(8,128)(2,1)S(1)} %get-tuple-element.16.low_ref), custom_call_target="tpu_custom_call" | custom-call | flops 4000000000 | bytes 10000000 | tf_op jit(solution)/shard_map/hist/pallas_call | solution.py:169
  34.5 0.4 collective-permute-start
  34.8 1.9 %slots.7 = (bf16[16,8192]{1,0:T(8,128)(2,1)S(1)}, bf16[16,8192]{1,0:T(8,128)(2,1)S(1)}) custom-call(s32[64,256]{1,0:T(8,128)S(1)} %copy-done.3, f32[64,8192]{1,0:T(8,128)S(1)} %copy-done.1), custom_call_target="tpu_custom_call" | custom-call | flops 10000000 | bytes 10000000 | tf_op jit(solution)/shard_map/slots/pallas_call | solution.py:100
  36.7 5.0 %hist.7 = f32[16,256]{1,0:T(8,128)S(1)} custom-call(f32[8,1024]{1,0:T(8,128)S(1)} %reshape.4.hess_ref, bf16[16,8192]{1,0:T(8,128)(2,1)S(1)} %get-tuple-element.19.top_ref, bf16[16,8192]{1,0:T(8,128)(2,1)S(1)} %get-tuple-element.20.low_ref), custom_call_target="tpu_custom_call" | custom-call | flops 4000000000 | bytes 10000000 | tf_op jit(solution)/shard_map/hist/pallas_call | solution.py:169
  41.8 2.6 %collective-permute-start.2 = (f32[16,256]{1,0:T(8,128)S(1)}, f32[16,256]{1,0:T(8,128)S(1)}, u32[]{:S(2)}, u32[]{:S(2)}) collective-permute-start(f32[16,256]{1,0:T(8,128)S(1)} %hist.7), channel_id=1, source_target_pairs={{0,192},{8,200},{16,208},{24,216},{32,224},{40,232},{48,240},{56,2... | collective-permute-start | bytes 49160 | tf_op jit(solution)/shard_map/ppermute | solution.py:278
  44.4 1.9 %slots.4 = (bf16[16,8192]{1,0:T(8,128)(2,1)S(1)}, bf16[16,8192]{1,0:T(8,128)(2,1)S(1)}) custom-call(s32[64,256]{1,0:T(8,128)S(1)} %copy-done.3, f32[64,8192]{1,0:T(8,128)S(1)} %copy-done.1), custom_call_target="tpu_custom_call" | custom-call | flops 10000000 | bytes 10000000 | tf_op jit(solution)/shard_map/slots/pallas_call | solution.py:100
  46.2 5.0 %hist.4 = f32[16,256]{1,0:T(8,128)S(1)} custom-call(f32[8,1024]{1,0:T(8,128)S(1)} %reshape.4.hess_ref, bf16[16,8192]{1,0:T(8,128)(2,1)S(1)} %get-tuple-element.13.top_ref, bf16[16,8192]{1,0:T(8,128)(2,1)S(1)} %get-tuple-element.14.low_ref), custom_call_target="tpu_custom_call" | custom-call | flops 4000000000 | bytes 10000000 | tf_op jit(solution)/shard_map/hist/pallas_call | solution.py:169
  51.3 0.0 collective-permute-done.1
  51.3 0.0 collective-permute-done
  51.3 0.0 collective-permute-done.2
  51.3 1.7 %collective-permute-start.3 = (f32[16,256]{1,0:T(8,128)S(1)}, f32[16,256]{1,0:T(8,128)S(1)}, u32[]{:S(2)}, u32[]{:S(2)}) collective-permute-start(f32[16,256]{1,0:T(8,128)S(1)} %add_add_fusion), channel_id=1, source_target_pairs={{0,8},{8,0},{16,24},{24,16},{32,40},{40,32},{48,56},{56,48},{64,72... | collective-permute-start | bytes 49160 | tf_op jit(solution)/shard_map/ppermute | solution.py:274
  53.1 1.1 collective-permute-done.3
  54.2 3.0 %collective-permute-start.4 = (f32[16,256]{1,0:T(8,128)S(1)}, f32[16,256]{1,0:T(8,128)S(1)}, u32[]{:S(2)}, u32[]{:S(2)}) collective-permute-start(f32[16,256]{1,0:T(8,128)S(1)} %add.18), channel_id=1, source_target_pairs={{0,16},{8,24},{16,0},{24,8},{32,48},{40,56},{48,32},{56,40},{64,80... | collective-permute-start | bytes 49160 | tf_op jit(solution)/shard_map/ppermute | solution.py:274
  57.2 1.1 collective-permute-done.4
  58.3 0.0 copy-start.5
  58.3 6.1 %collective-permute-start.5 = (f32[16,256]{1,0:T(8,128)S(1)}, f32[16,256]{1,0:T(8,128)S(1)}, u32[]{:S(2)}, u32[]{:S(2)}) collective-permute-start(f32[16,256]{1,0:T(8,128)S(1)} %add.19.first_ref), channel_id=1, source_target_pairs={{0,32},{8,40},{16,48},{24,56},{32,0},{40,8},{48,16},{56,24},{64,96... | collective-permute-start | bytes 49160 | tf_op jit(solution)/shard_map/ppermute | solution.py:274
  64.4 1.2 collective-permute-done.5.second_ref
  65.6 0.0 copy-done.5
  65.6 0.0 copy-start.6
  65.6 0.6 copy-done.6
  66.2 2.0 %cuts.1.c0 = f32[16,256]{1,0:T(8,128)} custom-call(s32[64,256]{1,0:T(8,128)} %codes_ref.1, s32[64,256]{1,0:T(8,128)} %ranks_ref.1, f32[16,256]{1,0:T(8,128)} %copy-done.5, f32[16,256]{1,0:T(8,128)} %copy-done.6), custom_call_target="tpu_custom_call" | custom-call | tf_op jit(solution)/shard_map/cuts/pallas_call | solution.py:211
  68.2 0.1 collective-permute-start.8
  68.2 0.8 collective-permute-start.7
  69.1 0.6 collective-permute-start.6
  69.7 1.3 %collective-permute-done.8.c3 = f32[16,256]{1,0:T(8,128)S(1)} collective-permute-done((f32[16,256]{1,0:T(8,128)}, f32[16,256]{1,0:T(8,128)S(1)}, u32[]{:S(2)}, u32[]{:S(2)}) %collective-permute-start.8) | collective-permute-done | bytes 16416 | tf_op jit(solution)/shard_map/ppermute | solution.py:278
  71.0 1.6 %collective-permute-done.7.c2 = f32[16,256]{1,0:T(8,128)S(1)} collective-permute-done((f32[16,256]{1,0:T(8,128)}, f32[16,256]{1,0:T(8,128)S(1)}, u32[]{:S(2)}, u32[]{:S(2)}) %collective-permute-start.7) | collective-permute-done | bytes 16416 | tf_op jit(solution)/shard_map/ppermute | solution.py:278
  72.5 0.9 collective-permute-done.6.c1
  73.4 0.0 copy-start.4
  73.4 0.7 copy-done.4
  74.1 10.5 %place.1 = f32[8,64,1024]{2,1,0:T(8,128)S(1)} custom-call(f32[16,256]{1,0:T(8,128)S(1)} %copy-done.4, f32[16,256]{1,0:T(8,128)S(1)} %collective-permute-done.6.c1, f32[16,256]{1,0:T(8,128)S(1)} %collective-permute-done.7.c2, f32[16,256]{1,0:T(8,128)S(1)} %collective-permute-done.8.c3, f32[64,8192]{1,0:T(8,128)S(1)} %copy-done.1), custom_call_target="tpu_custom_call" | custom-call | tf_op jit(solution)/shard_map/place/pallas_call | solution.py:262
  84.6 35.6 %all_to_all.5 = f32[8,64,1024]{2,1,0:T(8,128)S(1)} all-to-all(f32[8,64,1024]{2,1,0:T(8,128)S(1)} %place.1), channel_id=1, replica_groups=mesh['rows'=32,'feat'=8] {'feat'}, dimensions={0} | all-to-all | bytes 4194304 | tf_op jit(solution)/shard_map/all_to_all | solution.py:292
  120.2 1.3 %copy.6 = f32[512,1024]{1,0:T(8,128)} copy(f32[512,1024]{1,0:T(8,128)S(1)} %bitcast.1) | data formatting | bytes 4194304
  (4 shorter events, 0.0 us)
Async XLA Ops:
  16.5 1.6 %copy-start = (f32[64,8192]{1,0:T(8,128)S(1)}, f32[64,8192]{1,0:T(8,128)}, u32[]{:S(2)}) copy-start(f32[64,8192]{1,0:T(8,128)} %values_ref.1) | copy-start | bytes 6291460
  18.1 0.8 copy-start.2
  20.8 6.7 %copy-start.1 = (f32[64,8192]{1,0:T(8,128)S(1)}, f32[64,8192]{1,0:T(8,128)}, u32[]{:S(2)}) copy-start(f32[64,8192]{1,0:T(8,128)} %values_ref.1) | copy-start | bytes 6291460
  20.9 6.7 %copy-start.3 = (s32[64,256]{1,0:T(8,128)S(1)}, s32[64,256]{1,0:T(8,128)}, u32[]{:S(2)}) copy-start(s32[64,256]{1,0:T(8,128)} %codes_ref.1) | copy-start | bytes 196612
  25.9 25.4 %collective-permute-start.1 = (f32[16,256]{1,0:T(8,128)S(1)}, f32[16,256]{1,0:T(8,128)S(1)}, u32[]{:S(2)}, u32[]{:S(2)}) collective-permute-start(f32[16,256]{1,0:T(8,128)S(1)} %hist.6), channel_id=1, source_target_pairs={{0,128},{8,136},{16,144},{24,152},{32,160},{40,168},{48,176},{56,1... | collective-permute-start | bytes 49160 | tf_op jit(solution)/shard_map/ppermute | solution.py:278
  34.5 16.8 %collective-permute-start = (f32[16,256]{1,0:T(8,128)S(1)}, f32[16,256]{1,0:T(8,128)S(1)}, u32[]{:S(2)}, u32[]{:S(2)}) collective-permute-start(f32[16,256]{1,0:T(8,128)S(1)} %hist.5), channel_id=1, source_target_pairs={{0,64},{8,72},{16,80},{24,88},{32,96},{40,104},{48,112},{56,120},{... | collective-permute-start | bytes 49160 | tf_op jit(solution)/shard_map/ppermute | solution.py:278
  41.8 9.6 %collective-permute-start.2 = (f32[16,256]{1,0:T(8,128)S(1)}, f32[16,256]{1,0:T(8,128)S(1)}, u32[]{:S(2)}, u32[]{:S(2)}) collective-permute-start(f32[16,256]{1,0:T(8,128)S(1)} %hist.7), channel_id=1, source_target_pairs={{0,192},{8,200},{16,208},{24,216},{32,224},{40,232},{48,240},{56,2... | collective-permute-start | bytes 49160 | tf_op jit(solution)/shard_map/ppermute | solution.py:278
  51.3 2.9 %collective-permute-start.3 = (f32[16,256]{1,0:T(8,128)S(1)}, f32[16,256]{1,0:T(8,128)S(1)}, u32[]{:S(2)}, u32[]{:S(2)}) collective-permute-start(f32[16,256]{1,0:T(8,128)S(1)} %add_add_fusion), channel_id=1, source_target_pairs={{0,8},{8,0},{16,24},{24,16},{32,40},{40,32},{48,56},{56,48},{64,72... | collective-permute-start | bytes 49160 | tf_op jit(solution)/shard_map/ppermute | solution.py:274
  54.2 4.1 %collective-permute-start.4 = (f32[16,256]{1,0:T(8,128)S(1)}, f32[16,256]{1,0:T(8,128)S(1)}, u32[]{:S(2)}, u32[]{:S(2)}) collective-permute-start(f32[16,256]{1,0:T(8,128)S(1)} %add.18), channel_id=1, source_target_pairs={{0,16},{8,24},{16,0},{24,8},{32,48},{40,56},{48,32},{56,40},{64,80... | collective-permute-start | bytes 49160 | tf_op jit(solution)/shard_map/ppermute | solution.py:274
  58.3 7.3 %copy-start.5 = (f32[16,256]{1,0:T(8,128)}, f32[16,256]{1,0:T(8,128)S(1)}, u32[]{:S(2)}) copy-start(f32[16,256]{1,0:T(8,128)S(1)} %add.19.first_ref) | copy-start | bytes 49156
  58.3 7.3 %collective-permute-start.5 = (f32[16,256]{1,0:T(8,128)S(1)}, f32[16,256]{1,0:T(8,128)S(1)}, u32[]{:S(2)}, u32[]{:S(2)}) collective-permute-start(f32[16,256]{1,0:T(8,128)S(1)} %add.19.first_ref), channel_id=1, source_target_pairs={{0,32},{8,40},{16,48},{24,56},{32,0},{40,8},{48,16},{56,24},{64,96... | collective-permute-start | bytes 49160 | tf_op jit(solution)/shard_map/ppermute | solution.py:274
  65.6 0.6 copy-start.6
  68.2 2.8 %collective-permute-start.8 = (f32[16,256]{1,0:T(8,128)}, f32[16,256]{1,0:T(8,128)S(1)}, u32[]{:S(2)}, u32[]{:S(2)}) collective-permute-start(f32[16,256]{1,0:T(8,128)} %cuts.1.c0), channel_id=1, source_target_pairs={{0,192},{8,200},{16,208},{24,216},{32,224},{40,232},{48,240},{56,2... | collective-permute-start | bytes 49160 | tf_op jit(solution)/shard_map/ppermute | solution.py:278
  68.2 4.3 %collective-permute-start.7 = (f32[16,256]{1,0:T(8,128)}, f32[16,256]{1,0:T(8,128)S(1)}, u32[]{:S(2)}, u32[]{:S(2)}) collective-permute-start(f32[16,256]{1,0:T(8,128)} %cuts.1.c0), channel_id=1, source_target_pairs={{0,128},{8,136},{16,144},{24,152},{32,160},{40,168},{48,176},{56,1... | collective-permute-start | bytes 49160 | tf_op jit(solution)/shard_map/ppermute | solution.py:278
  69.1 4.3 %collective-permute-start.6 = (f32[16,256]{1,0:T(8,128)}, f32[16,256]{1,0:T(8,128)S(1)}, u32[]{:S(2)}, u32[]{:S(2)}) collective-permute-start(f32[16,256]{1,0:T(8,128)} %cuts.1.c0), channel_id=1, source_target_pairs={{0,64},{8,72},{16,80},{24,88},{32,96},{40,104},{48,112},{56,120},{... | collective-permute-start | bytes 49160 | tf_op jit(solution)/shard_map/ppermute | solution.py:278
  73.4 0.7 copy-start.4

commit v3 on v2

--- a/solution.py
+++ b/solution.py
@@ -119,8 +119,9 @@
     high = jnp.floor(scaled * (1.0 / 256.0))
     rest = scaled - high * 256.0
     wide = hess_ref.shape[1]
+    me = lax.axis_index("feat")
     for part in range(rows // wide):
-        own = slice(part * wide, (part + 1) * wide)
+        own = pl.ds(pl.multiple_of((part ^ me) * wide, wide), wide)
         high_ref[:, own] = jnp.broadcast_to(high[part : part + 1], (FEATS, wide)).astype(jnp.bfloat16)
         rest_ref[:, own] = jnp.broadcast_to(rest[part : part + 1], (FEATS, wide)).astype(jnp.bfloat16)
 
@@ -149,19 +150,20 @@
 
     lax.fori_loop(0, rows // SPAN, step, 0)
 
-    for parity in range(2):
-        point = 2 * lane + parity - 1
-        column = (point & 7) * FEATS + feat
-        result = jnp.zeros(shape, jnp.float32)
-        before = jnp.zeros(shape, jnp.float32)
-        for k in range(16):
-            large = sum_ref[k * FEATS : (k + 1) * FEATS]
-            small = sum_ref[(16 + k) * FEATS : (17 + k) * FEATS]
-            block = (large * 256.0 + small) * (1.0 / 65536.0)
+    points = [2 * lane - 1, 2 * lane]
+    columns = [(point & 7) * FEATS + feat for point in points]
+    results = [jnp.zeros(shape, jnp.float32)] * 2
+    before = jnp.zeros(shape, jnp.float32)
+    for k in range(16):
+        large = sum_ref[k * FEATS : (k + 1) * FEATS]
+        small = sum_ref[(16 + k) * FEATS : (17 + k) * FEATS]
+        block = (large * 256.0 + small) * (1.0 / 65536.0)
+        for parity, (point, column) in enumerate(zip(points, columns)):
             here = jnp.where((point & 15) < 8, lane_take(block[:, :LANES], column), lane_take(block[:, LANES:], column))
-            result = jnp.where((point >> 4) == k, before + here, result)
-            before = before + lane_take(block[:, LANES:], 7 * FEATS + feat)
-        mass_ref[:, parity * LANES : (parity + 1) * LANES] = result
+            results[parity] = jnp.where((point >> 4) == k, before + here, results[parity])
+        before = before + lane_take(block[:, LANES:], 7 * FEATS + feat)
+    mass_ref[:, :LANES] = results[0]
+    mass_ref[:, LANES:] = results[1]
 
 
 def find_mass(hess, top, low):
@@ -213,6 +215,7 @@
         in_specs=in_vmem(4),
         out_specs=in_vmem(1)[0],
         out_shape=jax.ShapeDtypeStruct((FEATS, 256), jnp.float32),
+        compiler_params=pltpu.CompilerParams(vmem_limit_bytes=4 << 20),
         name="cuts",
     )(edge_codes, cut_ranks, first, second)
 
@@ -236,20 +239,29 @@
         write(index, jnp.where(value >= last, 256.0 + (value - last) * inv_last, inside))
 
 
-def place_kernel(c0, c1, c2, c3, values_ref, out_ref, cuts_ref):
-    blocks, feats, wide = out_ref.shape
+def first_kernel(moves, c0, c1, c2, c3, values_ref, cuts_ref, *out_refs):
     mine = lax.axis_index("rows") // 8
     for turn, c_ref in enumerate((c0, c1, c2, c3)):
         group = (mine + 4 - turn) % 4
         cuts_ref[pl.ds(pl.multiple_of(group * FEATS, FEATS), FEATS), :] = c_ref[...]
+    place_kernel(moves, cuts_ref, values_ref, *out_refs)
+
+
+def place_kernel(moves, cuts_ref, values_ref, *out_refs):
+    feats, wide = out_refs[0].shape
+    bases = [owner(move) * wide for move in moves]
 
     def step(index, carry):
         at = pl.ds(pl.multiple_of(index * 8, 8), 8)
-        values = [values_ref[at, part * LANES : (part + 1) * LANES] for part in range(blocks * wide // LANES)]
+        values, places = [], []
+        for base, out_ref in zip(bases, out_refs):
+            for part in range(0, wide, LANES):
+                values.append(values_ref[at, pl.ds(pl.multiple_of(base + part, LANES), LANES)])
+                places.append((out_ref, part))
 
         def write(part, value):
-            lanes = part * LANES % wide
-            out_ref[part * LANES // wide, at, lanes : lanes + LANES] = value
+            out_ref, lanes = places[part]
+            out_ref[at, lanes : lanes + LANES] = value
 
         place_group(cuts_ref[at, :LANES], cuts_ref[at, LANES:], values, write)
         return carry
@@ -257,19 +269,63 @@
     lax.fori_loop(0, feats // 8, step, 0)
 
 
-def place(cuts, values):
+def place(moves, cuts, values):
     feats, rows = values.shape
-    return pl.pallas_call(
-        place_kernel,
-        in_specs=in_vmem(5),
-        out_specs=in_vmem(1)[0],
-        out_shape=jax.ShapeDtypeStruct((8, feats, rows // 8), jnp.float32),
-        scratch_shapes=[pltpu.VMEM((feats, 256), jnp.float32)],
+    block = jax.ShapeDtypeStruct((feats, rows // 8), jnp.float32)
+    first = len(cuts) > 1
+    kernel = first_kernel if first else place_kernel
+    outs = [jax.ShapeDtypeStruct((feats, 256), jnp.float32)] * first + [block] * len(moves)
+    return pl.pallas_call(
+        lambda *refs: kernel(moves, *refs),
+        in_specs=in_vmem(len(cuts) + 1),
+        out_specs=in_vmem(len(outs)),
+        out_shape=outs,
         compiler_params=pltpu.CompilerParams(vmem_limit_bytes=16 << 20),
+        cost_estimate=pl.CostEstimate(flops=10**7 * len(moves), bytes_accessed=10**6, transcendentals=0),
         name="place",
     )(*cuts, values)
 
 
+def join_kernel(moves, *refs):
+    *parts, out_ref, sems = refs
+    feats = parts[0].shape[0]
+    copies = []
+    for index, (move, part) in enumerate(zip(moves, parts)):
+        back = (-move[0], move[1])
+        rows = pl.ds(pl.multiple_of(owner(back) * feats, feats), feats)
+        copies.append(pltpu.make_async_copy(part, out_ref.at[rows, :], sems.at[index]))
+    for copy in copies:
+        copy.start()
+    for copy in copies:
+        copy.wait()
+
+
+def join(moves, parts):
+    feats, wide = parts[0].shape
+    return pl.pallas_call(
+        lambda *refs: join_kernel(moves, *refs),
+        in_specs=in_vmem(len(parts)),
+        out_specs=pl.BlockSpec(memory_space=pl.ANY),
+        out_shape=jax.ShapeDtypeStruct((len(parts) * feats, wide), jnp.float32),
+        scratch_shapes=[pltpu.SemaphoreType.DMA((len(parts),))],
+        compiler_params=pltpu.CompilerParams(vmem_limit_bytes=4 << 20),
+        name="join",
+    )(*parts)
+
+
+def owner(move):
+    me = lax.axis_index("feat")
+    return (me // 2 + move[0] + 4) % 4 * 2 + (me % 2 ^ move[1])
+
+
+def send_feat(array, move):
+    return lax.ppermute(array, "feat", [(i, (i // 2 + move[0]) % 4 * 2 + (i % 2 ^ move[1])) for i in range(8)])
+
+
+def flip_feat(array, flip):
+    return lax.ppermute(array, "feat", [(i, i ^ flip) for i in range(8)])
+
+
 def flip_rows(array, flip):
     return lax.ppermute(array, "rows", [(i, i ^ flip) for i in range(32)])
 
@@ -280,7 +336,9 @@
 
 def on_device(feature_values, hessian_codes, edge_codes, cut_ranks):
     hess_own = hessian_codes.astype(jnp.float32) * (1.0 / 65536.0)
-    hess = lax.all_gather(hess_own, "feat", axis=0)
+    hess = hess_own.reshape(1, -1)
+    for flip in (1, 2, 4):
+        hess = jnp.concatenate([hess, flip_feat(hess, flip)], axis=0)
     slots = [find_slots(turn, edge_codes, feature_values) for turn in range(4)]
     parts = [turn_rows(find_mass(hess, *slots[turn]), turn) for turn in (1, 2, 3)]
     mass = find_mass(hess, *slots[0]) + parts[0] + parts[1] + parts[2]
@@ -288,8 +346,16 @@
         mass = mass + flip_rows(mass, flip)
     cuts = find_cuts(edge_codes, cut_ranks, mass, flip_rows(mass, 4))
     cuts = [cuts] + [turn_rows(cuts, turn) for turn in (1, 2, 3)]
-    positions = place(cuts, feature_values)
-    return lax.all_to_all(positions, "feat", split_axis=0, concat_axis=0, tiled=True).reshape(512, -1)
+    stages = [[(2, 0), (2, 1)], [(1, 0), (3, 0)], [(1, 1), (3, 1)], [(0, 1), (0, 0)]]
+    moves, parts = [], []
+    for stage in stages:
+        outs = place(stage, cuts, feature_values)
+        if len(cuts) > 1:
+            cuts, *outs = outs
+            cuts = [cuts]
+        moves += stage
+        parts += [send_feat(out, move) if move != (0, 0) else out for out, move in zip(outs, stage)]
+    return join(moves, parts)
 
 
 def solution(mesh):

time: 122 us -> 106 us (0.87)
  blocking collectives: 51.4 us -> 0 us
  starting transfers between devices: 16.9 us -> 39.1 us
  waiting for transfers between devices: 7.22 us -> 16.2 us
  Pallas kernels: 40 us -> 46.6 us
  local copies, waits for them, and re-layouts: 5.09 us -> 2.44 us
    all_to_all x1 -> x0, blocking collectives: 35.6 us -> none  [on_device(): lax.all_to_all(positions, 'feat', split_axis=0, concat_axis=0, tiled=True)]
    ppermute x0 -> x10, starting transfers between devices: none -> 20.9 us  [the longest x7 16.3 us: send_feat(): lax.ppermute(array, 'feat', [(i, (i // 2 + move[0]) % 4 * 2 + (i % 2 ^ mo...]
    all_gather x1 -> x0, blocking collectives: 15.8 us -> none  [on_device(): hess = lax.all_gather(hess_own, 'feat', axis=0)]
    ppermute x0 -> x10, waiting for transfers between devices: none -> 9.25 us  [the longest x7 5.93 us: send_feat(): lax.ppermute(array, 'feat', [(i, (i // 2 + move[0]) % 4 * 2 + (i % 2 ^ mo...]
    pallas_call x1 -> x5, Pallas kernels: 10.5 us -> 18.6 us  [the longest x4 17.2 us: place(): pl.pallas_call(lambda *refs: kernel(moves, *refs), in_specs=in_vmem(len(c...]
    unnamed x15 -> x10, local copies, waits for them, and re-layouts: 5.08 us -> 2.44 us
    pallas_call x1, Pallas kernels: 1.96 us -> 0.49 us  [find_cuts(): pl.pallas_call(cuts_kernel, in_specs=in_vmem(4), out_specs=in_vmem(1)[0],...]
    ppermute x6, starting transfers between devices: 6.09 us -> 7.39 us  [turn_rows(): lax.ppermute(array, 'rows', [(i, (i + 8 * turn) % 32) for i in range(32)])]
  transfers between devices with their start and end apart: 9 -> 19, of which waited for: 6 -> 9; matrix products, arithmetic and copies ran while one was open for 0% -> 0% of each run, Pallas kernels for 17% -> 34%
where the time goes in v3:
time: 106 us; the launch traced here: 105 us
  Pallas kernels  46.6 us (44%)
  starting transfers between devices  39.1 us (37%)
  waiting for transfers between devices  16.2 us (15%)
  local copies, waits for them, and re-layouts  2.44 us (2%)
    pallas_call x4, Pallas kernels, find_mass(): pl.pallas_call(hist_kernel, in_specs=in_vmem(3), out_specs=in_vmem(1)[0],...  20.1 us
    pallas_call x4, Pallas kernels, place(): pl.pallas_call(lambda *refs: kernel(moves, *refs), in_specs=in_vmem(len(c...  17.2 us
    ppermute x7, starting transfers between devices, send_feat(): lax.ppermute(array, 'feat', [(i, (i // 2 + move[0]) % 4 * 2 + (i % 2 ^ mo...  16.3 us
    ppermute x3, starting transfers between devices, flip_rows(): return lax.ppermute(array, 'rows', [(i, i ^ flip) for i in range(32)])  10.8 us
    pallas_call x4, Pallas kernels, find_slots(): pl.pallas_call(lambda *refs: slot_kernel(turn, *refs), in_specs=in_vmem(2...  7.48 us
    ppermute x6, starting transfers between devices, turn_rows(): lax.ppermute(array, 'rows', [(i, (i + 8 * turn) % 32) for i in range(32)])  7.39 us
    ppermute x7, waiting for transfers between devices, send_feat(): lax.ppermute(array, 'feat', [(i, (i // 2 + move[0]) % 4 * 2 + (i % 2 ^ mo...  5.93 us
    ppermute x3, starting transfers between devices, flip_feat(): return lax.ppermute(array, 'feat', [(i, i ^ flip) for i in range(8)])  4.6 us
  transfers between devices with their start and end apart: 19, of which 9 were waited for; matrix products, arithmetic and copies ran while one was open for 0% of the time, Pallas kernels for 34%

profile of v3, /device:TPU:1, one launch (start us, length us, event | category | flops | bytes accessed | tf_op | source)
XLA Modules:
  0.0 105.4 jit_solution(6859492846872862211)
XLA Ops:
  0.0 0.7 convert_multiply_fusion
  0.7 3.2 %collective-permute-start = (f32[1,1024]{1,0:T(1,128)S(1)}, f32[1,1024]{1,0:T(1,128)S(1)}, u32[]{:S(2)}, u32[]{:S(2)}) collective-permute-start(f32[1,1024]{1,0:T(1,128)S(1)} %bitcast.1), channel_id=1, source_target_pairs={{0,1},{1,0},{2,3},{3,2},{4,5},{5,4},{6,7},{7,6},{8,9},{9,8},{10,11... | collective-permute-start | bytes 12296 | tf_op jit(solution)/shard_map/ppermute | solution.py:326
  3.9 0.8 collective-permute-done
  4.8 0.1 collective-permute-start.1
  4.9 2.5 %collective-permute-done.1 = f32[2,1024]{1,0:T(2,128)S(1)} collective-permute-done((f32[2,1024]{1,0:T(2,128)S(1)}, f32[2,1024]{1,0:T(2,128)S(1)}, u32[]{:S(2)}, u32[]{:S(2)}) %collective-permute-start.1) | collective-permute-done | bytes 8224 | tf_op jit(solution)/shard_map/ppermute | solution.py:326
  7.4 1.3 %collective-permute-start.2 = (f32[4,1024]{1,0:T(4,128)S(1)}, f32[4,1024]{1,0:T(4,128)S(1)}, u32[]{:S(2)}, u32[]{:S(2)}) collective-permute-start(f32[4,1024]{1,0:T(4,128)S(1)} %pad_maximum_fusion.1), channel_id=1, source_target_pairs={{0,4},{1,5},{2,6},{3,7},{4,0},{5,1},{6,2},{7,3},{8,12},{9,13},{10,... | collective-permute-start | bytes 49160 | tf_op jit(solution)/shard_map/ppermute | solution.py:326
  8.6 1.6 %copy-done = f32[64,8192]{1,0:T(8,128)S(1)} copy-done((f32[64,8192]{1,0:T(8,128)S(1)}, f32[64,8192]{1,0:T(8,128)}, u32[]{:S(2)}) %copy-start) | copy-done | bytes 2097176
  10.2 0.8 copy-done.2
  11.1 1.9 %slots.6 = (bf16[16,8192]{1,0:T(8,128)(2,1)S(1)}, bf16[16,8192]{1,0:T(8,128)(2,1)S(1)}) custom-call(s32[64,256]{1,0:T(8,128)S(1)} %copy-done.2, f32[64,8192]{1,0:T(8,128)S(1)} %copy-done), custom_call_target="tpu_custom_call" | custom-call | flops 10000000 | bytes 10000000 | tf_op jit(solution)/shard_map/slots/pallas_call | solution.py:100
  12.9 1.9 %slots.5 = (bf16[16,8192]{1,0:T(8,128)(2,1)S(1)}, bf16[16,8192]{1,0:T(8,128)(2,1)S(1)}) custom-call(s32[64,256]{1,0:T(8,128)S(1)} %copy-done.2, f32[64,8192]{1,0:T(8,128)S(1)} %copy-done), custom_call_target="tpu_custom_call" | custom-call | flops 10000000 | bytes 10000000 | tf_op jit(solution)/shard_map/slots/pallas_call | solution.py:100
  14.8 1.9 %slots.4 = (bf16[16,8192]{1,0:T(8,128)(2,1)S(1)}, bf16[16,8192]{1,0:T(8,128)(2,1)S(1)}) custom-call(s32[64,256]{1,0:T(8,128)S(1)} %copy-done.2, f32[64,8192]{1,0:T(8,128)S(1)} %copy-done), custom_call_target="tpu_custom_call" | custom-call | flops 10000000 | bytes 10000000 | tf_op jit(solution)/shard_map/slots/pallas_call | solution.py:100
  16.7 1.9 %slots.7 = (bf16[16,8192]{1,0:T(8,128)(2,1)S(1)}, bf16[16,8192]{1,0:T(8,128)(2,1)S(1)}) custom-call(s32[64,256]{1,0:T(8,128)S(1)} %copy-done.2, f32[64,8192]{1,0:T(8,128)S(1)} %copy-done), custom_call_target="tpu_custom_call" | custom-call | flops 10000000 | bytes 10000000 | tf_op jit(solution)/shard_map/slots/pallas_call | solution.py:100
  18.6 0.0 collective-permute-done.2
  18.6 5.0 %hist.6 = f32[16,256]{1,0:T(8,128)S(1)} custom-call(f32[8,1024]{1,0:T(8,128)S(1)} %pad_maximum_fusion.hess_ref, bf16[16,8192]{1,0:T(8,128)(2,1)S(1)} %get-tuple-element.26.top_ref, bf16[16,8192]{1,0:T(8,128)(2,1)S(1)} %get-tuple-element.27.low_ref), custom_call_target="tpu_custom_call" | custom-call | flops 4000000000 | bytes 10000000 | tf_op jit(solution)/shard_map/hist/pallas_call | solution.py:171
  23.7 2.8 %collective-permute-start.4 = (f32[16,256]{1,0:T(8,128)S(1)}, f32[16,256]{1,0:T(8,128)S(1)}, u32[]{:S(2)}, u32[]{:S(2)}) collective-permute-start(f32[16,256]{1,0:T(8,128)S(1)} %hist.6), channel_id=1, source_target_pairs={{0,128},{8,136},{16,144},{24,152},{32,160},{40,168},{48,176},{56,1... | collective-permute-start | bytes 49160 | tf_op jit(solution)/shard_map/ppermute | solution.py:334
  26.5 5.0 %hist.5 = f32[16,256]{1,0:T(8,128)S(1)} custom-call(f32[8,1024]{1,0:T(8,128)S(1)} %pad_maximum_fusion.hess_ref, bf16[16,8192]{1,0:T(8,128)(2,1)S(1)} %get-tuple-element.24.top_ref, bf16[16,8192]{1,0:T(8,128)(2,1)S(1)} %get-tuple-element.25.low_ref), custom_call_target="tpu_custom_call" | custom-call | flops 4000000000 | bytes 10000000 | tf_op jit(solution)/shard_map/hist/pallas_call | solution.py:171
  31.5 0.4 collective-permute-start.3
  31.9 5.0 %hist.7 = f32[16,256]{1,0:T(8,128)S(1)} custom-call(f32[8,1024]{1,0:T(8,128)S(1)} %pad_maximum_fusion.hess_ref, bf16[16,8192]{1,0:T(8,128)(2,1)S(1)} %get-tuple-element.28.top_ref, bf16[16,8192]{1,0:T(8,128)(2,1)S(1)} %get-tuple-element.29.low_ref), custom_call_target="tpu_custom_call" | custom-call | flops 4000000000 | bytes 10000000 | tf_op jit(solution)/shard_map/hist/pallas_call | solution.py:171
  36.9 2.6 %collective-permute-start.5 = (f32[16,256]{1,0:T(8,128)S(1)}, f32[16,256]{1,0:T(8,128)S(1)}, u32[]{:S(2)}, u32[]{:S(2)}) collective-permute-start(f32[16,256]{1,0:T(8,128)S(1)} %hist.7), channel_id=1, source_target_pairs={{0,192},{8,200},{16,208},{24,216},{32,224},{40,232},{48,240},{56,2... | collective-permute-start | bytes 49160 | tf_op jit(solution)/shard_map/ppermute | solution.py:334
  39.6 5.0 %hist.4 = f32[16,256]{1,0:T(8,128)S(1)} custom-call(f32[8,1024]{1,0:T(8,128)S(1)} %pad_maximum_fusion.hess_ref, bf16[16,8192]{1,0:T(8,128)(2,1)S(1)} %get-tuple-element.22.top_ref, bf16[16,8192]{1,0:T(8,128)(2,1)S(1)} %get-tuple-element.23.low_ref), custom_call_target="tpu_custom_call" | custom-call | flops 4000000000 | bytes 10000000 | tf_op jit(solution)/shard_map/hist/pallas_call | solution.py:171
  44.6 0.0 collective-permute-done.5
  44.6 1.7 %collective-permute-start.6 = (f32[16,256]{1,0:T(8,128)S(1)}, f32[16,256]{1,0:T(8,128)S(1)}, u32[]{:S(2)}, u32[]{:S(2)}) collective-permute-start(f32[16,256]{1,0:T(8,128)S(1)} %add_add_fusion), channel_id=1, source_target_pairs={{0,8},{8,0},{16,24},{24,16},{32,40},{40,32},{48,56},{56,48},{64,72... | collective-permute-start | bytes 49160 | tf_op jit(solution)/shard_map/ppermute | solution.py:330
  46.4 1.1 %collective-permute-done.6 = f32[16,256]{1,0:T(8,128)S(1)} collective-permute-done((f32[16,256]{1,0:T(8,128)S(1)}, f32[16,256]{1,0:T(8,128)S(1)}, u32[]{:S(2)}, u32[]{:S(2)}) %collective-permute-start.6) | collective-permute-done | bytes 16416 | tf_op jit(solution)/shard_map/ppermute | solution.py:330
  47.5 3.0 %collective-permute-start.7 = (f32[16,256]{1,0:T(8,128)S(1)}, f32[16,256]{1,0:T(8,128)S(1)}, u32[]{:S(2)}, u32[]{:S(2)}) collective-permute-start(f32[16,256]{1,0:T(8,128)S(1)} %add.18), channel_id=1, source_target_pairs={{0,16},{8,24},{16,0},{24,8},{32,48},{40,56},{48,32},{56,40},{64,80... | collective-permute-start | bytes 49160 | tf_op jit(solution)/shard_map/ppermute | solution.py:330
  50.5 1.1 %collective-permute-done.7 = f32[16,256]{1,0:T(8,128)S(1)} collective-permute-done((f32[16,256]{1,0:T(8,128)S(1)}, f32[16,256]{1,0:T(8,128)S(1)}, u32[]{:S(2)}, u32[]{:S(2)}) %collective-permute-start.7) | collective-permute-done | bytes 16416 | tf_op jit(solution)/shard_map/ppermute | solution.py:330
  51.6 6.1 %collective-permute-start.8 = (f32[16,256]{1,0:T(8,128)S(1)}, f32[16,256]{1,0:T(8,128)S(1)}, u32[]{:S(2)}, u32[]{:S(2)}) collective-permute-start(f32[16,256]{1,0:T(8,128)S(1)} %add.19.first_ref), channel_id=1, source_target_pairs={{0,32},{8,40},{16,48},{24,56},{32,0},{40,8},{48,16},{56,24},{64,96... | collective-permute-start | bytes 49160 | tf_op jit(solution)/shard_map/ppermute | solution.py:330
  57.7 1.1 %collective-permute-done.8.second_ref = f32[16,256]{1,0:T(8,128)S(1)} collective-permute-done((f32[16,256]{1,0:T(8,128)S(1)}, f32[16,256]{1,0:T(8,128)S(1)}, u32[]{:S(2)}, u32[]{:S(2)}) %collective-permute-start.8) | collective-permute-done | bytes 16416 | tf_op jit(solution)/shard_map/ppermute | solution.py:330
  58.9 0.5 cuts.1.refs_0_
  59.4 0.1 collective-permute-start.11
  59.5 0.8 collective-permute-start.10
  60.3 0.6 collective-permute-start.9
  60.9 1.4 %collective-permute-done.11.refs_3_ = f32[16,256]{1,0:T(8,128)S(1)} collective-permute-done((f32[16,256]{1,0:T(8,128)S(1)}, f32[16,256]{1,0:T(8,128)S(1)}, u32[]{:S(2)}, u32[]{:S(2)}) %collective-permute-start.11) | collective-permute-done | bytes 16416 | tf_op jit(solution)/shard_map/ppermute | solution.py:334
  62.3 1.6 %collective-permute-done.10.refs_2_ = f32[16,256]{1,0:T(8,128)S(1)} collective-permute-done((f32[16,256]{1,0:T(8,128)S(1)}, f32[16,256]{1,0:T(8,128)S(1)}, u32[]{:S(2)}, u32[]{:S(2)}) %collective-permute-start.10) | collective-permute-done | bytes 16416 | tf_op jit(solution)/shard_map/ppermute | solution.py:334
  63.9 0.5 collective-permute-done.9.refs_1_
  64.4 4.3 %place.4 = (f32[64,256]{1,0:T(8,128)S(1)}, f32[64,1024]{1,0:T(8,128)S(1)}, f32[64,1024]{1,0:T(8,128)S(1)}) custom-call(f32[16,256]{1,0:T(8,128)S(1)} %cuts.1.refs_0_, f32[16,256]{1,0:T(8,128)S(1)} %collective-permute-done.9.refs_1_, f32[16,256]{1,0:T(8,128)S(1)} %collective-permute-done.10.refs_2_, f32[16,256]{1,0:T(8,128)S(1)} %collective-permute-done.11.refs_3_, ...), custom_call_target="tpu_custom_call" | custom-call | flops 20000000 | bytes 1000000 | tf_op jit(solution)/shard_map/place/pallas_call | solution.py:278
  68.7 0.1 collective-permute-start.12
  68.9 10.3 %collective-permute-start.13 = (f32[64,1024]{1,0:T(8,128)S(1)}, f32[64,1024]{1,0:T(8,128)S(1)}, u32[]{:S(2)}, u32[]{:S(2)}) collective-permute-start(f32[64,1024]{1,0:T(8,128)S(1)} %get-tuple-element.31), channel_id=1, source_target_pairs={{0,5},{1,4},{2,7},{3,6},{4,1},{5,0},{6,3},{7,2},{8,13},{9,12},{10,... | collective-permute-start | bytes 786440 | tf_op jit(solution)/shard_map/ppermute | solution.py:322
  79.2 4.3 %place.7 = (f32[64,1024]{1,0:T(8,128)S(1)}, f32[64,1024]{1,0:T(8,128)S(1)}) custom-call(f32[64,256]{1,0:T(8,128)S(1)} %get-tuple-element.32.refs_0_, f32[64,8192]{1,0:T(8,128)S(1)} %copy-done.1), custom_call_target="tpu_custom_call" | custom-call | flops 20000000 | bytes 1000000 | tf_op jit(solution)/shard_map/place/pallas_call | solution.py:278
  83.4 0.1 collective-permute-start.18
  83.5 4.3 %place.6 = (f32[64,1024]{1,0:T(8,128)S(1)}, f32[64,1024]{1,0:T(8,128)S(1)}) custom-call(f32[64,256]{1,0:T(8,128)S(1)} %get-tuple-element.32.refs_0_, f32[64,8192]{1,0:T(8,128)S(1)} %copy-done.1), custom_call_target="tpu_custom_call" | custom-call | flops 20000000 | bytes 1000000 | tf_op jit(solution)/shard_map/place/pallas_call | solution.py:278
  87.9 0.8 collective-permute-start.16
  88.7 2.2 %collective-permute-start.17 = (f32[64,1024]{1,0:T(8,128)S(1)}, f32[64,1024]{1,0:T(8,128)S(1)}, u32[]{:S(2)}, u32[]{:S(2)}) collective-permute-start(f32[64,1024]{1,0:T(8,128)S(1)} %get-tuple-element.36), channel_id=1, source_target_pairs={{0,7},{1,6},{2,1},{3,0},{4,3},{5,2},{6,5},{7,4},{8,15},{9,14},{10,... | collective-permute-start | bytes 786440 | tf_op jit(solution)/shard_map/ppermute | solution.py:322
  90.9 4.3 %place.5 = (f32[64,1024]{1,0:T(8,128)S(1)}, f32[64,1024]{1,0:T(8,128)S(1)}) custom-call(f32[64,256]{1,0:T(8,128)S(1)} %get-tuple-element.32.refs_0_, f32[64,8192]{1,0:T(8,128)S(1)} %copy-done.1), custom_call_target="tpu_custom_call" | custom-call | flops 20000000 | bytes 1000000 | tf_op jit(solution)/shard_map/place/pallas_call | solution.py:278
  95.2 0.1 collective-permute-start.14
  95.3 2.7 %collective-permute-start.15 = (f32[64,1024]{1,0:T(8,128)S(1)}, f32[64,1024]{1,0:T(8,128)S(1)}, u32[]{:S(2)}, u32[]{:S(2)}) collective-permute-start(f32[64,1024]{1,0:T(8,128)S(1)} %get-tuple-element.34), channel_id=1, source_target_pairs={{0,6},{1,7},{2,0},{3,1},{4,2},{5,3},{6,4},{7,5},{8,14},{9,15},{10,... | collective-permute-start | bytes 786440 | tf_op jit(solution)/shard_map/ppermute | solution.py:322
  98.0 0.0 collective-permute-done.18.refs_6_
  98.0 5.9 %collective-permute-done.14.refs_2_ = f32[64,1024]{1,0:T(8,128)S(1)} collective-permute-done((f32[64,1024]{1,0:T(8,128)S(1)}, f32[64,1024]{1,0:T(8,128)S(1)}, u32[]{:S(2)}, u32[]{:S(2)}) %collective-permute-start.14) | collective-permute-done | bytes 262176 | tf_op jit(solution)/shard_map/ppermute | solution.py:322
  103.9 1.4 %join.1 = f32[512,1024]{1,0:T(8,128)} custom-call(f32[64,1024]{1,0:T(8,128)S(1)} %collective-permute-done.12.refs_0_, f32[64,1024]{1,0:T(8,128)S(1)} %collective-permute-done.13.refs_1_, f32[64,1024]{1,0:T(8,128)S(1)} %collective-permute-done.14.refs_2_, f32[64,1024]{1,0:T(8,128)S(1)} %collective-permute-done.15.refs_3_, ...), custom_call_target="tpu_custom_call" | custom-call | tf_op jit(solution)/shard_map/join/pallas_call | solution.py:305
  (21 shorter events, 0.1 us)
Async XLA Ops:
  0.7 4.1 %collective-permute-start = (f32[1,1024]{1,0:T(1,128)S(1)}, f32[1,1024]{1,0:T(1,128)S(1)}, u32[]{:S(2)}, u32[]{:S(2)}) collective-permute-start(f32[1,1024]{1,0:T(1,128)S(1)} %bitcast.1), channel_id=1, source_target_pairs={{0,1},{1,0},{2,3},{3,2},{4,5},{5,4},{6,7},{7,6},{8,9},{9,8},{10,11... | collective-permute-start | bytes 12296 | tf_op jit(solution)/shard_map/ppermute | solution.py:326
  4.8 2.6 %collective-permute-start.1 = (f32[2,1024]{1,0:T(2,128)S(1)}, f32[2,1024]{1,0:T(2,128)S(1)}, u32[]{:S(2)}, u32[]{:S(2)}) collective-permute-start(f32[2,1024]{1,0:T(2,128)S(1)} %pad_maximum_fusion.2), channel_id=1, source_target_pairs={{0,2},{1,3},{2,0},{3,1},{4,6},{5,7},{6,4},{7,5},{8,10},{9,11},{10,... | collective-permute-start | bytes 24584 | tf_op jit(solution)/shard_map/ppermute | solution.py:326
  7.4 11.2 %collective-permute-start.2 = (f32[4,1024]{1,0:T(4,128)S(1)}, f32[4,1024]{1,0:T(4,128)S(1)}, u32[]{:S(2)}, u32[]{:S(2)}) collective-permute-start(f32[4,1024]{1,0:T(4,128)S(1)} %pad_maximum_fusion.1), channel_id=1, source_target_pairs={{0,4},{1,5},{2,6},{3,7},{4,0},{5,1},{6,2},{7,3},{8,12},{9,13},{10,... | collective-permute-start | bytes 49160 | tf_op jit(solution)/shard_map/ppermute | solution.py:326
  8.6 1.6 %copy-start = (f32[64,8192]{1,0:T(8,128)S(1)}, f32[64,8192]{1,0:T(8,128)}, u32[]{:S(2)}) copy-start(f32[64,8192]{1,0:T(8,128)} %refs_1_.13) | copy-start | bytes 6291460
  10.2 0.8 copy-start.2
  23.7 20.9 %collective-permute-start.4 = (f32[16,256]{1,0:T(8,128)S(1)}, f32[16,256]{1,0:T(8,128)S(1)}, u32[]{:S(2)}, u32[]{:S(2)}) collective-permute-start(f32[16,256]{1,0:T(8,128)S(1)} %hist.6), channel_id=1, source_target_pairs={{0,128},{8,136},{16,144},{24,152},{32,160},{40,168},{48,176},{56,1... | collective-permute-start | bytes 49160 | tf_op jit(solution)/shard_map/ppermute | solution.py:334
  31.5 13.1 %collective-permute-start.3 = (f32[16,256]{1,0:T(8,128)S(1)}, f32[16,256]{1,0:T(8,128)S(1)}, u32[]{:S(2)}, u32[]{:S(2)}) collective-permute-start(f32[16,256]{1,0:T(8,128)S(1)} %hist.5), channel_id=1, source_target_pairs={{0,64},{8,72},{16,80},{24,88},{32,96},{40,104},{48,112},{56,120},{... | collective-permute-start | bytes 49160 | tf_op jit(solution)/shard_map/ppermute | solution.py:334
  36.9 7.7 %collective-permute-start.5 = (f32[16,256]{1,0:T(8,128)S(1)}, f32[16,256]{1,0:T(8,128)S(1)}, u32[]{:S(2)}, u32[]{:S(2)}) collective-permute-start(f32[16,256]{1,0:T(8,128)S(1)} %hist.7), channel_id=1, source_target_pairs={{0,192},{8,200},{16,208},{24,216},{32,224},{40,232},{48,240},{56,2... | collective-permute-start | bytes 49160 | tf_op jit(solution)/shard_map/ppermute | solution.py:334
  39.6 19.3 %copy-start.3 = (s32[64,256]{1,0:T(8,128)S(1)}, s32[64,256]{1,0:T(8,128)}, u32[]{:S(2)}) copy-start(s32[64,256]{1,0:T(8,128)} %codes_ref.1) | copy-start | bytes 196612
  39.6 19.3 %copy-start.4 = (s32[64,256]{1,0:T(8,128)S(1)}, s32[64,256]{1,0:T(8,128)}, u32[]{:S(2)}) copy-start(s32[64,256]{1,0:T(8,128)} %ranks_ref.1) | copy-start | bytes 196612
  39.6 24.9 %copy-start.1 = (f32[64,8192]{1,0:T(8,128)S(1)}, f32[64,8192]{1,0:T(8,128)}, u32[]{:S(2)}) copy-start(f32[64,8192]{1,0:T(8,128)} %refs_1_.13) | copy-start | bytes 6291460
  44.6 2.9 %collective-permute-start.6 = (f32[16,256]{1,0:T(8,128)S(1)}, f32[16,256]{1,0:T(8,128)S(1)}, u32[]{:S(2)}, u32[]{:S(2)}) collective-permute-start(f32[16,256]{1,0:T(8,128)S(1)} %add_add_fusion), channel_id=1, source_target_pairs={{0,8},{8,0},{16,24},{24,16},{32,40},{40,32},{48,56},{56,48},{64,72... | collective-permute-start | bytes 49160 | tf_op jit(solution)/shard_map/ppermute | solution.py:330
  47.5 4.1 %collective-permute-start.7 = (f32[16,256]{1,0:T(8,128)S(1)}, f32[16,256]{1,0:T(8,128)S(1)}, u32[]{:S(2)}, u32[]{:S(2)}) collective-permute-start(f32[16,256]{1,0:T(8,128)S(1)} %add.18), channel_id=1, source_target_pairs={{0,16},{8,24},{16,0},{24,8},{32,48},{40,56},{48,32},{56,40},{64,80... | collective-permute-start | bytes 49160 | tf_op jit(solution)/shard_map/ppermute | solution.py:330
  51.6 7.2 %collective-permute-start.8 = (f32[16,256]{1,0:T(8,128)S(1)}, f32[16,256]{1,0:T(8,128)S(1)}, u32[]{:S(2)}, u32[]{:S(2)}) collective-permute-start(f32[16,256]{1,0:T(8,128)S(1)} %add.19.first_ref), channel_id=1, source_target_pairs={{0,32},{8,40},{16,48},{24,56},{32,0},{40,8},{48,16},{56,24},{64,96... | collective-permute-start | bytes 49160 | tf_op jit(solution)/shard_map/ppermute | solution.py:330
  59.4 3.0 %collective-permute-start.11 = (f32[16,256]{1,0:T(8,128)S(1)}, f32[16,256]{1,0:T(8,128)S(1)}, u32[]{:S(2)}, u32[]{:S(2)}) collective-permute-start(f32[16,256]{1,0:T(8,128)S(1)} %cuts.1.refs_0_), channel_id=1, source_target_pairs={{0,192},{8,200},{16,208},{24,216},{32,224},{40,232},{48,240},{56,2... | collective-permute-start | bytes 49160 | tf_op jit(solution)/shard_map/ppermute | solution.py:334
  59.5 4.4 %collective-permute-start.10 = (f32[16,256]{1,0:T(8,128)S(1)}, f32[16,256]{1,0:T(8,128)S(1)}, u32[]{:S(2)}, u32[]{:S(2)}) collective-permute-start(f32[16,256]{1,0:T(8,128)S(1)} %cuts.1.refs_0_), channel_id=1, source_target_pairs={{0,128},{8,136},{16,144},{24,152},{32,160},{40,168},{48,176},{56,1... | collective-permute-start | bytes 49160 | tf_op jit(solution)/shard_map/ppermute | solution.py:334
  60.3 4.1 %collective-permute-start.9 = (f32[16,256]{1,0:T(8,128)S(1)}, f32[16,256]{1,0:T(8,128)S(1)}, u32[]{:S(2)}, u32[]{:S(2)}) collective-permute-start(f32[16,256]{1,0:T(8,128)S(1)} %cuts.1.refs_0_), channel_id=1, source_target_pairs={{0,64},{8,72},{16,80},{24,88},{32,96},{40,104},{48,112},{56,120},{... | collective-permute-start | bytes 49160 | tf_op jit(solution)/shard_map/ppermute | solution.py:334
  68.7 26.5 %collective-permute-start.12 = (f32[64,1024]{1,0:T(8,128)S(1)}, f32[64,1024]{1,0:T(8,128)S(1)}, u32[]{:S(2)}, u32[]{:S(2)}) collective-permute-start(f32[64,1024]{1,0:T(8,128)S(1)} %get-tuple-element.30), channel_id=1, source_target_pairs={{0,4},{1,5},{2,6},{3,7},{4,0},{5,1},{6,2},{7,3},{8,12},{9,13},{10,... | collective-permute-start | bytes 786440 | tf_op jit(solution)/shard_map/ppermute | solution.py:322
  68.9 26.4 %collective-permute-start.13 = (f32[64,1024]{1,0:T(8,128)S(1)}, f32[64,1024]{1,0:T(8,128)S(1)}, u32[]{:S(2)}, u32[]{:S(2)}) collective-permute-start(f32[64,1024]{1,0:T(8,128)S(1)} %get-tuple-element.31), channel_id=1, source_target_pairs={{0,5},{1,4},{2,7},{3,6},{4,1},{5,0},{6,3},{7,2},{8,13},{9,12},{10,... | collective-permute-start | bytes 786440 | tf_op jit(solution)/shard_map/ppermute | solution.py:322
  83.4 14.5 %collective-permute-start.18 = (f32[64,1024]{1,0:T(8,128)S(1)}, f32[64,1024]{1,0:T(8,128)S(1)}, u32[]{:S(2)}, u32[]{:S(2)}) collective-permute-start(f32[64,1024]{1,0:T(8,128)S(1)} %get-tuple-element.37), channel_id=1, source_target_pairs={{0,1},{1,0},{2,3},{3,2},{4,5},{5,4},{6,7},{7,6},{8,9},{9,8},{10,11... | collective-permute-start | bytes 786440 | tf_op jit(solution)/shard_map/ppermute | solution.py:322
  87.9 10.1 %collective-permute-start.16 = (f32[64,1024]{1,0:T(8,128)S(1)}, f32[64,1024]{1,0:T(8,128)S(1)}, u32[]{:S(2)}, u32[]{:S(2)}) collective-permute-start(f32[64,1024]{1,0:T(8,128)S(1)} %get-tuple-element.35), channel_id=1, source_target_pairs={{0,3},{1,2},{2,5},{3,4},{4,7},{5,6},{6,1},{7,0},{8,11},{9,10},{10,... | collective-permute-start | bytes 786440 | tf_op jit(solution)/shard_map/ppermute | solution.py:322
  88.7 9.3 %collective-permute-start.17 = (f32[64,1024]{1,0:T(8,128)S(1)}, f32[64,1024]{1,0:T(8,128)S(1)}, u32[]{:S(2)}, u32[]{:S(2)}) collective-permute-start(f32[64,1024]{1,0:T(8,128)S(1)} %get-tuple-element.36), channel_id=1, source_target_pairs={{0,7},{1,6},{2,1},{3,0},{4,3},{5,2},{6,5},{7,4},{8,15},{9,14},{10,... | collective-permute-start | bytes 786440 | tf_op jit(solution)/shard_map/ppermute | solution.py:322
  95.2 8.7 %collective-permute-start.14 = (f32[64,1024]{1,0:T(8,128)S(1)}, f32[64,1024]{1,0:T(8,128)S(1)}, u32[]{:S(2)}, u32[]{:S(2)}) collective-permute-start(f32[64,1024]{1,0:T(8,128)S(1)} %get-tuple-element.33), channel_id=1, source_target_pairs={{0,2},{1,3},{2,4},{3,5},{4,6},{5,7},{6,0},{7,1},{8,10},{9,11},{10,... | collective-permute-start | bytes 786440 | tf_op jit(solution)/shard_map/ppermute | solution.py:322
  95.3 8.6 %collective-permute-start.15 = (f32[64,1024]{1,0:T(8,128)S(1)}, f32[64,1024]{1,0:T(8,128)S(1)}, u32[]{:S(2)}, u32[]{:S(2)}) collective-permute-start(f32[64,1024]{1,0:T(8,128)S(1)} %get-tuple-element.34), channel_id=1, source_target_pairs={{0,6},{1,7},{2,0},{3,1},{4,2},{5,3},{6,4},{7,5},{8,14},{9,15},{10,... | collective-permute-start | bytes 786440 | tf_op jit(solution)/shard_map/ppermute | solution.py:322

commit v4 on v3

--- a/solution.py
+++ b/solution.py
@@ -8,7 +8,8 @@
 LANES = 128
 FEATS = 16
 DEPTH = 4
-SPAN = 2048
+TILE = 256
+UNROLL = 8
 
 
 def in_vmem(count):
@@ -67,13 +68,22 @@
     return pick_columns(edges, 2 * lane), pick_columns(edges, 2 * lane + 1)
 
 
-def slot_kernel(turn, codes_ref, values_ref, top_ref, low_ref):
+def slot_kernel(turn, codes_hbm, values_hbm, top_ref, low_ref, codes_ref, values_ref, sems):
     rows = values_ref.shape[1]
     width = 32
     group = (lax.axis_index("rows") // 8 + turn) % 4
+    own = pl.ds(pl.multiple_of(group * FEATS, FEATS), FEATS)
+    span = rows // 2
+    copies = [pltpu.make_async_copy(codes_hbm.at[own, :], codes_ref, sems.at[2])]
+    for part in range(2):
+        at = slice(part * span, (part + 1) * span)
+        copies.append(pltpu.make_async_copy(values_hbm.at[own, at], values_ref.at[:, at], sems.at[part]))
+    for copy in copies:
+        copy.start()
+    copies[0].wait()
     tables = []
     for half in range(2):
-        at = pl.ds(pl.multiple_of(group * FEATS + 8 * half, 8), 8)
+        at = slice(8 * half, 8 * half + 8)
         even, odd = even_odd(codes_ref[at, :])
         tables.append((at, odd, (even, spread(even))))
 
@@ -92,29 +102,39 @@
             low_ref[:, column] = jnp.concatenate(low, axis=0).astype(jnp.bfloat16)
         return carry
 
-    lax.fori_loop(0, rows // (width * LANES), chunk, 0)
+    steps = span // (width * LANES)
+    for part in range(2):
+        copies[1 + part].wait()
+        lax.fori_loop(part * steps, (part + 1) * steps, chunk, 0)
 
 
 def find_slots(turn, edge_codes, values):
-    slots = jax.ShapeDtypeStruct((FEATS, values.shape[1]), jnp.bfloat16)
+    rows = values.shape[1]
+    slots = jax.ShapeDtypeStruct((FEATS, rows), jnp.bfloat16)
     return pl.pallas_call(
         lambda *refs: slot_kernel(turn, *refs),
-        in_specs=in_vmem(2),
+        in_specs=[pl.BlockSpec(memory_space=pltpu.HBM)] * 2,
         out_specs=in_vmem(2),
         out_shape=[slots, slots],
+        scratch_shapes=[
+            pltpu.VMEM((FEATS, 256), jnp.int32),
+            pltpu.VMEM((FEATS, rows), jnp.float32),
+            pltpu.SemaphoreType.DMA((3,)),
+        ],
         compiler_params=pltpu.CompilerParams(vmem_limit_bytes=16 << 20),
         cost_estimate=pl.CostEstimate(flops=10**7, bytes_accessed=10**7, transcendentals=0),
         name="slots",
-    )(edge_codes, values)
-
-
-def hist_kernel(hess_ref, top_ref, low_ref, mass_ref, high_ref, rest_ref, sum_ref, a0, b0):
+    )(
+        pltpu.with_memory_space_constraint(edge_codes, pltpu.HBM),
+        pltpu.with_memory_space_constraint(values, pltpu.HBM),
+    )
+
+
+def hist_kernel(hess_ref, top_ref, low_ref, mass_ref, high_ref, rest_ref, sum_ref):
     rows = top_ref.shape[1]
     shape = (FEATS, LANES)
     lane = lane_iota(shape)
     feat = lax.broadcasted_iota(jnp.int32, shape, 0)
-    zero = jnp.zeros(shape, jnp.bfloat16)
-    one = jnp.ones(shape, jnp.bfloat16)
     scaled = hess_ref[...] * 65536.0
     high = jnp.floor(scaled * (1.0 / 256.0))
     rest = scaled - high * 256.0
@@ -125,39 +145,39 @@
         high_ref[:, own] = jnp.broadcast_to(high[part : part + 1], (FEATS, wide)).astype(jnp.bfloat16)
         rest_ref[:, own] = jnp.broadcast_to(rest[part : part + 1], (FEATS, wide)).astype(jnp.bfloat16)
 
-    def make(step, a_ref, b_ref):
-        for off in range(0, SPAN, LANES):
-            at = pl.ds(pl.multiple_of(step * SPAN + off, LANES), LANES)
-            own = slice(off, off + LANES)
-            top, low, w_high, w_rest = top_ref[:, at], low_ref[:, at], high_ref[:, at], rest_ref[:, at]
-            for k in range(16):
-                hit = top == k
-                a_ref[k * FEATS : (k + 1) * FEATS, own] = jnp.where(hit, w_high, zero)
-                a_ref[(16 + k) * FEATS : (17 + k) * FEATS, own] = jnp.where(hit, w_rest, zero)
-                b_ref[k * FEATS : (k + 1) * FEATS, own] = jnp.where(low <= k, one, zero)
-
-    def add(a_ref, b_ref):
-        sum_ref[...] += lax.dot_general(
-            a_ref[...], b_ref[...], (((1,), (1,)), ((), ())), preferred_element_type=jnp.float32
-        )
-
-    sum_ref[...] = jnp.zeros_like(sum_ref)
-
-    def step(index, carry):
-        make(index, a0, b0)
-        add(a0, b0)
-        return carry
-
-    lax.fori_loop(0, rows // SPAN, step, 0)
+    def multiply(*sums):
+        zero = jnp.zeros((FEATS, TILE), jnp.bfloat16)
+        one = jnp.ones((FEATS, TILE), jnp.bfloat16)
+        units = (sums[:16], sums[16:])
+
+        def step(index, carry):
+            for turn in range(UNROLL):
+                spots = [pl.ds(pl.multiple_of(((index * UNROLL + turn) * 2 + unit) * TILE, TILE), TILE) for unit in range(2)]
+                for unit, at in enumerate(spots):
+                    low = low_ref[:, at]
+                    below = jnp.concatenate([jnp.where(low <= k, one, zero) for k in range(16)], axis=0)
+                    pltpu.matmul_push_rhs(below, turn % 2, unit, transpose=True)
+                for unit, at in enumerate(spots):
+                    top, w_high, w_rest = top_ref[:, at], high_ref[:, at], rest_ref[:, at]
+                    for k in range(16):
+                        hit = top == k
+                        weighted = jnp.concatenate([jnp.where(hit, w_high, zero), jnp.where(hit, w_rest, zero)], axis=0)
+                        pltpu.matmul_acc_lhs(units[unit][k], weighted, load_staged_rhs=turn % 2 if k == 0 else None)
+            return carry
+
+        lax.fori_loop(0, rows // (2 * TILE * UNROLL), step, 0)
+        for k in range(16):
+            both = pltpu.matmul_pop(units[0][k]) + pltpu.matmul_pop(units[1][k])
+            sum_ref[k * FEATS : (k + 1) * FEATS] = both[:FEATS] * (1.0 / 256.0) + both[FEATS:] * (1.0 / 65536.0)
+
+    pl.run_scoped(multiply, *[pltpu.ACC(mxu_id=unit)((2 * FEATS, TILE), jnp.float32) for unit in range(2) for _ in range(16)])
 
     points = [2 * lane - 1, 2 * lane]
     columns = [(point & 7) * FEATS + feat for point in points]
     results = [jnp.zeros(shape, jnp.float32)] * 2
     before = jnp.zeros(shape, jnp.float32)
     for k in range(16):
-        large = sum_ref[k * FEATS : (k + 1) * FEATS]
-        small = sum_ref[(16 + k) * FEATS : (17 + k) * FEATS]
-        block = (large * 256.0 + small) * (1.0 / 65536.0)
+        block = sum_ref[k * FEATS : (k + 1) * FEATS]
         for parity, (point, column) in enumerate(zip(points, columns)):
             here = jnp.where((point & 15) < 8, lane_take(block[:, :LANES], column), lane_take(block[:, LANES:], column))
             results[parity] = jnp.where((point >> 4) == k, before + here, results[parity])
@@ -174,22 +194,21 @@
         out_specs=in_vmem(1)[0],
         out_shape=jax.ShapeDtypeStruct((FEATS, 256), jnp.float32),
         scratch_shapes=[pltpu.VMEM((FEATS, rows), jnp.bfloat16)] * 2
-        + [pltpu.VMEM((512, 256), jnp.float32)]
-        + [pltpu.VMEM((512, SPAN), jnp.bfloat16), pltpu.VMEM((256, SPAN), jnp.bfloat16)],
+        + [pltpu.VMEM((16 * FEATS, TILE), jnp.float32)],
         compiler_params=pltpu.CompilerParams(vmem_limit_bytes=24 << 20),
         cost_estimate=pl.CostEstimate(flops=4 * 10**9, bytes_accessed=10**7, transcendentals=0),
         name="hist",
     )(hess, top, low)
 
 
-def cuts_kernel(codes_ref, ranks_ref, first_ref, second_ref, cuts_ref):
+def cuts_kernel(codes_ref, ranks_ref, first_ref, second_ref, third_ref, cuts_ref):
     shape = (FEATS, LANES)
     lane = lane_iota(shape)
     group = lax.axis_index("rows") // 8
     at = pl.ds(pl.multiple_of(group * FEATS, FEATS), FEATS)
     edge_even, edge_odd = even_odd(codes_ref[at, :])
     edge_next = lane_take(edge_even, (lane + 1) & (LANES - 1))
-    mass = first_ref[...] + second_ref[...]
+    mass = first_ref[...] + second_ref[...] + third_ref[...]
     mass_even, mass_odd = mass[:, :LANES], mass[:, LANES:]
     mass_next = lane_take(mass_even, (lane + 1) & (LANES - 1))
     total = jnp.broadcast_to(mass_odd[:, LANES - 1 :], shape)
@@ -209,34 +228,39 @@
         cuts_ref[:, side * LANES : (side + 1) * LANES] = low_edge + part * (high_edge - low_edge)
 
 
-def find_cuts(edge_codes, cut_ranks, first, second):
+def find_cuts(edge_codes, cut_ranks, *sums):
     return pl.pallas_call(
         cuts_kernel,
-        in_specs=in_vmem(4),
+        in_specs=in_vmem(2 + len(sums)),
         out_specs=in_vmem(1)[0],
         out_shape=jax.ShapeDtypeStruct((FEATS, 256), jnp.float32),
         compiler_params=pltpu.CompilerParams(vmem_limit_bytes=4 << 20),
         name="cuts",
-    )(edge_codes, cut_ranks, first, second)
-
-
-def place_group(raw, odd, values, write):
-    shape = odd.shape
-    lane = lane_iota(shape)
-    last = jnp.broadcast_to(raw[:, :1], shape)
-    even = jnp.where(lane == 0, -16.0, raw)
-    after = jnp.where(lane == LANES - 1, last, lane_take(even, (lane + 1) & (LANES - 1)))
-    inv_low = 1.0 / (odd - even)
-    inv_high = 1.0 / (after - odd)
-    inv_last = 1.0 / (16.0 - last)
-    table = (even, spread(even))
-    pairs = search_pairs([table] * len(values), values)
-    knots = [lane_take(odd, pair) for pair in pairs]
-    highs = [lane_take(inv_high, pair) for pair in pairs]
-    lows = [lane_take(inv_low, pair) for pair in pairs]
-    for index, (value, pair, knot, high, low) in enumerate(zip(values, pairs, knots, highs, lows)):
+    )(edge_codes, cut_ranks, *sums)
+
+
+def place_groups(groups):
+    tables, all_values, rest = [], [], []
+    for raw, odd, values, writes in groups:
+        shape = odd.shape
+        lane = lane_iota(shape)
+        last = jnp.broadcast_to(raw[:, :1], shape)
+        even = jnp.where(lane == 0, -16.0, raw)
+        after = jnp.where(lane == LANES - 1, last, lane_take(even, (lane + 1) & (LANES - 1)))
+        inv_low = 1.0 / (odd - even)
+        inv_high = 1.0 / (after - odd)
+        inv_last = 1.0 / (16.0 - last)
+        tables += [(even, spread(even))] * len(values)
+        all_values += values
+        rest += [(odd, inv_low, inv_high, last, inv_last, write) for write in writes]
+    pairs = search_pairs(tables, all_values)
+    knots = [lane_take(item[0], pair) for item, pair in zip(rest, pairs)]
+    lows = [lane_take(item[1], pair) for item, pair in zip(rest, pairs)]
+    highs = [lane_take(item[2], pair) for item, pair in zip(rest, pairs)]
+    for item, value, pair, knot, low, high in zip(rest, all_values, pairs, knots, lows, highs):
+        last, inv_last, write = item[3:]
         inside = (2 * pair + 1).astype(jnp.float32) + (value - knot) * jnp.where(value >= knot, high, low)
-        write(index, jnp.where(value >= last, 256.0 + (value - last) * inv_last, inside))
+        write(jnp.where(value >= last, 256.0 + (value - last) * inv_last, inside))
 
 
 def first_kernel(moves, c0, c1, c2, c3, values_ref, cuts_ref, *out_refs):
@@ -251,22 +275,28 @@
     feats, wide = out_refs[0].shape
     bases = [owner(move) * wide for move in moves]
 
+    together = max(1, 8 // len(moves))
+
+    def store(out_ref, at, part):
+        def write(value):
+            out_ref[at, part : part + LANES] = value
+
+        return write
+
     def step(index, carry):
-        at = pl.ds(pl.multiple_of(index * 8, 8), 8)
-        values, places = [], []
-        for base, out_ref in zip(bases, out_refs):
-            for part in range(0, wide, LANES):
-                values.append(values_ref[at, pl.ds(pl.multiple_of(base + part, LANES), LANES)])
-                places.append((out_ref, part))
-
-        def write(part, value):
-            out_ref, lanes = places[part]
-            out_ref[at, lanes : lanes + LANES] = value
-
-        place_group(cuts_ref[at, :LANES], cuts_ref[at, LANES:], values, write)
+        groups = []
+        for turn in range(together):
+            at = pl.ds(pl.multiple_of((index * together + turn) * 8, 8), 8)
+            values, writes = [], []
+            for base, out_ref in zip(bases, out_refs):
+                for part in range(0, wide, LANES):
+                    values.append(values_ref[at, pl.ds(pl.multiple_of(base + part, LANES), LANES)])
+                    writes.append(store(out_ref, at, part))
+            groups.append((cuts_ref[at, :LANES], cuts_ref[at, LANES:], values, writes))
+        place_groups(groups)
         return carry
 
-    lax.fori_loop(0, feats // 8, step, 0)
+    lax.fori_loop(0, feats // (8 * together), step, 0)
 
 
 def place(moves, cuts, values):
@@ -326,8 +356,8 @@
     return lax.ppermute(array, "feat", [(i, i ^ flip) for i in range(8)])
 
 
-def flip_rows(array, flip):
-    return lax.ppermute(array, "rows", [(i, i ^ flip) for i in range(32)])
+def shift_rows(array, shift):
+    return lax.ppermute(array, "rows", [(i, i // 8 * 8 + (i + shift) % 8) for i in range(32)])
 
 
 def turn_rows(array, turn):
@@ -337,16 +367,22 @@
 def on_device(feature_values, hessian_codes, edge_codes, cut_ranks):
     hess_own = hessian_codes.astype(jnp.float32) * (1.0 / 65536.0)
     hess = hess_own.reshape(1, -1)
-    for flip in (1, 2, 4):
-        hess = jnp.concatenate([hess, flip_feat(hess, flip)], axis=0)
-    slots = [find_slots(turn, edge_codes, feature_values) for turn in range(4)]
+    slots = {}
+    codes = edge_codes
+    for flip, turns in ((1, (1,)), (2, (2,)), (4, (3, 0))):
+        other = flip_feat(hess, flip)
+        for turn in turns:
+            slots[turn] = find_slots(turn, codes, feature_values)
+        hess = jnp.concatenate([hess, other], axis=0)
+        if flip < 4:
+            hess, slots[turn], codes = lax.optimization_barrier((hess, slots[turn], codes))
     parts = [turn_rows(find_mass(hess, *slots[turn]), turn) for turn in (1, 2, 3)]
     mass = find_mass(hess, *slots[0]) + parts[0] + parts[1] + parts[2]
-    for flip in (1, 2):
-        mass = mass + flip_rows(mass, flip)
-    cuts = find_cuts(edge_codes, cut_ranks, mass, flip_rows(mass, 4))
+    before = mass + shift_rows(mass, 1)
+    around = before + shift_rows(mass, -1)
+    cuts = find_cuts(edge_codes, cut_ranks, around, shift_rows(around, -3), shift_rows(before, 2))
     cuts = [cuts] + [turn_rows(cuts, turn) for turn in (1, 2, 3)]
-    stages = [[(2, 0), (2, 1)], [(1, 0), (3, 0)], [(1, 1), (3, 1)], [(0, 1), (0, 0)]]
+    stages = [[(2, 0)], [(2, 1), (1, 0)], [(3, 0), (1, 1)], [(3, 1), (0, 1)], [(0, 0)]]
     moves, parts = [], []
     for stage in stages:
         outs = place(stage, cuts, feature_values)

time: 106 us -> 94.1 us (0.89)
  Pallas kernels: 46.6 us -> 34.8 us
  waiting for transfers between devices: 16.2 us -> 23.6 us
  starting transfers between devices: 39.1 us -> 34 us
  local copies, waits for them, and re-layouts: 2.44 us -> 0.01 us
    pallas_call x4, Pallas kernels: 20.1 us -> 11.4 us  [find_mass(): pl.pallas_call(hist_kernel, in_specs=in_vmem(3), out_specs=in_vmem(1)[0],...]
    ppermute x7, waiting for transfers between devices: 5.93 us -> 13.5 us  [send_feat(): lax.ppermute(array, 'feat', [(i, (i // 2 + move[0]) % 4 * 2 + (i % 2 ^ mo...]
    pallas_call x4 -> x5, Pallas kernels: 17.2 us -> 10.9 us  [place(): pl.pallas_call(lambda *refs: kernel(moves, *refs), in_specs=in_vmem(len(c...]
    ppermute x3, waiting for transfers between devices: 3.31 us -> 0.01 us  [flip_feat(): return lax.ppermute(array, 'feat', [(i, i ^ flip) for i in range(8)])]
    pallas_call x5, Pallas kernels: 7.97 us -> 11.1 us  [the longest x4 10.6 us: find_slots(): pl.pallas_call(lambda *refs: slot_kernel(turn, *refs), in_specs=[pl.Block...]
    ppermute x7, starting transfers between devices: 16.3 us -> 13.2 us  [send_feat(): lax.ppermute(array, 'feat', [(i, (i // 2 + move[0]) % 4 * 2 + (i % 2 ^ mo...]
    ppermute x3 -> x4, starting transfers between devices: 10.8 us -> 7.82 us  [shift_rows(): lax.ppermute(array, 'rows', [(i, i // 8 * 8 + (i + shift) % 8) for i in r...]
    ppermute x3 -> x4, waiting for transfers between devices: 3.38 us -> 6.33 us  [shift_rows(): lax.ppermute(array, 'rows', [(i, i // 8 * 8 + (i + shift) % 8) for i in r...]
  transfers between devices with their start and end apart: 19 -> 20, of which waited for: 9 -> 8; matrix products, arithmetic and copies ran while one was open for 0% -> 0% of each run, Pallas kernels for 34% -> 31%
where the time goes in v4:
time: 94.1 us; the launch traced here: 93.6 us
  Pallas kernels  34.8 us (37%)
  starting transfers between devices  34 us (36%)
  waiting for transfers between devices  23.6 us (25%)
    ppermute x7, waiting for transfers between devices, send_feat(): lax.ppermute(array, 'feat', [(i, (i // 2 + move[0]) % 4 * 2 + (i % 2 ^ mo...  13.5 us
    ppermute x7, starting transfers between devices, send_feat(): lax.ppermute(array, 'feat', [(i, (i // 2 + move[0]) % 4 * 2 + (i % 2 ^ mo...  13.2 us
    pallas_call x4, Pallas kernels, find_mass(): pl.pallas_call(hist_kernel, in_specs=in_vmem(3), out_specs=in_vmem(1)[0],...  11.4 us
    pallas_call x5, Pallas kernels, place(): pl.pallas_call(lambda *refs: kernel(moves, *refs), in_specs=in_vmem(len(c...  10.9 us
    pallas_call x4, Pallas kernels, find_slots(): pl.pallas_call(lambda *refs: slot_kernel(turn, *refs), in_specs=[pl.Block...  10.6 us
    ppermute x4, starting transfers between devices, shift_rows(): lax.ppermute(array, 'rows', [(i, i // 8 * 8 + (i + shift) % 8) for i in r...  7.82 us
    ppermute x6, starting transfers between devices, turn_rows(): lax.ppermute(array, 'rows', [(i, (i + 8 * turn) % 32) for i in range(32)])  7.42 us
    ppermute x4, waiting for transfers between devices, shift_rows(): lax.ppermute(array, 'rows', [(i, i // 8 * 8 + (i + shift) % 8) for i in r...  6.33 us
  transfers between devices with their start and end apart: 20, of which 8 were waited for; matrix products, arithmetic and copies ran while one was open for 0% of the time, Pallas kernels for 31%

profile of v4, /device:TPU:1, one launch (start us, length us, event | category | flops | bytes accessed | tf_op | source)
XLA Modules:
  0.0 93.6 jit_solution(1840591801589337624)
XLA Ops:
  0.0 0.7 convert_multiply_fusion
  0.7 3.2 %collective-permute-start = (f32[1,1024]{1,0:T(1,128)S(1)}, f32[1,1024]{1,0:T(1,128)S(1)}, u32[]{:S(2)}, u32[]{:S(2)}) collective-permute-start(f32[1,1024]{1,0:T(1,128)S(1)} %bitcast.1), channel_id=1, source_target_pairs={{0,1},{1,0},{2,3},{3,2},{4,5},{5,4},{6,7},{7,6},{8,9},{9,8},{10,11... | collective-permute-start | bytes 12296 | tf_op jit(solution)/shard_map/ppermute | solution.py:356
  3.9 2.6 %slots.4 = (bf16[16,8192]{1,0:T(8,128)(2,1)S(1)}, bf16[16,8192]{1,0:T(8,128)(2,1)S(1)}) custom-call(s32[64,256]{1,0:T(8,128)} %codes_ref.1, f32[64,8192]{1,0:T(8,128)} %refs_1_.15), custom_call_target="tpu_custom_call" | custom-call | flops 10000000 | bytes 10000000 | tf_op jit(solution)/shard_map/slots/pallas_call | solution.py:114
  6.6 0.0 collective-permute-done
  6.6 0.1 collective-permute-start.1
  6.7 2.7 %slots.5 = (bf16[16,8192]{1,0:T(8,128)(2,1)S(1)}, bf16[16,8192]{1,0:T(8,128)(2,1)S(1)}) custom-call(s32[64,256]{1,0:T(8,128)} %codes_ref.1, f32[64,8192]{1,0:T(8,128)} %refs_1_.15), custom_call_target="tpu_custom_call" | custom-call | flops 10000000 | bytes 10000000 | tf_op jit(solution)/shard_map/slots/pallas_call | solution.py:114
  9.4 2.2 %collective-permute-start.2 = (f32[4,1024]{1,0:T(4,128)S(1)}, f32[4,1024]{1,0:T(4,128)S(1)}, u32[]{:S(2)}, u32[]{:S(2)}) collective-permute-start(f32[4,1024]{1,0:T(4,128)S(1)} %pad_maximum_fusion.1), channel_id=1, source_target_pairs={{0,4},{1,5},{2,6},{3,7},{4,0},{5,1},{6,2},{7,3},{8,12},{9,13},{10,... | collective-permute-start | bytes 49160 | tf_op jit(solution)/shard_map/ppermute | solution.py:356
  11.6 2.6 %slots.7 = (bf16[16,8192]{1,0:T(8,128)(2,1)S(1)}, bf16[16,8192]{1,0:T(8,128)(2,1)S(1)}) custom-call(s32[64,256]{1,0:T(8,128)} %codes_ref.1, f32[64,8192]{1,0:T(8,128)} %refs_1_.15), custom_call_target="tpu_custom_call" | custom-call | flops 10000000 | bytes 10000000 | tf_op jit(solution)/shard_map/slots/pallas_call | solution.py:114
  14.3 2.7 %slots.6 = (bf16[16,8192]{1,0:T(8,128)(2,1)S(1)}, bf16[16,8192]{1,0:T(8,128)(2,1)S(1)}) custom-call(s32[64,256]{1,0:T(8,128)} %codes_ref.1, f32[64,8192]{1,0:T(8,128)} %refs_1_.15), custom_call_target="tpu_custom_call" | custom-call | flops 10000000 | bytes 10000000 | tf_op jit(solution)/shard_map/slots/pallas_call | solution.py:114
  17.0 2.9 %hist.5 = f32[16,256]{1,0:T(8,128)S(1)} custom-call(f32[8,1024]{1,0:T(8,128)S(1)} %pad_maximum_fusion.hess_ref, bf16[16,8192]{1,0:T(8,128)(2,1)S(1)} %get-tuple-element.39.top_ref, bf16[16,8192]{1,0:T(8,128)(2,1)S(1)} %get-tuple-element.40.low_ref), custom_call_target="tpu_custom_call" | custom-call | flops 4000000000 | bytes 10000000 | tf_op jit(solution)/shard_map/hist/pallas_call | solution.py:191
  19.9 1.5 %collective-permute-start.3 = (f32[16,256]{1,0:T(8,128)S(1)}, f32[16,256]{1,0:T(8,128)S(1)}, u32[]{:S(2)}, u32[]{:S(2)}) collective-permute-start(f32[16,256]{1,0:T(8,128)S(1)} %hist.5), channel_id=1, source_target_pairs={{0,64},{8,72},{16,80},{24,88},{32,96},{40,104},{48,112},{56,120},{... | collective-permute-start | bytes 49160 | tf_op jit(solution)/shard_map/ppermute | solution.py:364
  21.3 2.9 %hist.6 = f32[16,256]{1,0:T(8,128)S(1)} custom-call(f32[8,1024]{1,0:T(8,128)S(1)} %pad_maximum_fusion.hess_ref, bf16[16,8192]{1,0:T(8,128)(2,1)S(1)} %get-tuple-element.41.top_ref, bf16[16,8192]{1,0:T(8,128)(2,1)S(1)} %get-tuple-element.42.low_ref), custom_call_target="tpu_custom_call" | custom-call | flops 4000000000 | bytes 10000000 | tf_op jit(solution)/shard_map/hist/pallas_call | solution.py:191
  24.2 2.5 %collective-permute-start.4 = (f32[16,256]{1,0:T(8,128)S(1)}, f32[16,256]{1,0:T(8,128)S(1)}, u32[]{:S(2)}, u32[]{:S(2)}) collective-permute-start(f32[16,256]{1,0:T(8,128)S(1)} %hist.6), channel_id=1, source_target_pairs={{0,128},{8,136},{16,144},{24,152},{32,160},{40,168},{48,176},{56,1... | collective-permute-start | bytes 49160 | tf_op jit(solution)/shard_map/ppermute | solution.py:364
  26.7 2.9 %hist.7 = f32[16,256]{1,0:T(8,128)S(1)} custom-call(f32[8,1024]{1,0:T(8,128)S(1)} %pad_maximum_fusion.hess_ref, bf16[16,8192]{1,0:T(8,128)(2,1)S(1)} %get-tuple-element.43.top_ref, bf16[16,8192]{1,0:T(8,128)(2,1)S(1)} %get-tuple-element.44.low_ref), custom_call_target="tpu_custom_call" | custom-call | flops 4000000000 | bytes 10000000 | tf_op jit(solution)/shard_map/hist/pallas_call | solution.py:191
  29.6 1.3 %collective-permute-start.5 = (f32[16,256]{1,0:T(8,128)S(1)}, f32[16,256]{1,0:T(8,128)S(1)}, u32[]{:S(2)}, u32[]{:S(2)}) collective-permute-start(f32[16,256]{1,0:T(8,128)S(1)} %hist.7), channel_id=1, source_target_pairs={{0,192},{8,200},{16,208},{24,216},{32,224},{40,232},{48,240},{56,2... | collective-permute-start | bytes 49160 | tf_op jit(solution)/shard_map/ppermute | solution.py:364
  30.8 2.9 %hist.4 = f32[16,256]{1,0:T(8,128)S(1)} custom-call(f32[8,1024]{1,0:T(8,128)S(1)} %pad_maximum_fusion.hess_ref, bf16[16,8192]{1,0:T(8,128)(2,1)S(1)} %get-tuple-element.37.top_ref, bf16[16,8192]{1,0:T(8,128)(2,1)S(1)} %get-tuple-element.38.low_ref), custom_call_target="tpu_custom_call" | custom-call | flops 4000000000 | bytes 10000000 | tf_op jit(solution)/shard_map/hist/pallas_call | solution.py:191
  33.7 0.0 collective-permute-done.5
  33.8 5.7 %collective-permute-start.7 = (f32[16,256]{1,0:T(8,128)S(1)}, f32[16,256]{1,0:T(8,128)S(1)}, u32[]{:S(2)}, u32[]{:S(2)}) collective-permute-start(f32[16,256]{1,0:T(8,128)S(1)} %add_add_fusion), channel_id=1, source_target_pairs={{0,56},{8,0},{16,8},{24,16},{32,24},{40,32},{48,40},{56,48},{64,12... | collective-permute-start | bytes 49160 | tf_op jit(solution)/shard_map/ppermute | solution.py:360
  39.4 0.0 collective-permute-start.6
  39.4 0.9 collective-permute-done.7
  40.3 2.9 %collective-permute-done.6 = f32[16,256]{1,0:T(8,128)S(1)} collective-permute-done((f32[16,256]{1,0:T(8,128)S(1)}, f32[16,256]{1,0:T(8,128)S(1)}, u32[]{:S(2)}, u32[]{:S(2)}) %collective-permute-start.6) | collective-permute-done | bytes 16416 | tf_op jit(solution)/shard_map/ppermute | solution.py:360
  43.2 0.0 collective-permute-start.9
  43.2 2.2 %collective-permute-start.8 = (f32[16,256]{1,0:T(8,128)S(1)}, f32[16,256]{1,0:T(8,128)S(1)}, u32[]{:S(2)}, u32[]{:S(2)}) collective-permute-start(f32[16,256]{1,0:T(8,128)S(1)} %get-tuple-element.53.first_ref), channel_id=1, source_target_pairs={{0,40},{8,48},{16,56},{24,0},{32,8},{40,16},{48,24},{56,32},{64,10... | collective-permute-start | bytes 49160 | tf_op jit(solution)/shard_map/ppermute | solution.py:360
  45.4 2.5 %collective-permute-done.9.third_ref = f32[16,256]{1,0:T(8,128)S(1)} collective-permute-done((f32[16,256]{1,0:T(8,128)S(1)}, f32[16,256]{1,0:T(8,128)S(1)}, u32[]{:S(2)}, u32[]{:S(2)}) %collective-permute-start.9) | collective-permute-done | bytes 16416 | tf_op jit(solution)/shard_map/ppermute | solution.py:360
  47.9 0.5 cuts.1.refs_0_
  48.4 0.9 collective-permute-start.12
  49.3 1.3 %collective-permute-start.11 = (f32[16,256]{1,0:T(8,128)S(1)}, f32[16,256]{1,0:T(8,128)S(1)}, u32[]{:S(2)}, u32[]{:S(2)}) collective-permute-start(f32[16,256]{1,0:T(8,128)S(1)} %cuts.1.refs_0_), channel_id=1, source_target_pairs={{0,128},{8,136},{16,144},{24,152},{32,160},{40,168},{48,176},{56,1... | collective-permute-start | bytes 49160 | tf_op jit(solution)/shard_map/ppermute | solution.py:364
  50.6 0.0 collective-permute-start.10
  50.6 0.8 collective-permute-done.12.refs_3_
  51.4 2.0 %collective-permute-done.11.refs_2_ = f32[16,256]{1,0:T(8,128)S(1)} collective-permute-done((f32[16,256]{1,0:T(8,128)S(1)}, f32[16,256]{1,0:T(8,128)S(1)}, u32[]{:S(2)}, u32[]{:S(2)}) %collective-permute-start.11) | collective-permute-done | bytes 16416 | tf_op jit(solution)/shard_map/ppermute | solution.py:364
  53.4 1.0 %collective-permute-done.10.refs_1_ = f32[16,256]{1,0:T(8,128)S(1)} collective-permute-done((f32[16,256]{1,0:T(8,128)S(1)}, f32[16,256]{1,0:T(8,128)S(1)}, u32[]{:S(2)}, u32[]{:S(2)}) %collective-permute-start.10) | collective-permute-done | bytes 16416 | tf_op jit(solution)/shard_map/ppermute | solution.py:364
  54.4 1.4 %place.5 = (f32[64,256]{1,0:T(8,128)S(1)}, f32[64,1024]{1,0:T(8,128)S(1)}) custom-call(f32[16,256]{1,0:T(8,128)S(1)} %cuts.1.refs_0_, f32[16,256]{1,0:T(8,128)S(1)} %collective-permute-done.10.refs_1_, f32[16,256]{1,0:T(8,128)S(1)} %collective-permute-done.11.refs_2_, f32[16,256]{1,0:T(8,128)S(1)} %collective-permute-done.12.refs_3_, f32[64,8192]{1,0:T(8,128)S(1)} %copy-done), custom_call_target="tpu_custom_call" | custom-call | flops 10000000 | bytes 1000000 | tf_op jit(solution)/shard_map/place/pallas_call | solution.py:308
  55.8 0.6 collective-permute-start.13
  56.5 2.7 %place.8 = (f32[64,1024]{1,0:T(8,128)S(1)}, f32[64,1024]{1,0:T(8,128)S(1)}) custom-call(f32[64,256]{1,0:T(8,128)S(1)} %get-tuple-element.46.refs_0_, f32[64,8192]{1,0:T(8,128)S(1)} %copy-done), custom_call_target="tpu_custom_call" | custom-call | flops 20000000 | bytes 1000000 | tf_op jit(solution)/shard_map/place/pallas_call | solution.py:308
  59.2 8.2 %collective-permute-start.18 = (f32[64,1024]{1,0:T(8,128)S(1)}, f32[64,1024]{1,0:T(8,128)S(1)}, u32[]{:S(2)}, u32[]{:S(2)}) collective-permute-start(f32[64,1024]{1,0:T(8,128)S(1)} %get-tuple-element.51), channel_id=1, source_target_pairs={{0,7},{1,6},{2,1},{3,0},{4,3},{5,2},{6,5},{7,4},{8,15},{9,14},{10,... | collective-permute-start | bytes 786440 | tf_op jit(solution)/shard_map/ppermute | solution.py:352
  67.4 2.7 %place.7 = (f32[64,1024]{1,0:T(8,128)S(1)}, f32[64,1024]{1,0:T(8,128)S(1)}) custom-call(f32[64,256]{1,0:T(8,128)S(1)} %get-tuple-element.46.refs_0_, f32[64,8192]{1,0:T(8,128)S(1)} %copy-done), custom_call_target="tpu_custom_call" | custom-call | flops 20000000 | bytes 1000000 | tf_op jit(solution)/shard_map/place/pallas_call | solution.py:308
  70.0 0.7 collective-permute-start.16
  70.8 1.5 %collective-permute-start.17 = (f32[64,1024]{1,0:T(8,128)S(1)}, f32[64,1024]{1,0:T(8,128)S(1)}, u32[]{:S(2)}, u32[]{:S(2)}) collective-permute-start(f32[64,1024]{1,0:T(8,128)S(1)} %get-tuple-element.50), channel_id=1, source_target_pairs={{0,3},{1,2},{2,5},{3,4},{4,7},{5,6},{6,1},{7,0},{8,11},{9,10},{10,... | collective-permute-start | bytes 786440 | tf_op jit(solution)/shard_map/ppermute | solution.py:352
  72.3 2.7 %place.6 = (f32[64,1024]{1,0:T(8,128)S(1)}, f32[64,1024]{1,0:T(8,128)S(1)}) custom-call(f32[64,256]{1,0:T(8,128)S(1)} %get-tuple-element.46.refs_0_, f32[64,8192]{1,0:T(8,128)S(1)} %copy-done), custom_call_target="tpu_custom_call" | custom-call | flops 20000000 | bytes 1000000 | tf_op jit(solution)/shard_map/place/pallas_call | solution.py:308
  74.9 0.0 collective-permute-done.13.refs_0_
  75.0 0.3 collective-permute-start.14
  75.2 0.0 collective-permute-done.18.refs_5_
  75.2 1.9 %collective-permute-start.15 = (f32[64,1024]{1,0:T(8,128)S(1)}, f32[64,1024]{1,0:T(8,128)S(1)}, u32[]{:S(2)}, u32[]{:S(2)}) collective-permute-start(f32[64,1024]{1,0:T(8,128)S(1)} %get-tuple-element.48), channel_id=1, source_target_pairs={{0,2},{1,3},{2,4},{3,5},{4,6},{5,7},{6,0},{7,1},{8,10},{9,11},{10,... | collective-permute-start | bytes 786440 | tf_op jit(solution)/shard_map/ppermute | solution.py:352
  77.1 1.4 %place.9.refs_7_ = f32[64,1024]{1,0:T(8,128)S(1)} custom-call(f32[64,256]{1,0:T(8,128)S(1)} %get-tuple-element.46.refs_0_, f32[64,8192]{1,0:T(8,128)S(1)} %copy-done), custom_call_target="tpu_custom_call" | custom-call | flops 10000000 | bytes 1000000 | tf_op jit(solution)/shard_map/place/pallas_call | solution.py:308
  78.5 0.0 collective-permute-done.19.refs_6_
  78.5 7.9 %collective-permute-done.17.refs_4_ = f32[64,1024]{1,0:T(8,128)S(1)} collective-permute-done((f32[64,1024]{1,0:T(8,128)S(1)}, f32[64,1024]{1,0:T(8,128)S(1)}, u32[]{:S(2)}, u32[]{:S(2)}) %collective-permute-start.17) | collective-permute-done | bytes 262176 | tf_op jit(solution)/shard_map/ppermute | solution.py:352
  86.4 5.6 %collective-permute-done.15.refs_2_ = f32[64,1024]{1,0:T(8,128)S(1)} collective-permute-done((f32[64,1024]{1,0:T(8,128)S(1)}, f32[64,1024]{1,0:T(8,128)S(1)}, u32[]{:S(2)}, u32[]{:S(2)}) %collective-permute-start.15) | collective-permute-done | bytes 262176 | tf_op jit(solution)/shard_map/ppermute | solution.py:352
  92.0 1.4 %join.1 = f32[512,1024]{1,0:T(8,128)} custom-call(f32[64,1024]{1,0:T(8,128)S(1)} %collective-permute-done.13.refs_0_, f32[64,1024]{1,0:T(8,128)S(1)} %collective-permute-done.14.refs_1_, f32[64,1024]{1,0:T(8,128)S(1)} %collective-permute-done.15.refs_2_, f32[64,1024]{1,0:T(8,128)S(1)} %collective-permute-done.16.refs_3_, ...), custom_call_target="tpu_custom_call" | custom-call | tf_op jit(solution)/shard_map/join/pallas_call | solution.py:335
  (19 shorter events, 0.1 us)
Async XLA Ops:
  0.7 5.9 %collective-permute-start = (f32[1,1024]{1,0:T(1,128)S(1)}, f32[1,1024]{1,0:T(1,128)S(1)}, u32[]{:S(2)}, u32[]{:S(2)}) collective-permute-start(f32[1,1024]{1,0:T(1,128)S(1)} %bitcast.1), channel_id=1, source_target_pairs={{0,1},{1,0},{2,3},{3,2},{4,5},{5,4},{6,7},{7,6},{8,9},{9,8},{10,11... | collective-permute-start | bytes 12296 | tf_op jit(solution)/shard_map/ppermute | solution.py:356
  6.6 2.8 %collective-permute-start.1 = (f32[2,1024]{1,0:T(2,128)S(1)}, f32[2,1024]{1,0:T(2,128)S(1)}, u32[]{:S(2)}, u32[]{:S(2)}) collective-permute-start(f32[2,1024]{1,0:T(2,128)S(1)} %pad_maximum_fusion.2), channel_id=1, source_target_pairs={{0,2},{1,3},{2,0},{3,1},{4,6},{5,7},{6,4},{7,5},{8,10},{9,11},{10,... | collective-permute-start | bytes 24584 | tf_op jit(solution)/shard_map/ppermute | solution.py:356
  9.4 7.6 %collective-permute-start.2 = (f32[4,1024]{1,0:T(4,128)S(1)}, f32[4,1024]{1,0:T(4,128)S(1)}, u32[]{:S(2)}, u32[]{:S(2)}) collective-permute-start(f32[4,1024]{1,0:T(4,128)S(1)} %pad_maximum_fusion.1), channel_id=1, source_target_pairs={{0,4},{1,5},{2,6},{3,7},{4,0},{5,1},{6,2},{7,3},{8,12},{9,13},{10,... | collective-permute-start | bytes 49160 | tf_op jit(solution)/shard_map/ppermute | solution.py:356
  19.9 13.9 %collective-permute-start.3 = (f32[16,256]{1,0:T(8,128)S(1)}, f32[16,256]{1,0:T(8,128)S(1)}, u32[]{:S(2)}, u32[]{:S(2)}) collective-permute-start(f32[16,256]{1,0:T(8,128)S(1)} %hist.5), channel_id=1, source_target_pairs={{0,64},{8,72},{16,80},{24,88},{32,96},{40,104},{48,112},{56,120},{... | collective-permute-start | bytes 49160 | tf_op jit(solution)/shard_map/ppermute | solution.py:364
  24.2 9.5 %collective-permute-start.4 = (f32[16,256]{1,0:T(8,128)S(1)}, f32[16,256]{1,0:T(8,128)S(1)}, u32[]{:S(2)}, u32[]{:S(2)}) collective-permute-start(f32[16,256]{1,0:T(8,128)S(1)} %hist.6), channel_id=1, source_target_pairs={{0,128},{8,136},{16,144},{24,152},{32,160},{40,168},{48,176},{56,1... | collective-permute-start | bytes 49160 | tf_op jit(solution)/shard_map/ppermute | solution.py:364
  29.6 4.1 %collective-permute-start.5 = (f32[16,256]{1,0:T(8,128)S(1)}, f32[16,256]{1,0:T(8,128)S(1)}, u32[]{:S(2)}, u32[]{:S(2)}) collective-permute-start(f32[16,256]{1,0:T(8,128)S(1)} %hist.7), channel_id=1, source_target_pairs={{0,192},{8,200},{16,208},{24,216},{32,224},{40,232},{48,240},{56,2... | collective-permute-start | bytes 49160 | tf_op jit(solution)/shard_map/ppermute | solution.py:364
  30.8 17.1 %copy-start.1 = (s32[64,256]{1,0:T(8,128)S(1)}, s32[64,256]{1,0:T(8,128)}, u32[]{:S(2)}) copy-start(s32[64,256]{1,0:T(8,128)} %codes_ref.1) | copy-start | bytes 196612
  30.8 17.1 %copy-start.2 = (s32[64,256]{1,0:T(8,128)S(1)}, s32[64,256]{1,0:T(8,128)}, u32[]{:S(2)}) copy-start(s32[64,256]{1,0:T(8,128)} %ranks_ref.1) | copy-start | bytes 196612
  30.8 23.6 %copy-start = (f32[64,8192]{1,0:T(8,128)S(1)}, f32[64,8192]{1,0:T(8,128)}, u32[]{:S(2)}) copy-start(f32[64,8192]{1,0:T(8,128)} %refs_1_.15) | copy-start | bytes 6291460
  33.8 6.5 %collective-permute-start.7 = (f32[16,256]{1,0:T(8,128)S(1)}, f32[16,256]{1,0:T(8,128)S(1)}, u32[]{:S(2)}, u32[]{:S(2)}) collective-permute-start(f32[16,256]{1,0:T(8,128)S(1)} %add_add_fusion), channel_id=1, source_target_pairs={{0,56},{8,0},{16,8},{24,16},{32,24},{40,32},{48,40},{56,48},{64,12... | collective-permute-start | bytes 49160 | tf_op jit(solution)/shard_map/ppermute | solution.py:360
  39.4 3.8 %collective-permute-start.6 = (f32[16,256]{1,0:T(8,128)S(1)}, f32[16,256]{1,0:T(8,128)S(1)}, u32[]{:S(2)}, u32[]{:S(2)}) collective-permute-start(f32[16,256]{1,0:T(8,128)S(1)} %add_add_fusion), channel_id=1, source_target_pairs={{0,8},{8,16},{16,24},{24,32},{32,40},{40,48},{48,56},{56,0},{64,72... | collective-permute-start | bytes 49160 | tf_op jit(solution)/shard_map/ppermute | solution.py:360
  43.2 4.7 %collective-permute-start.9 = (f32[16,256]{1,0:T(8,128)S(1)}, f32[16,256]{1,0:T(8,128)S(1)}, u32[]{:S(2)}, u32[]{:S(2)}) collective-permute-start(f32[16,256]{1,0:T(8,128)S(1)} %get-tuple-element.54), channel_id=1, source_target_pairs={{0,16},{8,24},{16,32},{24,40},{32,48},{40,56},{48,0},{56,8},{64,80... | collective-permute-start | bytes 49160 | tf_op jit(solution)/shard_map/ppermute | solution.py:360
  43.2 4.7 %collective-permute-start.8 = (f32[16,256]{1,0:T(8,128)S(1)}, f32[16,256]{1,0:T(8,128)S(1)}, u32[]{:S(2)}, u32[]{:S(2)}) collective-permute-start(f32[16,256]{1,0:T(8,128)S(1)} %get-tuple-element.53.first_ref), channel_id=1, source_target_pairs={{0,40},{8,48},{16,56},{24,0},{32,8},{40,16},{48,24},{56,32},{64,10... | collective-permute-start | bytes 49160 | tf_op jit(solution)/shard_map/ppermute | solution.py:360
  48.4 3.0 %collective-permute-start.12 = (f32[16,256]{1,0:T(8,128)S(1)}, f32[16,256]{1,0:T(8,128)S(1)}, u32[]{:S(2)}, u32[]{:S(2)}) collective-permute-start(f32[16,256]{1,0:T(8,128)S(1)} %cuts.1.refs_0_), channel_id=1, source_target_pairs={{0,192},{8,200},{16,208},{24,216},{32,224},{40,232},{48,240},{56,2... | collective-permute-start | bytes 49160 | tf_op jit(solution)/shard_map/ppermute | solution.py:364
  49.3 4.1 %collective-permute-start.11 = (f32[16,256]{1,0:T(8,128)S(1)}, f32[16,256]{1,0:T(8,128)S(1)}, u32[]{:S(2)}, u32[]{:S(2)}) collective-permute-start(f32[16,256]{1,0:T(8,128)S(1)} %cuts.1.refs_0_), channel_id=1, source_target_pairs={{0,128},{8,136},{16,144},{24,152},{32,160},{40,168},{48,176},{56,1... | collective-permute-start | bytes 49160 | tf_op jit(solution)/shard_map/ppermute | solution.py:364
  50.6 3.8 %collective-permute-start.10 = (f32[16,256]{1,0:T(8,128)S(1)}, f32[16,256]{1,0:T(8,128)S(1)}, u32[]{:S(2)}, u32[]{:S(2)}) collective-permute-start(f32[16,256]{1,0:T(8,128)S(1)} %cuts.1.refs_0_), channel_id=1, source_target_pairs={{0,64},{8,72},{16,80},{24,88},{32,96},{40,104},{48,112},{56,120},{... | collective-permute-start | bytes 49160 | tf_op jit(solution)/shard_map/ppermute | solution.py:364
  55.8 19.1 %collective-permute-start.13 = (f32[64,1024]{1,0:T(8,128)S(1)}, f32[64,1024]{1,0:T(8,128)S(1)}, u32[]{:S(2)}, u32[]{:S(2)}) collective-permute-start(f32[64,1024]{1,0:T(8,128)S(1)} %get-tuple-element.45), channel_id=1, source_target_pairs={{0,4},{1,5},{2,6},{3,7},{4,0},{5,1},{6,2},{7,3},{8,12},{9,13},{10,... | collective-permute-start | bytes 786440 | tf_op jit(solution)/shard_map/ppermute | solution.py:352
  59.2 16.1 %collective-permute-start.18 = (f32[64,1024]{1,0:T(8,128)S(1)}, f32[64,1024]{1,0:T(8,128)S(1)}, u32[]{:S(2)}, u32[]{:S(2)}) collective-permute-start(f32[64,1024]{1,0:T(8,128)S(1)} %get-tuple-element.51), channel_id=1, source_target_pairs={{0,7},{1,6},{2,1},{3,0},{4,3},{5,2},{6,5},{7,4},{8,15},{9,14},{10,... | collective-permute-start | bytes 786440 | tf_op jit(solution)/shard_map/ppermute | solution.py:352
  67.4 11.1 %collective-permute-start.19 = (f32[64,1024]{1,0:T(8,128)S(1)}, f32[64,1024]{1,0:T(8,128)S(1)}, u32[]{:S(2)}, u32[]{:S(2)}) collective-permute-start(f32[64,1024]{1,0:T(8,128)S(1)} %get-tuple-element.52), channel_id=1, source_target_pairs={{0,1},{1,0},{2,3},{3,2},{4,5},{5,4},{6,7},{7,6},{8,9},{9,8},{10,11... | collective-permute-start | bytes 786440 | tf_op jit(solution)/shard_map/ppermute | solution.py:352
  70.0 8.5 %collective-permute-start.16 = (f32[64,1024]{1,0:T(8,128)S(1)}, f32[64,1024]{1,0:T(8,128)S(1)}, u32[]{:S(2)}, u32[]{:S(2)}) collective-permute-start(f32[64,1024]{1,0:T(8,128)S(1)} %get-tuple-element.49), channel_id=1, source_target_pairs={{0,6},{1,7},{2,0},{3,1},{4,2},{5,3},{6,4},{7,5},{8,14},{9,15},{10,... | collective-permute-start | bytes 786440 | tf_op jit(solution)/shard_map/ppermute | solution.py:352
  70.8 15.6 %collective-permute-start.17 = (f32[64,1024]{1,0:T(8,128)S(1)}, f32[64,1024]{1,0:T(8,128)S(1)}, u32[]{:S(2)}, u32[]{:S(2)}) collective-permute-start(f32[64,1024]{1,0:T(8,128)S(1)} %get-tuple-element.50), channel_id=1, source_target_pairs={{0,3},{1,2},{2,5},{3,4},{4,7},{5,6},{6,1},{7,0},{8,11},{9,10},{10,... | collective-permute-start | bytes 786440 | tf_op jit(solution)/shard_map/ppermute | solution.py:352
  75.0 11.4 %collective-permute-start.14 = (f32[64,1024]{1,0:T(8,128)S(1)}, f32[64,1024]{1,0:T(8,128)S(1)}, u32[]{:S(2)}, u32[]{:S(2)}) collective-permute-start(f32[64,1024]{1,0:T(8,128)S(1)} %get-tuple-element.47), channel_id=1, source_target_pairs={{0,5},{1,4},{2,7},{3,6},{4,1},{5,0},{6,3},{7,2},{8,13},{9,12},{10,... | collective-permute-start | bytes 786440 | tf_op jit(solution)/shard_map/ppermute | solution.py:352
  75.2 16.8 %collective-permute-start.15 = (f32[64,1024]{1,0:T(8,128)S(1)}, f32[64,1024]{1,0:T(8,128)S(1)}, u32[]{:S(2)}, u32[]{:S(2)}) collective-permute-start(f32[64,1024]{1,0:T(8,128)S(1)} %get-tuple-element.48), channel_id=1, source_target_pairs={{0,2},{1,3},{2,4},{3,5},{4,6},{5,7},{6,0},{7,1},{8,10},{9,11},{10,... | collective-permute-start | bytes 786440 | tf_op jit(solution)/shard_map/ppermute | solution.py:352

commit v5 on v4

--- a/solution.py
+++ b/solution.py
@@ -70,7 +70,6 @@
 
 def slot_kernel(turn, codes_hbm, values_hbm, top_ref, low_ref, codes_ref, values_ref, sems):
     rows = values_ref.shape[1]
-    width = 32
     group = (lax.axis_index("rows") // 8 + turn) % 4
     own = pl.ds(pl.multiple_of(group * FEATS, FEATS), FEATS)
     span = rows // 2
@@ -81,9 +80,17 @@
     for copy in copies:
         copy.start()
     copies[0].wait()
+    for part in range(2):
+        copies[1 + part].wait()
+        search_slots(0, codes_ref, values_ref, top_ref, low_ref, (part / 2, (part + 1) / 2))
+
+
+def search_slots(first, codes_ref, values_ref, top_ref, low_ref, share):
+    width = 32
+    steps = values_ref.shape[1] // (width * LANES)
     tables = []
     for half in range(2):
-        at = slice(8 * half, 8 * half + 8)
+        at = pl.ds(first + 8 * half, 8)
         even, odd = even_odd(codes_ref[at, :])
         tables.append((at, odd, (even, spread(even))))
 
@@ -102,10 +109,25 @@
             low_ref[:, column] = jnp.concatenate(low, axis=0).astype(jnp.bfloat16)
         return carry
 
-    steps = span // (width * LANES)
-    for part in range(2):
-        copies[1 + part].wait()
-        lax.fori_loop(part * steps, (part + 1) * steps, chunk, 0)
+    lax.fori_loop(int(share[0] * steps), int(share[1] * steps), chunk, 0)
+
+
+def near_slot_kernel(turn, codes_ref, values_ref, top_ref, low_ref):
+    group = (lax.axis_index("rows") // 8 + turn) % 4
+    search_slots(pl.multiple_of(group * FEATS, FEATS), codes_ref, values_ref, top_ref, low_ref, (0, 1))
+
+
+def find_near_slots(turn, edge_codes, values):
+    slots = jax.ShapeDtypeStruct((FEATS, values.shape[1]), jnp.bfloat16)
+    return pl.pallas_call(
+        lambda *refs: near_slot_kernel(turn, *refs),
+        in_specs=in_vmem(2),
+        out_specs=in_vmem(2),
+        out_shape=[slots, slots],
+        compiler_params=pltpu.CompilerParams(vmem_limit_bytes=16 << 20),
+        cost_estimate=pl.CostEstimate(flops=10**7, bytes_accessed=10**7, transcendentals=0),
+        name="slots",
+    )(edge_codes, values)
 
 
 def find_slots(turn, edge_codes, values):
@@ -263,19 +285,32 @@
         write(jnp.where(value >= last, 256.0 + (value - last) * inv_last, inside))
 
 
-def first_kernel(moves, c0, c1, c2, c3, values_ref, cuts_ref, *out_refs):
+def collect_kernel(c0, c1, c2, c3, cuts_ref):
     mine = lax.axis_index("rows") // 8
     for turn, c_ref in enumerate((c0, c1, c2, c3)):
         group = (mine + 4 - turn) % 4
         cuts_ref[pl.ds(pl.multiple_of(group * FEATS, FEATS), FEATS), :] = c_ref[...]
-    place_kernel(moves, cuts_ref, values_ref, *out_refs)
+
+
+def collect(parts):
+    return pl.pallas_call(
+        collect_kernel,
+        in_specs=in_vmem(4),
+        out_specs=in_vmem(1)[0],
+        out_shape=jax.ShapeDtypeStruct((4 * FEATS, 256), jnp.float32),
+        compiler_params=pltpu.CompilerParams(vmem_limit_bytes=4 << 20),
+        name="collect",
+    )(*parts)
 
 
 def place_kernel(moves, cuts_ref, values_ref, *out_refs):
+    wide = out_refs[0].shape[1]
+    place_blocks([owner(move) * wide for move in moves], cuts_ref, values_ref, out_refs)
+
+
+def place_blocks(bases, cuts_ref, values_ref, out_refs):
     feats, wide = out_refs[0].shape
-    bases = [owner(move) * wide for move in moves]
-
-    together = max(1, 8 // len(moves))
+    together = 4
 
     def store(out_ref, at, part):
         def write(value):
@@ -302,45 +337,76 @@
 def place(moves, cuts, values):
     feats, rows = values.shape
     block = jax.ShapeDtypeStruct((feats, rows // 8), jnp.float32)
-    first = len(cuts) > 1
-    kernel = first_kernel if first else place_kernel
-    outs = [jax.ShapeDtypeStruct((feats, 256), jnp.float32)] * first + [block] * len(moves)
-    return pl.pallas_call(
-        lambda *refs: kernel(moves, *refs),
-        in_specs=in_vmem(len(cuts) + 1),
-        out_specs=in_vmem(len(outs)),
-        out_shape=outs,
+    return pl.pallas_call(
+        lambda *refs: place_kernel(moves, *refs),
+        in_specs=in_vmem(2),
+        out_specs=in_vmem(len(moves)),
+        out_shape=[block] * len(moves),
         compiler_params=pltpu.CompilerParams(vmem_limit_bytes=16 << 20),
         cost_estimate=pl.CostEstimate(flops=10**7 * len(moves), bytes_accessed=10**6, transcendentals=0),
         name="place",
-    )(*cuts, values)
-
-
-def join_kernel(moves, *refs):
-    *parts, out_ref, sems = refs
-    feats = parts[0].shape[0]
+    )(cuts, values)
+
+
+def cut_kernel(moves, values_hbm, *refs):
+    *outs, sems = refs
+    wide = outs[0].shape[1]
     copies = []
-    for index, (move, part) in enumerate(zip(moves, parts)):
-        back = (-move[0], move[1])
-        rows = pl.ds(pl.multiple_of(owner(back) * feats, feats), feats)
-        copies.append(pltpu.make_async_copy(part, out_ref.at[rows, :], sems.at[index]))
+    for index, (move, out) in enumerate(zip(moves, outs)):
+        at = pl.ds(pl.multiple_of(owner(move) * wide, wide), wide)
+        copies.append(pltpu.make_async_copy(values_hbm.at[:, at], out, sems.at[index]))
     for copy in copies:
         copy.start()
     for copy in copies:
         copy.wait()
 
 
-def join(moves, parts):
+def cut_blocks(moves, values):
+    feats, rows = values.shape
+    return pl.pallas_call(
+        lambda *refs: cut_kernel(moves, *refs),
+        in_specs=[pl.BlockSpec(memory_space=pltpu.HBM)],
+        out_specs=in_vmem(len(moves)),
+        out_shape=[jax.ShapeDtypeStruct((feats, rows // 8), jnp.float32)] * len(moves),
+        scratch_shapes=[pltpu.SemaphoreType.DMA((len(moves),))],
+        compiler_params=pltpu.CompilerParams(vmem_limit_bytes=4 << 20),
+        name="cut",
+    )(pltpu.with_memory_space_constraint(values, pltpu.HBM))
+
+
+def finish_kernel(moves, far_moves, *refs):
+    count, far = len(moves), len(far_moves)
+    parts, far_cuts, far_values = refs[:count], refs[count : count + far], refs[count + far : count + 2 * far]
+    out_ref, *far_outs, sems = refs[count + 2 * far :]
+    feats = out_ref.shape[0] // (count + far)
+
+    def send(index, move, part):
+        rows = pl.ds(pl.multiple_of(owner((-move[0], move[1])) * feats, feats), feats)
+        copy = pltpu.make_async_copy(part, out_ref.at[rows, :], sems.at[index])
+        copy.start()
+        return copy
+
+    copies = [send(index, move, part) for index, (move, part) in enumerate(zip(moves, parts))]
+    for index, move in enumerate(far_moves):
+        place_blocks([0], far_cuts[index], far_values[index], [far_outs[index]])
+        copies.append(send(count + index, move, far_outs[index]))
+    for copy in copies:
+        copy.wait()
+
+
+def finish(moves, parts, far_moves, far_cuts, far_values):
     feats, wide = parts[0].shape
-    return pl.pallas_call(
-        lambda *refs: join_kernel(moves, *refs),
-        in_specs=in_vmem(len(parts)),
+    blocks = len(moves) + len(far_moves)
+    return pl.pallas_call(
+        lambda *refs: finish_kernel(moves, far_moves, *refs),
+        in_specs=in_vmem(len(parts) + 2 * len(far_moves)),
         out_specs=pl.BlockSpec(memory_space=pl.ANY),
-        out_shape=jax.ShapeDtypeStruct((len(parts) * feats, wide), jnp.float32),
-        scratch_shapes=[pltpu.SemaphoreType.DMA((len(parts),))],
-        compiler_params=pltpu.CompilerParams(vmem_limit_bytes=4 << 20),
-        name="join",
-    )(*parts)
+        out_shape=jax.ShapeDtypeStruct((blocks * feats, wide), jnp.float32),
+        scratch_shapes=[pltpu.VMEM((feats, wide), jnp.float32)] * len(far_moves)
+        + [pltpu.SemaphoreType.DMA((blocks,))],
+        compiler_params=pltpu.CompilerParams(vmem_limit_bytes=16 << 20),
+        name="finish",
+    )(*parts, *far_cuts, *far_values)
 
 
 def owner(move):
@@ -368,30 +434,35 @@
     hess_own = hessian_codes.astype(jnp.float32) * (1.0 / 65536.0)
     hess = hess_own.reshape(1, -1)
     slots = {}
-    codes = edge_codes
+    codes, values = edge_codes, feature_values
     for flip, turns in ((1, (1,)), (2, (2,)), (4, (3, 0))):
         other = flip_feat(hess, flip)
         for turn in turns:
-            slots[turn] = find_slots(turn, codes, feature_values)
+            search = find_slots if turn == 1 else find_near_slots
+            slots[turn] = search(turn, codes, values)
         hess = jnp.concatenate([hess, other], axis=0)
         if flip < 4:
             hess, slots[turn], codes = lax.optimization_barrier((hess, slots[turn], codes))
+    far_moves = [(2, 0), (2, 1)]
+    far_blocks, hess = lax.optimization_barrier((cut_blocks(far_moves, feature_values), hess))
+    far_values = [send_feat(block, move) for block, move in zip(far_blocks, far_moves)]
     parts = [turn_rows(find_mass(hess, *slots[turn]), turn) for turn in (1, 2, 3)]
     mass = find_mass(hess, *slots[0]) + parts[0] + parts[1] + parts[2]
     before = mass + shift_rows(mass, 1)
     around = before + shift_rows(mass, -1)
     cuts = find_cuts(edge_codes, cut_ranks, around, shift_rows(around, -3), shift_rows(before, 2))
+    cuts, far_values = lax.optimization_barrier((cuts, far_values))
     cuts = [cuts] + [turn_rows(cuts, turn) for turn in (1, 2, 3)]
-    stages = [[(2, 0)], [(2, 1), (1, 0)], [(3, 0), (1, 1)], [(3, 1), (0, 1)], [(0, 0)]]
+    cuts = collect(cuts)
+    far_cuts = [send_feat(cuts, move) for move in far_moves]
+    stages = [[(1, 0), (3, 0)], [(1, 1), (3, 1)], [(0, 1)], [(0, 0)]]
     moves, parts = [], []
     for stage in stages:
         outs = place(stage, cuts, feature_values)
-        if len(cuts) > 1:
-            cuts, *outs = outs
-            cuts = [cuts]
+        cuts, outs = lax.optimization_barrier((cuts, outs))
         moves += stage
         parts += [send_feat(out, move) if move != (0, 0) else out for out, move in zip(outs, stage)]
-    return join(moves, parts)
+    return finish(moves, parts, far_moves, far_cuts, far_values)
 
 
 def solution(mesh):

time: 94.1 us -> 88.1 us (0.936)
  waiting for transfers between devices: 23.6 us -> 15.8 us
  starting transfers between devices: 34 us -> 36.8 us
    ppermute x7 -> x9, waiting for transfers between devices: 13.5 us -> 5.03 us  [send_feat(): lax.ppermute(array, 'feat', [(i, (i // 2 + move[0]) % 4 * 2 + (i % 2 ^ mo...]
    pallas_call x4 -> x1, Pallas kernels: 10.6 us -> 3.03 us  [find_slots(): pl.pallas_call(lambda *refs: slot_kernel(turn, *refs), in_specs=[pl.Block...]
    pallas_call x6 -> x10, Pallas kernels: 12.2 us -> 19 us  [the longest x4 8.47 us: place(): pl.pallas_call(lambda *refs: place_kernel(moves, *refs), in_specs=in_vmem...]
    ppermute x7 -> x9, starting transfers between devices: 13.2 us -> 16.3 us  [send_feat(): lax.ppermute(array, 'feat', [(i, (i // 2 + move[0]) % 4 * 2 + (i % 2 ^ mo...]
  transfers between devices with their start and end apart: 20 -> 22, of which waited for: 8 -> 8; matrix products, arithmetic and copies ran while one was open for 0% -> 0% of each run, Pallas kernels for 31% -> 31%
where the time goes in v5:
time: 88.1 us; the launch traced here: 87.9 us
  starting transfers between devices  36.8 us (42%)
  Pallas kernels  33.9 us (38%)
  waiting for transfers between devices  15.8 us (18%)
  other arithmetic  0.89 us (1%)
    ppermute x9, starting transfers between devices, send_feat(): lax.ppermute(array, 'feat', [(i, (i // 2 + move[0]) % 4 * 2 + (i % 2 ^ mo...  16.3 us
    pallas_call x4, Pallas kernels, find_mass(): pl.pallas_call(hist_kernel, in_specs=in_vmem(3), out_specs=in_vmem(1)[0],...  11.4 us
    pallas_call x4, Pallas kernels, place(): pl.pallas_call(lambda *refs: place_kernel(moves, *refs), in_specs=in_vmem...  8.47 us
    ppermute x4, starting transfers between devices, shift_rows(): lax.ppermute(array, 'rows', [(i, i // 8 * 8 + (i + shift) % 8) for i in r...  8.11 us
    ppermute x6, starting transfers between devices, turn_rows(): lax.ppermute(array, 'rows', [(i, (i + 8 * turn) % 32) for i in range(32)])  7.43 us
    ppermute x4, waiting for transfers between devices, shift_rows(): lax.ppermute(array, 'rows', [(i, i // 8 * 8 + (i + shift) % 8) for i in r...  6.04 us
    pallas_call x3, Pallas kernels, find_near_slots(): pl.pallas_call(lambda *refs: near_slot_kernel(turn, *refs), in_specs=in_v...  5.62 us
    ppermute x9, waiting for transfers between devices, send_feat(): lax.ppermute(array, 'feat', [(i, (i // 2 + move[0]) % 4 * 2 + (i % 2 ^ mo...  5.03 us
  transfers between devices with their start and end apart: 22, of which 8 were waited for; matrix products, arithmetic and copies ran while one was open for 0% of the time, Pallas kernels for 31%

profile of v5, /device:TPU:1, one launch (start us, length us, event | category | flops | bytes accessed | tf_op | source)
XLA Modules:
  0.0 87.9 jit_solution(610645501611821097)
XLA Ops:
  0.0 0.8 convert_multiply_fusion
  0.8 3.2 %collective-permute-start = (f32[1,1024]{1,0:T(1,128)S(1)}, f32[1,1024]{1,0:T(1,128)S(1)}, u32[]{:S(2)}, u32[]{:S(2)}) collective-permute-start(f32[1,1024]{1,0:T(1,128)S(1)} %bitcast.1), channel_id=1, source_target_pairs={{0,1},{1,0},{2,3},{3,2},{4,5},{5,4},{6,7},{7,6},{8,9},{9,8},{10,11... | collective-permute-start | bytes 12296 | tf_op jit(solution)/shard_map/ppermute | solution.py:422
  4.1 3.0 %slots.4 = (bf16[16,8192]{1,0:T(8,128)(2,1)S(1)}, bf16[16,8192]{1,0:T(8,128)(2,1)S(1)}) custom-call(s32[64,256]{1,0:T(8,128)} %codes_ref.1, f32[64,8192]{1,0:T(8,128)} %refs_1_.15), custom_call_target="tpu_custom_call" | custom-call | flops 10000000 | bytes 10000000 | tf_op jit(solution)/shard_map/slots/pallas_call | solution.py:136
  7.2 0.0 copy-start.1
  7.2 0.1 collective-permute-start.1
  7.3 1.9 %slots.5 = (bf16[16,8192]{1,0:T(8,128)(2,1)S(1)}, bf16[16,8192]{1,0:T(8,128)(2,1)S(1)}) custom-call(s32[64,256]{1,0:T(8,128)S(1)} %copy-done.2, f32[64,8192]{1,0:T(8,128)S(1)} %copy-done), custom_call_target="tpu_custom_call" | custom-call | flops 10000000 | bytes 10000000 | tf_op jit(solution)/shard_map/slots/pallas_call | solution.py:122
  9.2 0.6 collective-permute-done.1
  9.8 1.7 %collective-permute-start.2 = (f32[4,1024]{1,0:T(4,128)S(1)}, f32[4,1024]{1,0:T(4,128)S(1)}, u32[]{:S(2)}, u32[]{:S(2)}) collective-permute-start(f32[4,1024]{1,0:T(4,128)S(1)} %pad_maximum_fusion.1), channel_id=1, source_target_pairs={{0,4},{1,5},{2,6},{3,7},{4,0},{5,1},{6,2},{7,3},{8,12},{9,13},{10,... | collective-permute-start | bytes 49160 | tf_op jit(solution)/shard_map/ppermute | solution.py:422
  11.4 1.0 %cut.1 = (f32[64,1024]{1,0:T(8,128)S(1)}, f32[64,1024]{1,0:T(8,128)S(1)}) custom-call(f32[64,8192]{1,0:T(8,128)} %refs_1_.15), custom_call_target="tpu_custom_call" | custom-call | tf_op jit(solution)/shard_map/cut/pallas_call | solution.py:366
  12.5 1.9 %slots.7 = (bf16[16,8192]{1,0:T(8,128)(2,1)S(1)}, bf16[16,8192]{1,0:T(8,128)(2,1)S(1)}) custom-call(s32[64,256]{1,0:T(8,128)S(1)} %copy-done.2, f32[64,8192]{1,0:T(8,128)S(1)} %copy-done.1), custom_call_target="tpu_custom_call" | custom-call | flops 10000000 | bytes 10000000 | tf_op jit(solution)/shard_map/slots/pallas_call | solution.py:122
  14.4 1.9 %slots.6 = (bf16[16,8192]{1,0:T(8,128)(2,1)S(1)}, bf16[16,8192]{1,0:T(8,128)(2,1)S(1)}) custom-call(s32[64,256]{1,0:T(8,128)S(1)} %copy-done.2, f32[64,8192]{1,0:T(8,128)S(1)} %copy-done.1), custom_call_target="tpu_custom_call" | custom-call | flops 10000000 | bytes 10000000 | tf_op jit(solution)/shard_map/slots/pallas_call | solution.py:122
  16.3 0.0 collective-permute-done.2
  16.3 2.9 %hist.5 = f32[16,256]{1,0:T(8,128)S(1)} custom-call(f32[8,1024]{1,0:T(8,128)S(1)} %pad_maximum_fusion.hess_ref, bf16[16,8192]{1,0:T(8,128)(2,1)S(1)} %get-tuple-element.55.top_ref, bf16[16,8192]{1,0:T(8,128)(2,1)S(1)} %get-tuple-element.56.low_ref), custom_call_target="tpu_custom_call" | custom-call | flops 4000000000 | bytes 10000000 | tf_op jit(solution)/shard_map/hist/pallas_call | solution.py:213
  19.2 1.3 %collective-permute-start.3 = (f32[16,256]{1,0:T(8,128)S(1)}, f32[16,256]{1,0:T(8,128)S(1)}, u32[]{:S(2)}, u32[]{:S(2)}) collective-permute-start(f32[16,256]{1,0:T(8,128)S(1)} %hist.5), channel_id=1, source_target_pairs={{0,64},{8,72},{16,80},{24,88},{32,96},{40,104},{48,112},{56,120},{... | collective-permute-start | bytes 49160 | tf_op jit(solution)/shard_map/ppermute | solution.py:430
  20.4 2.9 %hist.6 = f32[16,256]{1,0:T(8,128)S(1)} custom-call(f32[8,1024]{1,0:T(8,128)S(1)} %pad_maximum_fusion.hess_ref, bf16[16,8192]{1,0:T(8,128)(2,1)S(1)} %get-tuple-element.57.top_ref, bf16[16,8192]{1,0:T(8,128)(2,1)S(1)} %get-tuple-element.58.low_ref), custom_call_target="tpu_custom_call" | custom-call | flops 4000000000 | bytes 10000000 | tf_op jit(solution)/shard_map/hist/pallas_call | solution.py:213
  23.3 2.5 %collective-permute-start.4 = (f32[16,256]{1,0:T(8,128)S(1)}, f32[16,256]{1,0:T(8,128)S(1)}, u32[]{:S(2)}, u32[]{:S(2)}) collective-permute-start(f32[16,256]{1,0:T(8,128)S(1)} %hist.6), channel_id=1, source_target_pairs={{0,128},{8,136},{16,144},{24,152},{32,160},{40,168},{48,176},{56,1... | collective-permute-start | bytes 49160 | tf_op jit(solution)/shard_map/ppermute | solution.py:430
  25.8 2.9 %hist.7 = f32[16,256]{1,0:T(8,128)S(1)} custom-call(f32[8,1024]{1,0:T(8,128)S(1)} %pad_maximum_fusion.hess_ref, bf16[16,8192]{1,0:T(8,128)(2,1)S(1)} %get-tuple-element.59.top_ref, bf16[16,8192]{1,0:T(8,128)(2,1)S(1)} %get-tuple-element.60.low_ref), custom_call_target="tpu_custom_call" | custom-call | flops 4000000000 | bytes 10000000 | tf_op jit(solution)/shard_map/hist/pallas_call | solution.py:213
  28.7 1.4 %collective-permute-start.5 = (f32[16,256]{1,0:T(8,128)S(1)}, f32[16,256]{1,0:T(8,128)S(1)}, u32[]{:S(2)}, u32[]{:S(2)}) collective-permute-start(f32[16,256]{1,0:T(8,128)S(1)} %hist.7), channel_id=1, source_target_pairs={{0,192},{8,200},{16,208},{24,216},{32,224},{40,232},{48,240},{56,2... | collective-permute-start | bytes 49160 | tf_op jit(solution)/shard_map/ppermute | solution.py:430
  30.1 0.3 collective-permute-start.10
  30.5 4.7 %collective-permute-start.11 = (f32[64,1024]{1,0:T(8,128)S(1)}, f32[64,1024]{1,0:T(8,128)S(1)}, u32[]{:S(2)}, u32[]{:S(2)}) collective-permute-start(f32[64,1024]{1,0:T(8,128)S(1)} %get-tuple-element.62), channel_id=1, source_target_pairs={{0,5},{1,4},{2,7},{3,6},{4,1},{5,0},{6,3},{7,2},{8,13},{9,12},{10,... | collective-permute-start | bytes 786440 | tf_op jit(solution)/shard_map/ppermute | solution.py:418
  35.1 2.9 %hist.4 = f32[16,256]{1,0:T(8,128)S(1)} custom-call(f32[8,1024]{1,0:T(8,128)S(1)} %pad_maximum_fusion.hess_ref, bf16[16,8192]{1,0:T(8,128)(2,1)S(1)} %get-tuple-element.53.top_ref, bf16[16,8192]{1,0:T(8,128)(2,1)S(1)} %get-tuple-element.54.low_ref), custom_call_target="tpu_custom_call" | custom-call | flops 4000000000 | bytes 10000000 | tf_op jit(solution)/shard_map/hist/pallas_call | solution.py:213
  38.0 0.0 collective-permute-done.3
  38.0 0.0 collective-permute-done.5
  38.1 5.7 %collective-permute-start.7 = (f32[16,256]{1,0:T(8,128)S(1)}, f32[16,256]{1,0:T(8,128)S(1)}, u32[]{:S(2)}, u32[]{:S(2)}) collective-permute-start(f32[16,256]{1,0:T(8,128)S(1)} %add_add_fusion), channel_id=1, source_target_pairs={{0,56},{8,0},{16,8},{24,16},{32,24},{40,32},{48,40},{56,48},{64,12... | collective-permute-start | bytes 49160 | tf_op jit(solution)/shard_map/ppermute | solution.py:426
  43.7 0.0 collective-permute-start.6
  43.7 0.9 collective-permute-done.7
  44.6 2.9 %collective-permute-done.6 = f32[16,256]{1,0:T(8,128)S(1)} collective-permute-done((f32[16,256]{1,0:T(8,128)S(1)}, f32[16,256]{1,0:T(8,128)S(1)}, u32[]{:S(2)}, u32[]{:S(2)}) %collective-permute-start.6) | collective-permute-done | bytes 16416 | tf_op jit(solution)/shard_map/ppermute | solution.py:426
  47.5 2.5 %collective-permute-start.8 = (f32[16,256]{1,0:T(8,128)S(1)}, f32[16,256]{1,0:T(8,128)S(1)}, u32[]{:S(2)}, u32[]{:S(2)}) collective-permute-start(f32[16,256]{1,0:T(8,128)S(1)} %get-tuple-element.79.first_ref), channel_id=1, source_target_pairs={{0,40},{8,48},{16,56},{24,0},{32,8},{40,16},{48,24},{56,32},{64,10... | collective-permute-start | bytes 49160 | tf_op jit(solution)/shard_map/ppermute | solution.py:426
  50.0 2.2 %collective-permute-done.9.third_ref = f32[16,256]{1,0:T(8,128)S(1)} collective-permute-done((f32[16,256]{1,0:T(8,128)S(1)}, f32[16,256]{1,0:T(8,128)S(1)}, u32[]{:S(2)}, u32[]{:S(2)}) %collective-permute-start.9) | collective-permute-done | bytes 16416 | tf_op jit(solution)/shard_map/ppermute | solution.py:426
  52.2 0.5 cuts.1.c0
  52.7 0.1 collective-permute-start.14
  52.8 2.1 %collective-permute-start.13 = (f32[16,256]{1,0:T(8,128)S(1)}, f32[16,256]{1,0:T(8,128)S(1)}, u32[]{:S(2)}, u32[]{:S(2)}) collective-permute-start(f32[16,256]{1,0:T(8,128)S(1)} %cuts.1.c0), channel_id=1, source_target_pairs={{0,128},{8,136},{16,144},{24,152},{32,160},{40,168},{48,176},{56,1... | collective-permute-start | bytes 49160 | tf_op jit(solution)/shard_map/ppermute | solution.py:430
  54.9 0.5 collective-permute-done.14.c3
  55.4 1.6 %collective-permute-done.13.c2 = f32[16,256]{1,0:T(8,128)S(1)} collective-permute-done((f32[16,256]{1,0:T(8,128)S(1)}, f32[16,256]{1,0:T(8,128)S(1)}, u32[]{:S(2)}, u32[]{:S(2)}) %collective-permute-start.13) | collective-permute-done | bytes 16416 | tf_op jit(solution)/shard_map/ppermute | solution.py:430
  57.0 2.0 %collective-permute-done.12.c1 = f32[16,256]{1,0:T(8,128)S(1)} collective-permute-done((f32[16,256]{1,0:T(8,128)S(1)}, f32[16,256]{1,0:T(8,128)S(1)}, u32[]{:S(2)}, u32[]{:S(2)}) %collective-permute-start.12) | collective-permute-done | bytes 16416 | tf_op jit(solution)/shard_map/ppermute | solution.py:430
  59.0 4.1 %collective-permute-start.21 = (f32[64,256]{1,0:T(8,128)S(1)}, f32[64,256]{1,0:T(8,128)S(1)}, u32[]{:S(2)}, u32[]{:S(2)}) collective-permute-start(f32[64,256]{1,0:T(8,128)S(1)} %collect.1.refs_0_), channel_id=1, source_target_pairs={{0,5},{1,4},{2,7},{3,6},{4,1},{5,0},{6,3},{7,2},{8,13},{9,12},{10,... | collective-permute-start | bytes 196616 | tf_op jit(solution)/shard_map/ppermute | solution.py:418
  63.1 1.3 %collective-permute-start.20 = (f32[64,256]{1,0:T(8,128)S(1)}, f32[64,256]{1,0:T(8,128)S(1)}, u32[]{:S(2)}, u32[]{:S(2)}) collective-permute-start(f32[64,256]{1,0:T(8,128)S(1)} %collect.1.refs_0_), channel_id=1, source_target_pairs={{0,4},{1,5},{2,6},{3,7},{4,0},{5,1},{6,2},{7,3},{8,12},{9,13},{10,... | collective-permute-start | bytes 196616 | tf_op jit(solution)/shard_map/ppermute | solution.py:418
  64.5 2.7 %place.4 = (f32[64,1024]{1,0:T(8,128)S(1)}, f32[64,1024]{1,0:T(8,128)S(1)}) custom-call(f32[64,256]{1,0:T(8,128)S(1)} %collect.1.refs_0_, f32[64,8192]{1,0:T(8,128)S(1)} %copy-done.1), custom_call_target="tpu_custom_call" | custom-call | flops 20000000 | bytes 1000000 | tf_op jit(solution)/shard_map/place/pallas_call | solution.py:340
  67.2 0.4 collective-permute-start.15
  67.6 2.3 %collective-permute-start.16 = (f32[64,1024]{1,0:T(8,128)S(1)}, f32[64,1024]{1,0:T(8,128)S(1)}, u32[]{:S(2)}, u32[]{:S(2)}) collective-permute-start(f32[64,1024]{1,0:T(8,128)S(1)} %get-tuple-element.67), channel_id=1, source_target_pairs={{0,6},{1,7},{2,0},{3,1},{4,2},{5,3},{6,4},{7,5},{8,14},{9,15},{10,... | collective-permute-start | bytes 786440 | tf_op jit(solution)/shard_map/ppermute | solution.py:418
  69.9 2.7 %place.5 = (f32[64,1024]{1,0:T(8,128)S(1)}, f32[64,1024]{1,0:T(8,128)S(1)}) custom-call(f32[64,256]{1,0:T(8,128)S(1)} %collect.1.refs_0_, f32[64,8192]{1,0:T(8,128)S(1)} %copy-done.1), custom_call_target="tpu_custom_call" | custom-call | flops 20000000 | bytes 1000000 | tf_op jit(solution)/shard_map/place/pallas_call | solution.py:340
  72.6 1.6 %place.6 = f32[64,1024]{1,0:T(8,128)S(1)} custom-call(f32[64,256]{1,0:T(8,128)S(1)} %collect.1.refs_0_, f32[64,8192]{1,0:T(8,128)S(1)} %copy-done.1), custom_call_target="tpu_custom_call" | custom-call | flops 10000000 | bytes 1000000 | tf_op jit(solution)/shard_map/place/pallas_call | solution.py:340
  74.2 0.1 collective-permute-start.19
  74.3 0.1 collective-permute-start.17
  74.4 2.9 %collective-permute-start.18 = (f32[64,1024]{1,0:T(8,128)S(1)}, f32[64,1024]{1,0:T(8,128)S(1)}, u32[]{:S(2)}, u32[]{:S(2)}) collective-permute-start(f32[64,1024]{1,0:T(8,128)S(1)} %get-tuple-element.72), channel_id=1, source_target_pairs={{0,7},{1,6},{2,1},{3,0},{4,3},{5,2},{6,5},{7,4},{8,15},{9,14},{10,... | collective-permute-start | bytes 786440 | tf_op jit(solution)/shard_map/ppermute | solution.py:418
  77.3 1.5 %place.7.refs_5_ = f32[64,1024]{1,0:T(8,128)S(1)} custom-call(f32[64,256]{1,0:T(8,128)S(1)} %collect.1.refs_0_, f32[64,8192]{1,0:T(8,128)S(1)} %copy-done.1), custom_call_target="tpu_custom_call" | custom-call | flops 10000000 | bytes 1000000 | tf_op jit(solution)/shard_map/place/pallas_call | solution.py:340
  78.9 5.0 %collective-permute-done.17.refs_2_ = f32[64,1024]{1,0:T(8,128)S(1)} collective-permute-done((f32[64,1024]{1,0:T(8,128)S(1)}, f32[64,1024]{1,0:T(8,128)S(1)}, u32[]{:S(2)}, u32[]{:S(2)}) %collective-permute-start.17) | collective-permute-done | bytes 262176 | tf_op jit(solution)/shard_map/ppermute | solution.py:418
  83.9 3.8 %finish.1 = f32[512,1024]{1,0:T(8,128)} custom-call(f32[64,1024]{1,0:T(8,128)S(1)} %collective-permute-done.15.refs_0_, f32[64,1024]{1,0:T(8,128)S(1)} %collective-permute-done.16.refs_1_, f32[64,1024]{1,0:T(8,128)S(1)} %collective-permute-done.17.refs_2_, f32[64,1024]{1,0:T(8,128)S(1)} %collective-permute-done.18.refs_3_, ...), custom_call_target="tpu_custom_call" | custom-call | tf_op jit(solution)/shard_map/finish/pallas_call | solution.py:400
  (26 shorter events, 0.1 us)
Async XLA Ops:
  0.0 7.3 %copy-start = (f32[64,8192]{1,0:T(8,128)S(1)}, f32[64,8192]{1,0:T(8,128)}, u32[]{:S(2)}) copy-start(f32[64,8192]{1,0:T(8,128)} %refs_1_.15) | copy-start | bytes 6291460
  0.0 7.3 %copy-start.2 = (s32[64,256]{1,0:T(8,128)S(1)}, s32[64,256]{1,0:T(8,128)}, u32[]{:S(2)}) copy-start(s32[64,256]{1,0:T(8,128)} %codes_ref.1) | copy-start | bytes 196612
  0.8 6.3 %collective-permute-start = (f32[1,1024]{1,0:T(1,128)S(1)}, f32[1,1024]{1,0:T(1,128)S(1)}, u32[]{:S(2)}, u32[]{:S(2)}) collective-permute-start(f32[1,1024]{1,0:T(1,128)S(1)} %bitcast.1), channel_id=1, source_target_pairs={{0,1},{1,0},{2,3},{3,2},{4,5},{5,4},{6,7},{7,6},{8,9},{9,8},{10,11... | collective-permute-start | bytes 12296 | tf_op jit(solution)/shard_map/ppermute | solution.py:422
  7.2 5.3 %copy-start.1 = (f32[64,8192]{1,0:T(8,128)S(1)}, f32[64,8192]{1,0:T(8,128)}, u32[]{:S(2)}) copy-start(f32[64,8192]{1,0:T(8,128)} %refs_1_.15) | copy-start | bytes 6291460
  7.2 2.6 %collective-permute-start.1 = (f32[2,1024]{1,0:T(2,128)S(1)}, f32[2,1024]{1,0:T(2,128)S(1)}, u32[]{:S(2)}, u32[]{:S(2)}) collective-permute-start(f32[2,1024]{1,0:T(2,128)S(1)} %pad_maximum_fusion.2), channel_id=1, source_target_pairs={{0,2},{1,3},{2,0},{3,1},{4,6},{5,7},{6,4},{7,5},{8,10},{9,11},{10,... | collective-permute-start | bytes 24584 | tf_op jit(solution)/shard_map/ppermute | solution.py:422
  9.8 6.5 %collective-permute-start.2 = (f32[4,1024]{1,0:T(4,128)S(1)}, f32[4,1024]{1,0:T(4,128)S(1)}, u32[]{:S(2)}, u32[]{:S(2)}) collective-permute-start(f32[4,1024]{1,0:T(4,128)S(1)} %pad_maximum_fusion.1), channel_id=1, source_target_pairs={{0,4},{1,5},{2,6},{3,7},{4,0},{5,1},{6,2},{7,3},{8,12},{9,13},{10,... | collective-permute-start | bytes 49160 | tf_op jit(solution)/shard_map/ppermute | solution.py:422
  19.2 18.9 %collective-permute-start.3 = (f32[16,256]{1,0:T(8,128)S(1)}, f32[16,256]{1,0:T(8,128)S(1)}, u32[]{:S(2)}, u32[]{:S(2)}) collective-permute-start(f32[16,256]{1,0:T(8,128)S(1)} %hist.5), channel_id=1, source_target_pairs={{0,64},{8,72},{16,80},{24,88},{32,96},{40,104},{48,112},{56,120},{... | collective-permute-start | bytes 49160 | tf_op jit(solution)/shard_map/ppermute | solution.py:430
  23.3 14.7 %collective-permute-start.4 = (f32[16,256]{1,0:T(8,128)S(1)}, f32[16,256]{1,0:T(8,128)S(1)}, u32[]{:S(2)}, u32[]{:S(2)}) collective-permute-start(f32[16,256]{1,0:T(8,128)S(1)} %hist.6), channel_id=1, source_target_pairs={{0,128},{8,136},{16,144},{24,152},{32,160},{40,168},{48,176},{56,1... | collective-permute-start | bytes 49160 | tf_op jit(solution)/shard_map/ppermute | solution.py:430
  28.7 9.3 %collective-permute-start.5 = (f32[16,256]{1,0:T(8,128)S(1)}, f32[16,256]{1,0:T(8,128)S(1)}, u32[]{:S(2)}, u32[]{:S(2)}) collective-permute-start(f32[16,256]{1,0:T(8,128)S(1)} %hist.7), channel_id=1, source_target_pairs={{0,192},{8,200},{16,208},{24,216},{32,224},{40,232},{48,240},{56,2... | collective-permute-start | bytes 49160 | tf_op jit(solution)/shard_map/ppermute | solution.py:430
  30.1 22.6 %collective-permute-start.10 = (f32[64,1024]{1,0:T(8,128)S(1)}, f32[64,1024]{1,0:T(8,128)S(1)}, u32[]{:S(2)}, u32[]{:S(2)}) collective-permute-start(f32[64,1024]{1,0:T(8,128)S(1)} %get-tuple-element.61), channel_id=1, source_target_pairs={{0,4},{1,5},{2,6},{3,7},{4,0},{5,1},{6,2},{7,3},{8,12},{9,13},{10,... | collective-permute-start | bytes 786440 | tf_op jit(solution)/shard_map/ppermute | solution.py:418
  30.5 22.3 %collective-permute-start.11 = (f32[64,1024]{1,0:T(8,128)S(1)}, f32[64,1024]{1,0:T(8,128)S(1)}, u32[]{:S(2)}, u32[]{:S(2)}) collective-permute-start(f32[64,1024]{1,0:T(8,128)S(1)} %get-tuple-element.62), channel_id=1, source_target_pairs={{0,5},{1,4},{2,7},{3,6},{4,1},{5,0},{6,3},{7,2},{8,13},{9,12},{10,... | collective-permute-start | bytes 786440 | tf_op jit(solution)/shard_map/ppermute | solution.py:418
  35.1 17.1 %copy-start.3 = (s32[64,256]{1,0:T(8,128)S(1)}, s32[64,256]{1,0:T(8,128)}, u32[]{:S(2)}) copy-start(s32[64,256]{1,0:T(8,128)} %ranks_ref.1) | copy-start | bytes 196612
  38.1 6.5 %collective-permute-start.7 = (f32[16,256]{1,0:T(8,128)S(1)}, f32[16,256]{1,0:T(8,128)S(1)}, u32[]{:S(2)}, u32[]{:S(2)}) collective-permute-start(f32[16,256]{1,0:T(8,128)S(1)} %add_add_fusion), channel_id=1, source_target_pairs={{0,56},{8,0},{16,8},{24,16},{32,24},{40,32},{48,40},{56,48},{64,12... | collective-permute-start | bytes 49160 | tf_op jit(solution)/shard_map/ppermute | solution.py:426
  43.7 3.8 %collective-permute-start.6 = (f32[16,256]{1,0:T(8,128)S(1)}, f32[16,256]{1,0:T(8,128)S(1)}, u32[]{:S(2)}, u32[]{:S(2)}) collective-permute-start(f32[16,256]{1,0:T(8,128)S(1)} %add_add_fusion), channel_id=1, source_target_pairs={{0,8},{8,16},{16,24},{24,32},{32,40},{40,48},{48,56},{56,0},{64,72... | collective-permute-start | bytes 49160 | tf_op jit(solution)/shard_map/ppermute | solution.py:426
  47.5 4.7 %collective-permute-start.9 = (f32[16,256]{1,0:T(8,128)S(1)}, f32[16,256]{1,0:T(8,128)S(1)}, u32[]{:S(2)}, u32[]{:S(2)}) collective-permute-start(f32[16,256]{1,0:T(8,128)S(1)} %get-tuple-element.80), channel_id=1, source_target_pairs={{0,16},{8,24},{16,32},{24,40},{32,48},{40,56},{48,0},{56,8},{64,80... | collective-permute-start | bytes 49160 | tf_op jit(solution)/shard_map/ppermute | solution.py:426
  47.5 4.7 %collective-permute-start.8 = (f32[16,256]{1,0:T(8,128)S(1)}, f32[16,256]{1,0:T(8,128)S(1)}, u32[]{:S(2)}, u32[]{:S(2)}) collective-permute-start(f32[16,256]{1,0:T(8,128)S(1)} %get-tuple-element.79.first_ref), channel_id=1, source_target_pairs={{0,40},{8,48},{16,56},{24,0},{32,8},{40,16},{48,24},{56,32},{64,10... | collective-permute-start | bytes 49160 | tf_op jit(solution)/shard_map/ppermute | solution.py:426
  52.7 2.7 %collective-permute-start.14 = (f32[16,256]{1,0:T(8,128)S(1)}, f32[16,256]{1,0:T(8,128)S(1)}, u32[]{:S(2)}, u32[]{:S(2)}) collective-permute-start(f32[16,256]{1,0:T(8,128)S(1)} %cuts.1.c0), channel_id=1, source_target_pairs={{0,192},{8,200},{16,208},{24,216},{32,224},{40,232},{48,240},{56,2... | collective-permute-start | bytes 49160 | tf_op jit(solution)/shard_map/ppermute | solution.py:430
  52.8 4.2 %collective-permute-start.13 = (f32[16,256]{1,0:T(8,128)S(1)}, f32[16,256]{1,0:T(8,128)S(1)}, u32[]{:S(2)}, u32[]{:S(2)}) collective-permute-start(f32[16,256]{1,0:T(8,128)S(1)} %cuts.1.c0), channel_id=1, source_target_pairs={{0,128},{8,136},{16,144},{24,152},{32,160},{40,168},{48,176},{56,1... | collective-permute-start | bytes 49160 | tf_op jit(solution)/shard_map/ppermute | solution.py:430
  54.9 4.1 %collective-permute-start.12 = (f32[16,256]{1,0:T(8,128)S(1)}, f32[16,256]{1,0:T(8,128)S(1)}, u32[]{:S(2)}, u32[]{:S(2)}) collective-permute-start(f32[16,256]{1,0:T(8,128)S(1)} %cuts.1.c0), channel_id=1, source_target_pairs={{0,64},{8,72},{16,80},{24,88},{32,96},{40,104},{48,112},{56,120},{... | collective-permute-start | bytes 49160 | tf_op jit(solution)/shard_map/ppermute | solution.py:430
  59.0 15.2 %collective-permute-start.21 = (f32[64,256]{1,0:T(8,128)S(1)}, f32[64,256]{1,0:T(8,128)S(1)}, u32[]{:S(2)}, u32[]{:S(2)}) collective-permute-start(f32[64,256]{1,0:T(8,128)S(1)} %collect.1.refs_0_), channel_id=1, source_target_pairs={{0,5},{1,4},{2,7},{3,6},{4,1},{5,0},{6,3},{7,2},{8,13},{9,12},{10,... | collective-permute-start | bytes 196616 | tf_op jit(solution)/shard_map/ppermute | solution.py:418
  63.1 11.2 %collective-permute-start.20 = (f32[64,256]{1,0:T(8,128)S(1)}, f32[64,256]{1,0:T(8,128)S(1)}, u32[]{:S(2)}, u32[]{:S(2)}) collective-permute-start(f32[64,256]{1,0:T(8,128)S(1)} %collect.1.refs_0_), channel_id=1, source_target_pairs={{0,4},{1,5},{2,6},{3,7},{4,0},{5,1},{6,2},{7,3},{8,12},{9,13},{10,... | collective-permute-start | bytes 196616 | tf_op jit(solution)/shard_map/ppermute | solution.py:418
  67.2 11.7 %collective-permute-start.15 = (f32[64,1024]{1,0:T(8,128)S(1)}, f32[64,1024]{1,0:T(8,128)S(1)}, u32[]{:S(2)}, u32[]{:S(2)}) collective-permute-start(f32[64,1024]{1,0:T(8,128)S(1)} %get-tuple-element.66), channel_id=1, source_target_pairs={{0,2},{1,3},{2,4},{3,5},{4,6},{5,7},{6,0},{7,1},{8,10},{9,11},{10,... | collective-permute-start | bytes 786440 | tf_op jit(solution)/shard_map/ppermute | solution.py:418
  67.6 11.3 %collective-permute-start.16 = (f32[64,1024]{1,0:T(8,128)S(1)}, f32[64,1024]{1,0:T(8,128)S(1)}, u32[]{:S(2)}, u32[]{:S(2)}) collective-permute-start(f32[64,1024]{1,0:T(8,128)S(1)} %get-tuple-element.67), channel_id=1, source_target_pairs={{0,6},{1,7},{2,0},{3,1},{4,2},{5,3},{6,4},{7,5},{8,14},{9,15},{10,... | collective-permute-start | bytes 786440 | tf_op jit(solution)/shard_map/ppermute | solution.py:418
  74.2 4.7 %collective-permute-start.19 = (f32[64,1024]{1,0:T(8,128)S(1)}, f32[64,1024]{1,0:T(8,128)S(1)}, u32[]{:S(2)}, u32[]{:S(2)}) collective-permute-start(f32[64,1024]{1,0:T(8,128)S(1)} %place.6), channel_id=1, source_target_pairs={{0,1},{1,0},{2,3},{3,2},{4,5},{5,4},{6,7},{7,6},{8,9},{9,8},{10,11... | collective-permute-start | bytes 786440 | tf_op jit(solution)/shard_map/ppermute | solution.py:418
  74.3 9.6 %collective-permute-start.17 = (f32[64,1024]{1,0:T(8,128)S(1)}, f32[64,1024]{1,0:T(8,128)S(1)}, u32[]{:S(2)}, u32[]{:S(2)}) collective-permute-start(f32[64,1024]{1,0:T(8,128)S(1)} %get-tuple-element.71), channel_id=1, source_target_pairs={{0,3},{1,2},{2,5},{3,4},{4,7},{5,6},{6,1},{7,0},{8,11},{9,10},{10,... | collective-permute-start | bytes 786440 | tf_op jit(solution)/shard_map/ppermute | solution.py:418
  74.4 9.5 %collective-permute-start.18 = (f32[64,1024]{1,0:T(8,128)S(1)}, f32[64,1024]{1,0:T(8,128)S(1)}, u32[]{:S(2)}, u32[]{:S(2)}) collective-permute-start(f32[64,1024]{1,0:T(8,128)S(1)} %get-tuple-element.72), channel_id=1, source_target_pairs={{0,7},{1,6},{2,1},{3,0},{4,3},{5,2},{6,5},{7,4},{8,15},{9,14},{10,... | collective-permute-start | bytes 786440 | tf_op jit(solution)/shard_map/ppermute | solution.py:418

commit v6 on v4

--- a/solution.py
+++ b/solution.py
@@ -68,22 +68,35 @@
     return pick_columns(edges, 2 * lane), pick_columns(edges, 2 * lane + 1)
 
 
-def slot_kernel(turn, codes_hbm, values_hbm, top_ref, low_ref, codes_ref, values_ref, sems):
+def slot_kernel(group, moves, codes_hbm, values_hbm, top_ref, low_ref, *refs):
+    *blocks, codes_ref, values_ref, sems = refs
     rows = values_ref.shape[1]
-    width = 32
-    group = (lax.axis_index("rows") // 8 + turn) % 4
-    own = pl.ds(pl.multiple_of(group * FEATS, FEATS), FEATS)
+    wide = blocks[0].shape[1]
+    own = slice(group * FEATS, (group + 1) * FEATS)
     span = rows // 2
     copies = [pltpu.make_async_copy(codes_hbm.at[own, :], codes_ref, sems.at[2])]
     for part in range(2):
         at = slice(part * span, (part + 1) * span)
         copies.append(pltpu.make_async_copy(values_hbm.at[own, at], values_ref.at[:, at], sems.at[part]))
+    for index, (move, block) in enumerate(zip(moves, blocks)):
+        at = pl.ds(pl.multiple_of(owner(move) * wide, wide), wide)
+        copies.append(pltpu.make_async_copy(values_hbm.at[:, at], block, sems.at[3 + index]))
     for copy in copies:
         copy.start()
     copies[0].wait()
+    for part in range(2):
+        copies[1 + part].wait()
+        search_slots(0, codes_ref, values_ref, top_ref, low_ref, (part / 2, (part + 1) / 2))
+    for copy in copies[3:]:
+        copy.wait()
+
+
+def search_slots(first, codes_ref, values_ref, top_ref, low_ref, share):
+    width = 32
+    steps = values_ref.shape[1] // (width * LANES)
     tables = []
     for half in range(2):
-        at = slice(8 * half, 8 * half + 8)
+        at = pl.ds(first + 8 * half, 8)
         even, odd = even_odd(codes_ref[at, :])
         tables.append((at, odd, (even, spread(even))))
 
@@ -102,24 +115,40 @@
             low_ref[:, column] = jnp.concatenate(low, axis=0).astype(jnp.bfloat16)
         return carry
 
-    steps = span // (width * LANES)
-    for part in range(2):
-        copies[1 + part].wait()
-        lax.fori_loop(part * steps, (part + 1) * steps, chunk, 0)
-
-
-def find_slots(turn, edge_codes, values):
-    rows = values.shape[1]
+    lax.fori_loop(int(share[0] * steps), int(share[1] * steps), chunk, 0)
+
+
+def near_slot_kernel(groups, codes_ref, values_ref, *refs):
+    for index, group in enumerate(groups):
+        search_slots(group * FEATS, codes_ref, values_ref, *refs[2 * index : 2 * index + 2], (0, 1))
+
+
+def find_near_slots(groups, edge_codes, values):
+    slots = jax.ShapeDtypeStruct((FEATS, values.shape[1]), jnp.bfloat16)
+    return pl.pallas_call(
+        lambda *refs: near_slot_kernel(groups, *refs),
+        in_specs=in_vmem(2),
+        out_specs=in_vmem(2 * len(groups)),
+        out_shape=[slots] * (2 * len(groups)),
+        compiler_params=pltpu.CompilerParams(vmem_limit_bytes=16 << 20),
+        cost_estimate=pl.CostEstimate(flops=10**7, bytes_accessed=10**7, transcendentals=0),
+        name="slots",
+    )(edge_codes, values)
+
+
+def find_slots(group, moves, edge_codes, values):
+    feats, rows = values.shape
     slots = jax.ShapeDtypeStruct((FEATS, rows), jnp.bfloat16)
-    return pl.pallas_call(
-        lambda *refs: slot_kernel(turn, *refs),
+    block = jax.ShapeDtypeStruct((feats, rows // 8), jnp.float32)
+    return pl.pallas_call(
+        lambda *refs: slot_kernel(group, moves, *refs),
         in_specs=[pl.BlockSpec(memory_space=pltpu.HBM)] * 2,
-        out_specs=in_vmem(2),
-        out_shape=[slots, slots],
+        out_specs=in_vmem(2 + len(moves)),
+        out_shape=[slots] * 2 + [block] * len(moves),
         scratch_shapes=[
             pltpu.VMEM((FEATS, 256), jnp.int32),
             pltpu.VMEM((FEATS, rows), jnp.float32),
-            pltpu.SemaphoreType.DMA((3,)),
+            pltpu.SemaphoreType.DMA((3 + len(moves),)),
         ],
         compiler_params=pltpu.CompilerParams(vmem_limit_bytes=16 << 20),
         cost_estimate=pl.CostEstimate(flops=10**7, bytes_accessed=10**7, transcendentals=0),
@@ -130,11 +159,9 @@
     )
 
 
-def hist_kernel(hess_ref, top_ref, low_ref, mass_ref, high_ref, rest_ref, sum_ref):
-    rows = top_ref.shape[1]
-    shape = (FEATS, LANES)
-    lane = lane_iota(shape)
-    feat = lax.broadcasted_iota(jnp.int32, shape, 0)
+def hist_kernel(hess_ref, *refs):
+    *slots, mass_ref, high_ref, rest_ref, sum_ref = refs
+    rows = slots[0].shape[1]
     scaled = hess_ref[...] * 65536.0
     high = jnp.floor(scaled * (1.0 / 256.0))
     rest = scaled - high * 256.0
@@ -144,6 +171,16 @@
         own = pl.ds(pl.multiple_of((part ^ me) * wide, wide), wide)
         high_ref[:, own] = jnp.broadcast_to(high[part : part + 1], (FEATS, wide)).astype(jnp.bfloat16)
         rest_ref[:, own] = jnp.broadcast_to(rest[part : part + 1], (FEATS, wide)).astype(jnp.bfloat16)
+
+    for group in range(len(slots) // 2):
+        hist_group(group, *slots[2 * group : 2 * group + 2], mass_ref, high_ref, rest_ref, sum_ref)
+
+
+def hist_group(group, top_ref, low_ref, mass_ref, high_ref, rest_ref, sum_ref):
+    rows = top_ref.shape[1]
+    shape = (FEATS, LANES)
+    lane = lane_iota(shape)
+    feat = lax.broadcasted_iota(jnp.int32, shape, 0)
 
     def multiply(*sums):
         zero = jnp.zeros((FEATS, TILE), jnp.bfloat16)
@@ -182,33 +219,46 @@
             here = jnp.where((point & 15) < 8, lane_take(block[:, :LANES], column), lane_take(block[:, LANES:], column))
             results[parity] = jnp.where((point >> 4) == k, before + here, results[parity])
         before = before + lane_take(block[:, LANES:], 7 * FEATS + feat)
-    mass_ref[:, :LANES] = results[0]
-    mass_ref[:, LANES:] = results[1]
-
-
-def find_mass(hess, top, low):
-    rows = top.shape[1]
+    own = slice(group * FEATS, (group + 1) * FEATS)
+    mass_ref[own, :LANES] = results[0]
+    mass_ref[own, LANES:] = results[1]
+
+
+def find_mass(hess, slots):
+    rows = slots[0].shape[1]
+    feats = FEATS * len(slots) // 2
     return pl.pallas_call(
         hist_kernel,
-        in_specs=in_vmem(3),
+        in_specs=in_vmem(1 + len(slots)),
         out_specs=in_vmem(1)[0],
-        out_shape=jax.ShapeDtypeStruct((FEATS, 256), jnp.float32),
+        out_shape=jax.ShapeDtypeStruct((feats, 256), jnp.float32),
         scratch_shapes=[pltpu.VMEM((FEATS, rows), jnp.bfloat16)] * 2
         + [pltpu.VMEM((16 * FEATS, TILE), jnp.float32)],
         compiler_params=pltpu.CompilerParams(vmem_limit_bytes=24 << 20),
         cost_estimate=pl.CostEstimate(flops=4 * 10**9, bytes_accessed=10**7, transcendentals=0),
         name="hist",
-    )(hess, top, low)
-
-
-def cuts_kernel(codes_ref, ranks_ref, first_ref, second_ref, third_ref, cuts_ref):
+    )(hess, *slots)
+
+
+def cuts_kernel(codes_ref, ranks_ref, *refs):
+    *mass_refs, cuts_ref = refs
+
+    def step(group, carry):
+        at = pl.ds(pl.multiple_of(group * FEATS, FEATS), FEATS)
+        mass = mass_refs[0][at, :]
+        for mass_ref in mass_refs[1:]:
+            mass = mass + mass_ref[at, :]
+        cut_group(at, codes_ref, ranks_ref, mass, cuts_ref)
+        return carry
+
+    lax.fori_loop(0, codes_ref.shape[0] // FEATS, step, 0)
+
+
+def cut_group(at, codes_ref, ranks_ref, mass, cuts_ref):
     shape = (FEATS, LANES)
     lane = lane_iota(shape)
-    group = lax.axis_index("rows") // 8
-    at = pl.ds(pl.multiple_of(group * FEATS, FEATS), FEATS)
     edge_even, edge_odd = even_odd(codes_ref[at, :])
     edge_next = lane_take(edge_even, (lane + 1) & (LANES - 1))
-    mass = first_ref[...] + second_ref[...] + third_ref[...]
     mass_even, mass_odd = mass[:, :LANES], mass[:, LANES:]
     mass_next = lane_take(mass_even, (lane + 1) & (LANES - 1))
     total = jnp.broadcast_to(mass_odd[:, LANES - 1 :], shape)
@@ -225,7 +275,7 @@
         low_edge = jnp.where(above, mid_edge, lane_take(edge_even, pair))
         high_edge = jnp.where(above, lane_take(edge_next, pair), mid_edge)
         part = (target - low_mass) / (high_mass - low_mass)
-        cuts_ref[:, side * LANES : (side + 1) * LANES] = low_edge + part * (high_edge - low_edge)
+        cuts_ref[at, side * LANES : (side + 1) * LANES] = low_edge + part * (high_edge - low_edge)
 
 
 def find_cuts(edge_codes, cut_ranks, *sums):
@@ -233,7 +283,7 @@
         cuts_kernel,
         in_specs=in_vmem(2 + len(sums)),
         out_specs=in_vmem(1)[0],
-        out_shape=jax.ShapeDtypeStruct((FEATS, 256), jnp.float32),
+        out_shape=jax.ShapeDtypeStruct((edge_codes.shape[0], 256), jnp.float32),
         compiler_params=pltpu.CompilerParams(vmem_limit_bytes=4 << 20),
         name="cuts",
     )(edge_codes, cut_ranks, *sums)
@@ -263,19 +313,14 @@
         write(jnp.where(value >= last, 256.0 + (value - last) * inv_last, inside))
 
 
-def first_kernel(moves, c0, c1, c2, c3, values_ref, cuts_ref, *out_refs):
-    mine = lax.axis_index("rows") // 8
-    for turn, c_ref in enumerate((c0, c1, c2, c3)):
-        group = (mine + 4 - turn) % 4
-        cuts_ref[pl.ds(pl.multiple_of(group * FEATS, FEATS), FEATS), :] = c_ref[...]
-    place_kernel(moves, cuts_ref, values_ref, *out_refs)
-
-
 def place_kernel(moves, cuts_ref, values_ref, *out_refs):
+    wide = out_refs[0].shape[1]
+    place_blocks([owner(move) * wide for move in moves], cuts_ref, values_ref, out_refs)
+
+
+def place_blocks(bases, cuts_ref, values_ref, out_refs):
     feats, wide = out_refs[0].shape
-    bases = [owner(move) * wide for move in moves]
-
-    together = max(1, 8 // len(moves))
+    together = 4
 
     def store(out_ref, at, part):
         def write(value):
@@ -302,18 +347,33 @@
 def place(moves, cuts, values):
     feats, rows = values.shape
     block = jax.ShapeDtypeStruct((feats, rows // 8), jnp.float32)
-    first = len(cuts) > 1
-    kernel = first_kernel if first else place_kernel
-    outs = [jax.ShapeDtypeStruct((feats, 256), jnp.float32)] * first + [block] * len(moves)
-    return pl.pallas_call(
-        lambda *refs: kernel(moves, *refs),
-        in_specs=in_vmem(len(cuts) + 1),
-        out_specs=in_vmem(len(outs)),
-        out_shape=outs,
+    return pl.pallas_call(
+        lambda *refs: place_kernel(moves, *refs),
+        in_specs=in_vmem(2),
+        out_specs=in_vmem(len(moves)),
+        out_shape=[block] * len(moves),
         compiler_params=pltpu.CompilerParams(vmem_limit_bytes=16 << 20),
-        cost_estimate=pl.CostEstimate(flops=10**7 * len(moves), bytes_accessed=10**6, transcendentals=0),
+        cost_estimate=pl.CostEstimate(flops=10**5, bytes_accessed=10**4, transcendentals=0),
         name="place",
-    )(*cuts, values)
+    )(cuts, values)
+
+
+def far_kernel(*refs):
+    count = len(refs) // 3
+    for cuts_ref, values_ref, out_ref in zip(refs[:count], refs[count : 2 * count], refs[2 * count :]):
+        place_blocks([0], cuts_ref, values_ref, [out_ref])
+
+
+def place_far(cuts, values):
+    return pl.pallas_call(
+        far_kernel,
+        in_specs=in_vmem(2 * len(cuts)),
+        out_specs=in_vmem(len(cuts)),
+        out_shape=[jax.ShapeDtypeStruct(block.shape, jnp.float32) for block in values],
+        compiler_params=pltpu.CompilerParams(vmem_limit_bytes=16 << 20),
+        cost_estimate=pl.CostEstimate(flops=10**5, bytes_accessed=10**4, transcendentals=0),
+        name="far",
+    )(*cuts, *values)
 
 
 def join_kernel(moves, *refs):
@@ -321,8 +381,7 @@
     feats = parts[0].shape[0]
     copies = []
     for index, (move, part) in enumerate(zip(moves, parts)):
-        back = (-move[0], move[1])
-        rows = pl.ds(pl.multiple_of(owner(back) * feats, feats), feats)
+        rows = pl.ds(pl.multiple_of(owner((-move[0], move[1])) * feats, feats), feats)
         copies.append(pltpu.make_async_copy(part, out_ref.at[rows, :], sems.at[index]))
     for copy in copies:
         copy.start()
@@ -367,31 +426,40 @@
 def on_device(feature_values, hessian_codes, edge_codes, cut_ranks):
     hess_own = hessian_codes.astype(jnp.float32) * (1.0 / 65536.0)
     hess = hess_own.reshape(1, -1)
-    slots = {}
-    codes = edge_codes
-    for flip, turns in ((1, (1,)), (2, (2,)), (4, (3, 0))):
+    far_moves = [(2, 0), (2, 1)]
+    codes, slots = edge_codes, []
+    for flip, groups in ((1, (0,)), (2, (1,)), (4, (2, 3))):
         other = flip_feat(hess, flip)
-        for turn in turns:
-            slots[turn] = find_slots(turn, codes, feature_values)
+        if flip == 1:
+            top, low, *far_blocks = find_slots(0, far_moves, codes, feature_values)
+            slots += [top, low]
+        else:
+            slots += find_near_slots(groups, codes, feature_values)
         hess = jnp.concatenate([hess, other], axis=0)
         if flip < 4:
-            hess, slots[turn], codes = lax.optimization_barrier((hess, slots[turn], codes))
-    parts = [turn_rows(find_mass(hess, *slots[turn]), turn) for turn in (1, 2, 3)]
-    mass = find_mass(hess, *slots[0]) + parts[0] + parts[1] + parts[2]
+            hess, slots, codes = lax.optimization_barrier((hess, slots, codes))
+    far_blocks, hess = lax.optimization_barrier((far_blocks, hess))
+    far_values = [send_feat(block, move) for block, move in zip(far_blocks, far_moves)]
+    mass = find_mass(hess, slots)
     before = mass + shift_rows(mass, 1)
     around = before + shift_rows(mass, -1)
-    cuts = find_cuts(edge_codes, cut_ranks, around, shift_rows(around, -3), shift_rows(before, 2))
-    cuts = [cuts] + [turn_rows(cuts, turn) for turn in (1, 2, 3)]
-    stages = [[(2, 0)], [(2, 1), (1, 0)], [(3, 0), (1, 1)], [(3, 1), (0, 1)], [(0, 0)]]
+    mass = around + shift_rows(around, -3) + shift_rows(before, 2)
+    cuts = find_cuts(edge_codes, cut_ranks, mass, *[turn_rows(mass, turn) for turn in (1, 2, 3)])
+    cuts, far_values = lax.optimization_barrier((cuts, far_values))
+    far_cuts = [send_feat(cuts, move) for move in far_moves]
+    stages = [[(1, 0), (3, 0)], [(1, 1), (3, 1)], [(0, 1)], [(0, 0)]]
     moves, parts = [], []
     for stage in stages:
         outs = place(stage, cuts, feature_values)
-        if len(cuts) > 1:
-            cuts, *outs = outs
-            cuts = [cuts]
+        if stage[0] == (1, 1):
+            cuts, outs, far_cuts = lax.optimization_barrier((cuts, outs, far_cuts))
+        elif stage[0] == (0, 1):
+            cuts, outs, far_cuts, far_values = lax.optimization_barrier((cuts, outs, far_cuts, far_values))
+        else:
+            cuts, outs = lax.optimization_barrier((cuts, outs))
         moves += stage
         parts += [send_feat(out, move) if move != (0, 0) else out for out, move in zip(outs, stage)]
-    return join(moves, parts)
+    return join(moves + far_moves, parts + list(place_far(far_cuts, far_values)))
 
 
 def solution(mesh):

time: 94.1 us -> 82.3 us (0.87)
  waiting for transfers between devices: 23.6 us -> 11.1 us
    ppermute x7 -> x9, waiting for transfers between devices: 13.5 us -> 1.77 us  [send_feat(): lax.ppermute(array, 'feat', [(i, (i // 2 + move[0]) % 4 * 2 + (i % 2 ^ mo...]
    ppermute x7 -> x9, starting transfers between devices: 13.2 us -> 18.3 us  [send_feat(): lax.ppermute(array, 'feat', [(i, (i // 2 + move[0]) % 4 * 2 + (i % 2 ^ mo...]
    ppermute x6 -> x3, starting transfers between devices: 7.42 us -> 3.68 us  [turn_rows(): lax.ppermute(array, 'rows', [(i, (i + 8 * turn) % 32) for i in range(32)])]
    ppermute x4, waiting for transfers between devices: 6.33 us -> 4.33 us  [shift_rows(): lax.ppermute(array, 'rows', [(i, i // 8 * 8 + (i + shift) % 8) for i in r...]
    pallas_call x13 -> x9, Pallas kernels: 32.9 us -> 31.4 us  [the longest x1 11.3 us: find_mass(): pl.pallas_call(hist_kernel, in_specs=in_vmem(1 + len(slots)), out_specs=i...]
    pallas_call x1, Pallas kernels: 0.49 us -> 1.95 us  [find_cuts(): pl.pallas_call(cuts_kernel, in_specs=in_vmem(2 + len(sums)), out_specs=in...]
    ppermute x6 -> x3, waiting for transfers between devices: 3.8 us -> 4.38 us  [turn_rows(): lax.ppermute(array, 'rows', [(i, (i + 8 * turn) % 32) for i in range(32)])]
  transfers between devices with their start and end apart: 20 -> 19, of which waited for: 8 -> 7; matrix products, arithmetic and copies ran while one was open for 0% -> 0% of each run, Pallas kernels for 31% -> 27%
where the time goes in v6:
time: 82.3 us; the launch traced here: 82.1 us
  starting transfers between devices  34.9 us (42%)
  Pallas kernels  34.7 us (42%)
  waiting for transfers between devices  11.1 us (13%)
  other arithmetic  0.9 us (1%)
    ppermute x9, starting transfers between devices, send_feat(): lax.ppermute(array, 'feat', [(i, (i // 2 + move[0]) % 4 * 2 + (i % 2 ^ mo...  18.3 us
    pallas_call x1, Pallas kernels, find_mass(): pl.pallas_call(hist_kernel, in_specs=in_vmem(1 + len(slots)), out_specs=i...  11.3 us
    pallas_call x4, Pallas kernels, place(): pl.pallas_call(lambda *refs: place_kernel(moves, *refs), in_specs=in_vmem...  8.47 us
    ppermute x4, starting transfers between devices, shift_rows(): lax.ppermute(array, 'rows', [(i, i // 8 * 8 + (i + shift) % 8) for i in r...  8 us
    pallas_call x2, Pallas kernels, find_near_slots(): pl.pallas_call(lambda *refs: near_slot_kernel(groups, *refs), in_specs=in...  5.56 us
    ppermute x3, starting transfers between devices, flip_feat(): return lax.ppermute(array, 'feat', [(i, i ^ flip) for i in range(8)])  4.98 us
    ppermute x3, waiting for transfers between devices, turn_rows(): lax.ppermute(array, 'rows', [(i, (i + 8 * turn) % 32) for i in range(32)])  4.38 us
    ppermute x4, waiting for transfers between devices, shift_rows(): lax.ppermute(array, 'rows', [(i, i // 8 * 8 + (i + shift) % 8) for i in r...  4.33 us
  transfers between devices with their start and end apart: 19, of which 7 were waited for; matrix products, arithmetic and copies ran while one was open for 0% of the time, Pallas kernels for 27%

profile of v6, /device:TPU:1, one launch (start us, length us, event | category | flops | bytes accessed | tf_op | source)
XLA Modules:
  0.0 82.1 jit_solution(15071085642872820203)
XLA Ops:
  0.0 0.8 %convert_multiply_fusion = f32[1024]{0:T(1024)S(1)} fusion(s32[1024]{0:T(1024)} %param.5), kind=kLoop, calls=%fused_computation.4 | loop fusion | flops 2048 | bytes 8192 | tf_op jit(solution)/shard_map/mul | solution.py:427
  0.8 3.2 %collective-permute-start = (f32[1,1024]{1,0:T(1,128)S(1)}, f32[1,1024]{1,0:T(1,128)S(1)}, u32[]{:S(2)}, u32[]{:S(2)}) collective-permute-start(f32[1,1024]{1,0:T(1,128)S(1)} %bitcast.1), channel_id=1, source_target_pairs={{0,1},{1,0},{2,3},{3,2},{4,5},{5,4},{6,7},{7,6},{8,9},{9,8},{10,11... | collective-permute-start | bytes 12296 | tf_op jit(solution)/shard_map/ppermute | solution.py:415
  4.1 3.1 %slots.3 = (bf16[16,8192]{1,0:T(8,128)(2,1)S(1)}, bf16[16,8192]{1,0:T(8,128)(2,1)S(1)}, f32[64,1024]{1,0:T(8,128)S(1)}, f32[64,1024]{1,0:T(8,128)S(1)}) custom-call(s32[64,256]{1,0:T(8,128)} %codes_ref.1, f32[64,8192]{1,0:T(8,128)} %refs_1_.13), custom_call_target="tpu_custom_call" | custom-call | flops 10000000 | bytes 10000000 | tf_op jit(solution)/shard_map/slots/pallas_call | solution.py:143
  7.1 0.0 collective-permute-done
  7.2 0.1 collective-permute-start.1
  7.3 1.9 %slots.4 = (bf16[16,8192]{1,0:T(8,128)(2,1)S(1)}, bf16[16,8192]{1,0:T(8,128)(2,1)S(1)}) custom-call(s32[64,256]{1,0:T(8,128)S(1)} %copy-done.1, f32[64,8192]{1,0:T(8,128)S(1)} %copy-done), custom_call_target="tpu_custom_call" | custom-call | flops 10000000 | bytes 10000000 | tf_op jit(solution)/shard_map/slots/pallas_call | solution.py:128
  9.2 0.6 collective-permute-done.1
  9.8 1.6 %collective-permute-start.2 = (f32[4,1024]{1,0:T(4,128)S(1)}, f32[4,1024]{1,0:T(4,128)S(1)}, u32[]{:S(2)}, u32[]{:S(2)}) collective-permute-start(f32[4,1024]{1,0:T(4,128)S(1)} %pad_maximum_fusion.1), channel_id=1, source_target_pairs={{0,4},{1,5},{2,6},{3,7},{4,0},{5,1},{6,2},{7,3},{8,12},{9,13},{10,... | collective-permute-start | bytes 49160 | tf_op jit(solution)/shard_map/ppermute | solution.py:415
  11.4 3.7 %slots.5 = (bf16[16,8192]{1,0:T(8,128)(2,1)S(1)}, bf16[16,8192]{1,0:T(8,128)(2,1)S(1)}, bf16[16,8192]{1,0:T(8,128)(2,1)S(1)}, bf16[16,8192]{1,0:T(8,128)(2,1)S(1)}) custom-call(s32[64,256]{1,0:T(8,128)S(1)} %copy-done.1, f32[64,8192]{1,0:T(8,128)S(1)} %copy-done), custom_call_target="tpu_custom_call" | custom-call | flops 10000000 | bytes 10000000 | tf_op jit(solution)/shard_map/slots/pallas_call | solution.py:128
  15.1 0.0 collective-permute-done.2
  15.2 0.0 copy-start.2
  15.2 11.3 %hist.1 = f32[64,256]{1,0:T(8,128)S(1)} custom-call(f32[8,1024]{1,0:T(8,128)S(1)} %pad_maximum_fusion.hess_ref, bf16[16,8192]{1,0:T(8,128)(2,1)S(1)} %get-tuple-element.64.refs_0_, bf16[16,8192]{1,0:T(8,128)(2,1)S(1)} %get-tuple-element.65.refs_1_, bf16[16,8192]{1,0:T(8,128)(2,1)S(1)} %get-tuple-element.66.refs_2_, ...), custom_call_target="tpu_custom_call" | custom-call | flops 4000000000 | bytes 10000000 | tf_op jit(solution)/shard_map/hist/pallas_call | solution.py:230
  26.5 5.8 %collective-permute-start.4 = (f32[64,256]{1,0:T(8,128)S(1)}, f32[64,256]{1,0:T(8,128)S(1)}, u32[]{:S(2)}, u32[]{:S(2)}) collective-permute-start(f32[64,256]{1,0:T(8,128)S(1)} %hist.1), channel_id=1, source_target_pairs={{0,56},{8,0},{16,8},{24,16},{32,24},{40,32},{48,40},{56,48},{64,12... | collective-permute-start | bytes 196616 | tf_op jit(solution)/shard_map/ppermute | solution.py:419
  32.3 1.3 %collective-permute-done.4 = f32[64,256]{1,0:T(8,128)S(1)} collective-permute-done((f32[64,256]{1,0:T(8,128)S(1)}, f32[64,256]{1,0:T(8,128)S(1)}, u32[]{:S(2)}, u32[]{:S(2)}) %collective-permute-start.4) | collective-permute-done | bytes 65568 | tf_op jit(solution)/shard_map/ppermute | solution.py:419
  33.7 3.0 %collective-permute-done.3 = f32[64,256]{1,0:T(8,128)S(1)} collective-permute-done((f32[64,256]{1,0:T(8,128)S(1)}, f32[64,256]{1,0:T(8,128)S(1)}, u32[]{:S(2)}, u32[]{:S(2)}) %collective-permute-start.3) | collective-permute-done | bytes 65568 | tf_op jit(solution)/shard_map/ppermute | solution.py:419
  36.7 0.1 collective-permute-start.6
  36.8 2.1 %collective-permute-start.5 = (f32[64,256]{1,0:T(8,128)S(1)}, f32[64,256]{1,0:T(8,128)S(1)}, u32[]{:S(2)}, u32[]{:S(2)}) collective-permute-start(f32[64,256]{1,0:T(8,128)S(1)} %get-tuple-element.99), channel_id=1, source_target_pairs={{0,40},{8,48},{16,56},{24,0},{32,8},{40,16},{48,24},{56,32},{64,10... | collective-permute-start | bytes 196616 | tf_op jit(solution)/shard_map/ppermute | solution.py:419
  38.8 0.4 collective-permute-start.10
  39.2 5.5 %collective-permute-start.11 = (f32[64,1024]{1,0:T(8,128)S(1)}, f32[64,1024]{1,0:T(8,128)S(1)}, u32[]{:S(2)}, u32[]{:S(2)}) collective-permute-start(f32[64,1024]{1,0:T(8,128)S(1)} %get-tuple-element.74), channel_id=1, source_target_pairs={{0,5},{1,4},{2,7},{3,6},{4,1},{5,0},{6,3},{7,2},{8,13},{9,12},{10,... | collective-permute-start | bytes 786440 | tf_op jit(solution)/shard_map/ppermute | solution.py:411
  44.7 0.0 collective-permute-done.6
  44.7 0.0 collective-permute-done.5
  44.8 2.5 %collective-permute-start.9 = (f32[64,256]{1,0:T(8,128)S(1)}, f32[64,256]{1,0:T(8,128)S(1)}, u32[]{:S(2)}, u32[]{:S(2)}) collective-permute-start(f32[64,256]{1,0:T(8,128)S(1)} %add_add_fusion.refs_0_), channel_id=1, source_target_pairs={{0,192},{8,200},{16,208},{24,216},{32,224},{40,232},{48,240},{56,2... | collective-permute-start | bytes 196616 | tf_op jit(solution)/shard_map/ppermute | solution.py:423
  47.3 0.5 collective-permute-start.8
  47.8 0.6 collective-permute-start.7
  48.4 0.2 collective-permute-done.9.refs_3_
  48.6 3.6 %collective-permute-done.8.refs_2_ = f32[64,256]{1,0:T(8,128)S(1)} collective-permute-done((f32[64,256]{1,0:T(8,128)S(1)}, f32[64,256]{1,0:T(8,128)S(1)}, u32[]{:S(2)}, u32[]{:S(2)}) %collective-permute-start.8) | collective-permute-done | bytes 65568 | tf_op jit(solution)/shard_map/ppermute | solution.py:423
  52.2 0.6 collective-permute-done.7.refs_1_
  52.8 2.0 %cuts.1.refs_0_ = f32[64,256]{1,0:T(8,128)S(1)} custom-call(s32[64,256]{1,0:T(8,128)S(1)} %copy-done.1, s32[64,256]{1,0:T(8,128)S(1)} %copy-done.2, f32[64,256]{1,0:T(8,128)S(1)} %add_add_fusion.refs_0_, f32[64,256]{1,0:T(8,128)S(1)} %collective-permute-done.7.refs_1_, f32[64,256]{1,0:T(8,128)S(1)} %collective-permute-done.8.refs_2_, ...), custom_call_target="tpu_custom_call" | custom-call | tf_op jit(solution)/shard_map/cuts/pallas_call | solution.py:282
  54.8 0.0 collective-permute-done.11.refs_3_
  54.8 3.9 %collective-permute-start.15 = (f32[64,256]{1,0:T(8,128)S(1)}, f32[64,256]{1,0:T(8,128)S(1)}, u32[]{:S(2)}, u32[]{:S(2)}) collective-permute-start(f32[64,256]{1,0:T(8,128)S(1)} %cuts.1.refs_0_), channel_id=1, source_target_pairs={{0,5},{1,4},{2,7},{3,6},{4,1},{5,0},{6,3},{7,2},{8,13},{9,12},{10,... | collective-permute-start | bytes 196616 | tf_op jit(solution)/shard_map/ppermute | solution.py:411
  58.7 2.4 %collective-permute-start.14 = (f32[64,256]{1,0:T(8,128)S(1)}, f32[64,256]{1,0:T(8,128)S(1)}, u32[]{:S(2)}, u32[]{:S(2)}) collective-permute-start(f32[64,256]{1,0:T(8,128)S(1)} %cuts.1.refs_0_), channel_id=1, source_target_pairs={{0,4},{1,5},{2,6},{3,7},{4,0},{5,1},{6,2},{7,3},{8,12},{9,13},{10,... | collective-permute-start | bytes 196616 | tf_op jit(solution)/shard_map/ppermute | solution.py:411
  61.1 2.7 %place.4 = (f32[64,1024]{1,0:T(8,128)S(1)}, f32[64,1024]{1,0:T(8,128)S(1)}) custom-call(f32[64,256]{1,0:T(8,128)S(1)} %cuts.1.refs_0_, f32[64,8192]{1,0:T(8,128)S(1)} %copy-done), custom_call_target="tpu_custom_call" | custom-call | flops 100000 | bytes 10000 | tf_op jit(solution)/shard_map/place/pallas_call | solution.py:350
  63.8 0.4 collective-permute-start.12
  64.1 2.4 %collective-permute-start.13 = (f32[64,1024]{1,0:T(8,128)S(1)}, f32[64,1024]{1,0:T(8,128)S(1)}, u32[]{:S(2)}, u32[]{:S(2)}) collective-permute-start(f32[64,1024]{1,0:T(8,128)S(1)} %get-tuple-element.79), channel_id=1, source_target_pairs={{0,6},{1,7},{2,0},{3,1},{4,2},{5,3},{6,4},{7,5},{8,14},{9,15},{10,... | collective-permute-start | bytes 786440 | tf_op jit(solution)/shard_map/ppermute | solution.py:411
  66.5 2.7 %place.5 = (f32[64,1024]{1,0:T(8,128)S(1)}, f32[64,1024]{1,0:T(8,128)S(1)}) custom-call(f32[64,256]{1,0:T(8,128)S(1)} %cuts.1.refs_0_, f32[64,8192]{1,0:T(8,128)S(1)} %copy-done), custom_call_target="tpu_custom_call" | custom-call | flops 100000 | bytes 10000 | tf_op jit(solution)/shard_map/place/pallas_call | solution.py:350
  69.2 0.0 collective-permute-done.15.refs_1_
  69.2 0.0 collective-permute-done.14.refs_0_
  69.2 1.6 %place.6 = f32[64,1024]{1,0:T(8,128)S(1)} custom-call(f32[64,256]{1,0:T(8,128)S(1)} %cuts.1.refs_0_, f32[64,8192]{1,0:T(8,128)S(1)} %copy-done), custom_call_target="tpu_custom_call" | custom-call | flops 100000 | bytes 10000 | tf_op jit(solution)/shard_map/place/pallas_call | solution.py:350
  70.8 0.1 collective-permute-start.18
  70.9 0.3 collective-permute-start.16
  71.2 2.9 %collective-permute-start.17 = (f32[64,1024]{1,0:T(8,128)S(1)}, f32[64,1024]{1,0:T(8,128)S(1)}, u32[]{:S(2)}, u32[]{:S(2)}) collective-permute-start(f32[64,1024]{1,0:T(8,128)S(1)} %get-tuple-element.84), channel_id=1, source_target_pairs={{0,7},{1,6},{2,1},{3,0},{4,3},{5,2},{6,5},{7,4},{8,15},{9,14},{10,... | collective-permute-start | bytes 786440 | tf_op jit(solution)/shard_map/ppermute | solution.py:411
  74.2 1.5 %place.7.refs_5_ = f32[64,1024]{1,0:T(8,128)S(1)} custom-call(f32[64,256]{1,0:T(8,128)S(1)} %cuts.1.refs_0_, f32[64,8192]{1,0:T(8,128)S(1)} %copy-done), custom_call_target="tpu_custom_call" | custom-call | flops 100000 | bytes 10000 | tf_op jit(solution)/shard_map/place/pallas_call | solution.py:350
  75.7 3.0 %far.1 = (f32[64,1024]{1,0:T(8,128)S(1)}, f32[64,1024]{1,0:T(8,128)S(1)}) custom-call(f32[64,256]{1,0:T(8,128)S(1)} %collective-permute-done.14.refs_0_, f32[64,256]{1,0:T(8,128)S(1)} %collective-permute-done.15.refs_1_, f32[64,1024]{1,0:T(8,128)S(1)} %collective-permute-done.10.refs_2_, f32[64,1024]{1,0:T(8,128)S(1)} %collective-permute-done.11.refs_3_), custom_call_target="tpu_custom_call" | custom-call | flops 100000 | bytes 10000 | tf_op jit(solution)/shard_map/far/pallas_call | solution.py:368
  78.8 0.0 collective-permute-done.12.refs_0_
  78.8 0.0 collective-permute-done.18.refs_4_
  78.8 1.7 %collective-permute-done.16.refs_2_ = f32[64,1024]{1,0:T(8,128)S(1)} collective-permute-done((f32[64,1024]{1,0:T(8,128)S(1)}, f32[64,1024]{1,0:T(8,128)S(1)}, u32[]{:S(2)}, u32[]{:S(2)}) %collective-permute-start.16) | collective-permute-done | bytes 262176 | tf_op jit(solution)/shard_map/ppermute | solution.py:411
  80.5 0.0 collective-permute-done.17.refs_3_
  80.5 1.4 %join.1 = f32[512,1024]{1,0:T(8,128)} custom-call(f32[64,1024]{1,0:T(8,128)S(1)} %collective-permute-done.12.refs_0_, f32[64,1024]{1,0:T(8,128)S(1)} %collective-permute-done.13.refs_1_, f32[64,1024]{1,0:T(8,128)S(1)} %collective-permute-done.16.refs_2_, f32[64,1024]{1,0:T(8,128)S(1)} %collective-permute-done.17.refs_3_, ...), custom_call_target="tpu_custom_call" | custom-call | tf_op jit(solution)/shard_map/join/pallas_call | solution.py:394
  (13 shorter events, 0.1 us)
Async XLA Ops:
  0.0 7.3 %copy-start = (f32[64,8192]{1,0:T(8,128)S(1)}, f32[64,8192]{1,0:T(8,128)}, u32[]{:S(2)}) copy-start(f32[64,8192]{1,0:T(8,128)} %refs_1_.13) | copy-start | bytes 6291460
  0.0 7.3 %copy-start.1 = (s32[64,256]{1,0:T(8,128)S(1)}, s32[64,256]{1,0:T(8,128)}, u32[]{:S(2)}) copy-start(s32[64,256]{1,0:T(8,128)} %codes_ref.1) | copy-start | bytes 196612
  0.8 6.3 %collective-permute-start = (f32[1,1024]{1,0:T(1,128)S(1)}, f32[1,1024]{1,0:T(1,128)S(1)}, u32[]{:S(2)}, u32[]{:S(2)}) collective-permute-start(f32[1,1024]{1,0:T(1,128)S(1)} %bitcast.1), channel_id=1, source_target_pairs={{0,1},{1,0},{2,3},{3,2},{4,5},{5,4},{6,7},{7,6},{8,9},{9,8},{10,11... | collective-permute-start | bytes 12296 | tf_op jit(solution)/shard_map/ppermute | solution.py:415
  7.2 2.6 %collective-permute-start.1 = (f32[2,1024]{1,0:T(2,128)S(1)}, f32[2,1024]{1,0:T(2,128)S(1)}, u32[]{:S(2)}, u32[]{:S(2)}) collective-permute-start(f32[2,1024]{1,0:T(2,128)S(1)} %pad_maximum_fusion.2), channel_id=1, source_target_pairs={{0,2},{1,3},{2,0},{3,1},{4,6},{5,7},{6,4},{7,5},{8,10},{9,11},{10,... | collective-permute-start | bytes 24584 | tf_op jit(solution)/shard_map/ppermute | solution.py:415
  9.8 5.4 %collective-permute-start.2 = (f32[4,1024]{1,0:T(4,128)S(1)}, f32[4,1024]{1,0:T(4,128)S(1)}, u32[]{:S(2)}, u32[]{:S(2)}) collective-permute-start(f32[4,1024]{1,0:T(4,128)S(1)} %pad_maximum_fusion.1), channel_id=1, source_target_pairs={{0,4},{1,5},{2,6},{3,7},{4,0},{5,1},{6,2},{7,3},{8,12},{9,13},{10,... | collective-permute-start | bytes 49160 | tf_op jit(solution)/shard_map/ppermute | solution.py:415
  15.2 37.7 %copy-start.2 = (s32[64,256]{1,0:T(8,128)S(1)}, s32[64,256]{1,0:T(8,128)}, u32[]{:S(2)}) copy-start(s32[64,256]{1,0:T(8,128)} %ranks_ref.1) | copy-start | bytes 196612
  26.5 7.2 %collective-permute-start.4 = (f32[64,256]{1,0:T(8,128)S(1)}, f32[64,256]{1,0:T(8,128)S(1)}, u32[]{:S(2)}, u32[]{:S(2)}) collective-permute-start(f32[64,256]{1,0:T(8,128)S(1)} %hist.1), channel_id=1, source_target_pairs={{0,56},{8,0},{16,8},{24,16},{32,24},{40,32},{48,40},{56,48},{64,12... | collective-permute-start | bytes 196616 | tf_op jit(solution)/shard_map/ppermute | solution.py:419
  32.3 4.3 %collective-permute-start.3 = (f32[64,256]{1,0:T(8,128)S(1)}, f32[64,256]{1,0:T(8,128)S(1)}, u32[]{:S(2)}, u32[]{:S(2)}) collective-permute-start(f32[64,256]{1,0:T(8,128)S(1)} %hist.1), channel_id=1, source_target_pairs={{0,8},{8,16},{16,24},{24,32},{32,40},{40,48},{48,56},{56,0},{64,72... | collective-permute-start | bytes 196616 | tf_op jit(solution)/shard_map/ppermute | solution.py:419
  36.7 8.1 %collective-permute-start.6 = (f32[64,256]{1,0:T(8,128)S(1)}, f32[64,256]{1,0:T(8,128)S(1)}, u32[]{:S(2)}, u32[]{:S(2)}) collective-permute-start(f32[64,256]{1,0:T(8,128)S(1)} %get-tuple-element.100), channel_id=1, source_target_pairs={{0,16},{8,24},{16,32},{24,40},{32,48},{40,56},{48,0},{56,8},{64,80... | collective-permute-start | bytes 196616 | tf_op jit(solution)/shard_map/ppermute | solution.py:419
  36.8 8.0 %collective-permute-start.5 = (f32[64,256]{1,0:T(8,128)S(1)}, f32[64,256]{1,0:T(8,128)S(1)}, u32[]{:S(2)}, u32[]{:S(2)}) collective-permute-start(f32[64,256]{1,0:T(8,128)S(1)} %get-tuple-element.99), channel_id=1, source_target_pairs={{0,40},{8,48},{16,56},{24,0},{32,8},{40,16},{48,24},{56,32},{64,10... | collective-permute-start | bytes 196616 | tf_op jit(solution)/shard_map/ppermute | solution.py:419
  38.8 16.0 %collective-permute-start.10 = (f32[64,1024]{1,0:T(8,128)S(1)}, f32[64,1024]{1,0:T(8,128)S(1)}, u32[]{:S(2)}, u32[]{:S(2)}) collective-permute-start(f32[64,1024]{1,0:T(8,128)S(1)} %get-tuple-element.73), channel_id=1, source_target_pairs={{0,4},{1,5},{2,6},{3,7},{4,0},{5,1},{6,2},{7,3},{8,12},{9,13},{10,... | collective-permute-start | bytes 786440 | tf_op jit(solution)/shard_map/ppermute | solution.py:411
  39.2 15.6 %collective-permute-start.11 = (f32[64,1024]{1,0:T(8,128)S(1)}, f32[64,1024]{1,0:T(8,128)S(1)}, u32[]{:S(2)}, u32[]{:S(2)}) collective-permute-start(f32[64,1024]{1,0:T(8,128)S(1)} %get-tuple-element.74), channel_id=1, source_target_pairs={{0,5},{1,4},{2,7},{3,6},{4,1},{5,0},{6,3},{7,2},{8,13},{9,12},{10,... | collective-permute-start | bytes 786440 | tf_op jit(solution)/shard_map/ppermute | solution.py:411
  44.8 3.9 %collective-permute-start.9 = (f32[64,256]{1,0:T(8,128)S(1)}, f32[64,256]{1,0:T(8,128)S(1)}, u32[]{:S(2)}, u32[]{:S(2)}) collective-permute-start(f32[64,256]{1,0:T(8,128)S(1)} %add_add_fusion.refs_0_), channel_id=1, source_target_pairs={{0,192},{8,200},{16,208},{24,216},{32,224},{40,232},{48,240},{56,2... | collective-permute-start | bytes 196616 | tf_op jit(solution)/shard_map/ppermute | solution.py:423
  47.3 4.9 %collective-permute-start.8 = (f32[64,256]{1,0:T(8,128)S(1)}, f32[64,256]{1,0:T(8,128)S(1)}, u32[]{:S(2)}, u32[]{:S(2)}) collective-permute-start(f32[64,256]{1,0:T(8,128)S(1)} %add_add_fusion.refs_0_), channel_id=1, source_target_pairs={{0,128},{8,136},{16,144},{24,152},{32,160},{40,168},{48,176},{56,1... | collective-permute-start | bytes 196616 | tf_op jit(solution)/shard_map/ppermute | solution.py:423
  47.8 5.0 %collective-permute-start.7 = (f32[64,256]{1,0:T(8,128)S(1)}, f32[64,256]{1,0:T(8,128)S(1)}, u32[]{:S(2)}, u32[]{:S(2)}) collective-permute-start(f32[64,256]{1,0:T(8,128)S(1)} %add_add_fusion.refs_0_), channel_id=1, source_target_pairs={{0,64},{8,72},{16,80},{24,88},{32,96},{40,104},{48,112},{56,120},{... | collective-permute-start | bytes 196616 | tf_op jit(solution)/shard_map/ppermute | solution.py:423
  54.8 14.4 %collective-permute-start.15 = (f32[64,256]{1,0:T(8,128)S(1)}, f32[64,256]{1,0:T(8,128)S(1)}, u32[]{:S(2)}, u32[]{:S(2)}) collective-permute-start(f32[64,256]{1,0:T(8,128)S(1)} %cuts.1.refs_0_), channel_id=1, source_target_pairs={{0,5},{1,4},{2,7},{3,6},{4,1},{5,0},{6,3},{7,2},{8,13},{9,12},{10,... | collective-permute-start | bytes 196616 | tf_op jit(solution)/shard_map/ppermute | solution.py:411
  58.7 10.5 %collective-permute-start.14 = (f32[64,256]{1,0:T(8,128)S(1)}, f32[64,256]{1,0:T(8,128)S(1)}, u32[]{:S(2)}, u32[]{:S(2)}) collective-permute-start(f32[64,256]{1,0:T(8,128)S(1)} %cuts.1.refs_0_), channel_id=1, source_target_pairs={{0,4},{1,5},{2,6},{3,7},{4,0},{5,1},{6,2},{7,3},{8,12},{9,13},{10,... | collective-permute-start | bytes 196616 | tf_op jit(solution)/shard_map/ppermute | solution.py:411
  63.8 15.0 %collective-permute-start.12 = (f32[64,1024]{1,0:T(8,128)S(1)}, f32[64,1024]{1,0:T(8,128)S(1)}, u32[]{:S(2)}, u32[]{:S(2)}) collective-permute-start(f32[64,1024]{1,0:T(8,128)S(1)} %get-tuple-element.78), channel_id=1, source_target_pairs={{0,2},{1,3},{2,4},{3,5},{4,6},{5,7},{6,0},{7,1},{8,10},{9,11},{10,... | collective-permute-start | bytes 786440 | tf_op jit(solution)/shard_map/ppermute | solution.py:411
  64.1 14.6 %collective-permute-start.13 = (f32[64,1024]{1,0:T(8,128)S(1)}, f32[64,1024]{1,0:T(8,128)S(1)}, u32[]{:S(2)}, u32[]{:S(2)}) collective-permute-start(f32[64,1024]{1,0:T(8,128)S(1)} %get-tuple-element.79), channel_id=1, source_target_pairs={{0,6},{1,7},{2,0},{3,1},{4,2},{5,3},{6,4},{7,5},{8,14},{9,15},{10,... | collective-permute-start | bytes 786440 | tf_op jit(solution)/shard_map/ppermute | solution.py:411
  70.8 8.0 %collective-permute-start.18 = (f32[64,1024]{1,0:T(8,128)S(1)}, f32[64,1024]{1,0:T(8,128)S(1)}, u32[]{:S(2)}, u32[]{:S(2)}) collective-permute-start(f32[64,1024]{1,0:T(8,128)S(1)} %place.6), channel_id=1, source_target_pairs={{0,1},{1,0},{2,3},{3,2},{4,5},{5,4},{6,7},{7,6},{8,9},{9,8},{10,11... | collective-permute-start | bytes 786440 | tf_op jit(solution)/shard_map/ppermute | solution.py:411
  70.9 9.6 %collective-permute-start.16 = (f32[64,1024]{1,0:T(8,128)S(1)}, f32[64,1024]{1,0:T(8,128)S(1)}, u32[]{:S(2)}, u32[]{:S(2)}) collective-permute-start(f32[64,1024]{1,0:T(8,128)S(1)} %get-tuple-element.83), channel_id=1, source_target_pairs={{0,3},{1,2},{2,5},{3,4},{4,7},{5,6},{6,1},{7,0},{8,11},{9,10},{10,... | collective-permute-start | bytes 786440 | tf_op jit(solution)/shard_map/ppermute | solution.py:411
  71.2 9.3 %collective-permute-start.17 = (f32[64,1024]{1,0:T(8,128)S(1)}, f32[64,1024]{1,0:T(8,128)S(1)}, u32[]{:S(2)}, u32[]{:S(2)}) collective-permute-start(f32[64,1024]{1,0:T(8,128)S(1)} %get-tuple-element.84), channel_id=1, source_target_pairs={{0,7},{1,6},{2,1},{3,0},{4,3},{5,2},{6,5},{7,4},{8,15},{9,14},{10,... | collective-permute-start | bytes 786440 | tf_op jit(solution)/shard_map/ppermute | solution.py:411

commit v7 on v6

--- a/solution.py
+++ b/solution.py
@@ -159,24 +159,55 @@
     )
 
 
+def factor_kernel(codes_hbm, out_ref, codes_ref, sem):
+    copy = pltpu.make_async_copy(codes_hbm, codes_ref, sem)
+    copy.start()
+    copy.wait()
+    weight = codes_ref[...].astype(jnp.float32)
+    first = jnp.ones_like(weight)
+    second = weight.astype(jnp.bfloat16).astype(jnp.float32)
+    error = jnp.abs(second - weight)
+    for index in range(1, 128):
+        left = 1.0 + index / 128.0
+        right = (weight * (1.0 / left)).astype(jnp.bfloat16).astype(jnp.float32)
+        off = jnp.abs(left * right - weight)
+        better = off < error
+        error = jnp.minimum(off, error)
+        first = jnp.where(better, left, first)
+        second = jnp.where(better, right, second)
+    out_ref[0] = first
+    out_ref[1] = second * (1.0 / 65536.0)
+
+
+def factor_weights(codes):
+    return pl.pallas_call(
+        factor_kernel,
+        in_specs=[pl.BlockSpec(memory_space=pltpu.HBM)],
+        out_specs=in_vmem(1)[0],
+        out_shape=jax.ShapeDtypeStruct((2,) + codes.shape, jnp.float32),
+        scratch_shapes=[pltpu.VMEM(codes.shape, jnp.int32), pltpu.SemaphoreType.DMA],
+        compiler_params=pltpu.CompilerParams(vmem_limit_bytes=4 << 20),
+        name="factor",
+    )(pltpu.with_memory_space_constraint(codes, pltpu.HBM))
+
+
 def hist_kernel(hess_ref, *refs):
-    *slots, mass_ref, high_ref, rest_ref, sum_ref = refs
-    rows = slots[0].shape[1]
-    scaled = hess_ref[...] * 65536.0
-    high = jnp.floor(scaled * (1.0 / 256.0))
-    rest = scaled - high * 256.0
-    wide = hess_ref.shape[1]
+    *slots, mass_ref, first_ref, second_ref, sum_ref = refs
+    blocks, tiles, lanes = hess_ref.shape
+    wide = tiles * lanes
     me = lax.axis_index("feat")
-    for part in range(rows // wide):
-        own = pl.ds(pl.multiple_of((part ^ me) * wide, wide), wide)
-        high_ref[:, own] = jnp.broadcast_to(high[part : part + 1], (FEATS, wide)).astype(jnp.bfloat16)
-        rest_ref[:, own] = jnp.broadcast_to(rest[part : part + 1], (FEATS, wide)).astype(jnp.bfloat16)
+    for block in range(blocks // 2):
+        for tile in range(tiles):
+            own = pl.ds(pl.multiple_of((block ^ me) * wide + tile * lanes, lanes), lanes)
+            for ref, part in ((first_ref, 0), (second_ref, 1)):
+                row = hess_ref[2 * block + part, tile : tile + 1, :]
+                ref[:, own] = jnp.broadcast_to(row, (FEATS, lanes)).astype(jnp.bfloat16)
 
     for group in range(len(slots) // 2):
-        hist_group(group, *slots[2 * group : 2 * group + 2], mass_ref, high_ref, rest_ref, sum_ref)
-
-
-def hist_group(group, top_ref, low_ref, mass_ref, high_ref, rest_ref, sum_ref):
+        hist_group(group, *slots[2 * group : 2 * group + 2], mass_ref, first_ref, second_ref, sum_ref)
+
+
+def hist_group(group, top_ref, low_ref, mass_ref, first_ref, second_ref, sum_ref):
     rows = top_ref.shape[1]
     shape = (FEATS, LANES)
     lane = lane_iota(shape)
@@ -184,30 +215,27 @@
 
     def multiply(*sums):
         zero = jnp.zeros((FEATS, TILE), jnp.bfloat16)
-        one = jnp.ones((FEATS, TILE), jnp.bfloat16)
         units = (sums[:16], sums[16:])
 
         def step(index, carry):
             for turn in range(UNROLL):
                 spots = [pl.ds(pl.multiple_of(((index * UNROLL + turn) * 2 + unit) * TILE, TILE), TILE) for unit in range(2)]
                 for unit, at in enumerate(spots):
-                    low = low_ref[:, at]
-                    below = jnp.concatenate([jnp.where(low <= k, one, zero) for k in range(16)], axis=0)
+                    low, second = low_ref[:, at], second_ref[:, at]
+                    below = jnp.concatenate([jnp.where(low <= k, second, zero) for k in range(16)], axis=0)
                     pltpu.matmul_push_rhs(below, turn % 2, unit, transpose=True)
                 for unit, at in enumerate(spots):
-                    top, w_high, w_rest = top_ref[:, at], high_ref[:, at], rest_ref[:, at]
+                    top, first = top_ref[:, at], first_ref[:, at]
                     for k in range(16):
-                        hit = top == k
-                        weighted = jnp.concatenate([jnp.where(hit, w_high, zero), jnp.where(hit, w_rest, zero)], axis=0)
+                        weighted = jnp.where(top == k, first, zero)
                         pltpu.matmul_acc_lhs(units[unit][k], weighted, load_staged_rhs=turn % 2 if k == 0 else None)
             return carry
 
         lax.fori_loop(0, rows // (2 * TILE * UNROLL), step, 0)
         for k in range(16):
-            both = pltpu.matmul_pop(units[0][k]) + pltpu.matmul_pop(units[1][k])
-            sum_ref[k * FEATS : (k + 1) * FEATS] = both[:FEATS] * (1.0 / 256.0) + both[FEATS:] * (1.0 / 65536.0)
-
-    pl.run_scoped(multiply, *[pltpu.ACC(mxu_id=unit)((2 * FEATS, TILE), jnp.float32) for unit in range(2) for _ in range(16)])
+            sum_ref[k * FEATS : (k + 1) * FEATS] = pltpu.matmul_pop(units[0][k]) + pltpu.matmul_pop(units[1][k])
+
+    pl.run_scoped(multiply, *[pltpu.ACC(mxu_id=unit)((FEATS, TILE), jnp.float32) for unit in range(2) for _ in range(16)])
 
     points = [2 * lane - 1, 2 * lane]
     columns = [(point & 7) * FEATS + feat for point in points]
@@ -243,19 +271,21 @@
 def cuts_kernel(codes_ref, ranks_ref, *refs):
     *mass_refs, cuts_ref = refs
 
+    together = 32
+
     def step(group, carry):
-        at = pl.ds(pl.multiple_of(group * FEATS, FEATS), FEATS)
+        at = pl.ds(pl.multiple_of(group * together, together), together)
         mass = mass_refs[0][at, :]
         for mass_ref in mass_refs[1:]:
             mass = mass + mass_ref[at, :]
         cut_group(at, codes_ref, ranks_ref, mass, cuts_ref)
         return carry
 
-    lax.fori_loop(0, codes_ref.shape[0] // FEATS, step, 0)
+    lax.fori_loop(0, codes_ref.shape[0] // together, step, 0)
 
 
 def cut_group(at, codes_ref, ranks_ref, mass, cuts_ref):
-    shape = (FEATS, LANES)
+    shape = (mass.shape[0], LANES)
     lane = lane_iota(shape)
     edge_even, edge_odd = even_odd(codes_ref[at, :])
     edge_next = lane_take(edge_even, (lane + 1) & (LANES - 1))
@@ -358,22 +388,25 @@
     )(cuts, values)
 
 
-def far_kernel(*refs):
-    count = len(refs) // 3
-    for cuts_ref, values_ref, out_ref in zip(refs[:count], refs[count : 2 * count], refs[2 * count :]):
-        place_blocks([0], cuts_ref, values_ref, [out_ref])
-
-
-def place_far(cuts, values):
-    return pl.pallas_call(
-        far_kernel,
-        in_specs=in_vmem(2 * len(cuts)),
-        out_specs=in_vmem(len(cuts)),
-        out_shape=[jax.ShapeDtypeStruct(block.shape, jnp.float32) for block in values],
+def rest_kernel(cuts_ref, values_ref, *refs):
+    count = (len(refs) - 1) // 3
+    outs = refs[2 * count :]
+    for far_cuts, far_values, out_ref in zip(refs[:count], refs[count : 2 * count], outs):
+        place_blocks([0], far_cuts, far_values, [out_ref])
+    place_blocks([owner((0, 0)) * outs[count].shape[1]], cuts_ref, values_ref, [outs[count]])
+
+
+def place_rest(cuts, values, far_cuts, far_values):
+    block = jax.ShapeDtypeStruct(far_values[0].shape, jnp.float32)
+    return pl.pallas_call(
+        rest_kernel,
+        in_specs=in_vmem(2 + 2 * len(far_cuts)),
+        out_specs=in_vmem(len(far_cuts) + 1),
+        out_shape=[block] * (len(far_cuts) + 1),
         compiler_params=pltpu.CompilerParams(vmem_limit_bytes=16 << 20),
         cost_estimate=pl.CostEstimate(flops=10**5, bytes_accessed=10**4, transcendentals=0),
-        name="far",
-    )(*cuts, *values)
+        name="rest",
+    )(cuts, values, *far_cuts, *far_values)
 
 
 def join_kernel(moves, *refs):
@@ -424,9 +457,8 @@
 
 
 def on_device(feature_values, hessian_codes, edge_codes, cut_ranks):
-    hess_own = hessian_codes.astype(jnp.float32) * (1.0 / 65536.0)
-    hess = hess_own.reshape(1, -1)
-    far_moves = [(2, 0), (2, 1)]
+    hess = factor_weights(hessian_codes.reshape(-1, LANES))
+    far_moves = [(2, 0), (2, 1), (0, 1)]
     codes, slots = edge_codes, []
     for flip, groups in ((1, (0,)), (2, (1,)), (4, (2, 3))):
         other = flip_feat(hess, flip)
@@ -441,25 +473,24 @@
     far_blocks, hess = lax.optimization_barrier((far_blocks, hess))
     far_values = [send_feat(block, move) for block, move in zip(far_blocks, far_moves)]
     mass = find_mass(hess, slots)
+    mass, far_values[2] = lax.optimization_barrier((mass, far_values[2]))
     before = mass + shift_rows(mass, 1)
     around = before + shift_rows(mass, -1)
     mass = around + shift_rows(around, -3) + shift_rows(before, 2)
     cuts = find_cuts(edge_codes, cut_ranks, mass, *[turn_rows(mass, turn) for turn in (1, 2, 3)])
     cuts, far_values = lax.optimization_barrier((cuts, far_values))
     far_cuts = [send_feat(cuts, move) for move in far_moves]
-    stages = [[(1, 0), (3, 0)], [(1, 1), (3, 1)], [(0, 1)], [(0, 0)]]
     moves, parts = [], []
-    for stage in stages:
+    for stage in ([(1, 0), (3, 0)], [(1, 1), (3, 1)]):
         outs = place(stage, cuts, feature_values)
-        if stage[0] == (1, 1):
-            cuts, outs, far_cuts = lax.optimization_barrier((cuts, outs, far_cuts))
-        elif stage[0] == (0, 1):
+        if parts:
             cuts, outs, far_cuts, far_values = lax.optimization_barrier((cuts, outs, far_cuts, far_values))
         else:
             cuts, outs = lax.optimization_barrier((cuts, outs))
         moves += stage
-        parts += [send_feat(out, move) if move != (0, 0) else out for out, move in zip(outs, stage)]
-    return join(moves + far_moves, parts + list(place_far(far_cuts, far_values)))
+        parts += [send_feat(out, move) for out, move in zip(outs, stage)]
+    rest = place_rest(cuts, feature_values, far_cuts, far_values)
+    return join(moves + far_moves + [(0, 0)], parts + list(rest))
 
 
 def solution(mesh):

time: 82.3 us -> 75.9 us (0.922)
  Pallas kernels: 34.7 us -> 31.1 us
  starting transfers between devices: 34.9 us -> 32.8 us
  other arithmetic: 0.9 us -> 0.04 us
    pallas_call x1 -> x2, Pallas kernels: 3.03 us -> 7.11 us  [the longest x1 6.1 us: place_rest(): pl.pallas_call(rest_kernel, in_specs=in_vmem(2 + 2 * len(far_cuts)), out_...]
    pallas_call x1, Pallas kernels: 11.3 us -> 7.32 us  [find_mass(): pl.pallas_call(hist_kernel, in_specs=in_vmem(1 + len(slots)), out_specs=i...]
    pallas_call x4 -> x2, Pallas kernels: 8.47 us -> 5.36 us  [place(): pl.pallas_call(lambda *refs: place_kernel(moves, *refs), in_specs=in_vmem...]
    ppermute x9 -> x10, starting transfers between devices: 18.3 us -> 15.7 us  [send_feat(): lax.ppermute(array, 'feat', [(i, (i // 2 + move[0]) % 4 * 2 + (i % 2 ^ mo...]
    mul x1 -> x0, other arithmetic: 0.84 us -> none  [on_device(): hess_own = hessian_codes.astype(jnp.float32) * (1.0 / 65536.0)]
    ppermute x9 -> x10, waiting for transfers between devices: 1.77 us -> 1.61 us  [send_feat(): lax.ppermute(array, 'feat', [(i, (i // 2 + move[0]) % 4 * 2 + (i % 2 ^ mo...]
  transfers between devices with their start and end apart: 19 -> 20, of which waited for: 7 -> 8; matrix products, arithmetic and copies ran while one was open for 0% -> 0% of each run, Pallas kernels for 27% -> 38%
where the time goes in v7:
time: 75.9 us; the launch traced here: 75.5 us
  starting transfers between devices  32.8 us (43%)
  Pallas kernels  31.1 us (41%)
  waiting for transfers between devices  11.1 us (15%)
    ppermute x10, starting transfers between devices, send_feat(): lax.ppermute(array, 'feat', [(i, (i // 2 + move[0]) % 4 * 2 + (i % 2 ^ mo...  15.7 us
    ppermute x4, starting transfers between devices, shift_rows(): lax.ppermute(array, 'rows', [(i, i // 8 * 8 + (i + shift) % 8) for i in r...  8.43 us
    pallas_call x1, Pallas kernels, find_mass(): pl.pallas_call(hist_kernel, in_specs=in_vmem(1 + len(slots)), out_specs=i...  7.32 us
    pallas_call x1, Pallas kernels, place_rest(): pl.pallas_call(rest_kernel, in_specs=in_vmem(2 + 2 * len(far_cuts)), out_...  6.1 us
    pallas_call x2, Pallas kernels, find_near_slots(): pl.pallas_call(lambda *refs: near_slot_kernel(groups, *refs), in_specs=in...  5.56 us
    pallas_call x2, Pallas kernels, place(): pl.pallas_call(lambda *refs: place_kernel(moves, *refs), in_specs=in_vmem...  5.36 us
    ppermute x3, starting transfers between devices, flip_feat(): return lax.ppermute(array, 'feat', [(i, i ^ flip) for i in range(8)])  4.98 us
    ppermute x3, waiting for transfers between devices, turn_rows(): lax.ppermute(array, 'rows', [(i, (i + 8 * turn) % 32) for i in range(32)])  4.49 us
  transfers between devices with their start and end apart: 20, of which 8 were waited for; matrix products, arithmetic and copies ran while one was open for 0% of the time, Pallas kernels for 38%

profile of v7, /device:TPU:1, one launch (start us, length us, event | category | flops | bytes accessed | tf_op | source)
XLA Modules:
  0.0 75.5 jit_solution(1195376663945069760)
XLA Ops:
  0.0 1.0 %factor.1 = f32[2,8,128]{2,1,0:T(8,128)S(1)} custom-call(s32[8,128]{1,0:T(8,128)} %bitcast.1), custom_call_target="tpu_custom_call" | custom-call | tf_op jit(solution)/shard_map/factor/pallas_call | solution.py:183
  1.0 3.3 %collective-permute-start = (f32[2,8,128]{2,1,0:T(8,128)S(1)}, f32[2,8,128]{2,1,0:T(8,128)S(1)}, u32[]{:S(2)}, u32[]{:S(2)}) collective-permute-start(f32[2,8,128]{2,1,0:T(8,128)S(1)} %factor.1), channel_id=1, source_target_pairs={{0,1},{1,0},{2,3},{3,2},{4,5},{5,4},{6,7},{7,6},{8,9},{9,8},{10,11... | collective-permute-start | bytes 24584 | tf_op jit(solution)/shard_map/ppermute | solution.py:448
  4.4 3.1 %slots.3 = (bf16[16,8192]{1,0:T(8,128)(2,1)S(1)}, bf16[16,8192]{1,0:T(8,128)(2,1)S(1)}, f32[64,1024]{1,0:T(8,128)S(1)}, f32[64,1024]{1,0:T(8,128)S(1)}, f32[64,1024]{1,0:T(8,128)S(1)}) custom-call(s32[64,256]{1,0:T(8,128)} %codes_ref.1, f32[64,8192]{1,0:T(8,128)} %values_ref.1), custom_call_target="tpu_custom_call" | custom-call | flops 10000000 | bytes 10000000 | tf_op jit(solution)/shard_map/slots/pallas_call | solution.py:143
  7.4 0.0 collective-permute-done
  7.5 0.1 collective-permute-start.1
  7.6 1.9 %slots.4 = (bf16[16,8192]{1,0:T(8,128)(2,1)S(1)}, bf16[16,8192]{1,0:T(8,128)(2,1)S(1)}) custom-call(s32[64,256]{1,0:T(8,128)S(1)} %copy-done.1, f32[64,8192]{1,0:T(8,128)S(1)} %copy-done), custom_call_target="tpu_custom_call" | custom-call | flops 10000000 | bytes 10000000 | tf_op jit(solution)/shard_map/slots/pallas_call | solution.py:128
  9.4 0.7 collective-permute-done.1
  10.1 1.6 %collective-permute-start.2 = (f32[8,8,128]{2,1,0:T(8,128)S(1)}, f32[8,8,128]{2,1,0:T(8,128)S(1)}, u32[]{:S(2)}, u32[]{:S(2)}) collective-permute-start(f32[8,8,128]{2,1,0:T(8,128)S(1)} %pad_maximum_fusion.1), channel_id=1, source_target_pairs={{0,4},{1,5},{2,6},{3,7},{4,0},{5,1},{6,2},{7,3},{8,12},{9,13},{10,... | collective-permute-start | bytes 98312 | tf_op jit(solution)/shard_map/ppermute | solution.py:448
  11.7 3.7 %slots.5 = (bf16[16,8192]{1,0:T(8,128)(2,1)S(1)}, bf16[16,8192]{1,0:T(8,128)(2,1)S(1)}, bf16[16,8192]{1,0:T(8,128)(2,1)S(1)}, bf16[16,8192]{1,0:T(8,128)(2,1)S(1)}) custom-call(s32[64,256]{1,0:T(8,128)S(1)} %copy-done.1, f32[64,8192]{1,0:T(8,128)S(1)} %copy-done), custom_call_target="tpu_custom_call" | custom-call | flops 10000000 | bytes 10000000 | tf_op jit(solution)/shard_map/slots/pallas_call | solution.py:128
  15.4 0.0 collective-permute-done.2
  15.4 1.3 %collective-permute-start.3 = (f32[64,1024]{1,0:T(8,128)S(1)}, f32[64,1024]{1,0:T(8,128)S(1)}, u32[]{:S(2)}, u32[]{:S(2)}) collective-permute-start(f32[64,1024]{1,0:T(8,128)S(1)} %get-tuple-element.78), channel_id=1, source_target_pairs={{0,1},{1,0},{2,3},{3,2},{4,5},{5,4},{6,7},{7,6},{8,9},{9,8},{10,11... | collective-permute-start | bytes 786440 | tf_op jit(solution)/shard_map/ppermute | solution.py:444
  16.7 7.3 %hist.1 = f32[64,256]{1,0:T(8,128)S(1)} custom-call(f32[16,8,128]{2,1,0:T(8,128)S(1)} %pad_maximum_fusion.hess_ref, bf16[16,8192]{1,0:T(8,128)(2,1)S(1)} %get-tuple-element.69.refs_0_, bf16[16,8192]{1,0:T(8,128)(2,1)S(1)} %get-tuple-element.70.refs_1_, bf16[16,8192]{1,0:T(8,128)(2,1)S(1)} %get-tuple-element.71.refs_2_, ...), custom_call_target="tpu_custom_call" | custom-call | flops 4000000000 | bytes 10000000 | tf_op jit(solution)/shard_map/hist/pallas_call | solution.py:258
  24.1 0.0 collective-permute-done.3.refs_5_
  24.1 5.5 %collective-permute-start.5 = (f32[64,256]{1,0:T(8,128)S(1)}, f32[64,256]{1,0:T(8,128)S(1)}, u32[]{:S(2)}, u32[]{:S(2)}) collective-permute-start(f32[64,256]{1,0:T(8,128)S(1)} %hist.1), channel_id=1, source_target_pairs={{0,56},{8,0},{16,8},{24,16},{32,24},{40,32},{48,40},{56,48},{64,12... | collective-permute-start | bytes 196616 | tf_op jit(solution)/shard_map/ppermute | solution.py:452
  29.6 0.0 collective-permute-start.4
  29.6 1.3 %collective-permute-done.5 = f32[64,256]{1,0:T(8,128)S(1)} collective-permute-done((f32[64,256]{1,0:T(8,128)S(1)}, f32[64,256]{1,0:T(8,128)S(1)}, u32[]{:S(2)}, u32[]{:S(2)}) %collective-permute-start.5) | collective-permute-done | bytes 65568 | tf_op jit(solution)/shard_map/ppermute | solution.py:452
  30.9 3.0 %collective-permute-done.4 = f32[64,256]{1,0:T(8,128)S(1)} collective-permute-done((f32[64,256]{1,0:T(8,128)S(1)}, f32[64,256]{1,0:T(8,128)S(1)}, u32[]{:S(2)}, u32[]{:S(2)}) %collective-permute-start.4) | collective-permute-done | bytes 65568 | tf_op jit(solution)/shard_map/ppermute | solution.py:452
  33.9 0.3 collective-permute-start.7
  34.2 2.6 %collective-permute-start.6 = (f32[64,256]{1,0:T(8,128)S(1)}, f32[64,256]{1,0:T(8,128)S(1)}, u32[]{:S(2)}, u32[]{:S(2)}) collective-permute-start(f32[64,256]{1,0:T(8,128)S(1)} %get-tuple-element.107), channel_id=1, source_target_pairs={{0,40},{8,48},{16,56},{24,0},{32,8},{40,16},{48,24},{56,32},{64,10... | collective-permute-start | bytes 196616 | tf_op jit(solution)/shard_map/ppermute | solution.py:452
  36.8 1.3 %collective-permute-start.11 = (f32[64,1024]{1,0:T(8,128)S(1)}, f32[64,1024]{1,0:T(8,128)S(1)}, u32[]{:S(2)}, u32[]{:S(2)}) collective-permute-start(f32[64,1024]{1,0:T(8,128)S(1)} %get-tuple-element.80), channel_id=1, source_target_pairs={{0,4},{1,5},{2,6},{3,7},{4,0},{5,1},{6,2},{7,3},{8,12},{9,13},{10,... | collective-permute-start | bytes 786440 | tf_op jit(solution)/shard_map/ppermute | solution.py:444
  38.2 3.2 %collective-permute-start.12 = (f32[64,1024]{1,0:T(8,128)S(1)}, f32[64,1024]{1,0:T(8,128)S(1)}, u32[]{:S(2)}, u32[]{:S(2)}) collective-permute-start(f32[64,1024]{1,0:T(8,128)S(1)} %get-tuple-element.81), channel_id=1, source_target_pairs={{0,5},{1,4},{2,7},{3,6},{4,1},{5,0},{6,3},{7,2},{8,13},{9,12},{10,... | collective-permute-start | bytes 786440 | tf_op jit(solution)/shard_map/ppermute | solution.py:444
  41.4 0.0 collective-permute-done.7
  41.4 2.5 %collective-permute-start.10 = (f32[64,256]{1,0:T(8,128)S(1)}, f32[64,256]{1,0:T(8,128)S(1)}, u32[]{:S(2)}, u32[]{:S(2)}) collective-permute-start(f32[64,256]{1,0:T(8,128)S(1)} %add_add_fusion.refs_0_), channel_id=1, source_target_pairs={{0,192},{8,200},{16,208},{24,216},{32,224},{40,232},{48,240},{56,2... | collective-permute-start | bytes 196616 | tf_op jit(solution)/shard_map/ppermute | solution.py:456
  43.9 0.5 collective-permute-start.9
  44.5 0.6 collective-permute-start.8
  45.1 0.2 collective-permute-done.10.refs_3_
  45.3 3.6 %collective-permute-done.9.refs_2_ = f32[64,256]{1,0:T(8,128)S(1)} collective-permute-done((f32[64,256]{1,0:T(8,128)S(1)}, f32[64,256]{1,0:T(8,128)S(1)}, u32[]{:S(2)}, u32[]{:S(2)}) %collective-permute-start.9) | collective-permute-done | bytes 65568 | tf_op jit(solution)/shard_map/ppermute | solution.py:456
  48.8 0.7 collective-permute-done.8.refs_1_
  49.5 1.3 %cuts.1.refs_0_.cuts_ref = f32[64,256]{1,0:T(8,128)S(1)} custom-call(s32[64,256]{1,0:T(8,128)S(1)} %copy-done.1, s32[64,256]{1,0:T(8,128)S(1)} %copy-done.2, f32[64,256]{1,0:T(8,128)S(1)} %add_add_fusion.refs_0_, f32[64,256]{1,0:T(8,128)S(1)} %collective-permute-done.8.refs_1_, f32[64,256]{1,0:T(8,128)S(1)} %collective-permute-done.9.refs_2_, ...), custom_call_target="tpu_custom_call" | custom-call | tf_op jit(solution)/shard_map/cuts/pallas_call | solution.py:312
  50.9 0.0 collective-permute-done.11.refs_3_
  50.9 1.1 %collective-permute-done.12.refs_4_ = f32[64,1024]{1,0:T(8,128)S(1)} collective-permute-done((f32[64,1024]{1,0:T(8,128)S(1)}, f32[64,1024]{1,0:T(8,128)S(1)}, u32[]{:S(2)}, u32[]{:S(2)}) %collective-permute-start.12) | collective-permute-done | bytes 262176 | tf_op jit(solution)/shard_map/ppermute | solution.py:444
  52.0 1.2 %collective-permute-start.17 = (f32[64,256]{1,0:T(8,128)S(1)}, f32[64,256]{1,0:T(8,128)S(1)}, u32[]{:S(2)}, u32[]{:S(2)}) collective-permute-start(f32[64,256]{1,0:T(8,128)S(1)} %cuts.1.refs_0_.cuts_ref), channel_id=1, source_target_pairs={{0,1},{1,0},{2,3},{3,2},{4,5},{5,4},{6,7},{7,6},{8,9},{9,8},{10,11... | collective-permute-start | bytes 196616 | tf_op jit(solution)/shard_map/ppermute | solution.py:444
  53.2 1.3 %collective-permute-start.16 = (f32[64,256]{1,0:T(8,128)S(1)}, f32[64,256]{1,0:T(8,128)S(1)}, u32[]{:S(2)}, u32[]{:S(2)}) collective-permute-start(f32[64,256]{1,0:T(8,128)S(1)} %cuts.1.refs_0_.cuts_ref), channel_id=1, source_target_pairs={{0,5},{1,4},{2,7},{3,6},{4,1},{5,0},{6,3},{7,2},{8,13},{9,12},{10,... | collective-permute-start | bytes 196616 | tf_op jit(solution)/shard_map/ppermute | solution.py:444
  54.5 1.7 %collective-permute-start.15 = (f32[64,256]{1,0:T(8,128)S(1)}, f32[64,256]{1,0:T(8,128)S(1)}, u32[]{:S(2)}, u32[]{:S(2)}) collective-permute-start(f32[64,256]{1,0:T(8,128)S(1)} %cuts.1.refs_0_.cuts_ref), channel_id=1, source_target_pairs={{0,4},{1,5},{2,6},{3,7},{4,0},{5,1},{6,2},{7,3},{8,12},{9,13},{10,... | collective-permute-start | bytes 196616 | tf_op jit(solution)/shard_map/ppermute | solution.py:444
  56.1 2.7 %place.2 = (f32[64,1024]{1,0:T(8,128)S(1)}, f32[64,1024]{1,0:T(8,128)S(1)}) custom-call(f32[64,256]{1,0:T(8,128)S(1)} %cuts.1.refs_0_.cuts_ref, f32[64,8192]{1,0:T(8,128)S(1)} %copy-done), custom_call_target="tpu_custom_call" | custom-call | flops 100000 | bytes 10000 | tf_op jit(solution)/shard_map/place/pallas_call | solution.py:380
  58.8 0.5 collective-permute-start.13
  59.3 2.3 %collective-permute-start.14 = (f32[64,1024]{1,0:T(8,128)S(1)}, f32[64,1024]{1,0:T(8,128)S(1)}, u32[]{:S(2)}, u32[]{:S(2)}) collective-permute-start(f32[64,1024]{1,0:T(8,128)S(1)} %get-tuple-element.87), channel_id=1, source_target_pairs={{0,6},{1,7},{2,0},{3,1},{4,2},{5,3},{6,4},{7,5},{8,14},{9,15},{10,... | collective-permute-start | bytes 786440 | tf_op jit(solution)/shard_map/ppermute | solution.py:444
  61.6 2.7 %place.3 = (f32[64,1024]{1,0:T(8,128)S(1)}, f32[64,1024]{1,0:T(8,128)S(1)}) custom-call(f32[64,256]{1,0:T(8,128)S(1)} %cuts.1.refs_0_.cuts_ref, f32[64,8192]{1,0:T(8,128)S(1)} %copy-done), custom_call_target="tpu_custom_call" | custom-call | flops 100000 | bytes 10000 | tf_op jit(solution)/shard_map/place/pallas_call | solution.py:380
  64.3 0.0 collective-permute-done.17.refs_2_
  64.3 0.0 collective-permute-done.15.refs_0_
  64.3 0.4 collective-permute-start.18
  64.7 2.6 %collective-permute-start.19 = (f32[64,1024]{1,0:T(8,128)S(1)}, f32[64,1024]{1,0:T(8,128)S(1)}, u32[]{:S(2)}, u32[]{:S(2)}) collective-permute-start(f32[64,1024]{1,0:T(8,128)S(1)} %get-tuple-element.95), channel_id=1, source_target_pairs={{0,7},{1,6},{2,1},{3,0},{4,3},{5,2},{6,5},{7,4},{8,15},{9,14},{10,... | collective-permute-start | bytes 786440 | tf_op jit(solution)/shard_map/ppermute | solution.py:444
  67.3 6.1 %rest.1 = (f32[64,1024]{1,0:T(8,128)S(1)}, f32[64,1024]{1,0:T(8,128)S(1)}, f32[64,1024]{1,0:T(8,128)S(1)}, f32[64,1024]{1,0:T(8,128)S(1)}) custom-call(f32[64,256]{1,0:T(8,128)S(1)} %cuts.1.refs_0_.cuts_ref, f32[64,8192]{1,0:T(8,128)S(1)} %copy-done, f32[64,256]{1,0:T(8,128)S(1)} %collective-permute-done.15.refs_0_, ...), custom_call_target="tpu_custom_call" | custom-call | flops 100000 | bytes 10000 | tf_op jit(solution)/shard_map/rest/pallas_call | solution.py:401
  73.4 0.0 collective-permute-done.13.refs_0_
  73.5 0.0 collective-permute-done.14.refs_1_
  73.5 0.5 collective-permute-done.18.refs_2_
  74.0 0.0 collective-permute-done.19.refs_3_
  74.0 1.4 %join.1 = f32[512,1024]{1,0:T(8,128)} custom-call(f32[64,1024]{1,0:T(8,128)S(1)} %collective-permute-done.13.refs_0_, f32[64,1024]{1,0:T(8,128)S(1)} %collective-permute-done.14.refs_1_, f32[64,1024]{1,0:T(8,128)S(1)} %collective-permute-done.18.refs_2_, f32[64,1024]{1,0:T(8,128)S(1)} %collective-permute-done.19.refs_3_, ...), custom_call_target="tpu_custom_call" | custom-call | tf_op jit(solution)/shard_map/join/pallas_call | solution.py:427
  (13 shorter events, 0.1 us)
Async XLA Ops:
  0.0 7.6 %copy-start = (f32[64,8192]{1,0:T(8,128)S(1)}, f32[64,8192]{1,0:T(8,128)}, u32[]{:S(2)}) copy-start(f32[64,8192]{1,0:T(8,128)} %values_ref.1) | copy-start | bytes 6291460
  0.0 7.6 %copy-start.1 = (s32[64,256]{1,0:T(8,128)S(1)}, s32[64,256]{1,0:T(8,128)}, u32[]{:S(2)}) copy-start(s32[64,256]{1,0:T(8,128)} %codes_ref.1) | copy-start | bytes 196612
  1.0 6.4 %collective-permute-start = (f32[2,8,128]{2,1,0:T(8,128)S(1)}, f32[2,8,128]{2,1,0:T(8,128)S(1)}, u32[]{:S(2)}, u32[]{:S(2)}) collective-permute-start(f32[2,8,128]{2,1,0:T(8,128)S(1)} %factor.1), channel_id=1, source_target_pairs={{0,1},{1,0},{2,3},{3,2},{4,5},{5,4},{6,7},{7,6},{8,9},{9,8},{10,11... | collective-permute-start | bytes 24584 | tf_op jit(solution)/shard_map/ppermute | solution.py:448
  7.5 2.7 %collective-permute-start.1 = (f32[4,8,128]{2,1,0:T(8,128)S(1)}, f32[4,8,128]{2,1,0:T(8,128)S(1)}, u32[]{:S(2)}, u32[]{:S(2)}) collective-permute-start(f32[4,8,128]{2,1,0:T(8,128)S(1)} %pad_maximum_fusion.2), channel_id=1, source_target_pairs={{0,2},{1,3},{2,0},{3,1},{4,6},{5,7},{6,4},{7,5},{8,10},{9,11},{10,... | collective-permute-start | bytes 49160 | tf_op jit(solution)/shard_map/ppermute | solution.py:448
  10.1 5.3 %collective-permute-start.2 = (f32[8,8,128]{2,1,0:T(8,128)S(1)}, f32[8,8,128]{2,1,0:T(8,128)S(1)}, u32[]{:S(2)}, u32[]{:S(2)}) collective-permute-start(f32[8,8,128]{2,1,0:T(8,128)S(1)} %pad_maximum_fusion.1), channel_id=1, source_target_pairs={{0,4},{1,5},{2,6},{3,7},{4,0},{5,1},{6,2},{7,3},{8,12},{9,13},{10,... | collective-permute-start | bytes 98312 | tf_op jit(solution)/shard_map/ppermute | solution.py:448
  15.4 8.6 %collective-permute-start.3 = (f32[64,1024]{1,0:T(8,128)S(1)}, f32[64,1024]{1,0:T(8,128)S(1)}, u32[]{:S(2)}, u32[]{:S(2)}) collective-permute-start(f32[64,1024]{1,0:T(8,128)S(1)} %get-tuple-element.78), channel_id=1, source_target_pairs={{0,1},{1,0},{2,3},{3,2},{4,5},{5,4},{6,7},{7,6},{8,9},{9,8},{10,11... | collective-permute-start | bytes 786440 | tf_op jit(solution)/shard_map/ppermute | solution.py:444
  16.7 32.8 %copy-start.2 = (s32[64,256]{1,0:T(8,128)S(1)}, s32[64,256]{1,0:T(8,128)}, u32[]{:S(2)}) copy-start(s32[64,256]{1,0:T(8,128)} %ranks_ref.1) | copy-start | bytes 196612
  24.1 6.8 %collective-permute-start.5 = (f32[64,256]{1,0:T(8,128)S(1)}, f32[64,256]{1,0:T(8,128)S(1)}, u32[]{:S(2)}, u32[]{:S(2)}) collective-permute-start(f32[64,256]{1,0:T(8,128)S(1)} %hist.1), channel_id=1, source_target_pairs={{0,56},{8,0},{16,8},{24,16},{32,24},{40,32},{48,40},{56,48},{64,12... | collective-permute-start | bytes 196616 | tf_op jit(solution)/shard_map/ppermute | solution.py:452
  29.6 4.3 %collective-permute-start.4 = (f32[64,256]{1,0:T(8,128)S(1)}, f32[64,256]{1,0:T(8,128)S(1)}, u32[]{:S(2)}, u32[]{:S(2)}) collective-permute-start(f32[64,256]{1,0:T(8,128)S(1)} %hist.1), channel_id=1, source_target_pairs={{0,8},{8,16},{16,24},{24,32},{32,40},{40,48},{48,56},{56,0},{64,72... | collective-permute-start | bytes 196616 | tf_op jit(solution)/shard_map/ppermute | solution.py:452
  33.9 7.4 %collective-permute-start.7 = (f32[64,256]{1,0:T(8,128)S(1)}, f32[64,256]{1,0:T(8,128)S(1)}, u32[]{:S(2)}, u32[]{:S(2)}) collective-permute-start(f32[64,256]{1,0:T(8,128)S(1)} %get-tuple-element.108), channel_id=1, source_target_pairs={{0,16},{8,24},{16,32},{24,40},{32,48},{40,56},{48,0},{56,8},{64,80... | collective-permute-start | bytes 196616 | tf_op jit(solution)/shard_map/ppermute | solution.py:452
  34.2 7.2 %collective-permute-start.6 = (f32[64,256]{1,0:T(8,128)S(1)}, f32[64,256]{1,0:T(8,128)S(1)}, u32[]{:S(2)}, u32[]{:S(2)}) collective-permute-start(f32[64,256]{1,0:T(8,128)S(1)} %get-tuple-element.107), channel_id=1, source_target_pairs={{0,40},{8,48},{16,56},{24,0},{32,8},{40,16},{48,24},{56,32},{64,10... | collective-permute-start | bytes 196616 | tf_op jit(solution)/shard_map/ppermute | solution.py:452
  36.8 14.1 %collective-permute-start.11 = (f32[64,1024]{1,0:T(8,128)S(1)}, f32[64,1024]{1,0:T(8,128)S(1)}, u32[]{:S(2)}, u32[]{:S(2)}) collective-permute-start(f32[64,1024]{1,0:T(8,128)S(1)} %get-tuple-element.80), channel_id=1, source_target_pairs={{0,4},{1,5},{2,6},{3,7},{4,0},{5,1},{6,2},{7,3},{8,12},{9,13},{10,... | collective-permute-start | bytes 786440 | tf_op jit(solution)/shard_map/ppermute | solution.py:444
  38.2 13.8 %collective-permute-start.12 = (f32[64,1024]{1,0:T(8,128)S(1)}, f32[64,1024]{1,0:T(8,128)S(1)}, u32[]{:S(2)}, u32[]{:S(2)}) collective-permute-start(f32[64,1024]{1,0:T(8,128)S(1)} %get-tuple-element.81), channel_id=1, source_target_pairs={{0,5},{1,4},{2,7},{3,6},{4,1},{5,0},{6,3},{7,2},{8,13},{9,12},{10,... | collective-permute-start | bytes 786440 | tf_op jit(solution)/shard_map/ppermute | solution.py:444
  41.4 3.9 %collective-permute-start.10 = (f32[64,256]{1,0:T(8,128)S(1)}, f32[64,256]{1,0:T(8,128)S(1)}, u32[]{:S(2)}, u32[]{:S(2)}) collective-permute-start(f32[64,256]{1,0:T(8,128)S(1)} %add_add_fusion.refs_0_), channel_id=1, source_target_pairs={{0,192},{8,200},{16,208},{24,216},{32,224},{40,232},{48,240},{56,2... | collective-permute-start | bytes 196616 | tf_op jit(solution)/shard_map/ppermute | solution.py:456
  43.9 4.9 %collective-permute-start.9 = (f32[64,256]{1,0:T(8,128)S(1)}, f32[64,256]{1,0:T(8,128)S(1)}, u32[]{:S(2)}, u32[]{:S(2)}) collective-permute-start(f32[64,256]{1,0:T(8,128)S(1)} %add_add_fusion.refs_0_), channel_id=1, source_target_pairs={{0,128},{8,136},{16,144},{24,152},{32,160},{40,168},{48,176},{56,1... | collective-permute-start | bytes 196616 | tf_op jit(solution)/shard_map/ppermute | solution.py:456
  44.5 5.1 %collective-permute-start.8 = (f32[64,256]{1,0:T(8,128)S(1)}, f32[64,256]{1,0:T(8,128)S(1)}, u32[]{:S(2)}, u32[]{:S(2)}) collective-permute-start(f32[64,256]{1,0:T(8,128)S(1)} %add_add_fusion.refs_0_), channel_id=1, source_target_pairs={{0,64},{8,72},{16,80},{24,88},{32,96},{40,104},{48,112},{56,120},{... | collective-permute-start | bytes 196616 | tf_op jit(solution)/shard_map/ppermute | solution.py:456
  52.0 12.3 %collective-permute-start.17 = (f32[64,256]{1,0:T(8,128)S(1)}, f32[64,256]{1,0:T(8,128)S(1)}, u32[]{:S(2)}, u32[]{:S(2)}) collective-permute-start(f32[64,256]{1,0:T(8,128)S(1)} %cuts.1.refs_0_.cuts_ref), channel_id=1, source_target_pairs={{0,1},{1,0},{2,3},{3,2},{4,5},{5,4},{6,7},{7,6},{8,9},{9,8},{10,11... | collective-permute-start | bytes 196616 | tf_op jit(solution)/shard_map/ppermute | solution.py:444
  53.2 11.1 %collective-permute-start.16 = (f32[64,256]{1,0:T(8,128)S(1)}, f32[64,256]{1,0:T(8,128)S(1)}, u32[]{:S(2)}, u32[]{:S(2)}) collective-permute-start(f32[64,256]{1,0:T(8,128)S(1)} %cuts.1.refs_0_.cuts_ref), channel_id=1, source_target_pairs={{0,5},{1,4},{2,7},{3,6},{4,1},{5,0},{6,3},{7,2},{8,13},{9,12},{10,... | collective-permute-start | bytes 196616 | tf_op jit(solution)/shard_map/ppermute | solution.py:444
  54.5 9.8 %collective-permute-start.15 = (f32[64,256]{1,0:T(8,128)S(1)}, f32[64,256]{1,0:T(8,128)S(1)}, u32[]{:S(2)}, u32[]{:S(2)}) collective-permute-start(f32[64,256]{1,0:T(8,128)S(1)} %cuts.1.refs_0_.cuts_ref), channel_id=1, source_target_pairs={{0,4},{1,5},{2,6},{3,7},{4,0},{5,1},{6,2},{7,3},{8,12},{9,13},{10,... | collective-permute-start | bytes 196616 | tf_op jit(solution)/shard_map/ppermute | solution.py:444
  58.8 14.6 %collective-permute-start.13 = (f32[64,1024]{1,0:T(8,128)S(1)}, f32[64,1024]{1,0:T(8,128)S(1)}, u32[]{:S(2)}, u32[]{:S(2)}) collective-permute-start(f32[64,1024]{1,0:T(8,128)S(1)} %get-tuple-element.86), channel_id=1, source_target_pairs={{0,2},{1,3},{2,4},{3,5},{4,6},{5,7},{6,0},{7,1},{8,10},{9,11},{10,... | collective-permute-start | bytes 786440 | tf_op jit(solution)/shard_map/ppermute | solution.py:444
  59.3 14.1 %collective-permute-start.14 = (f32[64,1024]{1,0:T(8,128)S(1)}, f32[64,1024]{1,0:T(8,128)S(1)}, u32[]{:S(2)}, u32[]{:S(2)}) collective-permute-start(f32[64,1024]{1,0:T(8,128)S(1)} %get-tuple-element.87), channel_id=1, source_target_pairs={{0,6},{1,7},{2,0},{3,1},{4,2},{5,3},{6,4},{7,5},{8,14},{9,15},{10,... | collective-permute-start | bytes 786440 | tf_op jit(solution)/shard_map/ppermute | solution.py:444
  64.3 9.7 %collective-permute-start.18 = (f32[64,1024]{1,0:T(8,128)S(1)}, f32[64,1024]{1,0:T(8,128)S(1)}, u32[]{:S(2)}, u32[]{:S(2)}) collective-permute-start(f32[64,1024]{1,0:T(8,128)S(1)} %get-tuple-element.94), channel_id=1, source_target_pairs={{0,3},{1,2},{2,5},{3,4},{4,7},{5,6},{6,1},{7,0},{8,11},{9,10},{10,... | collective-permute-start | bytes 786440 | tf_op jit(solution)/shard_map/ppermute | solution.py:444
  64.7 9.3 %collective-permute-start.19 = (f32[64,1024]{1,0:T(8,128)S(1)}, f32[64,1024]{1,0:T(8,128)S(1)}, u32[]{:S(2)}, u32[]{:S(2)}) collective-permute-start(f32[64,1024]{1,0:T(8,128)S(1)} %get-tuple-element.95), channel_id=1, source_target_pairs={{0,7},{1,6},{2,1},{3,0},{4,3},{5,2},{6,5},{7,4},{8,15},{9,14},{10,... | collective-permute-start | bytes 786440 | tf_op jit(solution)/shard_map/ppermute | solution.py:444

commit v8 on v7

--- a/solution.py
+++ b/solution.py
@@ -350,7 +350,7 @@
 
 def place_blocks(bases, cuts_ref, values_ref, out_refs):
     feats, wide = out_refs[0].shape
-    together = 4
+    together = 8 // len(bases)
 
     def store(out_ref, at, part):
         def write(value):
@@ -388,25 +388,23 @@
     )(cuts, values)
 
 
-def rest_kernel(cuts_ref, values_ref, *refs):
-    count = (len(refs) - 1) // 3
-    outs = refs[2 * count :]
-    for far_cuts, far_values, out_ref in zip(refs[:count], refs[count : 2 * count], outs):
-        place_blocks([0], far_cuts, far_values, [out_ref])
-    place_blocks([owner((0, 0)) * outs[count].shape[1]], cuts_ref, values_ref, [outs[count]])
-
-
-def place_rest(cuts, values, far_cuts, far_values):
-    block = jax.ShapeDtypeStruct(far_values[0].shape, jnp.float32)
-    return pl.pallas_call(
-        rest_kernel,
-        in_specs=in_vmem(2 + 2 * len(far_cuts)),
-        out_specs=in_vmem(len(far_cuts) + 1),
-        out_shape=[block] * (len(far_cuts) + 1),
+def far_kernel(far_ref, core_ref, *refs):
+    feats = far_ref.shape[0]
+    cuts_refs = [far_ref, core_ref.at[:feats, :], core_ref.at[feats:, :]]
+    for cuts_ref, values_ref, out_ref in zip(cuts_refs, refs[:3], refs[3:]):
+        place_blocks([0], cuts_ref, values_ref, [out_ref])
+
+
+def place_far(far_cuts, core_cuts, values):
+    return pl.pallas_call(
+        far_kernel,
+        in_specs=in_vmem(2 + len(values)),
+        out_specs=in_vmem(len(values)),
+        out_shape=[jax.ShapeDtypeStruct(block.shape, jnp.float32) for block in values],
         compiler_params=pltpu.CompilerParams(vmem_limit_bytes=16 << 20),
         cost_estimate=pl.CostEstimate(flops=10**5, bytes_accessed=10**4, transcendentals=0),
-        name="rest",
-    )(cuts, values, *far_cuts, *far_values)
+        name="far",
+    )(far_cuts, core_cuts, *values)
 
 
 def join_kernel(moves, *refs):
@@ -479,18 +477,20 @@
     mass = around + shift_rows(around, -3) + shift_rows(before, 2)
     cuts = find_cuts(edge_codes, cut_ranks, mass, *[turn_rows(mass, turn) for turn in (1, 2, 3)])
     cuts, far_values = lax.optimization_barrier((cuts, far_values))
-    far_cuts = [send_feat(cuts, move) for move in far_moves]
-    moves, parts = [], []
-    for stage in ([(1, 0), (3, 0)], [(1, 1), (3, 1)]):
-        outs = place(stage, cuts, feature_values)
-        if parts:
-            cuts, outs, far_cuts, far_values = lax.optimization_barrier((cuts, outs, far_cuts, far_values))
-        else:
-            cuts, outs = lax.optimization_barrier((cuts, outs))
-        moves += stage
-        parts += [send_feat(out, move) for out, move in zip(outs, stage)]
-    rest = place_rest(cuts, feature_values, far_cuts, far_values)
-    return join(moves + far_moves + [(0, 0)], parts + list(rest))
+    far_cuts, moves, parts = send_feat(cuts, (2, 0)), [], []
+    for index, stage in enumerate(((0, 0), (1, 0), (3, 0), (1, 1), (3, 1))):
+        (out,) = place([stage], cuts, feature_values)
+        cuts, out = lax.optimization_barrier((cuts, out))
+        if index == 2:
+            cuts, far_cuts = lax.optimization_barrier((cuts, far_cuts))
+            core_cuts = send_feat(jnp.concatenate([far_cuts, cuts], axis=0), (0, 1))
+        elif index == 3:
+            cuts, parts[1] = lax.optimization_barrier((cuts, parts[1]))
+        elif index == 4:
+            cuts, far_values, parts[2] = lax.optimization_barrier((cuts, far_values, parts[2]))
+        moves.append(stage)
+        parts.append(send_feat(out, stage) if stage != (0, 0) else out)
+    return join(moves + far_moves, parts + list(place_far(far_cuts, core_cuts, far_values)))
 
 
 def solution(mesh):

time: 75.9 us -> 79.7 us (1.050)
  waiting for transfers between devices: 11.1 us -> 15.4 us
    ppermute x10 -> x9, waiting for transfers between devices: 1.61 us -> 5.85 us  [send_feat(): lax.ppermute(array, 'feat', [(i, (i // 2 + move[0]) % 4 * 2 + (i % 2 ^ mo...]
    pallas_call x1, Pallas kernels: 6.1 us -> 4.05 us  [place_far(): pl.pallas_call(far_kernel, in_specs=in_vmem(2 + len(values)), out_specs=i...]
    pallas_call x2 -> x5, Pallas kernels: 5.36 us -> 7.04 us  [place(): pl.pallas_call(lambda *refs: place_kernel(moves, *refs), in_specs=in_vmem...]
    ppermute x10 -> x9, starting transfers between devices: 15.7 us -> 15.2 us  [send_feat(): lax.ppermute(array, 'feat', [(i, (i // 2 + move[0]) % 4 * 2 + (i % 2 ^ mo...]
  transfers between devices with their start and end apart: 20 -> 19, of which waited for: 8 -> 9; matrix products, arithmetic and copies ran while one was open for 0% -> 0% of each run, Pallas kernels for 38% -> 32%
where the time goes in v8:
time: 79.7 us; the launch traced here: 78.9 us
  starting transfers between devices  32.3 us (41%)
  Pallas kernels  30.8 us (39%)
  waiting for transfers between devices  15.4 us (19%)
    ppermute x9, starting transfers between devices, send_feat(): lax.ppermute(array, 'feat', [(i, (i // 2 + move[0]) % 4 * 2 + (i % 2 ^ mo...  15.2 us
    ppermute x4, starting transfers between devices, shift_rows(): lax.ppermute(array, 'rows', [(i, i // 8 * 8 + (i + shift) % 8) for i in r...  8.43 us
    pallas_call x1, Pallas kernels, find_mass(): pl.pallas_call(hist_kernel, in_specs=in_vmem(1 + len(slots)), out_specs=i...  7.32 us
    pallas_call x5, Pallas kernels, place(): pl.pallas_call(lambda *refs: place_kernel(moves, *refs), in_specs=in_vmem...  7.04 us
    ppermute x9, waiting for transfers between devices, send_feat(): lax.ppermute(array, 'feat', [(i, (i // 2 + move[0]) % 4 * 2 + (i % 2 ^ mo...  5.85 us
    pallas_call x2, Pallas kernels, find_near_slots(): pl.pallas_call(lambda *refs: near_slot_kernel(groups, *refs), in_specs=in...  5.56 us
    ppermute x3, starting transfers between devices, flip_feat(): return lax.ppermute(array, 'feat', [(i, i ^ flip) for i in range(8)])  4.98 us
    ppermute x3, waiting for transfers between devices, turn_rows(): lax.ppermute(array, 'rows', [(i, (i + 8 * turn) % 32) for i in range(32)])  4.49 us
  transfers between devices with their start and end apart: 19, of which 9 were waited for; matrix products, arithmetic and copies ran while one was open for 0% of the time, Pallas kernels for 32%

profile of v8, /device:TPU:1, one launch (start us, length us, event | category | flops | bytes accessed | tf_op | source)
XLA Modules:
  0.0 78.9 jit_solution(756812617803140490)
XLA Ops:
  0.0 1.0 %factor.1 = f32[2,8,128]{2,1,0:T(8,128)S(1)} custom-call(s32[8,128]{1,0:T(8,128)} %bitcast.1), custom_call_target="tpu_custom_call" | custom-call | tf_op jit(solution)/shard_map/factor/pallas_call | solution.py:183
  1.0 3.3 %collective-permute-start = (f32[2,8,128]{2,1,0:T(8,128)S(1)}, f32[2,8,128]{2,1,0:T(8,128)S(1)}, u32[]{:S(2)}, u32[]{:S(2)}) collective-permute-start(f32[2,8,128]{2,1,0:T(8,128)S(1)} %factor.1), channel_id=1, source_target_pairs={{0,1},{1,0},{2,3},{3,2},{4,5},{5,4},{6,7},{7,6},{8,9},{9,8},{10,11... | collective-permute-start | bytes 24584 | tf_op jit(solution)/shard_map/ppermute | solution.py:446
  4.4 3.1 %slots.3 = (bf16[16,8192]{1,0:T(8,128)(2,1)S(1)}, bf16[16,8192]{1,0:T(8,128)(2,1)S(1)}, f32[64,1024]{1,0:T(8,128)S(1)}, f32[64,1024]{1,0:T(8,128)S(1)}, f32[64,1024]{1,0:T(8,128)S(1)}) custom-call(s32[64,256]{1,0:T(8,128)} %codes_ref.1, f32[64,8192]{1,0:T(8,128)} %refs_1_.15), custom_call_target="tpu_custom_call" | custom-call | flops 10000000 | bytes 10000000 | tf_op jit(solution)/shard_map/slots/pallas_call | solution.py:143
  7.4 0.0 collective-permute-done
  7.5 0.1 collective-permute-start.1
  7.6 1.9 %slots.4 = (bf16[16,8192]{1,0:T(8,128)(2,1)S(1)}, bf16[16,8192]{1,0:T(8,128)(2,1)S(1)}) custom-call(s32[64,256]{1,0:T(8,128)S(1)} %copy-done.1, f32[64,8192]{1,0:T(8,128)S(1)} %copy-done), custom_call_target="tpu_custom_call" | custom-call | flops 10000000 | bytes 10000000 | tf_op jit(solution)/shard_map/slots/pallas_call | solution.py:128
  9.4 0.7 collective-permute-done.1
  10.1 1.6 %collective-permute-start.2 = (f32[8,8,128]{2,1,0:T(8,128)S(1)}, f32[8,8,128]{2,1,0:T(8,128)S(1)}, u32[]{:S(2)}, u32[]{:S(2)}) collective-permute-start(f32[8,8,128]{2,1,0:T(8,128)S(1)} %pad_maximum_fusion.2), channel_id=1, source_target_pairs={{0,4},{1,5},{2,6},{3,7},{4,0},{5,1},{6,2},{7,3},{8,12},{9,13},{10,... | collective-permute-start | bytes 98312 | tf_op jit(solution)/shard_map/ppermute | solution.py:446
  11.7 3.7 %slots.5 = (bf16[16,8192]{1,0:T(8,128)(2,1)S(1)}, bf16[16,8192]{1,0:T(8,128)(2,1)S(1)}, bf16[16,8192]{1,0:T(8,128)(2,1)S(1)}, bf16[16,8192]{1,0:T(8,128)(2,1)S(1)}) custom-call(s32[64,256]{1,0:T(8,128)S(1)} %copy-done.1, f32[64,8192]{1,0:T(8,128)S(1)} %copy-done), custom_call_target="tpu_custom_call" | custom-call | flops 10000000 | bytes 10000000 | tf_op jit(solution)/shard_map/slots/pallas_call | solution.py:128
  15.4 0.0 collective-permute-done.2
  15.4 1.3 %collective-permute-start.3 = (f32[64,1024]{1,0:T(8,128)S(1)}, f32[64,1024]{1,0:T(8,128)S(1)}, u32[]{:S(2)}, u32[]{:S(2)}) collective-permute-start(f32[64,1024]{1,0:T(8,128)S(1)} %get-tuple-element.78), channel_id=1, source_target_pairs={{0,1},{1,0},{2,3},{3,2},{4,5},{5,4},{6,7},{7,6},{8,9},{9,8},{10,11... | collective-permute-start | bytes 786440 | tf_op jit(solution)/shard_map/ppermute | solution.py:442
  16.7 7.3 %hist.1 = f32[64,256]{1,0:T(8,128)S(1)} custom-call(f32[16,8,128]{2,1,0:T(8,128)S(1)} %pad_maximum_fusion.1.hess_ref, bf16[16,8192]{1,0:T(8,128)(2,1)S(1)} %get-tuple-element.69.refs_0_, bf16[16,8192]{1,0:T(8,128)(2,1)S(1)} %get-tuple-element.70.refs_1_, bf16[16,8192]{1,0:T(8,128)(2,1)S(1)} %get-tuple-element.71.refs_2_, ...), custom_call_target="tpu_custom_call" | custom-call | flops 4000000000 | bytes 10000000 | tf_op jit(solution)/shard_map/hist/pallas_call | solution.py:258
  24.1 0.0 collective-permute-done.3.refs_2_
  24.1 5.5 %collective-permute-start.5 = (f32[64,256]{1,0:T(8,128)S(1)}, f32[64,256]{1,0:T(8,128)S(1)}, u32[]{:S(2)}, u32[]{:S(2)}) collective-permute-start(f32[64,256]{1,0:T(8,128)S(1)} %hist.1), channel_id=1, source_target_pairs={{0,56},{8,0},{16,8},{24,16},{32,24},{40,32},{48,40},{56,48},{64,12... | collective-permute-start | bytes 196616 | tf_op jit(solution)/shard_map/ppermute | solution.py:450
  29.6 0.0 collective-permute-start.4
  29.6 1.3 %collective-permute-done.5 = f32[64,256]{1,0:T(8,128)S(1)} collective-permute-done((f32[64,256]{1,0:T(8,128)S(1)}, f32[64,256]{1,0:T(8,128)S(1)}, u32[]{:S(2)}, u32[]{:S(2)}) %collective-permute-start.5) | collective-permute-done | bytes 65568 | tf_op jit(solution)/shard_map/ppermute | solution.py:450
  30.9 3.0 %collective-permute-done.4 = f32[64,256]{1,0:T(8,128)S(1)} collective-permute-done((f32[64,256]{1,0:T(8,128)S(1)}, f32[64,256]{1,0:T(8,128)S(1)}, u32[]{:S(2)}, u32[]{:S(2)}) %collective-permute-start.4) | collective-permute-done | bytes 65568 | tf_op jit(solution)/shard_map/ppermute | solution.py:450
  33.9 0.3 collective-permute-start.7
  34.2 2.6 %collective-permute-start.6 = (f32[64,256]{1,0:T(8,128)S(1)}, f32[64,256]{1,0:T(8,128)S(1)}, u32[]{:S(2)}, u32[]{:S(2)}) collective-permute-start(f32[64,256]{1,0:T(8,128)S(1)} %get-tuple-element.107), channel_id=1, source_target_pairs={{0,40},{8,48},{16,56},{24,0},{32,8},{40,16},{48,24},{56,32},{64,10... | collective-permute-start | bytes 196616 | tf_op jit(solution)/shard_map/ppermute | solution.py:450
  36.8 1.3 %collective-permute-start.11 = (f32[64,1024]{1,0:T(8,128)S(1)}, f32[64,1024]{1,0:T(8,128)S(1)}, u32[]{:S(2)}, u32[]{:S(2)}) collective-permute-start(f32[64,1024]{1,0:T(8,128)S(1)} %get-tuple-element.80), channel_id=1, source_target_pairs={{0,4},{1,5},{2,6},{3,7},{4,0},{5,1},{6,2},{7,3},{8,12},{9,13},{10,... | collective-permute-start | bytes 786440 | tf_op jit(solution)/shard_map/ppermute | solution.py:442
  38.2 3.2 %collective-permute-start.12 = (f32[64,1024]{1,0:T(8,128)S(1)}, f32[64,1024]{1,0:T(8,128)S(1)}, u32[]{:S(2)}, u32[]{:S(2)}) collective-permute-start(f32[64,1024]{1,0:T(8,128)S(1)} %get-tuple-element.81), channel_id=1, source_target_pairs={{0,5},{1,4},{2,7},{3,6},{4,1},{5,0},{6,3},{7,2},{8,13},{9,12},{10,... | collective-permute-start | bytes 786440 | tf_op jit(solution)/shard_map/ppermute | solution.py:442
  41.4 0.0 collective-permute-done.7
  41.4 2.5 %collective-permute-start.10 = (f32[64,256]{1,0:T(8,128)S(1)}, f32[64,256]{1,0:T(8,128)S(1)}, u32[]{:S(2)}, u32[]{:S(2)}) collective-permute-start(f32[64,256]{1,0:T(8,128)S(1)} %add_add_fusion.refs_0_), channel_id=1, source_target_pairs={{0,192},{8,200},{16,208},{24,216},{32,224},{40,232},{48,240},{56,2... | collective-permute-start | bytes 196616 | tf_op jit(solution)/shard_map/ppermute | solution.py:454
  43.9 0.5 collective-permute-start.9
  44.5 0.6 collective-permute-start.8
  45.1 0.2 collective-permute-done.10.refs_3_
  45.3 3.6 %collective-permute-done.9.refs_2_ = f32[64,256]{1,0:T(8,128)S(1)} collective-permute-done((f32[64,256]{1,0:T(8,128)S(1)}, f32[64,256]{1,0:T(8,128)S(1)}, u32[]{:S(2)}, u32[]{:S(2)}) %collective-permute-start.9) | collective-permute-done | bytes 65568 | tf_op jit(solution)/shard_map/ppermute | solution.py:454
  48.8 0.7 collective-permute-done.8.refs_1_
  49.5 1.4 %cuts.1.refs_0_ = f32[64,256]{1,0:T(8,128)S(1)} custom-call(s32[64,256]{1,0:T(8,128)S(1)} %copy-done.1, s32[64,256]{1,0:T(8,128)S(1)} %copy-done.2, f32[64,256]{1,0:T(8,128)S(1)} %add_add_fusion.refs_0_, f32[64,256]{1,0:T(8,128)S(1)} %collective-permute-done.8.refs_1_, f32[64,256]{1,0:T(8,128)S(1)} %collective-permute-done.9.refs_2_, ...), custom_call_target="tpu_custom_call" | custom-call | tf_op jit(solution)/shard_map/cuts/pallas_call | solution.py:312
  50.9 1.1 %collective-permute-done.12.refs_1_ = f32[64,1024]{1,0:T(8,128)S(1)} collective-permute-done((f32[64,1024]{1,0:T(8,128)S(1)}, f32[64,1024]{1,0:T(8,128)S(1)}, u32[]{:S(2)}, u32[]{:S(2)}) %collective-permute-start.12) | collective-permute-done | bytes 262176 | tf_op jit(solution)/shard_map/ppermute | solution.py:442
  52.0 1.4 %place.5.refs_0_ = f32[64,1024]{1,0:T(8,128)S(1)} custom-call(f32[64,256]{1,0:T(8,128)S(1)} %cuts.1.refs_0_, f32[64,8192]{1,0:T(8,128)S(1)} %copy-done), custom_call_target="tpu_custom_call" | custom-call | flops 100000 | bytes 10000 | tf_op jit(solution)/shard_map/place/pallas_call | solution.py:380
  53.4 1.4 %place.6 = f32[64,1024]{1,0:T(8,128)S(1)} custom-call(f32[64,256]{1,0:T(8,128)S(1)} %cuts.1.refs_0_, f32[64,8192]{1,0:T(8,128)S(1)} %copy-done), custom_call_target="tpu_custom_call" | custom-call | flops 100000 | bytes 10000 | tf_op jit(solution)/shard_map/place/pallas_call | solution.py:380
  54.8 0.5 collective-permute-start.14
  55.3 1.9 %collective-permute-start.13 = (f32[64,256]{1,0:T(8,128)S(1)}, f32[64,256]{1,0:T(8,128)S(1)}, u32[]{:S(2)}, u32[]{:S(2)}) collective-permute-start(f32[64,256]{1,0:T(8,128)S(1)} %cuts.1.refs_0_), channel_id=1, source_target_pairs={{0,4},{1,5},{2,6},{3,7},{4,0},{5,1},{6,2},{7,3},{8,12},{9,13},{10,... | collective-permute-start | bytes 196616 | tf_op jit(solution)/shard_map/ppermute | solution.py:442
  57.2 1.4 %place.7 = f32[64,1024]{1,0:T(8,128)S(1)} custom-call(f32[64,256]{1,0:T(8,128)S(1)} %cuts.1.refs_0_, f32[64,8192]{1,0:T(8,128)S(1)} %copy-done), custom_call_target="tpu_custom_call" | custom-call | flops 100000 | bytes 10000 | tf_op jit(solution)/shard_map/place/pallas_call | solution.py:380
  58.6 1.1 %collective-permute-start.15 = (f32[64,1024]{1,0:T(8,128)S(1)}, f32[64,1024]{1,0:T(8,128)S(1)}, u32[]{:S(2)}, u32[]{:S(2)}) collective-permute-start(f32[64,1024]{1,0:T(8,128)S(1)} %place.7), channel_id=1, source_target_pairs={{0,6},{1,7},{2,0},{3,1},{4,2},{5,3},{6,4},{7,5},{8,14},{9,15},{10,... | collective-permute-start | bytes 786440 | tf_op jit(solution)/shard_map/ppermute | solution.py:442
  59.8 3.8 %collective-permute-done.13.far_ref = f32[64,256]{1,0:T(8,128)S(1)} collective-permute-done((f32[64,256]{1,0:T(8,128)S(1)}, f32[64,256]{1,0:T(8,128)S(1)}, u32[]{:S(2)}, u32[]{:S(2)}) %collective-permute-start.13) | collective-permute-done | bytes 65568 | tf_op jit(solution)/shard_map/ppermute | solution.py:442
  63.6 1.4 %place.8 = f32[64,1024]{1,0:T(8,128)S(1)} custom-call(f32[64,256]{1,0:T(8,128)S(1)} %cuts.1.refs_0_, f32[64,8192]{1,0:T(8,128)S(1)} %copy-done), custom_call_target="tpu_custom_call" | custom-call | flops 100000 | bytes 10000 | tf_op jit(solution)/shard_map/place/pallas_call | solution.py:380
  65.0 0.4 collective-permute-start.16
  65.4 1.4 %place.9 = f32[64,1024]{1,0:T(8,128)S(1)} custom-call(f32[64,256]{1,0:T(8,128)S(1)} %cuts.1.refs_0_, f32[64,8192]{1,0:T(8,128)S(1)} %copy-done), custom_call_target="tpu_custom_call" | custom-call | flops 100000 | bytes 10000 | tf_op jit(solution)/shard_map/place/pallas_call | solution.py:380
  66.8 3.0 %collective-permute-start.17 = (f32[64,1024]{1,0:T(8,128)S(1)}, f32[64,1024]{1,0:T(8,128)S(1)}, u32[]{:S(2)}, u32[]{:S(2)}) collective-permute-start(f32[64,1024]{1,0:T(8,128)S(1)} %place.9), channel_id=1, source_target_pairs={{0,7},{1,6},{2,1},{3,0},{4,3},{5,2},{6,5},{7,4},{8,15},{9,14},{10,... | collective-permute-start | bytes 786440 | tf_op jit(solution)/shard_map/ppermute | solution.py:442
  69.7 2.5 %collective-permute-start.18 = (f32[128,256]{1,0:T(8,128)S(1)}, f32[128,256]{1,0:T(8,128)S(1)}, u32[]{:S(2)}, u32[]{:S(2)}) collective-permute-start(f32[128,256]{1,0:T(8,128)S(1)} %pad_maximum_fusion), channel_id=1, source_target_pairs={{0,1},{1,0},{2,3},{3,2},{4,5},{5,4},{6,7},{7,6},{8,9},{9,8},{10,11... | collective-permute-start | bytes 393224 | tf_op jit(solution)/shard_map/ppermute | solution.py:442
  72.3 0.0 collective-permute-done.15.refs_2_
  72.3 1.0 %collective-permute-done.18.core_ref = f32[128,256]{1,0:T(8,128)S(1)} collective-permute-done((f32[128,256]{1,0:T(8,128)S(1)}, f32[128,256]{1,0:T(8,128)S(1)}, u32[]{:S(2)}, u32[]{:S(2)}) %collective-permute-start.18) | collective-permute-done | bytes 131104 | tf_op jit(solution)/shard_map/ppermute | solution.py:442
  73.2 4.1 %far.1 = (f32[64,1024]{1,0:T(8,128)S(1)}, f32[64,1024]{1,0:T(8,128)S(1)}, f32[64,1024]{1,0:T(8,128)S(1)}) custom-call(f32[64,256]{1,0:T(8,128)S(1)} %collective-permute-done.13.far_ref, f32[128,256]{1,0:T(8,128)S(1)} %collective-permute-done.18.core_ref, f32[64,1024]{1,0:T(8,128)S(1)} %collective-permute-done.11.refs_0_, ...), custom_call_target="tpu_custom_call" | custom-call | flops 100000 | bytes 10000 | tf_op jit(solution)/shard_map/far/pallas_call | solution.py:399
  77.3 0.0 collective-permute-done.16.refs_3_
  77.3 0.0 collective-permute-done.17.refs_4_
  77.3 1.4 %join.1 = f32[512,1024]{1,0:T(8,128)} custom-call(f32[64,1024]{1,0:T(8,128)S(1)} %place.5.refs_0_, f32[64,1024]{1,0:T(8,128)S(1)} %collective-permute-done.14.refs_1_, f32[64,1024]{1,0:T(8,128)S(1)} %collective-permute-done.15.refs_2_, f32[64,1024]{1,0:T(8,128)S(1)} %collective-permute-done.16.refs_3_, f32[64,1024]{1,0:T(8,128)S(1)} %collective-permute-done.17.refs_4_, ...), custom_call_target="tpu_custom_call" | custom-call | tf_op jit(solution)/shard_map/join/pallas_call | solution.py:425
  (15 shorter events, 0.1 us)
Async XLA Ops:
  0.0 7.6 %copy-start = (f32[64,8192]{1,0:T(8,128)S(1)}, f32[64,8192]{1,0:T(8,128)}, u32[]{:S(2)}) copy-start(f32[64,8192]{1,0:T(8,128)} %refs_1_.15) | copy-start | bytes 6291460
  0.0 7.6 %copy-start.1 = (s32[64,256]{1,0:T(8,128)S(1)}, s32[64,256]{1,0:T(8,128)}, u32[]{:S(2)}) copy-start(s32[64,256]{1,0:T(8,128)} %codes_ref.1) | copy-start | bytes 196612
  1.0 6.4 %collective-permute-start = (f32[2,8,128]{2,1,0:T(8,128)S(1)}, f32[2,8,128]{2,1,0:T(8,128)S(1)}, u32[]{:S(2)}, u32[]{:S(2)}) collective-permute-start(f32[2,8,128]{2,1,0:T(8,128)S(1)} %factor.1), channel_id=1, source_target_pairs={{0,1},{1,0},{2,3},{3,2},{4,5},{5,4},{6,7},{7,6},{8,9},{9,8},{10,11... | collective-permute-start | bytes 24584 | tf_op jit(solution)/shard_map/ppermute | solution.py:446
  7.5 2.7 %collective-permute-start.1 = (f32[4,8,128]{2,1,0:T(8,128)S(1)}, f32[4,8,128]{2,1,0:T(8,128)S(1)}, u32[]{:S(2)}, u32[]{:S(2)}) collective-permute-start(f32[4,8,128]{2,1,0:T(8,128)S(1)} %pad_maximum_fusion.3), channel_id=1, source_target_pairs={{0,2},{1,3},{2,0},{3,1},{4,6},{5,7},{6,4},{7,5},{8,10},{9,11},{10,... | collective-permute-start | bytes 49160 | tf_op jit(solution)/shard_map/ppermute | solution.py:446
  10.1 5.3 %collective-permute-start.2 = (f32[8,8,128]{2,1,0:T(8,128)S(1)}, f32[8,8,128]{2,1,0:T(8,128)S(1)}, u32[]{:S(2)}, u32[]{:S(2)}) collective-permute-start(f32[8,8,128]{2,1,0:T(8,128)S(1)} %pad_maximum_fusion.2), channel_id=1, source_target_pairs={{0,4},{1,5},{2,6},{3,7},{4,0},{5,1},{6,2},{7,3},{8,12},{9,13},{10,... | collective-permute-start | bytes 98312 | tf_op jit(solution)/shard_map/ppermute | solution.py:446
  15.4 8.6 %collective-permute-start.3 = (f32[64,1024]{1,0:T(8,128)S(1)}, f32[64,1024]{1,0:T(8,128)S(1)}, u32[]{:S(2)}, u32[]{:S(2)}) collective-permute-start(f32[64,1024]{1,0:T(8,128)S(1)} %get-tuple-element.78), channel_id=1, source_target_pairs={{0,1},{1,0},{2,3},{3,2},{4,5},{5,4},{6,7},{7,6},{8,9},{9,8},{10,11... | collective-permute-start | bytes 786440 | tf_op jit(solution)/shard_map/ppermute | solution.py:442
  16.7 32.8 %copy-start.2 = (s32[64,256]{1,0:T(8,128)S(1)}, s32[64,256]{1,0:T(8,128)}, u32[]{:S(2)}) copy-start(s32[64,256]{1,0:T(8,128)} %ranks_ref.1) | copy-start | bytes 196612
  24.1 6.8 %collective-permute-start.5 = (f32[64,256]{1,0:T(8,128)S(1)}, f32[64,256]{1,0:T(8,128)S(1)}, u32[]{:S(2)}, u32[]{:S(2)}) collective-permute-start(f32[64,256]{1,0:T(8,128)S(1)} %hist.1), channel_id=1, source_target_pairs={{0,56},{8,0},{16,8},{24,16},{32,24},{40,32},{48,40},{56,48},{64,12... | collective-permute-start | bytes 196616 | tf_op jit(solution)/shard_map/ppermute | solution.py:450
  29.6 4.3 %collective-permute-start.4 = (f32[64,256]{1,0:T(8,128)S(1)}, f32[64,256]{1,0:T(8,128)S(1)}, u32[]{:S(2)}, u32[]{:S(2)}) collective-permute-start(f32[64,256]{1,0:T(8,128)S(1)} %hist.1), channel_id=1, source_target_pairs={{0,8},{8,16},{16,24},{24,32},{32,40},{40,48},{48,56},{56,0},{64,72... | collective-permute-start | bytes 196616 | tf_op jit(solution)/shard_map/ppermute | solution.py:450
  33.9 7.4 %collective-permute-start.7 = (f32[64,256]{1,0:T(8,128)S(1)}, f32[64,256]{1,0:T(8,128)S(1)}, u32[]{:S(2)}, u32[]{:S(2)}) collective-permute-start(f32[64,256]{1,0:T(8,128)S(1)} %get-tuple-element.108), channel_id=1, source_target_pairs={{0,16},{8,24},{16,32},{24,40},{32,48},{40,56},{48,0},{56,8},{64,80... | collective-permute-start | bytes 196616 | tf_op jit(solution)/shard_map/ppermute | solution.py:450
  34.2 7.2 %collective-permute-start.6 = (f32[64,256]{1,0:T(8,128)S(1)}, f32[64,256]{1,0:T(8,128)S(1)}, u32[]{:S(2)}, u32[]{:S(2)}) collective-permute-start(f32[64,256]{1,0:T(8,128)S(1)} %get-tuple-element.107), channel_id=1, source_target_pairs={{0,40},{8,48},{16,56},{24,0},{32,8},{40,16},{48,24},{56,32},{64,10... | collective-permute-start | bytes 196616 | tf_op jit(solution)/shard_map/ppermute | solution.py:450
  36.8 14.1 %collective-permute-start.11 = (f32[64,1024]{1,0:T(8,128)S(1)}, f32[64,1024]{1,0:T(8,128)S(1)}, u32[]{:S(2)}, u32[]{:S(2)}) collective-permute-start(f32[64,1024]{1,0:T(8,128)S(1)} %get-tuple-element.80), channel_id=1, source_target_pairs={{0,4},{1,5},{2,6},{3,7},{4,0},{5,1},{6,2},{7,3},{8,12},{9,13},{10,... | collective-permute-start | bytes 786440 | tf_op jit(solution)/shard_map/ppermute | solution.py:442
  38.2 13.8 %collective-permute-start.12 = (f32[64,1024]{1,0:T(8,128)S(1)}, f32[64,1024]{1,0:T(8,128)S(1)}, u32[]{:S(2)}, u32[]{:S(2)}) collective-permute-start(f32[64,1024]{1,0:T(8,128)S(1)} %get-tuple-element.81), channel_id=1, source_target_pairs={{0,5},{1,4},{2,7},{3,6},{4,1},{5,0},{6,3},{7,2},{8,13},{9,12},{10,... | collective-permute-start | bytes 786440 | tf_op jit(solution)/shard_map/ppermute | solution.py:442
  41.4 3.9 %collective-permute-start.10 = (f32[64,256]{1,0:T(8,128)S(1)}, f32[64,256]{1,0:T(8,128)S(1)}, u32[]{:S(2)}, u32[]{:S(2)}) collective-permute-start(f32[64,256]{1,0:T(8,128)S(1)} %add_add_fusion.refs_0_), channel_id=1, source_target_pairs={{0,192},{8,200},{16,208},{24,216},{32,224},{40,232},{48,240},{56,2... | collective-permute-start | bytes 196616 | tf_op jit(solution)/shard_map/ppermute | solution.py:454
  43.9 4.9 %collective-permute-start.9 = (f32[64,256]{1,0:T(8,128)S(1)}, f32[64,256]{1,0:T(8,128)S(1)}, u32[]{:S(2)}, u32[]{:S(2)}) collective-permute-start(f32[64,256]{1,0:T(8,128)S(1)} %add_add_fusion.refs_0_), channel_id=1, source_target_pairs={{0,128},{8,136},{16,144},{24,152},{32,160},{40,168},{48,176},{56,1... | collective-permute-start | bytes 196616 | tf_op jit(solution)/shard_map/ppermute | solution.py:454
  44.5 5.1 %collective-permute-start.8 = (f32[64,256]{1,0:T(8,128)S(1)}, f32[64,256]{1,0:T(8,128)S(1)}, u32[]{:S(2)}, u32[]{:S(2)}) collective-permute-start(f32[64,256]{1,0:T(8,128)S(1)} %add_add_fusion.refs_0_), channel_id=1, source_target_pairs={{0,64},{8,72},{16,80},{24,88},{32,96},{40,104},{48,112},{56,120},{... | collective-permute-start | bytes 196616 | tf_op jit(solution)/shard_map/ppermute | solution.py:454
  54.8 10.5 %collective-permute-start.14 = (f32[64,1024]{1,0:T(8,128)S(1)}, f32[64,1024]{1,0:T(8,128)S(1)}, u32[]{:S(2)}, u32[]{:S(2)}) collective-permute-start(f32[64,1024]{1,0:T(8,128)S(1)} %place.6), channel_id=1, source_target_pairs={{0,2},{1,3},{2,4},{3,5},{4,6},{5,7},{6,0},{7,1},{8,10},{9,11},{10,... | collective-permute-start | bytes 786440 | tf_op jit(solution)/shard_map/ppermute | solution.py:442
  55.3 8.3 %collective-permute-start.13 = (f32[64,256]{1,0:T(8,128)S(1)}, f32[64,256]{1,0:T(8,128)S(1)}, u32[]{:S(2)}, u32[]{:S(2)}) collective-permute-start(f32[64,256]{1,0:T(8,128)S(1)} %cuts.1.refs_0_), channel_id=1, source_target_pairs={{0,4},{1,5},{2,6},{3,7},{4,0},{5,1},{6,2},{7,3},{8,12},{9,13},{10,... | collective-permute-start | bytes 196616 | tf_op jit(solution)/shard_map/ppermute | solution.py:442
  58.6 13.6 %collective-permute-start.15 = (f32[64,1024]{1,0:T(8,128)S(1)}, f32[64,1024]{1,0:T(8,128)S(1)}, u32[]{:S(2)}, u32[]{:S(2)}) collective-permute-start(f32[64,1024]{1,0:T(8,128)S(1)} %place.7), channel_id=1, source_target_pairs={{0,6},{1,7},{2,0},{3,1},{4,2},{5,3},{6,4},{7,5},{8,14},{9,15},{10,... | collective-permute-start | bytes 786440 | tf_op jit(solution)/shard_map/ppermute | solution.py:442
  65.0 12.3 %collective-permute-start.16 = (f32[64,1024]{1,0:T(8,128)S(1)}, f32[64,1024]{1,0:T(8,128)S(1)}, u32[]{:S(2)}, u32[]{:S(2)}) collective-permute-start(f32[64,1024]{1,0:T(8,128)S(1)} %place.8), channel_id=1, source_target_pairs={{0,3},{1,2},{2,5},{3,4},{4,7},{5,6},{6,1},{7,0},{8,11},{9,10},{10,... | collective-permute-start | bytes 786440 | tf_op jit(solution)/shard_map/ppermute | solution.py:442
  66.8 10.5 %collective-permute-start.17 = (f32[64,1024]{1,0:T(8,128)S(1)}, f32[64,1024]{1,0:T(8,128)S(1)}, u32[]{:S(2)}, u32[]{:S(2)}) collective-permute-start(f32[64,1024]{1,0:T(8,128)S(1)} %place.9), channel_id=1, source_target_pairs={{0,7},{1,6},{2,1},{3,0},{4,3},{5,2},{6,5},{7,4},{8,15},{9,14},{10,... | collective-permute-start | bytes 786440 | tf_op jit(solution)/shard_map/ppermute | solution.py:442
  69.7 3.5 %collective-permute-start.18 = (f32[128,256]{1,0:T(8,128)S(1)}, f32[128,256]{1,0:T(8,128)S(1)}, u32[]{:S(2)}, u32[]{:S(2)}) collective-permute-start(f32[128,256]{1,0:T(8,128)S(1)} %pad_maximum_fusion), channel_id=1, source_target_pairs={{0,1},{1,0},{2,3},{3,2},{4,5},{5,4},{6,7},{7,6},{8,9},{9,8},{10,11... | collective-permute-start | bytes 393224 | tf_op jit(solution)/shard_map/ppermute | solution.py:442

commit v9 on v8

--- a/solution.py
+++ b/solution.py
@@ -388,23 +388,22 @@
     )(cuts, values)
 
 
-def far_kernel(far_ref, core_ref, *refs):
-    feats = far_ref.shape[0]
-    cuts_refs = [far_ref, core_ref.at[:feats, :], core_ref.at[feats:, :]]
-    for cuts_ref, values_ref, out_ref in zip(cuts_refs, refs[:3], refs[3:]):
+def far_kernel(*refs):
+    count = len(refs) // 3
+    for cuts_ref, values_ref, out_ref in zip(refs[:count], refs[count : 2 * count], refs[2 * count :]):
         place_blocks([0], cuts_ref, values_ref, [out_ref])
 
 
-def place_far(far_cuts, core_cuts, values):
+def place_far(cuts, values):
     return pl.pallas_call(
         far_kernel,
-        in_specs=in_vmem(2 + len(values)),
-        out_specs=in_vmem(len(values)),
+        in_specs=in_vmem(2 * len(cuts)),
+        out_specs=in_vmem(len(cuts)),
         out_shape=[jax.ShapeDtypeStruct(block.shape, jnp.float32) for block in values],
         compiler_params=pltpu.CompilerParams(vmem_limit_bytes=16 << 20),
         cost_estimate=pl.CostEstimate(flops=10**5, bytes_accessed=10**4, transcendentals=0),
         name="far",
-    )(far_cuts, core_cuts, *values)
+    )(*cuts, *values)
 
 
 def join_kernel(moves, *refs):
@@ -490,7 +489,9 @@
             cuts, far_values, parts[2] = lax.optimization_barrier((cuts, far_values, parts[2]))
         moves.append(stage)
         parts.append(send_feat(out, stage) if stage != (0, 0) else out)
-    return join(moves + far_moves, parts + list(place_far(far_cuts, core_cuts, far_values)))
+    feats = cuts.shape[0]
+    cuts_there = [far_cuts, core_cuts[:feats], core_cuts[feats:]]
+    return join(moves + far_moves, parts + list(place_far(cuts_there, far_values)))
 
 
 def solution(mesh):

time: 79.7 us -> 77.1 us (0.967)
  waiting for transfers between devices: 15.4 us -> 12.2 us
    ppermute x9, waiting for transfers between devices: 5.85 us -> 2.68 us  [send_feat(): lax.ppermute(array, 'feat', [(i, (i // 2 + move[0]) % 4 * 2 + (i % 2 ^ mo...]
  transfers between devices with their start and end apart: 19 -> 19, of which waited for: 9 -> 9; matrix products, arithmetic and copies ran while one was open for 0% -> 0% of each run, Pallas kernels for 32% -> 38%
where the time goes in v9:
time: 77.1 us; the launch traced here: 75.6 us
  starting transfers between devices  32.2 us (42%)
  Pallas kernels  30.8 us (40%)
  waiting for transfers between devices  12.2 us (16%)
    ppermute x9, starting transfers between devices, send_feat(): lax.ppermute(array, 'feat', [(i, (i // 2 + move[0]) % 4 * 2 + (i % 2 ^ mo...  15.1 us
    ppermute x4, starting transfers between devices, shift_rows(): lax.ppermute(array, 'rows', [(i, i // 8 * 8 + (i + shift) % 8) for i in r...  8.43 us
    pallas_call x1, Pallas kernels, find_mass(): pl.pallas_call(hist_kernel, in_specs=in_vmem(1 + len(slots)), out_specs=i...  7.32 us
    pallas_call x5, Pallas kernels, place(): pl.pallas_call(lambda *refs: place_kernel(moves, *refs), in_specs=in_vmem...  7.04 us
    pallas_call x2, Pallas kernels, find_near_slots(): pl.pallas_call(lambda *refs: near_slot_kernel(groups, *refs), in_specs=in...  5.56 us
    ppermute x3, starting transfers between devices, flip_feat(): return lax.ppermute(array, 'feat', [(i, i ^ flip) for i in range(8)])  4.98 us
    ppermute x3, waiting for transfers between devices, turn_rows(): lax.ppermute(array, 'rows', [(i, (i + 8 * turn) % 32) for i in range(32)])  4.49 us
    ppermute x4, waiting for transfers between devices, shift_rows(): lax.ppermute(array, 'rows', [(i, i // 8 * 8 + (i + shift) % 8) for i in r...  4.33 us
  transfers between devices with their start and end apart: 19, of which 9 were waited for; matrix products, arithmetic and copies ran while one was open for 0% of the time, Pallas kernels for 38%

profile of v9, /device:TPU:1, one launch (start us, length us, event | category | flops | bytes accessed | tf_op | source)
XLA Modules:
  0.0 75.6 jit_solution(18315881020230223248)
XLA Ops:
  0.0 1.0 %factor.1 = f32[2,8,128]{2,1,0:T(8,128)S(1)} custom-call(s32[8,128]{1,0:T(8,128)} %bitcast.1), custom_call_target="tpu_custom_call" | custom-call | tf_op jit(solution)/shard_map/factor/pallas_call | solution.py:183
  1.0 3.3 %collective-permute-start = (f32[2,8,128]{2,1,0:T(8,128)S(1)}, f32[2,8,128]{2,1,0:T(8,128)S(1)}, u32[]{:S(2)}, u32[]{:S(2)}) collective-permute-start(f32[2,8,128]{2,1,0:T(8,128)S(1)} %factor.1), channel_id=1, source_target_pairs={{0,1},{1,0},{2,3},{3,2},{4,5},{5,4},{6,7},{7,6},{8,9},{9,8},{10,11... | collective-permute-start | bytes 24584 | tf_op jit(solution)/shard_map/ppermute | solution.py:445
  4.4 3.1 %slots.3 = (bf16[16,8192]{1,0:T(8,128)(2,1)S(1)}, bf16[16,8192]{1,0:T(8,128)(2,1)S(1)}, f32[64,1024]{1,0:T(8,128)S(1)}, f32[64,1024]{1,0:T(8,128)S(1)}, f32[64,1024]{1,0:T(8,128)S(1)}) custom-call(s32[64,256]{1,0:T(8,128)} %codes_ref.1, f32[64,8192]{1,0:T(8,128)} %refs_1_.15), custom_call_target="tpu_custom_call" | custom-call | flops 10000000 | bytes 10000000 | tf_op jit(solution)/shard_map/slots/pallas_call | solution.py:143
  7.4 0.0 collective-permute-done
  7.5 0.1 collective-permute-start.1
  7.6 1.9 %slots.4 = (bf16[16,8192]{1,0:T(8,128)(2,1)S(1)}, bf16[16,8192]{1,0:T(8,128)(2,1)S(1)}) custom-call(s32[64,256]{1,0:T(8,128)S(1)} %copy-done.1, f32[64,8192]{1,0:T(8,128)S(1)} %copy-done), custom_call_target="tpu_custom_call" | custom-call | flops 10000000 | bytes 10000000 | tf_op jit(solution)/shard_map/slots/pallas_call | solution.py:128
  9.4 0.7 collective-permute-done.1
  10.1 1.6 %collective-permute-start.2 = (f32[8,8,128]{2,1,0:T(8,128)S(1)}, f32[8,8,128]{2,1,0:T(8,128)S(1)}, u32[]{:S(2)}, u32[]{:S(2)}) collective-permute-start(f32[8,8,128]{2,1,0:T(8,128)S(1)} %pad_maximum_fusion.2), channel_id=1, source_target_pairs={{0,4},{1,5},{2,6},{3,7},{4,0},{5,1},{6,2},{7,3},{8,12},{9,13},{10,... | collective-permute-start | bytes 98312 | tf_op jit(solution)/shard_map/ppermute | solution.py:445
  11.7 3.7 %slots.5 = (bf16[16,8192]{1,0:T(8,128)(2,1)S(1)}, bf16[16,8192]{1,0:T(8,128)(2,1)S(1)}, bf16[16,8192]{1,0:T(8,128)(2,1)S(1)}, bf16[16,8192]{1,0:T(8,128)(2,1)S(1)}) custom-call(s32[64,256]{1,0:T(8,128)S(1)} %copy-done.1, f32[64,8192]{1,0:T(8,128)S(1)} %copy-done), custom_call_target="tpu_custom_call" | custom-call | flops 10000000 | bytes 10000000 | tf_op jit(solution)/shard_map/slots/pallas_call | solution.py:128
  15.4 0.0 collective-permute-done.2
  15.4 1.3 %collective-permute-start.3 = (f32[64,1024]{1,0:T(8,128)S(1)}, f32[64,1024]{1,0:T(8,128)S(1)}, u32[]{:S(2)}, u32[]{:S(2)}) collective-permute-start(f32[64,1024]{1,0:T(8,128)S(1)} %get-tuple-element.78), channel_id=1, source_target_pairs={{0,1},{1,0},{2,3},{3,2},{4,5},{5,4},{6,7},{7,6},{8,9},{9,8},{10,11... | collective-permute-start | bytes 786440 | tf_op jit(solution)/shard_map/ppermute | solution.py:441
  16.7 7.3 %hist.1 = f32[64,256]{1,0:T(8,128)S(1)} custom-call(f32[16,8,128]{2,1,0:T(8,128)S(1)} %pad_maximum_fusion.1.hess_ref, bf16[16,8192]{1,0:T(8,128)(2,1)S(1)} %get-tuple-element.69.refs_0_, bf16[16,8192]{1,0:T(8,128)(2,1)S(1)} %get-tuple-element.70.refs_1_, bf16[16,8192]{1,0:T(8,128)(2,1)S(1)} %get-tuple-element.71.refs_2_, ...), custom_call_target="tpu_custom_call" | custom-call | flops 4000000000 | bytes 10000000 | tf_op jit(solution)/shard_map/hist/pallas_call | solution.py:258
  24.1 0.0 collective-permute-done.3.refs_5_
  24.1 5.5 %collective-permute-start.5 = (f32[64,256]{1,0:T(8,128)S(1)}, f32[64,256]{1,0:T(8,128)S(1)}, u32[]{:S(2)}, u32[]{:S(2)}) collective-permute-start(f32[64,256]{1,0:T(8,128)S(1)} %hist.1), channel_id=1, source_target_pairs={{0,56},{8,0},{16,8},{24,16},{32,24},{40,32},{48,40},{56,48},{64,12... | collective-permute-start | bytes 196616 | tf_op jit(solution)/shard_map/ppermute | solution.py:449
  29.6 0.0 collective-permute-start.4
  29.6 1.3 %collective-permute-done.5 = f32[64,256]{1,0:T(8,128)S(1)} collective-permute-done((f32[64,256]{1,0:T(8,128)S(1)}, f32[64,256]{1,0:T(8,128)S(1)}, u32[]{:S(2)}, u32[]{:S(2)}) %collective-permute-start.5) | collective-permute-done | bytes 65568 | tf_op jit(solution)/shard_map/ppermute | solution.py:449
  30.9 3.0 %collective-permute-done.4 = f32[64,256]{1,0:T(8,128)S(1)} collective-permute-done((f32[64,256]{1,0:T(8,128)S(1)}, f32[64,256]{1,0:T(8,128)S(1)}, u32[]{:S(2)}, u32[]{:S(2)}) %collective-permute-start.4) | collective-permute-done | bytes 65568 | tf_op jit(solution)/shard_map/ppermute | solution.py:449
  33.9 0.3 collective-permute-start.7
  34.2 2.6 %collective-permute-start.6 = (f32[64,256]{1,0:T(8,128)S(1)}, f32[64,256]{1,0:T(8,128)S(1)}, u32[]{:S(2)}, u32[]{:S(2)}) collective-permute-start(f32[64,256]{1,0:T(8,128)S(1)} %get-tuple-element.107), channel_id=1, source_target_pairs={{0,40},{8,48},{16,56},{24,0},{32,8},{40,16},{48,24},{56,32},{64,10... | collective-permute-start | bytes 196616 | tf_op jit(solution)/shard_map/ppermute | solution.py:449
  36.8 1.3 %collective-permute-start.11 = (f32[64,1024]{1,0:T(8,128)S(1)}, f32[64,1024]{1,0:T(8,128)S(1)}, u32[]{:S(2)}, u32[]{:S(2)}) collective-permute-start(f32[64,1024]{1,0:T(8,128)S(1)} %get-tuple-element.80), channel_id=1, source_target_pairs={{0,4},{1,5},{2,6},{3,7},{4,0},{5,1},{6,2},{7,3},{8,12},{9,13},{10,... | collective-permute-start | bytes 786440 | tf_op jit(solution)/shard_map/ppermute | solution.py:441
  38.2 3.2 %collective-permute-start.12 = (f32[64,1024]{1,0:T(8,128)S(1)}, f32[64,1024]{1,0:T(8,128)S(1)}, u32[]{:S(2)}, u32[]{:S(2)}) collective-permute-start(f32[64,1024]{1,0:T(8,128)S(1)} %get-tuple-element.81), channel_id=1, source_target_pairs={{0,5},{1,4},{2,7},{3,6},{4,1},{5,0},{6,3},{7,2},{8,13},{9,12},{10,... | collective-permute-start | bytes 786440 | tf_op jit(solution)/shard_map/ppermute | solution.py:441
  41.4 0.0 collective-permute-done.7
  41.4 0.0 collective-permute-done.6
  41.4 2.5 %collective-permute-start.10 = (f32[64,256]{1,0:T(8,128)S(1)}, f32[64,256]{1,0:T(8,128)S(1)}, u32[]{:S(2)}, u32[]{:S(2)}) collective-permute-start(f32[64,256]{1,0:T(8,128)S(1)} %add_add_fusion.refs_0_), channel_id=1, source_target_pairs={{0,192},{8,200},{16,208},{24,216},{32,224},{40,232},{48,240},{56,2... | collective-permute-start | bytes 196616 | tf_op jit(solution)/shard_map/ppermute | solution.py:453
  43.9 0.5 collective-permute-start.9
  44.5 0.6 collective-permute-start.8
  45.1 0.2 collective-permute-done.10.refs_3_
  45.3 3.6 %collective-permute-done.9.refs_2_ = f32[64,256]{1,0:T(8,128)S(1)} collective-permute-done((f32[64,256]{1,0:T(8,128)S(1)}, f32[64,256]{1,0:T(8,128)S(1)}, u32[]{:S(2)}, u32[]{:S(2)}) %collective-permute-start.9) | collective-permute-done | bytes 65568 | tf_op jit(solution)/shard_map/ppermute | solution.py:453
  48.8 0.7 collective-permute-done.8.refs_1_
  49.5 1.4 %cuts.1.refs_0_ = f32[64,256]{1,0:T(8,128)S(1)} custom-call(s32[64,256]{1,0:T(8,128)S(1)} %copy-done.1, s32[64,256]{1,0:T(8,128)S(1)} %copy-done.2, f32[64,256]{1,0:T(8,128)S(1)} %add_add_fusion.refs_0_, f32[64,256]{1,0:T(8,128)S(1)} %collective-permute-done.8.refs_1_, f32[64,256]{1,0:T(8,128)S(1)} %collective-permute-done.9.refs_2_, ...), custom_call_target="tpu_custom_call" | custom-call | tf_op jit(solution)/shard_map/cuts/pallas_call | solution.py:312
  50.9 0.0 collective-permute-done.11.refs_3_
  50.9 1.1 %collective-permute-done.12.refs_4_ = f32[64,1024]{1,0:T(8,128)S(1)} collective-permute-done((f32[64,1024]{1,0:T(8,128)S(1)}, f32[64,1024]{1,0:T(8,128)S(1)}, u32[]{:S(2)}, u32[]{:S(2)}) %collective-permute-start.12) | collective-permute-done | bytes 262176 | tf_op jit(solution)/shard_map/ppermute | solution.py:441
  52.0 1.3 %collective-permute-start.13 = (f32[64,256]{1,0:T(8,128)S(1)}, f32[64,256]{1,0:T(8,128)S(1)}, u32[]{:S(2)}, u32[]{:S(2)}) collective-permute-start(f32[64,256]{1,0:T(8,128)S(1)} %cuts.1.refs_0_), channel_id=1, source_target_pairs={{0,4},{1,5},{2,6},{3,7},{4,0},{5,1},{6,2},{7,3},{8,12},{9,13},{10,... | collective-permute-start | bytes 196616 | tf_op jit(solution)/shard_map/ppermute | solution.py:441
  53.3 1.4 %place.5.refs_0_ = f32[64,1024]{1,0:T(8,128)S(1)} custom-call(f32[64,256]{1,0:T(8,128)S(1)} %cuts.1.refs_0_, f32[64,8192]{1,0:T(8,128)S(1)} %copy-done), custom_call_target="tpu_custom_call" | custom-call | flops 100000 | bytes 10000 | tf_op jit(solution)/shard_map/place/pallas_call | solution.py:380
  54.7 1.4 %place.6 = f32[64,1024]{1,0:T(8,128)S(1)} custom-call(f32[64,256]{1,0:T(8,128)S(1)} %cuts.1.refs_0_, f32[64,8192]{1,0:T(8,128)S(1)} %copy-done), custom_call_target="tpu_custom_call" | custom-call | flops 100000 | bytes 10000 | tf_op jit(solution)/shard_map/place/pallas_call | solution.py:380
  56.1 0.5 collective-permute-start.14
  56.6 1.4 %place.7 = f32[64,1024]{1,0:T(8,128)S(1)} custom-call(f32[64,256]{1,0:T(8,128)S(1)} %cuts.1.refs_0_, f32[64,8192]{1,0:T(8,128)S(1)} %copy-done), custom_call_target="tpu_custom_call" | custom-call | flops 100000 | bytes 10000 | tf_op jit(solution)/shard_map/place/pallas_call | solution.py:380
  58.1 1.8 %collective-permute-start.18 = (f32[128,256]{1,0:T(8,128)S(1)}, f32[128,256]{1,0:T(8,128)S(1)}, u32[]{:S(2)}, u32[]{:S(2)}) collective-permute-start(f32[128,256]{1,0:T(8,128)S(1)} %pad_maximum_fusion), channel_id=1, source_target_pairs={{0,1},{1,0},{2,3},{3,2},{4,5},{5,4},{6,7},{7,6},{8,9},{9,8},{10,11... | collective-permute-start | bytes 393224 | tf_op jit(solution)/shard_map/ppermute | solution.py:441
  59.9 2.3 %collective-permute-start.15 = (f32[64,1024]{1,0:T(8,128)S(1)}, f32[64,1024]{1,0:T(8,128)S(1)}, u32[]{:S(2)}, u32[]{:S(2)}) collective-permute-start(f32[64,1024]{1,0:T(8,128)S(1)} %place.7), channel_id=1, source_target_pairs={{0,6},{1,7},{2,0},{3,1},{4,2},{5,3},{6,4},{7,5},{8,14},{9,15},{10,... | collective-permute-start | bytes 786440 | tf_op jit(solution)/shard_map/ppermute | solution.py:441
  62.2 1.4 %place.8 = f32[64,1024]{1,0:T(8,128)S(1)} custom-call(f32[64,256]{1,0:T(8,128)S(1)} %cuts.1.refs_0_, f32[64,8192]{1,0:T(8,128)S(1)} %copy-done), custom_call_target="tpu_custom_call" | custom-call | flops 100000 | bytes 10000 | tf_op jit(solution)/shard_map/place/pallas_call | solution.py:380
  63.6 0.3 collective-permute-start.16
  63.9 1.4 %place.9 = f32[64,1024]{1,0:T(8,128)S(1)} custom-call(f32[64,256]{1,0:T(8,128)S(1)} %cuts.1.refs_0_, f32[64,8192]{1,0:T(8,128)S(1)} %copy-done), custom_call_target="tpu_custom_call" | custom-call | flops 100000 | bytes 10000 | tf_op jit(solution)/shard_map/place/pallas_call | solution.py:380
  65.3 3.0 %collective-permute-start.17 = (f32[64,1024]{1,0:T(8,128)S(1)}, f32[64,1024]{1,0:T(8,128)S(1)}, u32[]{:S(2)}, u32[]{:S(2)}) collective-permute-start(f32[64,1024]{1,0:T(8,128)S(1)} %place.9), channel_id=1, source_target_pairs={{0,7},{1,6},{2,1},{3,0},{4,3},{5,2},{6,5},{7,4},{8,15},{9,14},{10,... | collective-permute-start | bytes 786440 | tf_op jit(solution)/shard_map/ppermute | solution.py:441
  68.4 0.0 collective-permute-done.15.refs_2_
  68.4 4.1 %far.1 = (f32[64,1024]{1,0:T(8,128)S(1)}, f32[64,1024]{1,0:T(8,128)S(1)}, f32[64,1024]{1,0:T(8,128)S(1)}) custom-call(f32[64,256]{1,0:T(8,128)S(1)} %collective-permute-done.13.refs_0_, f32[64,256]{1,0:T(8,128)S(1)} %get-tuple-element.110.refs_1_, f32[64,256]{1,0:T(8,128)S(1)} %get-tuple-element.109.refs_2_, f32[64,1024]{1,0:T(8,128)S(1)} %collective-permute-done.11.refs_3_, ...), custom_call_target="tpu_custom_call" | custom-call | flops 100000 | bytes 10000 | tf_op jit(solution)/shard_map/far/pallas_call | solution.py:398
  72.5 0.9 %collective-permute-done.16.refs_3_ = f32[64,1024]{1,0:T(8,128)S(1)} collective-permute-done((f32[64,1024]{1,0:T(8,128)S(1)}, f32[64,1024]{1,0:T(8,128)S(1)}, u32[]{:S(2)}, u32[]{:S(2)}) %collective-permute-start.16) | collective-permute-done | bytes 262176 | tf_op jit(solution)/shard_map/ppermute | solution.py:441
  73.4 0.7 collective-permute-done.17.refs_4_
  74.0 1.4 %join.1 = f32[512,1024]{1,0:T(8,128)} custom-call(f32[64,1024]{1,0:T(8,128)S(1)} %place.5.refs_0_, f32[64,1024]{1,0:T(8,128)S(1)} %collective-permute-done.14.refs_1_, f32[64,1024]{1,0:T(8,128)S(1)} %collective-permute-done.15.refs_2_, f32[64,1024]{1,0:T(8,128)S(1)} %collective-permute-done.16.refs_3_, f32[64,1024]{1,0:T(8,128)S(1)} %collective-permute-done.17.refs_4_, ...), custom_call_target="tpu_custom_call" | custom-call | tf_op jit(solution)/shard_map/join/pallas_call | solution.py:424
  (16 shorter events, 0.1 us)
Async XLA Ops:
  0.0 7.6 %copy-start = (f32[64,8192]{1,0:T(8,128)S(1)}, f32[64,8192]{1,0:T(8,128)}, u32[]{:S(2)}) copy-start(f32[64,8192]{1,0:T(8,128)} %refs_1_.15) | copy-start | bytes 6291460
  0.0 7.6 %copy-start.1 = (s32[64,256]{1,0:T(8,128)S(1)}, s32[64,256]{1,0:T(8,128)}, u32[]{:S(2)}) copy-start(s32[64,256]{1,0:T(8,128)} %codes_ref.1) | copy-start | bytes 196612
  1.0 6.4 %collective-permute-start = (f32[2,8,128]{2,1,0:T(8,128)S(1)}, f32[2,8,128]{2,1,0:T(8,128)S(1)}, u32[]{:S(2)}, u32[]{:S(2)}) collective-permute-start(f32[2,8,128]{2,1,0:T(8,128)S(1)} %factor.1), channel_id=1, source_target_pairs={{0,1},{1,0},{2,3},{3,2},{4,5},{5,4},{6,7},{7,6},{8,9},{9,8},{10,11... | collective-permute-start | bytes 24584 | tf_op jit(solution)/shard_map/ppermute | solution.py:445
  7.5 2.7 %collective-permute-start.1 = (f32[4,8,128]{2,1,0:T(8,128)S(1)}, f32[4,8,128]{2,1,0:T(8,128)S(1)}, u32[]{:S(2)}, u32[]{:S(2)}) collective-permute-start(f32[4,8,128]{2,1,0:T(8,128)S(1)} %pad_maximum_fusion.3), channel_id=1, source_target_pairs={{0,2},{1,3},{2,0},{3,1},{4,6},{5,7},{6,4},{7,5},{8,10},{9,11},{10,... | collective-permute-start | bytes 49160 | tf_op jit(solution)/shard_map/ppermute | solution.py:445
  10.1 5.3 %collective-permute-start.2 = (f32[8,8,128]{2,1,0:T(8,128)S(1)}, f32[8,8,128]{2,1,0:T(8,128)S(1)}, u32[]{:S(2)}, u32[]{:S(2)}) collective-permute-start(f32[8,8,128]{2,1,0:T(8,128)S(1)} %pad_maximum_fusion.2), channel_id=1, source_target_pairs={{0,4},{1,5},{2,6},{3,7},{4,0},{5,1},{6,2},{7,3},{8,12},{9,13},{10,... | collective-permute-start | bytes 98312 | tf_op jit(solution)/shard_map/ppermute | solution.py:445
  15.4 8.6 %collective-permute-start.3 = (f32[64,1024]{1,0:T(8,128)S(1)}, f32[64,1024]{1,0:T(8,128)S(1)}, u32[]{:S(2)}, u32[]{:S(2)}) collective-permute-start(f32[64,1024]{1,0:T(8,128)S(1)} %get-tuple-element.78), channel_id=1, source_target_pairs={{0,1},{1,0},{2,3},{3,2},{4,5},{5,4},{6,7},{7,6},{8,9},{9,8},{10,11... | collective-permute-start | bytes 786440 | tf_op jit(solution)/shard_map/ppermute | solution.py:441
  16.7 32.8 %copy-start.2 = (s32[64,256]{1,0:T(8,128)S(1)}, s32[64,256]{1,0:T(8,128)}, u32[]{:S(2)}) copy-start(s32[64,256]{1,0:T(8,128)} %ranks_ref.1) | copy-start | bytes 196612
  24.1 6.8 %collective-permute-start.5 = (f32[64,256]{1,0:T(8,128)S(1)}, f32[64,256]{1,0:T(8,128)S(1)}, u32[]{:S(2)}, u32[]{:S(2)}) collective-permute-start(f32[64,256]{1,0:T(8,128)S(1)} %hist.1), channel_id=1, source_target_pairs={{0,56},{8,0},{16,8},{24,16},{32,24},{40,32},{48,40},{56,48},{64,12... | collective-permute-start | bytes 196616 | tf_op jit(solution)/shard_map/ppermute | solution.py:449
  29.6 4.3 %collective-permute-start.4 = (f32[64,256]{1,0:T(8,128)S(1)}, f32[64,256]{1,0:T(8,128)S(1)}, u32[]{:S(2)}, u32[]{:S(2)}) collective-permute-start(f32[64,256]{1,0:T(8,128)S(1)} %hist.1), channel_id=1, source_target_pairs={{0,8},{8,16},{16,24},{24,32},{32,40},{40,48},{48,56},{56,0},{64,72... | collective-permute-start | bytes 196616 | tf_op jit(solution)/shard_map/ppermute | solution.py:449
  33.9 7.4 %collective-permute-start.7 = (f32[64,256]{1,0:T(8,128)S(1)}, f32[64,256]{1,0:T(8,128)S(1)}, u32[]{:S(2)}, u32[]{:S(2)}) collective-permute-start(f32[64,256]{1,0:T(8,128)S(1)} %get-tuple-element.108), channel_id=1, source_target_pairs={{0,16},{8,24},{16,32},{24,40},{32,48},{40,56},{48,0},{56,8},{64,80... | collective-permute-start | bytes 196616 | tf_op jit(solution)/shard_map/ppermute | solution.py:449
  34.2 7.2 %collective-permute-start.6 = (f32[64,256]{1,0:T(8,128)S(1)}, f32[64,256]{1,0:T(8,128)S(1)}, u32[]{:S(2)}, u32[]{:S(2)}) collective-permute-start(f32[64,256]{1,0:T(8,128)S(1)} %get-tuple-element.107), channel_id=1, source_target_pairs={{0,40},{8,48},{16,56},{24,0},{32,8},{40,16},{48,24},{56,32},{64,10... | collective-permute-start | bytes 196616 | tf_op jit(solution)/shard_map/ppermute | solution.py:449
  36.8 14.1 %collective-permute-start.11 = (f32[64,1024]{1,0:T(8,128)S(1)}, f32[64,1024]{1,0:T(8,128)S(1)}, u32[]{:S(2)}, u32[]{:S(2)}) collective-permute-start(f32[64,1024]{1,0:T(8,128)S(1)} %get-tuple-element.80), channel_id=1, source_target_pairs={{0,4},{1,5},{2,6},{3,7},{4,0},{5,1},{6,2},{7,3},{8,12},{9,13},{10,... | collective-permute-start | bytes 786440 | tf_op jit(solution)/shard_map/ppermute | solution.py:441
  38.2 13.8 %collective-permute-start.12 = (f32[64,1024]{1,0:T(8,128)S(1)}, f32[64,1024]{1,0:T(8,128)S(1)}, u32[]{:S(2)}, u32[]{:S(2)}) collective-permute-start(f32[64,1024]{1,0:T(8,128)S(1)} %get-tuple-element.81), channel_id=1, source_target_pairs={{0,5},{1,4},{2,7},{3,6},{4,1},{5,0},{6,3},{7,2},{8,13},{9,12},{10,... | collective-permute-start | bytes 786440 | tf_op jit(solution)/shard_map/ppermute | solution.py:441
  41.4 3.9 %collective-permute-start.10 = (f32[64,256]{1,0:T(8,128)S(1)}, f32[64,256]{1,0:T(8,128)S(1)}, u32[]{:S(2)}, u32[]{:S(2)}) collective-permute-start(f32[64,256]{1,0:T(8,128)S(1)} %add_add_fusion.refs_0_), channel_id=1, source_target_pairs={{0,192},{8,200},{16,208},{24,216},{32,224},{40,232},{48,240},{56,2... | collective-permute-start | bytes 196616 | tf_op jit(solution)/shard_map/ppermute | solution.py:453
  43.9 4.9 %collective-permute-start.9 = (f32[64,256]{1,0:T(8,128)S(1)}, f32[64,256]{1,0:T(8,128)S(1)}, u32[]{:S(2)}, u32[]{:S(2)}) collective-permute-start(f32[64,256]{1,0:T(8,128)S(1)} %add_add_fusion.refs_0_), channel_id=1, source_target_pairs={{0,128},{8,136},{16,144},{24,152},{32,160},{40,168},{48,176},{56,1... | collective-permute-start | bytes 196616 | tf_op jit(solution)/shard_map/ppermute | solution.py:453
  44.5 5.1 %collective-permute-start.8 = (f32[64,256]{1,0:T(8,128)S(1)}, f32[64,256]{1,0:T(8,128)S(1)}, u32[]{:S(2)}, u32[]{:S(2)}) collective-permute-start(f32[64,256]{1,0:T(8,128)S(1)} %add_add_fusion.refs_0_), channel_id=1, source_target_pairs={{0,64},{8,72},{16,80},{24,88},{32,96},{40,104},{48,112},{56,120},{... | collective-permute-start | bytes 196616 | tf_op jit(solution)/shard_map/ppermute | solution.py:453
  52.0 6.0 %collective-permute-start.13 = (f32[64,256]{1,0:T(8,128)S(1)}, f32[64,256]{1,0:T(8,128)S(1)}, u32[]{:S(2)}, u32[]{:S(2)}) collective-permute-start(f32[64,256]{1,0:T(8,128)S(1)} %cuts.1.refs_0_), channel_id=1, source_target_pairs={{0,4},{1,5},{2,6},{3,7},{4,0},{5,1},{6,2},{7,3},{8,12},{9,13},{10,... | collective-permute-start | bytes 196616 | tf_op jit(solution)/shard_map/ppermute | solution.py:441
  56.1 7.8 %collective-permute-start.14 = (f32[64,1024]{1,0:T(8,128)S(1)}, f32[64,1024]{1,0:T(8,128)S(1)}, u32[]{:S(2)}, u32[]{:S(2)}) collective-permute-start(f32[64,1024]{1,0:T(8,128)S(1)} %place.6), channel_id=1, source_target_pairs={{0,2},{1,3},{2,4},{3,5},{4,6},{5,7},{6,0},{7,1},{8,10},{9,11},{10,... | collective-permute-start | bytes 786440 | tf_op jit(solution)/shard_map/ppermute | solution.py:441
  58.1 10.3 %collective-permute-start.18 = (f32[128,256]{1,0:T(8,128)S(1)}, f32[128,256]{1,0:T(8,128)S(1)}, u32[]{:S(2)}, u32[]{:S(2)}) collective-permute-start(f32[128,256]{1,0:T(8,128)S(1)} %pad_maximum_fusion), channel_id=1, source_target_pairs={{0,1},{1,0},{2,3},{3,2},{4,5},{5,4},{6,7},{7,6},{8,9},{9,8},{10,11... | collective-permute-start | bytes 393224 | tf_op jit(solution)/shard_map/ppermute | solution.py:441
  59.9 8.5 %collective-permute-start.15 = (f32[64,1024]{1,0:T(8,128)S(1)}, f32[64,1024]{1,0:T(8,128)S(1)}, u32[]{:S(2)}, u32[]{:S(2)}) collective-permute-start(f32[64,1024]{1,0:T(8,128)S(1)} %place.7), channel_id=1, source_target_pairs={{0,6},{1,7},{2,0},{3,1},{4,2},{5,3},{6,4},{7,5},{8,14},{9,15},{10,... | collective-permute-start | bytes 786440 | tf_op jit(solution)/shard_map/ppermute | solution.py:441
  63.6 9.8 %collective-permute-start.16 = (f32[64,1024]{1,0:T(8,128)S(1)}, f32[64,1024]{1,0:T(8,128)S(1)}, u32[]{:S(2)}, u32[]{:S(2)}) collective-permute-start(f32[64,1024]{1,0:T(8,128)S(1)} %place.8), channel_id=1, source_target_pairs={{0,3},{1,2},{2,5},{3,4},{4,7},{5,6},{6,1},{7,0},{8,11},{9,10},{10,... | collective-permute-start | bytes 786440 | tf_op jit(solution)/shard_map/ppermute | solution.py:441
  65.3 8.7 %collective-permute-start.17 = (f32[64,1024]{1,0:T(8,128)S(1)}, f32[64,1024]{1,0:T(8,128)S(1)}, u32[]{:S(2)}, u32[]{:S(2)}) collective-permute-start(f32[64,1024]{1,0:T(8,128)S(1)} %place.9), channel_id=1, source_target_pairs={{0,7},{1,6},{2,1},{3,0},{4,3},{5,2},{6,5},{7,4},{8,15},{9,14},{10,... | collective-permute-start | bytes 786440 | tf_op jit(solution)/shard_map/ppermute | solution.py:441

commit v10 on v9

--- a/solution.py
+++ b/solution.py
@@ -477,16 +477,18 @@
     cuts = find_cuts(edge_codes, cut_ranks, mass, *[turn_rows(mass, turn) for turn in (1, 2, 3)])
     cuts, far_values = lax.optimization_barrier((cuts, far_values))
     far_cuts, moves, parts = send_feat(cuts, (2, 0)), [], []
-    for index, stage in enumerate(((0, 0), (1, 0), (3, 0), (1, 1), (3, 1))):
+    for index, stage in enumerate(((1, 0), (3, 0), (1, 1), (3, 1), (0, 0))):
         (out,) = place([stage], cuts, feature_values)
         cuts, out = lax.optimization_barrier((cuts, out))
-        if index == 2:
+        if index == 1:
             cuts, far_cuts = lax.optimization_barrier((cuts, far_cuts))
             core_cuts = send_feat(jnp.concatenate([far_cuts, cuts], axis=0), (0, 1))
+        elif index == 2:
+            cuts, far_values = lax.optimization_barrier((cuts, far_values))
         elif index == 3:
-            cuts, parts[1] = lax.optimization_barrier((cuts, parts[1]))
+            cuts, parts[0] = lax.optimization_barrier((cuts, parts[0]))
         elif index == 4:
-            cuts, far_values, parts[2] = lax.optimization_barrier((cuts, far_values, parts[2]))
+            cuts, far_values, parts[1], parts[2] = lax.optimization_barrier((cuts, far_values, parts[1], parts[2]))
         moves.append(stage)
         parts.append(send_feat(out, stage) if stage != (0, 0) else out)
     feats = cuts.shape[0]

time: 77.1 us -> 79.8 us (1.035); the launches traced: 75.6 us -> 79.6 us
  waiting for transfers between devices: 12.2 us -> 15.7 us
    ppermute x9, waiting for transfers between devices: 2.68 us -> 6.14 us  [send_feat(): lax.ppermute(array, 'feat', [(i, (i // 2 + move[0]) % 4 * 2 + (i % 2 ^ mo...]
  transfers between devices with their start and end apart: 19 -> 19, of which waited for: 9 -> 10; matrix products, arithmetic and copies ran while one was open for 0% -> 0% of each run, Pallas kernels for 38% -> 36%
where the time goes in v10:
time: 79.8 us; the launch traced here: 79.6 us
  starting transfers between devices  32.7 us (41%)
  Pallas kernels  30.8 us (39%)
  waiting for transfers between devices  15.7 us (20%)
    ppermute x9, starting transfers between devices, send_feat(): lax.ppermute(array, 'feat', [(i, (i // 2 + move[0]) % 4 * 2 + (i % 2 ^ mo...  15.6 us
    ppermute x4, starting transfers between devices, shift_rows(): lax.ppermute(array, 'rows', [(i, i // 8 * 8 + (i + shift) % 8) for i in r...  8.43 us
    pallas_call x1, Pallas kernels, find_mass(): pl.pallas_call(hist_kernel, in_specs=in_vmem(1 + len(slots)), out_specs=i...  7.32 us
    pallas_call x5, Pallas kernels, place(): pl.pallas_call(lambda *refs: place_kernel(moves, *refs), in_specs=in_vmem...  7.04 us
    ppermute x9, waiting for transfers between devices, send_feat(): lax.ppermute(array, 'feat', [(i, (i // 2 + move[0]) % 4 * 2 + (i % 2 ^ mo...  6.14 us
    pallas_call x2, Pallas kernels, find_near_slots(): pl.pallas_call(lambda *refs: near_slot_kernel(groups, *refs), in_specs=in...  5.56 us
    ppermute x3, starting transfers between devices, flip_feat(): return lax.ppermute(array, 'feat', [(i, i ^ flip) for i in range(8)])  4.98 us
    ppermute x3, waiting for transfers between devices, turn_rows(): lax.ppermute(array, 'rows', [(i, (i + 8 * turn) % 32) for i in range(32)])  4.49 us
  transfers between devices with their start and end apart: 19, of which 10 were waited for; matrix products, arithmetic and copies ran while one was open for 0% of the time, Pallas kernels for 36%

profile of v10, /device:TPU:1, one launch (start us, length us, event | category | flops | bytes accessed | tf_op | source)
XLA Modules:
  0.0 79.6 jit_solution(17598487962605918980)
XLA Ops:
  0.0 1.0 %factor.1 = f32[2,8,128]{2,1,0:T(8,128)S(1)} custom-call(s32[8,128]{1,0:T(8,128)} %bitcast.1), custom_call_target="tpu_custom_call" | custom-call | tf_op jit(solution)/shard_map/factor/pallas_call | solution.py:183
  1.0 3.3 %collective-permute-start = (f32[2,8,128]{2,1,0:T(8,128)S(1)}, f32[2,8,128]{2,1,0:T(8,128)S(1)}, u32[]{:S(2)}, u32[]{:S(2)}) collective-permute-start(f32[2,8,128]{2,1,0:T(8,128)S(1)} %factor.1), channel_id=1, source_target_pairs={{0,1},{1,0},{2,3},{3,2},{4,5},{5,4},{6,7},{7,6},{8,9},{9,8},{10,11... | collective-permute-start | bytes 24584 | tf_op jit(solution)/shard_map/ppermute | solution.py:445
  4.4 3.1 %slots.3 = (bf16[16,8192]{1,0:T(8,128)(2,1)S(1)}, bf16[16,8192]{1,0:T(8,128)(2,1)S(1)}, f32[64,1024]{1,0:T(8,128)S(1)}, f32[64,1024]{1,0:T(8,128)S(1)}, f32[64,1024]{1,0:T(8,128)S(1)}) custom-call(s32[64,256]{1,0:T(8,128)} %codes_ref.1, f32[64,8192]{1,0:T(8,128)} %refs_1_.15), custom_call_target="tpu_custom_call" | custom-call | flops 10000000 | bytes 10000000 | tf_op jit(solution)/shard_map/slots/pallas_call | solution.py:143
  7.4 0.0 collective-permute-done
  7.5 0.1 collective-permute-start.1
  7.6 1.9 %slots.4 = (bf16[16,8192]{1,0:T(8,128)(2,1)S(1)}, bf16[16,8192]{1,0:T(8,128)(2,1)S(1)}) custom-call(s32[64,256]{1,0:T(8,128)S(1)} %copy-done.1, f32[64,8192]{1,0:T(8,128)S(1)} %copy-done), custom_call_target="tpu_custom_call" | custom-call | flops 10000000 | bytes 10000000 | tf_op jit(solution)/shard_map/slots/pallas_call | solution.py:128
  9.4 0.7 collective-permute-done.1
  10.1 1.6 %collective-permute-start.2 = (f32[8,8,128]{2,1,0:T(8,128)S(1)}, f32[8,8,128]{2,1,0:T(8,128)S(1)}, u32[]{:S(2)}, u32[]{:S(2)}) collective-permute-start(f32[8,8,128]{2,1,0:T(8,128)S(1)} %pad_maximum_fusion.2), channel_id=1, source_target_pairs={{0,4},{1,5},{2,6},{3,7},{4,0},{5,1},{6,2},{7,3},{8,12},{9,13},{10,... | collective-permute-start | bytes 98312 | tf_op jit(solution)/shard_map/ppermute | solution.py:445
  11.7 3.7 %slots.5 = (bf16[16,8192]{1,0:T(8,128)(2,1)S(1)}, bf16[16,8192]{1,0:T(8,128)(2,1)S(1)}, bf16[16,8192]{1,0:T(8,128)(2,1)S(1)}, bf16[16,8192]{1,0:T(8,128)(2,1)S(1)}) custom-call(s32[64,256]{1,0:T(8,128)S(1)} %copy-done.1, f32[64,8192]{1,0:T(8,128)S(1)} %copy-done), custom_call_target="tpu_custom_call" | custom-call | flops 10000000 | bytes 10000000 | tf_op jit(solution)/shard_map/slots/pallas_call | solution.py:128
  15.4 1.3 %collective-permute-start.3 = (f32[64,1024]{1,0:T(8,128)S(1)}, f32[64,1024]{1,0:T(8,128)S(1)}, u32[]{:S(2)}, u32[]{:S(2)}) collective-permute-start(f32[64,1024]{1,0:T(8,128)S(1)} %get-tuple-element.83), channel_id=1, source_target_pairs={{0,1},{1,0},{2,3},{3,2},{4,5},{5,4},{6,7},{7,6},{8,9},{9,8},{10,11... | collective-permute-start | bytes 786440 | tf_op jit(solution)/shard_map/ppermute | solution.py:441
  16.7 7.3 %hist.1 = f32[64,256]{1,0:T(8,128)S(1)} custom-call(f32[16,8,128]{2,1,0:T(8,128)S(1)} %pad_maximum_fusion.1.hess_ref, bf16[16,8192]{1,0:T(8,128)(2,1)S(1)} %get-tuple-element.74.refs_0_, bf16[16,8192]{1,0:T(8,128)(2,1)S(1)} %get-tuple-element.75.refs_1_, bf16[16,8192]{1,0:T(8,128)(2,1)S(1)} %get-tuple-element.76.refs_2_, ...), custom_call_target="tpu_custom_call" | custom-call | flops 4000000000 | bytes 10000000 | tf_op jit(solution)/shard_map/hist/pallas_call | solution.py:258
  24.1 0.0 collective-permute-done.3.refs_5_
  24.1 5.5 %collective-permute-start.5 = (f32[64,256]{1,0:T(8,128)S(1)}, f32[64,256]{1,0:T(8,128)S(1)}, u32[]{:S(2)}, u32[]{:S(2)}) collective-permute-start(f32[64,256]{1,0:T(8,128)S(1)} %hist.1), channel_id=1, source_target_pairs={{0,56},{8,0},{16,8},{24,16},{32,24},{40,32},{48,40},{56,48},{64,12... | collective-permute-start | bytes 196616 | tf_op jit(solution)/shard_map/ppermute | solution.py:449
  29.6 0.0 collective-permute-start.4
  29.6 1.3 %collective-permute-done.5 = f32[64,256]{1,0:T(8,128)S(1)} collective-permute-done((f32[64,256]{1,0:T(8,128)S(1)}, f32[64,256]{1,0:T(8,128)S(1)}, u32[]{:S(2)}, u32[]{:S(2)}) %collective-permute-start.5) | collective-permute-done | bytes 65568 | tf_op jit(solution)/shard_map/ppermute | solution.py:449
  30.9 3.0 %collective-permute-done.4 = f32[64,256]{1,0:T(8,128)S(1)} collective-permute-done((f32[64,256]{1,0:T(8,128)S(1)}, f32[64,256]{1,0:T(8,128)S(1)}, u32[]{:S(2)}, u32[]{:S(2)}) %collective-permute-start.4) | collective-permute-done | bytes 65568 | tf_op jit(solution)/shard_map/ppermute | solution.py:449
  33.9 0.3 collective-permute-start.7
  34.2 2.6 %collective-permute-start.6 = (f32[64,256]{1,0:T(8,128)S(1)}, f32[64,256]{1,0:T(8,128)S(1)}, u32[]{:S(2)}, u32[]{:S(2)}) collective-permute-start(f32[64,256]{1,0:T(8,128)S(1)} %get-tuple-element.117), channel_id=1, source_target_pairs={{0,40},{8,48},{16,56},{24,0},{32,8},{40,16},{48,24},{56,32},{64,10... | collective-permute-start | bytes 196616 | tf_op jit(solution)/shard_map/ppermute | solution.py:449
  36.8 1.3 %collective-permute-start.11 = (f32[64,1024]{1,0:T(8,128)S(1)}, f32[64,1024]{1,0:T(8,128)S(1)}, u32[]{:S(2)}, u32[]{:S(2)}) collective-permute-start(f32[64,1024]{1,0:T(8,128)S(1)} %get-tuple-element.85), channel_id=1, source_target_pairs={{0,4},{1,5},{2,6},{3,7},{4,0},{5,1},{6,2},{7,3},{8,12},{9,13},{10,... | collective-permute-start | bytes 786440 | tf_op jit(solution)/shard_map/ppermute | solution.py:441
  38.2 3.2 %collective-permute-start.12 = (f32[64,1024]{1,0:T(8,128)S(1)}, f32[64,1024]{1,0:T(8,128)S(1)}, u32[]{:S(2)}, u32[]{:S(2)}) collective-permute-start(f32[64,1024]{1,0:T(8,128)S(1)} %get-tuple-element.86), channel_id=1, source_target_pairs={{0,5},{1,4},{2,7},{3,6},{4,1},{5,0},{6,3},{7,2},{8,13},{9,12},{10,... | collective-permute-start | bytes 786440 | tf_op jit(solution)/shard_map/ppermute | solution.py:441
  41.4 0.0 collective-permute-done.7
  41.4 0.0 collective-permute-done.6
  41.4 2.5 %collective-permute-start.10 = (f32[64,256]{1,0:T(8,128)S(1)}, f32[64,256]{1,0:T(8,128)S(1)}, u32[]{:S(2)}, u32[]{:S(2)}) collective-permute-start(f32[64,256]{1,0:T(8,128)S(1)} %add_add_fusion.refs_0_), channel_id=1, source_target_pairs={{0,192},{8,200},{16,208},{24,216},{32,224},{40,232},{48,240},{56,2... | collective-permute-start | bytes 196616 | tf_op jit(solution)/shard_map/ppermute | solution.py:453
  43.9 0.5 collective-permute-start.9
  44.5 0.6 collective-permute-start.8
  45.1 0.2 collective-permute-done.10.refs_3_
  45.3 3.6 %collective-permute-done.9.refs_2_ = f32[64,256]{1,0:T(8,128)S(1)} collective-permute-done((f32[64,256]{1,0:T(8,128)S(1)}, f32[64,256]{1,0:T(8,128)S(1)}, u32[]{:S(2)}, u32[]{:S(2)}) %collective-permute-start.9) | collective-permute-done | bytes 65568 | tf_op jit(solution)/shard_map/ppermute | solution.py:453
  48.8 0.7 collective-permute-done.8.refs_1_
  49.5 1.4 %cuts.1.refs_0_ = f32[64,256]{1,0:T(8,128)S(1)} custom-call(s32[64,256]{1,0:T(8,128)S(1)} %copy-done.1, s32[64,256]{1,0:T(8,128)S(1)} %copy-done.2, f32[64,256]{1,0:T(8,128)S(1)} %add_add_fusion.refs_0_, f32[64,256]{1,0:T(8,128)S(1)} %collective-permute-done.8.refs_1_, f32[64,256]{1,0:T(8,128)S(1)} %collective-permute-done.9.refs_2_, ...), custom_call_target="tpu_custom_call" | custom-call | tf_op jit(solution)/shard_map/cuts/pallas_call | solution.py:312
  50.9 0.0 collective-permute-done.11.refs_3_
  50.9 1.1 %collective-permute-done.12.refs_4_ = f32[64,1024]{1,0:T(8,128)S(1)} collective-permute-done((f32[64,1024]{1,0:T(8,128)S(1)}, f32[64,1024]{1,0:T(8,128)S(1)}, u32[]{:S(2)}, u32[]{:S(2)}) %collective-permute-start.12) | collective-permute-done | bytes 262176 | tf_op jit(solution)/shard_map/ppermute | solution.py:441
  52.0 1.3 %collective-permute-start.13 = (f32[64,256]{1,0:T(8,128)S(1)}, f32[64,256]{1,0:T(8,128)S(1)}, u32[]{:S(2)}, u32[]{:S(2)}) collective-permute-start(f32[64,256]{1,0:T(8,128)S(1)} %cuts.1.refs_0_), channel_id=1, source_target_pairs={{0,4},{1,5},{2,6},{3,7},{4,0},{5,1},{6,2},{7,3},{8,12},{9,13},{10,... | collective-permute-start | bytes 196616 | tf_op jit(solution)/shard_map/ppermute | solution.py:441
  53.3 1.4 %place.5 = f32[64,1024]{1,0:T(8,128)S(1)} custom-call(f32[64,256]{1,0:T(8,128)S(1)} %cuts.1.refs_0_, f32[64,8192]{1,0:T(8,128)S(1)} %copy-done), custom_call_target="tpu_custom_call" | custom-call | flops 100000 | bytes 10000 | tf_op jit(solution)/shard_map/place/pallas_call | solution.py:380
  54.7 1.4 %place.6 = f32[64,1024]{1,0:T(8,128)S(1)} custom-call(f32[64,256]{1,0:T(8,128)S(1)} %cuts.1.refs_0_, f32[64,8192]{1,0:T(8,128)S(1)} %copy-done), custom_call_target="tpu_custom_call" | custom-call | flops 100000 | bytes 10000 | tf_op jit(solution)/shard_map/place/pallas_call | solution.py:380
  56.1 0.5 collective-permute-done.13.refs_0_
  56.6 2.4 %collective-permute-start.18 = (f32[128,256]{1,0:T(8,128)S(1)}, f32[128,256]{1,0:T(8,128)S(1)}, u32[]{:S(2)}, u32[]{:S(2)}) collective-permute-start(f32[128,256]{1,0:T(8,128)S(1)} %pad_maximum_fusion), channel_id=1, source_target_pairs={{0,1},{1,0},{2,3},{3,2},{4,5},{5,4},{6,7},{7,6},{8,9},{9,8},{10,11... | collective-permute-start | bytes 393224 | tf_op jit(solution)/shard_map/ppermute | solution.py:441
  59.1 0.4 collective-permute-start.14
  59.5 2.3 %collective-permute-start.15 = (f32[64,1024]{1,0:T(8,128)S(1)}, f32[64,1024]{1,0:T(8,128)S(1)}, u32[]{:S(2)}, u32[]{:S(2)}) collective-permute-start(f32[64,1024]{1,0:T(8,128)S(1)} %place.6), channel_id=1, source_target_pairs={{0,6},{1,7},{2,0},{3,1},{4,2},{5,3},{6,4},{7,5},{8,14},{9,15},{10,... | collective-permute-start | bytes 786440 | tf_op jit(solution)/shard_map/ppermute | solution.py:441
  61.8 1.4 %place.7 = f32[64,1024]{1,0:T(8,128)S(1)} custom-call(f32[64,256]{1,0:T(8,128)S(1)} %cuts.1.refs_0_, f32[64,8192]{1,0:T(8,128)S(1)} %copy-done), custom_call_target="tpu_custom_call" | custom-call | flops 100000 | bytes 10000 | tf_op jit(solution)/shard_map/place/pallas_call | solution.py:380
  63.2 0.3 collective-permute-start.16
  63.5 1.4 %place.8 = f32[64,1024]{1,0:T(8,128)S(1)} custom-call(f32[64,256]{1,0:T(8,128)S(1)} %cuts.1.refs_0_, f32[64,8192]{1,0:T(8,128)S(1)} %copy-done), custom_call_target="tpu_custom_call" | custom-call | flops 100000 | bytes 10000 | tf_op jit(solution)/shard_map/place/pallas_call | solution.py:380
  64.9 3.0 %collective-permute-start.17 = (f32[64,1024]{1,0:T(8,128)S(1)}, f32[64,1024]{1,0:T(8,128)S(1)}, u32[]{:S(2)}, u32[]{:S(2)}) collective-permute-start(f32[64,1024]{1,0:T(8,128)S(1)} %place.8), channel_id=1, source_target_pairs={{0,7},{1,6},{2,1},{3,0},{4,3},{5,2},{6,5},{7,4},{8,15},{9,14},{10,... | collective-permute-start | bytes 786440 | tf_op jit(solution)/shard_map/ppermute | solution.py:441
  67.9 0.2 collective-permute-done.14.refs_0_
  68.1 1.4 %place.9.refs_4_ = f32[64,1024]{1,0:T(8,128)S(1)} custom-call(f32[64,256]{1,0:T(8,128)S(1)} %cuts.1.refs_0_, f32[64,8192]{1,0:T(8,128)S(1)} %copy-done), custom_call_target="tpu_custom_call" | custom-call | flops 100000 | bytes 10000 | tf_op jit(solution)/shard_map/place/pallas_call | solution.py:380
  69.6 0.0 collective-permute-done.15.refs_1_
  69.6 4.4 %collective-permute-done.16.refs_2_ = f32[64,1024]{1,0:T(8,128)S(1)} collective-permute-done((f32[64,1024]{1,0:T(8,128)S(1)}, f32[64,1024]{1,0:T(8,128)S(1)}, u32[]{:S(2)}, u32[]{:S(2)}) %collective-permute-start.16) | collective-permute-done | bytes 262176 | tf_op jit(solution)/shard_map/ppermute | solution.py:441
  73.9 4.1 %far.1 = (f32[64,1024]{1,0:T(8,128)S(1)}, f32[64,1024]{1,0:T(8,128)S(1)}, f32[64,1024]{1,0:T(8,128)S(1)}) custom-call(f32[64,256]{1,0:T(8,128)S(1)} %collective-permute-done.13.refs_0_, f32[64,256]{1,0:T(8,128)S(1)} %get-tuple-element.120.refs_1_, f32[64,256]{1,0:T(8,128)S(1)} %get-tuple-element.119.refs_2_, f32[64,1024]{1,0:T(8,128)S(1)} %collective-permute-done.11.refs_3_, ...), custom_call_target="tpu_custom_call" | custom-call | flops 100000 | bytes 10000 | tf_op jit(solution)/shard_map/far/pallas_call | solution.py:398
  78.0 1.4 %join.1 = f32[512,1024]{1,0:T(8,128)} custom-call(f32[64,1024]{1,0:T(8,128)S(1)} %collective-permute-done.14.refs_0_, f32[64,1024]{1,0:T(8,128)S(1)} %collective-permute-done.15.refs_1_, f32[64,1024]{1,0:T(8,128)S(1)} %collective-permute-done.16.refs_2_, f32[64,1024]{1,0:T(8,128)S(1)} %collective-permute-done.17.refs_3_, f32[64,1024]{1,0:T(8,128)S(1)} %place.9.refs_4_, ...), custom_call_target="tpu_custom_call" | custom-call | tf_op jit(solution)/shard_map/join/pallas_call | solution.py:424
  (16 shorter events, 0.1 us)
Async XLA Ops:
  0.0 7.6 %copy-start = (f32[64,8192]{1,0:T(8,128)S(1)}, f32[64,8192]{1,0:T(8,128)}, u32[]{:S(2)}) copy-start(f32[64,8192]{1,0:T(8,128)} %refs_1_.15) | copy-start | bytes 6291460
  0.0 7.6 %copy-start.1 = (s32[64,256]{1,0:T(8,128)S(1)}, s32[64,256]{1,0:T(8,128)}, u32[]{:S(2)}) copy-start(s32[64,256]{1,0:T(8,128)} %codes_ref.1) | copy-start | bytes 196612
  1.0 6.4 %collective-permute-start = (f32[2,8,128]{2,1,0:T(8,128)S(1)}, f32[2,8,128]{2,1,0:T(8,128)S(1)}, u32[]{:S(2)}, u32[]{:S(2)}) collective-permute-start(f32[2,8,128]{2,1,0:T(8,128)S(1)} %factor.1), channel_id=1, source_target_pairs={{0,1},{1,0},{2,3},{3,2},{4,5},{5,4},{6,7},{7,6},{8,9},{9,8},{10,11... | collective-permute-start | bytes 24584 | tf_op jit(solution)/shard_map/ppermute | solution.py:445
  7.5 2.7 %collective-permute-start.1 = (f32[4,8,128]{2,1,0:T(8,128)S(1)}, f32[4,8,128]{2,1,0:T(8,128)S(1)}, u32[]{:S(2)}, u32[]{:S(2)}) collective-permute-start(f32[4,8,128]{2,1,0:T(8,128)S(1)} %pad_maximum_fusion.3), channel_id=1, source_target_pairs={{0,2},{1,3},{2,0},{3,1},{4,6},{5,7},{6,4},{7,5},{8,10},{9,11},{10,... | collective-permute-start | bytes 49160 | tf_op jit(solution)/shard_map/ppermute | solution.py:445
  10.1 5.3 %collective-permute-start.2 = (f32[8,8,128]{2,1,0:T(8,128)S(1)}, f32[8,8,128]{2,1,0:T(8,128)S(1)}, u32[]{:S(2)}, u32[]{:S(2)}) collective-permute-start(f32[8,8,128]{2,1,0:T(8,128)S(1)} %pad_maximum_fusion.2), channel_id=1, source_target_pairs={{0,4},{1,5},{2,6},{3,7},{4,0},{5,1},{6,2},{7,3},{8,12},{9,13},{10,... | collective-permute-start | bytes 98312 | tf_op jit(solution)/shard_map/ppermute | solution.py:445
  15.4 8.6 %collective-permute-start.3 = (f32[64,1024]{1,0:T(8,128)S(1)}, f32[64,1024]{1,0:T(8,128)S(1)}, u32[]{:S(2)}, u32[]{:S(2)}) collective-permute-start(f32[64,1024]{1,0:T(8,128)S(1)} %get-tuple-element.83), channel_id=1, source_target_pairs={{0,1},{1,0},{2,3},{3,2},{4,5},{5,4},{6,7},{7,6},{8,9},{9,8},{10,11... | collective-permute-start | bytes 786440 | tf_op jit(solution)/shard_map/ppermute | solution.py:441
  16.7 32.8 %copy-start.2 = (s32[64,256]{1,0:T(8,128)S(1)}, s32[64,256]{1,0:T(8,128)}, u32[]{:S(2)}) copy-start(s32[64,256]{1,0:T(8,128)} %ranks_ref.1) | copy-start | bytes 196612
  24.1 6.8 %collective-permute-start.5 = (f32[64,256]{1,0:T(8,128)S(1)}, f32[64,256]{1,0:T(8,128)S(1)}, u32[]{:S(2)}, u32[]{:S(2)}) collective-permute-start(f32[64,256]{1,0:T(8,128)S(1)} %hist.1), channel_id=1, source_target_pairs={{0,56},{8,0},{16,8},{24,16},{32,24},{40,32},{48,40},{56,48},{64,12... | collective-permute-start | bytes 196616 | tf_op jit(solution)/shard_map/ppermute | solution.py:449
  29.6 4.3 %collective-permute-start.4 = (f32[64,256]{1,0:T(8,128)S(1)}, f32[64,256]{1,0:T(8,128)S(1)}, u32[]{:S(2)}, u32[]{:S(2)}) collective-permute-start(f32[64,256]{1,0:T(8,128)S(1)} %hist.1), channel_id=1, source_target_pairs={{0,8},{8,16},{16,24},{24,32},{32,40},{40,48},{48,56},{56,0},{64,72... | collective-permute-start | bytes 196616 | tf_op jit(solution)/shard_map/ppermute | solution.py:449
  33.9 7.4 %collective-permute-start.7 = (f32[64,256]{1,0:T(8,128)S(1)}, f32[64,256]{1,0:T(8,128)S(1)}, u32[]{:S(2)}, u32[]{:S(2)}) collective-permute-start(f32[64,256]{1,0:T(8,128)S(1)} %get-tuple-element.118), channel_id=1, source_target_pairs={{0,16},{8,24},{16,32},{24,40},{32,48},{40,56},{48,0},{56,8},{64,80... | collective-permute-start | bytes 196616 | tf_op jit(solution)/shard_map/ppermute | solution.py:449
  34.2 7.2 %collective-permute-start.6 = (f32[64,256]{1,0:T(8,128)S(1)}, f32[64,256]{1,0:T(8,128)S(1)}, u32[]{:S(2)}, u32[]{:S(2)}) collective-permute-start(f32[64,256]{1,0:T(8,128)S(1)} %get-tuple-element.117), channel_id=1, source_target_pairs={{0,40},{8,48},{16,56},{24,0},{32,8},{40,16},{48,24},{56,32},{64,10... | collective-permute-start | bytes 196616 | tf_op jit(solution)/shard_map/ppermute | solution.py:449
  36.8 14.1 %collective-permute-start.11 = (f32[64,1024]{1,0:T(8,128)S(1)}, f32[64,1024]{1,0:T(8,128)S(1)}, u32[]{:S(2)}, u32[]{:S(2)}) collective-permute-start(f32[64,1024]{1,0:T(8,128)S(1)} %get-tuple-element.85), channel_id=1, source_target_pairs={{0,4},{1,5},{2,6},{3,7},{4,0},{5,1},{6,2},{7,3},{8,12},{9,13},{10,... | collective-permute-start | bytes 786440 | tf_op jit(solution)/shard_map/ppermute | solution.py:441
  38.2 13.8 %collective-permute-start.12 = (f32[64,1024]{1,0:T(8,128)S(1)}, f32[64,1024]{1,0:T(8,128)S(1)}, u32[]{:S(2)}, u32[]{:S(2)}) collective-permute-start(f32[64,1024]{1,0:T(8,128)S(1)} %get-tuple-element.86), channel_id=1, source_target_pairs={{0,5},{1,4},{2,7},{3,6},{4,1},{5,0},{6,3},{7,2},{8,13},{9,12},{10,... | collective-permute-start | bytes 786440 | tf_op jit(solution)/shard_map/ppermute | solution.py:441
  41.4 3.9 %collective-permute-start.10 = (f32[64,256]{1,0:T(8,128)S(1)}, f32[64,256]{1,0:T(8,128)S(1)}, u32[]{:S(2)}, u32[]{:S(2)}) collective-permute-start(f32[64,256]{1,0:T(8,128)S(1)} %add_add_fusion.refs_0_), channel_id=1, source_target_pairs={{0,192},{8,200},{16,208},{24,216},{32,224},{40,232},{48,240},{56,2... | collective-permute-start | bytes 196616 | tf_op jit(solution)/shard_map/ppermute | solution.py:453
  43.9 4.9 %collective-permute-start.9 = (f32[64,256]{1,0:T(8,128)S(1)}, f32[64,256]{1,0:T(8,128)S(1)}, u32[]{:S(2)}, u32[]{:S(2)}) collective-permute-start(f32[64,256]{1,0:T(8,128)S(1)} %add_add_fusion.refs_0_), channel_id=1, source_target_pairs={{0,128},{8,136},{16,144},{24,152},{32,160},{40,168},{48,176},{56,1... | collective-permute-start | bytes 196616 | tf_op jit(solution)/shard_map/ppermute | solution.py:453
  44.5 5.1 %collective-permute-start.8 = (f32[64,256]{1,0:T(8,128)S(1)}, f32[64,256]{1,0:T(8,128)S(1)}, u32[]{:S(2)}, u32[]{:S(2)}) collective-permute-start(f32[64,256]{1,0:T(8,128)S(1)} %add_add_fusion.refs_0_), channel_id=1, source_target_pairs={{0,64},{8,72},{16,80},{24,88},{32,96},{40,104},{48,112},{56,120},{... | collective-permute-start | bytes 196616 | tf_op jit(solution)/shard_map/ppermute | solution.py:453
  52.0 4.6 %collective-permute-start.13 = (f32[64,256]{1,0:T(8,128)S(1)}, f32[64,256]{1,0:T(8,128)S(1)}, u32[]{:S(2)}, u32[]{:S(2)}) collective-permute-start(f32[64,256]{1,0:T(8,128)S(1)} %cuts.1.refs_0_), channel_id=1, source_target_pairs={{0,4},{1,5},{2,6},{3,7},{4,0},{5,1},{6,2},{7,3},{8,12},{9,13},{10,... | collective-permute-start | bytes 196616 | tf_op jit(solution)/shard_map/ppermute | solution.py:441
  56.6 11.3 %collective-permute-start.18 = (f32[128,256]{1,0:T(8,128)S(1)}, f32[128,256]{1,0:T(8,128)S(1)}, u32[]{:S(2)}, u32[]{:S(2)}) collective-permute-start(f32[128,256]{1,0:T(8,128)S(1)} %pad_maximum_fusion), channel_id=1, source_target_pairs={{0,1},{1,0},{2,3},{3,2},{4,5},{5,4},{6,7},{7,6},{8,9},{9,8},{10,11... | collective-permute-start | bytes 393224 | tf_op jit(solution)/shard_map/ppermute | solution.py:441
  59.1 9.1 %collective-permute-start.14 = (f32[64,1024]{1,0:T(8,128)S(1)}, f32[64,1024]{1,0:T(8,128)S(1)}, u32[]{:S(2)}, u32[]{:S(2)}) collective-permute-start(f32[64,1024]{1,0:T(8,128)S(1)} %place.5), channel_id=1, source_target_pairs={{0,2},{1,3},{2,4},{3,5},{4,6},{5,7},{6,0},{7,1},{8,10},{9,11},{10,... | collective-permute-start | bytes 786440 | tf_op jit(solution)/shard_map/ppermute | solution.py:441
  59.5 10.1 %collective-permute-start.15 = (f32[64,1024]{1,0:T(8,128)S(1)}, f32[64,1024]{1,0:T(8,128)S(1)}, u32[]{:S(2)}, u32[]{:S(2)}) collective-permute-start(f32[64,1024]{1,0:T(8,128)S(1)} %place.6), channel_id=1, source_target_pairs={{0,6},{1,7},{2,0},{3,1},{4,2},{5,3},{6,4},{7,5},{8,14},{9,15},{10,... | collective-permute-start | bytes 786440 | tf_op jit(solution)/shard_map/ppermute | solution.py:441
  63.2 10.8 %collective-permute-start.16 = (f32[64,1024]{1,0:T(8,128)S(1)}, f32[64,1024]{1,0:T(8,128)S(1)}, u32[]{:S(2)}, u32[]{:S(2)}) collective-permute-start(f32[64,1024]{1,0:T(8,128)S(1)} %place.7), channel_id=1, source_target_pairs={{0,3},{1,2},{2,5},{3,4},{4,7},{5,6},{6,1},{7,0},{8,11},{9,10},{10,... | collective-permute-start | bytes 786440 | tf_op jit(solution)/shard_map/ppermute | solution.py:441
  64.9 13.1 %collective-permute-start.17 = (f32[64,1024]{1,0:T(8,128)S(1)}, f32[64,1024]{1,0:T(8,128)S(1)}, u32[]{:S(2)}, u32[]{:S(2)}) collective-permute-start(f32[64,1024]{1,0:T(8,128)S(1)} %place.8), channel_id=1, source_target_pairs={{0,7},{1,6},{2,1},{3,0},{4,3},{5,2},{6,5},{7,4},{8,15},{9,14},{10,... | collective-permute-start | bytes 786440 | tf_op jit(solution)/shard_map/ppermute | solution.py:441
